TPU v7x, 32 devices: a whole 2x2x4 slice. The times are simulated.
32 devices in a mesh: ctx: 8 (over z, core), fsdp: 4 (over y, x).
Axes of the slice: x: 2, y: 2, z: 4, core: 2. Of those that a mesh axis runs over, the one named last changes fastest.
Arguments:
- inputs: bfloat16 [4, 2048, 1024], P('fsdp', 'ctx'), may hold values from -6 to 6
- encoder: bfloat16 [4, 512, 1024], P('fsdp', 'ctx'), may hold values from -6 to 6
- teacher: bfloat16 [4, 2048, 1024], P('fsdp', 'ctx'), may hold values from -6 to 6
- valid_mask: int32 [4, 2048], P('fsdp', 'ctx'), may hold values from 0 to 1, as said below
- doc_ids: int32 [4, 2048], P('fsdp'), may hold values from 0 to 2, never falling along the last dimension, each value on 1 to 1024 neighbouring positions
- block_order: int32 [16], replicated, may hold values from 0 to 15, as said below
- buckets: int32 [4096], replicated, may hold values from 0 to 31, as said below
- gain_self: bfloat16 [1024], P('fsdp'), may hold values from 0.5 to 1.5
- w_query: bfloat16 [1024, 1024], P('fsdp'), may hold values from -0.078125 to 0.078125
- w_key: bfloat16 [1024, 512], P('fsdp'), may hold values from -0.078125 to 0.078125
- w_value: bfloat16 [1024, 512], P('fsdp'), may hold values from -0.1875 to 0.1875
- w_out: bfloat16 [1024, 1024], P('fsdp'), may hold values from -1.5 to 1.5
- gain_cross: bfloat16 [1024], P('fsdp'), may hold values from 0.5 to 1.5
- c_query: bfloat16 [1024, 1024], P('fsdp'), may hold values from -0.078125 to 0.078125
- c_key: bfloat16 [1024, 512], P('fsdp'), may hold values from -0.078125 to 0.078125
- c_value: bfloat16 [1024, 512], P('fsdp'), may hold values from -0.1875 to 0.1875
- c_out: bfloat16 [1024, 1024], P('fsdp'), may hold values from -0.75 to 0.75
- gain_ffn: bfloat16 [1024], P('fsdp'), may hold values from 0.5 to 1.5
- w_gate: bfloat16 [1024, 2816], P('fsdp'), may hold values from -0.1875 to 0.1875
- w_up: bfloat16 [1024, 2816], P('fsdp'), may hold values from -0.1875 to 0.1875
- w_down: bfloat16 [2816, 1024], P('fsdp'), may hold values from -0.109375 to 0.109375
- bias_table: bfloat16 [32, 16], P('fsdp'), may hold values from -4 to 4
Outputs:
- layer_out: bfloat16 [4, 2048, 1024], P('fsdp', 'ctx')
- loss: float32 [], replicated
- grad_inputs: float32 [4, 2048, 1024], P('fsdp', 'ctx')
- grad_encoder: float32 [4, 512, 1024], P('fsdp', 'ctx')
- grad_gain_self: float32 [1024], P('fsdp')
- grad_w_query: float32 [1024, 1024], P('fsdp')
- grad_w_key: float32 [1024, 512], P('fsdp')
- grad_w_value: float32 [1024, 512], P('fsdp')
- grad_w_out: float32 [1024, 1024], P('fsdp')
- grad_gain_cross: float32 [1024], P('fsdp')
- grad_c_query: float32 [1024, 1024], P('fsdp')
- grad_c_key: float32 [1024, 512], P('fsdp')
- grad_c_value: float32 [1024, 512], P('fsdp')
- grad_c_out: float32 [1024, 1024], P('fsdp')
- grad_gain_ffn: float32 [1024], P('fsdp')
- grad_w_gate: float32 [1024, 2816], P('fsdp')
- grad_w_up: float32 [1024, 2816], P('fsdp')
- grad_w_down: float32 [2816, 1024], P('fsdp')
- grad_bias_table: float32 [32, 16], P('fsdp')
Inputs may be any that keep to these rules, and one draw needn't show every extreme that they name: `valid_mask`: 1 marks a token whose teacher state counts. `block_order`: a permutation in which stored blocks 2 c and 2 c + 1, those of index c of ctx, hold natural blocks b and 15 - b for some b. `buckets`: entry 2048 + d is the bucket of the offset d from a query's position to a key's, for all offsets of one sequence; all offsets of one sign with |d| of 128 or more share one bucket; entry 0 is unused.
All inputs are finite; a program needn't handle non-finite values.
Results may differ from a plain program's by a relative error of at most 0.028.
Values may be sent and summed in bfloat16 or wider, within the bound.
No kernel may reach another device: no remote copies, remote signals or barrier semaphores. Data moves between devices by JAX's collectives and lax.ppermute only.
A program may use at most 256 MiB of HBM per device.

v0:
```python
import jax
import jax.numpy as jnp
from jax import lax
from jax.sharding import PartitionSpec as P

D = 1024
HEADS = 16
KV_HEADS = 8
HEAD = 64
BUCKETS = 32
BLOCK = 128


EPS = 1e-06
NEGATIVE = -1e30


def matmul(left, right):
    return jnp.dot(left, right, preferred_element_type=jnp.float32)


def left_matmul(left, right):
    return lax.dot_general(
        left, right, (((0,), (0,)), ((), ())), preferred_element_type=jnp.float32
    )


def right_matmul(left, right):
    return lax.dot_general(
        left, right, (((1,), (1,)), ((), ())), preferred_element_type=jnp.float32
    )


def norm_rows(values, gain):
    scale = lax.rsqrt(jnp.mean(values * values, axis=-1, keepdims=True) + EPS)
    normed = values * scale
    return (normed, scale, (normed * gain).astype(jnp.bfloat16))


def norm_back(grad_out, normed, scale, gain):
    grad_gain = jnp.sum(grad_out * normed, axis=0)
    inner = grad_out * gain
    grad_in = scale * (inner - normed * jnp.mean(inner * normed, axis=-1, keepdims=True))
    return (grad_in, grad_gain)


def gelu_tanh(value):
    return jax.nn.gelu(value, approximate=True)


def natural_blocks(block_order, first_slot, count):
    slots = first_slot + jnp.arange(count, dtype=jnp.int32)
    table = jnp.arange(block_order.shape[0], dtype=jnp.int32)
    match = slots[:, None] == table[None, :]
    return jnp.sum(jnp.where(match, block_order[None, :], 0), axis=1)


def block_docs(doc_ids, blocks, block):
    parts = [
        lax.dynamic_slice_in_dim(doc_ids, blocks[index] * block, block, axis=1)
        for index in range(blocks.shape[0])
    ]
    return jnp.concatenate(parts, axis=1)


def toeplitz(vectors, block):
    lead = vectors.shape[:-1]
    padded = jnp.concatenate([vectors, jnp.zeros(lead + (1,), vectors.dtype)], axis=-1)
    tiled = jnp.tile(padded, (1,) * len(lead) + (block,))
    flat = tiled[..., block - 1 : block - 1 + block * (2 * block - 1)]
    return flat.reshape(lead + (block, 2 * block - 1))[..., :block]


def diagonal_sums(grid, block):
    lead = grid.shape[:-2]
    flipped = jnp.flip(grid, axis=-2)
    padded = jnp.concatenate([flipped, jnp.zeros(lead + (block, block), grid.dtype)], axis=-1)
    flat = padded.reshape(lead + (2 * block * block,))[..., : block * (2 * block - 1)]
    return jnp.sum(flat.reshape(lead + (block, 2 * block - 1)), axis=-2)


def tile_bias(distance, query_blocks, key_blocks, block):
    half = distance.shape[1] // 2
    offsets = (key_blocks[None, :] - query_blocks[:, None]) * block + half - (block - 1)

    def cut(offset):
        return lax.dynamic_slice_in_dim(distance, offset, 2 * block - 1, axis=1)

    vectors = jax.vmap(jax.vmap(cut))(offsets)
    grid = toeplitz(vectors, block)
    heads = distance.shape[0]
    return grid.transpose(2, 0, 3, 1, 4).reshape(
        heads, query_blocks.shape[0] * block, key_blocks.shape[0] * block
    )


def bias_grad(grad_bias, grad_score, query_blocks, key_blocks, block):
    heads = grad_bias.shape[0]
    half = grad_bias.shape[1] // 2
    query_count = query_blocks.shape[0]
    key_count = key_blocks.shape[0]
    summed = jnp.sum(grad_score, axis=0, dtype=jnp.float32).reshape(
        heads, query_count, block, key_count, block
    )
    sums = diagonal_sums(summed.transpose(1, 3, 0, 2, 4), block)
    for first in range(query_count):
        for second in range(key_count):
            offset = (key_blocks[second] - query_blocks[first]) * block + half - (block - 1)
            current = lax.dynamic_slice_in_dim(grad_bias, offset, 2 * block - 1, axis=1)
            grad_bias = lax.dynamic_update_slice_in_dim(
                grad_bias, current + sums[first, second], offset, axis=1
            )
    return grad_bias


def over_pieces(step_fn, carry, piece, width):
    count = piece.shape[1] // width
    parts = jnp.moveaxis(piece.reshape((piece.shape[0], count, width) + piece.shape[2:]), 1, 0)

    def advance(state, item):
        part, index = item
        return (step_fn(state, part, index * width), None)

    result, unused = lax.scan(advance, carry, (parts, jnp.arange(count, dtype=jnp.int32)))
    return result


def fetch_weights(parts):
    return (
        lax.all_gather(parts[0], "fsdp", axis=0, tiled=True),
        lax.all_gather(parts[1], "fsdp", axis=0, tiled=True),
        lax.all_gather(parts[2], "fsdp", axis=0, tiled=True),
        lax.all_gather(parts[3], "fsdp", axis=0, tiled=True),
        lax.all_gather(parts[4], "fsdp", axis=0, tiled=True),
        lax.all_gather(parts[5], "fsdp", axis=0, tiled=True),
        lax.all_gather(parts[6], "fsdp", axis=0, tiled=True),
        lax.all_gather(parts[7], "fsdp", axis=0, tiled=True),
        lax.all_gather(parts[8], "fsdp", axis=0, tiled=True),
        lax.all_gather(parts[9], "fsdp", axis=0, tiled=True),
        lax.all_gather(parts[10], "fsdp", axis=0, tiled=True),
        lax.all_gather(parts[11], "fsdp", axis=0, tiled=True),
        lax.all_gather(parts[12], "fsdp", axis=0, tiled=True),
        lax.all_gather(parts[13], "fsdp", axis=0, tiled=True),
        lax.all_gather(parts[14], "fsdp", axis=0, tiled=True),
    )


def pack_grads(grads, shards):
    return jnp.concatenate([grad.reshape(shards, -1) for grad in grads], axis=1)


def unpack_grads(flat, grads, shards):
    pieces = []
    offset = 0
    for grad in grads:
        amount = grad.size // shards
        shape = (grad.shape[0] // shards,) + grad.shape[1:]
        pieces.append(flat[offset : offset + amount].reshape(shape))
        offset = offset + amount
    return pieces


def body(
    inputs,
    encoder,
    teacher,
    valid_mask,
    doc_ids,
    block_order,
    buckets,
    gain_self,
    w_query,
    w_key,
    w_value,
    w_out,
    gain_cross,
    c_query,
    c_key,
    c_value,
    c_out,
    gain_ffn,
    w_gate,
    w_up,
    w_down,
    bias_table,
):
    sequences, rows, width = inputs.shape
    contexts = lax.axis_size("ctx")
    shards = lax.axis_size("fsdp")
    length = rows * contexts
    groups = HEADS // KV_HEADS
    key_width = KV_HEADS * HEAD
    head_width = HEADS * HEAD
    pair = rows // BLOCK
    token_total = sequences * length * shards
    local = (
        gain_self,
        w_query,
        w_key,
        w_value,
        w_out,
        gain_cross,
        c_query,
        c_key,
        c_value,
        c_out,
        gain_ffn,
        w_gate,
        w_up,
        w_down,
        bias_table,
    )
    query_blocks = lax.dynamic_slice_in_dim(block_order, lax.axis_index("ctx") * pair, pair)
    query_docs = block_docs(doc_ids, query_blocks, BLOCK)
    bucket_match = buckets[:, None] == jnp.arange(BUCKETS, dtype=jnp.int32)[None, :]
    (
        gain_one,
        query_weight,
        key_weight,
        value_weight,
        out_weight,
        gain_two,
        cross_query,
        cross_key,
        cross_value,
        cross_out,
        gain_three,
        gate_weight,
        up_weight,
        down_weight,
        table_whole,
    ) = fetch_weights(local)
    flat_in = inputs.reshape(sequences * rows, width).astype(jnp.float32)
    normed_one, scale_one, hidden_one = norm_rows(flat_in, gain_one.astype(jnp.float32))
    query = matmul(hidden_one, query_weight).astype(jnp.bfloat16)
    key_rows = matmul(hidden_one, key_weight).astype(jnp.bfloat16)
    value_rows = matmul(hidden_one, value_weight).astype(jnp.bfloat16)
    local_pairs = jnp.concatenate([key_rows, value_rows], axis=1).reshape(
        sequences, rows, 2 * key_width
    )
    query_tile = query.reshape(sequences, rows, KV_HEADS, groups, HEAD)
    distance = lax.dot_general(
        table_whole,
        bucket_match.astype(jnp.bfloat16),
        (((0,), (1,)), ((), ())),
        preferred_element_type=jnp.float32,
    )

    def tile_setup(piece, start):
        count = piece.shape[1]
        key_blocks = natural_blocks(block_order, start // BLOCK, count // BLOCK)
        key_docs = block_docs(doc_ids, key_blocks, BLOCK)
        keys = piece[..., :key_width].reshape(sequences, count, KV_HEADS, HEAD)
        values = piece[..., key_width:].reshape(sequences, count, KV_HEADS, HEAD)
        raw = jnp.einsum("sqgrd,skgd->sgrqk", query_tile, keys, preferred_element_type=jnp.float32)
        bias = tile_bias(distance, query_blocks, key_blocks, BLOCK).reshape(
            KV_HEADS, groups, rows, count
        )
        block_ok = key_blocks[None, :] <= query_blocks[:, None]
        block_ok = jnp.broadcast_to(
            block_ok[:, None, :, None], (pair, BLOCK, count // BLOCK, BLOCK)
        ).reshape(rows, count)
        allowed = (block_ok[None] & (query_docs[:, :, None] == key_docs[:, None, :]))[:, None, None]
        scores = jnp.where(allowed, raw + bias[None], NEGATIVE)
        return (keys, values, allowed, scores, key_blocks)

    def forward_tile(carry, piece, start):
        top, total, accum = carry
        keys, values, allowed, scores, key_blocks = tile_setup(piece, start)
        new_top = jnp.maximum(top, jnp.max(scores, axis=-1))
        factor = jnp.exp(top - new_top)
        weights = jnp.where(allowed, jnp.exp(scores - new_top[..., None]), 0.0)
        total = total * factor + jnp.sum(weights, axis=-1)
        update = jnp.einsum(
            "sgrqk,skgd->sgrqd",
            weights.astype(jnp.bfloat16),
            values,
            preferred_element_type=jnp.float32,
        )
        return (new_top, total, accum * factor[..., None] + update)

    start_state = (
        jnp.full((sequences, KV_HEADS, groups, rows), NEGATIVE, jnp.float32),
        jnp.zeros((sequences, KV_HEADS, groups, rows), jnp.float32),
        jnp.zeros((sequences, KV_HEADS, groups, rows, HEAD), jnp.float32),
    )
    top, total, accum = over_pieces(
        forward_tile, start_state, lax.all_gather(local_pairs, "ctx", axis=1, tiled=True), rows
    )
    attention = accum / total[..., None]
    log_total = top + jnp.log(total)
    attention_low = (
        attention.transpose(0, 3, 1, 2, 4)
        .reshape(sequences * rows, head_width)
        .astype(jnp.bfloat16)
    )
    mid_one = flat_in + matmul(attention_low, out_weight)
    normed_two, scale_two, hidden_two = norm_rows(mid_one, gain_two.astype(jnp.float32))
    cross_q = (
        matmul(hidden_two, cross_query)
        .astype(jnp.bfloat16)
        .reshape(sequences, rows, KV_HEADS, groups, HEAD)
    )
    encoder_local = encoder.shape[1]
    encoder_rows = encoder.reshape(sequences * encoder_local, width)
    encoder_pairs = (
        jnp.concatenate(
            [matmul(encoder_rows, cross_key), matmul(encoder_rows, cross_value)], axis=1
        )
        .astype(jnp.bfloat16)
        .reshape(sequences, encoder_local, 2 * key_width)
    )
    encoder_whole = lax.all_gather(encoder_pairs, "ctx", axis=1, tiled=True)
    encoder_count = encoder_whole.shape[1]
    encoder_keys = encoder_whole[..., :key_width].reshape(sequences, encoder_count, KV_HEADS, HEAD)
    encoder_values = encoder_whole[..., key_width:].reshape(
        sequences, encoder_count, KV_HEADS, HEAD
    )
    cross_raw = jnp.einsum(
        "sqgrd,skgd->sgrqk", cross_q, encoder_keys, preferred_element_type=jnp.float32
    )
    cross_top = jnp.max(cross_raw, axis=-1, keepdims=True)
    cross_exp = jnp.exp(cross_raw - cross_top)
    cross_total = jnp.sum(cross_exp, axis=-1, keepdims=True)
    cross_prob = cross_exp / cross_total
    cross_log = cross_top + jnp.log(cross_total)
    cross_rows = (
        jnp.einsum(
            "sgrqk,skgd->sqgrd",
            cross_prob.astype(jnp.bfloat16),
            encoder_values,
            preferred_element_type=jnp.float32,
        )
        .reshape(sequences * rows, head_width)
        .astype(jnp.bfloat16)
    )
    mid_two = mid_one + matmul(cross_rows, cross_out)
    normed_three, scale_three, hidden_three = norm_rows(mid_two, gain_three.astype(jnp.float32))
    gate = matmul(hidden_three, gate_weight)
    up = matmul(hidden_three, up_weight)
    active, gelu_pull = jax.vjp(gelu_tanh, gate)
    mixed = (active * up).astype(jnp.bfloat16)
    result = mid_two + matmul(mixed, down_weight)
    layer_out = result.reshape(sequences, rows, width).astype(jnp.bfloat16)
    target = teacher.reshape(sequences * rows, width).astype(jnp.float32)
    mask_rows = valid_mask.reshape(sequences * rows).astype(jnp.float32)
    diff = result - target
    squared_local = jnp.sum(mask_rows[:, None] * diff * diff)
    count_local = jnp.sum(mask_rows)
    squared, count = lax.psum((squared_local, count_local), ("ctx", "fsdp"))
    count = jnp.maximum(count, 1.0)
    loss = squared / (D * count)
    grad_result = token_total / count * mask_rows[:, None] * diff
    (
        gain_one,
        query_weight,
        key_weight,
        value_weight,
        out_weight,
        gain_two,
        cross_query,
        cross_key,
        cross_value,
        cross_out,
        gain_three,
        gate_weight,
        up_weight,
        down_weight,
        table_whole,
    ) = fetch_weights(local)
    grad_branch_three = grad_result.astype(jnp.bfloat16)
    grad_down = left_matmul(mixed, grad_branch_three)
    grad_mixed = right_matmul(grad_branch_three, down_weight)
    (gelu_slope,) = gelu_pull(grad_mixed * up)
    grad_gate = gelu_slope.astype(jnp.bfloat16)
    grad_up = (grad_mixed * active).astype(jnp.bfloat16)
    grad_gate_weight = left_matmul(hidden_three, grad_gate)
    grad_up_weight = left_matmul(hidden_three, grad_up)
    grad_hidden_three = right_matmul(grad_gate, gate_weight) + right_matmul(grad_up, up_weight)
    grad_norm_three, grad_gain_three = norm_back(
        grad_hidden_three, normed_three, scale_three, gain_three.astype(jnp.float32)
    )
    grad_mid_two = grad_result + grad_norm_three
    grad_branch_two = grad_mid_two.astype(jnp.bfloat16)
    grad_cross_out = left_matmul(cross_rows, grad_branch_two)
    grad_cross = (
        right_matmul(grad_branch_two, cross_out)
        .astype(jnp.bfloat16)
        .reshape(sequences, rows, KV_HEADS, groups, HEAD)
    )
    cross_again = jnp.einsum(
        "sqgrd,skgd->sgrqk", cross_q, encoder_keys, preferred_element_type=jnp.float32
    )
    cross_back = jnp.exp(cross_again - cross_log)
    cross_grad_prob = jnp.einsum(
        "sqgrd,skgd->sgrqk", grad_cross, encoder_values, preferred_element_type=jnp.float32
    )
    cross_delta = jnp.sum(cross_back * cross_grad_prob, axis=-1, keepdims=True)
    cross_grad_score = (cross_back * (cross_grad_prob - cross_delta)).astype(jnp.bfloat16)
    grad_cross_rows = (
        jnp.einsum(
            "sgrqk,skgd->sqgrd", cross_grad_score, encoder_keys, preferred_element_type=jnp.float32
        )
        .reshape(sequences * rows, head_width)
        .astype(jnp.bfloat16)
    )
    grad_encoder_keys = jnp.einsum(
        "sgrqk,sqgrd->skgd", cross_grad_score, cross_q, preferred_element_type=jnp.float32
    )
    grad_encoder_values = jnp.einsum(
        "sgrqk,sqgrd->skgd",
        cross_back.astype(jnp.bfloat16),
        grad_cross,
        preferred_element_type=jnp.float32,
    )
    encoder_grad = jnp.concatenate(
        [
            grad_encoder_keys.reshape(sequences, encoder_count, key_width),
            grad_encoder_values.reshape(sequences, encoder_count, key_width),
        ],
        axis=2,
    )
    encoder_mine = (
        lax.psum_scatter(encoder_grad.astype(jnp.bfloat16), "ctx", scatter_dimension=1, tiled=True)
        .astype(jnp.float32)
        .reshape(sequences * encoder_local, 2 * key_width)
        .astype(jnp.bfloat16)
    )
    grad_key_encoder = encoder_mine[:, :key_width]
    grad_value_encoder = encoder_mine[:, key_width:]
    grad_cross_key = left_matmul(encoder_rows, grad_key_encoder)
    grad_cross_value = left_matmul(encoder_rows, grad_value_encoder)
    grad_encoder = right_matmul(grad_key_encoder, cross_key) + right_matmul(
        grad_value_encoder, cross_value
    )
    grad_cross_query = left_matmul(hidden_two, grad_cross_rows)
    grad_hidden_two = right_matmul(grad_cross_rows, cross_query)
    grad_norm_two, grad_gain_two = norm_back(
        grad_hidden_two, normed_two, scale_two, gain_two.astype(jnp.float32)
    )
    grad_mid_one = grad_mid_two + grad_norm_two
    grad_branch_one = grad_mid_one.astype(jnp.bfloat16)
    grad_out_weight = left_matmul(attention_low, grad_branch_one)
    grad_attention = right_matmul(grad_branch_one, out_weight).astype(jnp.bfloat16)
    grad_attention = grad_attention.reshape(sequences, rows, KV_HEADS, groups, HEAD).transpose(
        0, 2, 3, 1, 4
    )
    delta = jnp.sum(grad_attention.astype(jnp.float32) * attention, axis=-1)

    def backward_tile(carry, piece, start):
        grad_query, grad_pairs, grad_bias = carry
        keys, values, allowed, scores, key_blocks = tile_setup(piece, start)
        prob = jnp.where(allowed, jnp.exp(scores - log_total[..., None]), 0.0)
        grad_values = jnp.einsum(
            "sgrqk,sgrqd->skgd",
            prob.astype(jnp.bfloat16),
            grad_attention,
            preferred_element_type=jnp.float32,
        )
        grad_prob = jnp.einsum(
            "sgrqd,skgd->sgrqk", grad_attention, values, preferred_element_type=jnp.float32
        )
        grad_score = (prob * (grad_prob - delta[..., None])).astype(jnp.bfloat16)
        grad_query = grad_query + jnp.einsum(
            "sgrqk,skgd->sgrqd", grad_score, keys, preferred_element_type=jnp.float32
        )
        grad_keys = jnp.einsum(
            "sgrqk,sqgrd->skgd", grad_score, query_tile, preferred_element_type=jnp.float32
        )
        count = piece.shape[1]
        block_grad = jnp.concatenate(
            [
                grad_keys.reshape(sequences, count, key_width),
                grad_values.reshape(sequences, count, key_width),
            ],
            axis=2,
        )
        grad_pairs = lax.dynamic_update_slice_in_dim(grad_pairs, block_grad, start, axis=1)
        grad_bias = bias_grad(grad_bias, grad_score, query_blocks, key_blocks, BLOCK)
        return (grad_query, grad_pairs, grad_bias)

    back_state = (
        jnp.zeros((sequences, KV_HEADS, groups, rows, HEAD), jnp.float32),
        jnp.zeros((sequences, length, 2 * key_width), jnp.float32),
        jnp.zeros((HEADS, distance.shape[1]), jnp.float32),
    )
    grad_query, grad_pairs, grad_bias = over_pieces(
        backward_tile, back_state, lax.all_gather(local_pairs, "ctx", axis=1, tiled=True), rows
    )
    grad_query_rows = (
        grad_query.transpose(0, 3, 1, 2, 4)
        .reshape(sequences * rows, head_width)
        .astype(jnp.bfloat16)
    )
    grad_local_pairs = (
        lax.psum_scatter(grad_pairs.astype(jnp.bfloat16), "ctx", scatter_dimension=1, tiled=True)
        .astype(jnp.float32)
        .reshape(sequences * rows, 2 * key_width)
        .astype(jnp.bfloat16)
    )
    grad_key_rows = grad_local_pairs[:, :key_width]
    grad_value_rows = grad_local_pairs[:, key_width:]
    grad_table = lax.dot_general(
        bucket_match.astype(jnp.float32),
        grad_bias,
        (((0,), (1,)), ((), ())),
        precision=lax.Precision.HIGHEST,
        preferred_element_type=jnp.float32,
    )
    grad_query_weight = left_matmul(hidden_one, grad_query_rows)
    grad_key_weight = left_matmul(hidden_one, grad_key_rows)
    grad_value_weight = left_matmul(hidden_one, grad_value_rows)
    grad_hidden_one = (
        right_matmul(grad_query_rows, query_weight)
        + right_matmul(grad_key_rows, key_weight)
        + right_matmul(grad_value_rows, value_weight)
    )
    grad_norm_one, grad_gain_one = norm_back(
        grad_hidden_one, normed_one, scale_one, gain_one.astype(jnp.float32)
    )
    grad_inputs = grad_mid_one + grad_norm_one
    grads = (
        grad_gain_one,
        grad_query_weight,
        grad_key_weight,
        grad_value_weight,
        grad_out_weight,
        grad_gain_two,
        grad_cross_query,
        grad_cross_key,
        grad_cross_value,
        grad_cross_out,
        grad_gain_three,
        grad_gate_weight,
        grad_up_weight,
        grad_down,
        grad_table,
    )
    packed = pack_grads(grads, shards)
    shard_sum = lax.psum_scatter(
        packed.reshape(-1).astype(jnp.bfloat16), "fsdp", scatter_dimension=0, tiled=True
    )
    piece_sum = lax.psum_scatter(shard_sum, "ctx", scatter_dimension=0, tiled=True).astype(
        jnp.float32
    )
    flat = lax.all_gather(piece_sum.astype(jnp.bfloat16), "ctx", axis=0, tiled=True).astype(
        piece_sum.dtype
    )
    weights_out = unpack_grads(flat, grads, shards)
    return (
        layer_out,
        loss,
        grad_inputs.reshape(sequences, rows, width),
        grad_encoder.reshape(sequences, encoder_local, width),
    ) + tuple(weights_out)


def solution(mesh):
    in_specs = (
        P("fsdp", "ctx", None),
        P("fsdp", "ctx", None),
        P("fsdp", "ctx", None),
        P("fsdp", "ctx"),
        P("fsdp", None),
        P(),
        P(),
        P("fsdp"),
        P("fsdp", None),
        P("fsdp", None),
        P("fsdp", None),
        P("fsdp", None),
        P("fsdp"),
        P("fsdp", None),
        P("fsdp", None),
        P("fsdp", None),
        P("fsdp", None),
        P("fsdp"),
        P("fsdp", None),
        P("fsdp", None),
        P("fsdp", None),
        P("fsdp", None),
    )
    out_specs = (
        P("fsdp", "ctx", None),
        P(),
        P("fsdp", "ctx", None),
        P("fsdp", "ctx", None),
        P("fsdp"),
        P("fsdp", None),
        P("fsdp", None),
        P("fsdp", None),
        P("fsdp", None),
        P("fsdp"),
        P("fsdp", None),
        P("fsdp", None),
        P("fsdp", None),
        P("fsdp", None),
        P("fsdp"),
        P("fsdp", None),
        P("fsdp", None),
        P("fsdp", None),
        P("fsdp", None),
    )
    return jax.shard_map(body, mesh=mesh, in_specs=in_specs, out_specs=out_specs, check_vma=False)
```

profile of v0, /device:TPU:0, one launch (start us, length us, event | category | flops | bytes accessed | tf_op | source)
XLA Modules:
  0.0 3626.7 jit_solution(12760938814210380592)
XLA Ops:
  10.7 28.5 all-gather.28.cloned.1.call-done
  40.7 26.8 all-gather.26.cloned.1.call-done
  78.0 17.8 all-gather.20.cloned.1.call-done
  97.6 26.5 all-gather.18.cloned.1.call-done
  163.8 21.7 all-gather.30.cloned.1.call-done
  188.8 45.3 %all-gather.42.cloned.1.call-done = bf16[2048,1024]{1,0:T(8,128)(2,1)} async-done(((bf16[256,1024]{1,0:T(8,128)(2,1)}), bf16[2048,1024]{1,0:T(8,128)(2,1)}) %all-gather.42.cloned.1.call-update) | async-done | bytes 4194320 | tf_op jit(solution)/shard_map/all_gather | solution.py:288
  240.6 620.6 %while.46 = (s32[]{:T(128)}, f32[1,8,2,256]{3,2,1,0:T(2,128)S(1)}, f32[1,8,2,256]{3,2,1,0:T(2,128)S(1)}, f32[1,8,2,256,64]{3,4,2,1,0:T(8,128)S(1)}, s32[8]{0:T(1...) while((s32[]{:T(128)}, f32[1,8,2,256]{3,2,1,0:T(2,128)S(1)}, ...), condition=%wide.region_5.6_spmd.clone, body=%wide.region_1.5_spmd.clone.sunk | while | flops 278815136 | bytes 123574976 | solution.py:124
  269.9 16.0 reshape.1231
  347.8 16.0 reshape.1231
  657.9 16.0 reshape.1231
  903.4 39.7 %all-reduce.8 = (f32[]{:T(128)}, f32[]{:T(128)}) all-reduce(f32[]{:T(128)} %get-tuple-element.957, f32[]{:T(128)} %convert_reduce_fusion), channel_id=1, replica_groups=mesh['ctx'=8,'fsdp'=4] {'ctx','fsdp'}, use_global_device_ids=true, to_apply=%region_11.12 | all-reduce | flops 2 | bytes 16 | tf_op jit(solution)/shard_map/psum | solution.py:350
  999.6 1487.1 %while.48 = (s32[]{:T(128)}, f32[1,8,2,256,64]{3,4,2,1,0:T(8,128)}, bf16[1,2048,1024]{1,2,0:T(8,128)(2,1)}, f32[16,4096]{1,0:T(8,128)}, s32[8]{0:T(128)S(1)}, /*...) while((s32[]{:T(128)}, f32[1,8,2,256,64]{3,4,2,1,0:T(8,128)}, ...), condition=%wide.region_21.22_spmd.clone, body=%wide.region_18.21_spmd.clone.sunk | while | flops 683270592 | bytes 231970768 | solution.py:124
  1094.4 32.3 rev.13
  1280.4 32.3 rev.13
  1466.3 32.3 rev.13
  1652.3 32.3 rev.13
  1838.2 32.3 rev.13
  2024.2 32.3 rev.13
  2210.2 32.3 rev.13
  2396.1 32.3 rev.13
  2623.2 89.1 %convert_element_type.280 = bf16[14945792]{0:T(1024)(128)(2,1)} reshape(bf16[4,3736448]{1,0:T(4,128)(2,1)} %constant_dynamic-update-slice_fusion) | data formatting | bytes 59783168 | tf_op jit(solution)/shard_map/convert_element_type | solution.py:541
  2714.1 518.1 %all-reduce.15.cloned.1.call-done = bf16[14945792]{0:T(1024)(128)(2,1)} async-done(((bf16[14945792]{0:T(1024)(128)(2,1)}), bf16[14945792]{0:T(1024)(128)(2,1)}) %all-reduce.15.cloned.1.call-update) | async-done | bytes 29891600
  3243.3 159.1 %all-reduce.17.cloned.1.call-done = bf16[3736448]{0:T(1024)(128)(2,1)} async-done(((bf16[3736448]{0:T(1024)(128)(2,1)}), bf16[3736448]{0:T(1024)(128)(2,1)}) %all-reduce.17.cloned.1.call-update) | async-done | bytes 7472912
  3428.4 153.0 %all-reduce.13.cloned.1.call-done = bf16[3736448]{0:T(1024)(128)(2,1)} async-done(((bf16[3736448]{0:T(1024)(128)(2,1)}), bf16[3736448]{0:T(1024)(128)(2,1)}) %all-reduce.13.cloned.1.call-update) | async-done | bytes 7472912
  (1366 shorter events, 2183.3 us)
Async XLA Ops:
  7.2 70.6 %copy-start.14 = (bf16[1,256,1024]{2,1,0:T(8,128)(2,1)S(1)}, bf16[1,256,1024]{2,1,0:T(8,128)(2,1)}, u32[]{:S(2)}) copy-start(bf16[1,256,1024]{2,1,0:T(8,128)(2,1)} %param.26) | copy-start | bytes 1572868
  7.2 31.9 all-gather.28.cloned.1.call-start
  8.0 59.5 %all-gather.26.cloned.1.call-start = ((), (), s32[]{:S(2)}) async-start(), calls=%async_computation.6 | async-start | bytes 1310720 | tf_op jit(solution)/shard_map/all_gather | solution.py:137
  8.7 87.2 %all-gather.20.cloned.1.call-start = ((), (), s32[]{:S(2)}) async-start(), calls=%async_computation.3 | async-start | bytes 1310720 | tf_op jit(solution)/shard_map/all_gather | solution.py:133
  9.4 114.7 %all-gather.18.cloned.1.call-start = ((), (), s32[]{:S(2)}) async-start(), calls=%async_computation.2 | async-start | bytes 1310720 | tf_op jit(solution)/shard_map/all_gather | solution.py:132
  10.0 151.2 %all-gather.22.cloned.1.call-start = ((), (), s32[]{:S(2)}) async-start(), calls=%async_computation.4 | async-start | bytes 2621440 | tf_op jit(solution)/shard_map/all_gather | solution.py:131
  10.6 174.9 %all-gather.30.cloned.1.call-start = ((), (), s32[]{:S(2)}) async-start(), calls=%async_computation.8 | async-start | bytes 1179648 | tf_op jit(solution)/shard_map/all_gather | solution.py:313
  69.7 164.4 %all-gather.42.cloned.1.call-start = ((), (), s32[]{:S(2)}) async-start(), calls=%async_computation.15 | async-start | bytes 4718592 | tf_op jit(solution)/shard_map/all_gather | solution.py:288
  77.8 83.4 %copy-start.73 = (f32[4,1,256]{2,1,0:T(1,128)}, f32[4,1,256]{2,1,0:T(1,128)S(1)}, u32[]{:S(2)}) copy-start(f32[4,1,256]{2,1,0:T(1,128)S(1)} %convert_element_type.284) | copy-start | bytes 12292
  78.0 83.2 %copy-start.77 = (f32[256]{0:T(256)}, f32[256]{0:T(256)S(1)}, u32[]{:S(2)}) copy-start(f32[256]{0:T(256)S(1)} %add_rsqrt_fusion.2) | copy-start | bytes 3076
  126.8 735.4 %all-gather.24.cloned.1.call-start = ((), (), s32[]{:S(2)}) async-start(), calls=%async_computation.5 | async-start | bytes 2621440 | tf_op jit(solution)/shard_map/all_gather | solution.py:134
  127.5 737.8 %all-gather.32.cloned.1.call-start = ((), (), s32[]{:S(2)}) async-start(), calls=%async_computation.9 | async-start | bytes 2621440 | tf_op jit(solution)/shard_map/all_gather | solution.py:136
  128.3 750.4 %all-gather.34.cloned.1.call-start = ((), (), s32[]{:S(2)}) async-start(), calls=%async_computation.10 | async-start | bytes 2621440 | tf_op jit(solution)/shard_map/all_gather | solution.py:139
  128.9 754.4 %all-gather.36.cloned.1.call-start = ((), (), s32[]{:S(2)}) async-start(), calls=%async_computation.11 | async-start | bytes 7208960 | tf_op jit(solution)/shard_map/all_gather | solution.py:141
  129.6 759.7 %all-gather.38.cloned.1.call-start = ((), (), s32[]{:S(2)}) async-start(), calls=%async_computation.12 | async-start | bytes 7208960 | tf_op jit(solution)/shard_map/all_gather | solution.py:142
  130.2 766.5 %all-gather.40.cloned.1.call-start = ((), (), s32[]{:S(2)}) async-start(), calls=%async_computation.13 | async-start | bytes 7208960 | tf_op jit(solution)/shard_map/all_gather | solution.py:143
  130.9 2436.0 %reduce-scatter.7.cloned.1.call-start = ((), (), s32[]{:S(2)}) async-start(), calls=%async_computation.17 | async-start | bytes 1179648
  240.6 621.6 %copy-start.15 = (bf16[1,256,1024]{2,1,0:T(8,128)(2,1)S(1)}, bf16[1,256,1024]{2,1,0:T(8,128)(2,1)}, u32[]{:S(2)}) copy-start(bf16[1,256,1024]{2,1,0:T(8,128)(2,1)} %param.26) | copy-start | bytes 1572868
  864.8 120.3 %copy-start.7 = (f32[256,1024]{1,0:T(8,128)}, f32[256,1024]{1,0:T(8,128)S(1)}, u32[]{:S(2)}) copy-start(f32[256,1024]{1,0:T(8,128)S(1)} %get-tuple-element.950) | copy-start | bytes 3145732
  996.2 1583.4 %reduce-scatter.5.cloned.1.call-start = ((), (), s32[]{:S(2)}) async-start(), calls=%async_computation.14 | async-start | bytes 4718592 | tf_op jit(solution)/shard_map/reduce_scatter | solution.py:496
  1000.0 69.6 %copy-start.4 = (bf16[1,256,8,2,64]{1,4,3,2,0:T(8,128)(2,1)}, bf16[1,256,8,2,64]{1,4,3,2,0:T(8,128)(2,1)S(1)}, u32[]{:S(2)}) copy-start(bf16[1,256,8,2,64]{1,4,3,2,0:T(8,128)(2,1)S(1)} %get-tuple-element.1396) | copy-start | bytes 1572868 | tf_op jit(solution)/shard_map/while
  2486.7 745.6 %all-reduce.15.cloned.1.call-start = ((), (), s32[]{:S(2)}) async-start(), calls=%async_computation.18 | async-start | bytes 59785216
  2712.3 690.1 %all-reduce.17.cloned.1.call-start = ((), (), s32[]{:S(2)}) async-start(), calls=%async_computation.19 | async-start | bytes 14946304
  3240.8 340.7 %all-reduce.13.cloned.1.call-start = ((), (), s32[]{:S(2)}) async-start(), calls=%async_computation.16 | async-start | bytes 14946304
  (171 other events, 2959.9 us)
Sparse Core Ops, SparseCore 0:
  9.9 29.2 all-gather.27
  41.0 26.4 all-gather.25
  69.4 26.4 all-gather.19
  97.6 26.4 all-gather.17
  125.8 35.3 all-gather.21
  163.2 22.2 all-gather.29
  187.7 46.4 all-gather.41
  235.9 34.0 all-gather.23
  271.9 35.1 all-gather.31
  308.8 35.1 all-gather.33
  345.8 65.6 all-gather.35
  413.2 65.6 all-gather.37
  480.8 65.6 all-gather.39
  996.3 32.6 reduce-scatter.6
  2486.8 49.9 reduce-scatter.4
  2712.4 519.8 all-reduce.14
  3240.9 161.4 all-reduce.16
  3422.5 158.9 all-reduce.12
where the time goes:
time: 3670 us; the launch traced here: 3630 us
  local copies, waits for them, and re-layouts  2060 us (56%)
  waiting for transfers between devices  1000 us (27%)
  matrix products  263 us (7%)
  other arithmetic  131 us (4%)
  loops' own time  75.2 us (2%)
  blocking collectives  71.6 us (2%)
    unnamed x22, waiting for transfers between devices  837 us
    rev x8, local copies, waits for them, and re-layouts, diagonal_sums(): flipped = jnp.flip(grid, axis=-2)  258 us
    reshape x16, local copies, waits for them, and re-layouts, toeplitz(): return flat.reshape(lead + (block, 2 * block - 1))[..., :block]  256 us
    another operation x32, local copies, waits for them, and re-layouts, toeplitz(): tiled = jnp.tile(padded, (1,) * len(lead) + (block,))  215 us
    transpose x32, local copies, waits for them, and re-layouts, tile_bias(): grid.transpose(2, 0, 3, 1, 4)  192 us
    slice x16, local copies, waits for them, and re-layouts, toeplitz(): flat = tiled[..., block - 1:block - 1 + block * (2 * block - 1)]  143 us
    reshape x8, local copies, waits for them, and re-layouts, diagonal_sums(): return jnp.sum(flat.reshape(lead + (block, 2 * block - 1)), axis=-2)  128 us
    reshape x16, local copies, waits for them, and re-layouts, tile_setup(): scores = jnp.where(allowed, raw + bias[None], NEGATIVE)  103 us
  transfers between devices with their start and end apart: 18, of which 10 were waited for; matrix products, arithmetic and copies ran while one was open for 60% of the time, Pallas kernels for 0%

commit v1 on v0

v1 whole, which is shorter than its diff:
```python
import functools
import jax
import jax.numpy as jnp
from jax import lax
from jax.experimental import pallas as pl
from jax.experimental.pallas import tpu as pltpu
from jax.sharding import Mesh
from jax.sharding import PartitionSpec as P

HEAD = 64
BLOCK = 128
NEGATIVE = -1e30
SPAN = 512
F32 = jnp.float32
BF16 = jnp.bfloat16


def nt(left, right):
    return lax.dot_general(left, right, (((1,), (1,)), ((), ())), preferred_element_type=F32)


def nn(left, right):
    return jnp.dot(left, right, preferred_element_type=F32)


def pad_heads(block):
    wide = block.astype(F32)
    lane = lax.broadcasted_iota(jnp.int32, (BLOCK, BLOCK), 1)
    parts = []
    for group in range(2):
        slab = wide[:, group * BLOCK : (group + 1) * BLOCK]
        turned = pltpu.roll(slab, HEAD, 1)
        keep = (lane < HEAD) if group == 0 else (lane >= HEAD)
        for part in range(2):
            source = slab if part == group else turned
            parts.append(jnp.where(keep, source, 0.0))
    return jnp.concatenate(parts, axis=0).astype(BF16)


def unpad_heads(turned):
    parts = [turned[:, index * BLOCK : (index + 1) * BLOCK].T for index in range(4)]
    return jnp.concatenate(parts, axis=1)


def fill_bias(vectors_ref, bias_ref):
    for head in range(4):
        row = jnp.broadcast_to(vectors_ref[0, head : head + 1, :], (BLOCK, SPAN))
        turned = pltpu.roll(row, 0, 1, stride=1, stride_axis=0)
        lanes = slice(head * BLOCK, (head + 1) * BLOCK)
        bias_ref[0, :, lanes] = turned[:, :BLOCK]
        bias_ref[1, :, lanes] = turned[:, BLOCK : 2 * BLOCK]
        bias_ref[2, :, lanes] = jnp.broadcast_to(row[:, BLOCK : BLOCK + 1], (BLOCK, BLOCK))


def four(tile):
    return jnp.concatenate([tile] * 4, axis=1)


def forward_kernel(masked, table, *refs):
    if masked:
        q_ref, k_ref, v_ref, vec_ref, low_ref, high_ref, a_ref, o_ref, l_ref, bias_ref, acc_ref = refs
        fill_bias(vec_ref, bias_ref)
    else:
        q_ref, k_ref, v_ref, a_ref, o_ref, l_ref, acc_ref = refs
    pairs = q_ref.shape[0] // BLOCK
    steps = k_ref.shape[0] // BLOCK
    row = lax.broadcasted_iota(jnp.int32, (BLOCK, BLOCK), 0)
    for index in range(pairs):
        rows = slice(index * BLOCK, (index + 1) * BLOCK)
        query = pad_heads(q_ref[rows, :])
        if masked:
            mine = table[index]
            first = table[pairs + index]
            low = low_ref[index : index + 1, :]
            high = high_ref[index : index + 1, :]

        def scores(step, near):
            if not masked:
                place = pl.multiple_of(step * BLOCK, BLOCK)
                return place, nt(k_ref[pl.ds(place, BLOCK), :], query)
            block = mine - step
            place = pl.multiple_of(table[2 * pairs + block] * BLOCK, BLOCK)
            raw = nt(k_ref[pl.ds(place, BLOCK), :], query)
            position = row + block * BLOCK
            allowed = position >= low
            if near:
                allowed = allowed & (position <= high)
                raw = raw + bias_ref[0]
            else:
                raw = raw + bias_ref[jnp.minimum(step, 2)]
            return place, jnp.where(four(allowed), raw, NEGATIVE)

        def gather(place, weight):
            turned = v_ref[pl.ds(place, BLOCK), :].astype(F32).T.astype(BF16)
            low_half = nn(turned[:HEAD], weight[:, : 2 * BLOCK])
            high_half = nn(turned[HEAD:], weight[:, 2 * BLOCK :])
            return jnp.concatenate([low_half, high_half], axis=1)

        place, raw = scores(0, True)
        top = jnp.max(raw, axis=0, keepdims=True)
        weight = jnp.exp(raw - top)
        total = jnp.sum(weight, axis=0, keepdims=True)
        acc_ref[...] = gather(place, weight.astype(BF16))

        def advance(step, carry):
            top, total = carry
            place, raw = scores(step, False)
            new_top = jnp.maximum(top, jnp.max(raw, axis=0, keepdims=True))
            factor = jnp.exp(top - new_top)
            weight = jnp.exp(raw - new_top)
            total = total * factor + jnp.sum(weight, axis=0, keepdims=True)
            acc_ref[...] = acc_ref[...] * factor + gather(place, weight.astype(BF16))
            return new_top, total

        count = mine - first + 1 if masked else steps
        top, total = lax.fori_loop(1, count, advance, (top, total))
        out = acc_ref[...] / total
        o_ref[0, index] = out
        l_ref[0, index] = jnp.broadcast_to(top + jnp.log(total), (8, 4 * BLOCK))
        a_ref[rows, :] = unpad_heads(out).astype(BF16)


def backward_kernel(masked, table, *refs):
    if masked:
        (q_ref, k_ref, v_ref, g_ref, o_ref, l_ref, vec_ref, low_ref, high_ref,
         dq_ref, dkv_ref, dvec_ref, bias_ref, dk_acc, dv_acc, dq_acc, near_ref, far_ref) = refs
        fill_bias(vec_ref, bias_ref)
        near_ref[...] = jnp.zeros_like(near_ref)
        far_ref[...] = jnp.zeros_like(far_ref)
    else:
        (q_ref, k_ref, v_ref, g_ref, o_ref, l_ref, dq_ref, dkv_ref, dk_acc, dv_acc, dq_acc) = refs
    pairs = q_ref.shape[0] // BLOCK
    steps = k_ref.shape[0] // BLOCK
    dk_acc[...] = jnp.zeros_like(dk_acc)
    dv_acc[...] = jnp.zeros_like(dv_acc)
    row = lax.broadcasted_iota(jnp.int32, (BLOCK, BLOCK), 0)
    for index in range(pairs):
        rows = slice(index * BLOCK, (index + 1) * BLOCK)
        query = pad_heads(q_ref[rows, :])
        grad = pad_heads(g_ref[rows, :])
        log_total = l_ref[0, index, :1, :]
        raw_grad = g_ref[rows, :].astype(F32)
        turned_grad = jnp.concatenate(
            [raw_grad[:, head * HEAD : (head + 1) * HEAD].T for head in range(4)], axis=1
        )
        delta = jnp.sum(turned_grad * o_ref[0, index], axis=0, keepdims=True)
        if masked:
            mine = table[index]
            first = table[pairs + index]
            low = low_ref[index : index + 1, :]
            high = high_ref[index : index + 1, :]

        def tile(step, near, start):
            if masked:
                block = mine - step
                place = pl.multiple_of(table[2 * pairs + block] * BLOCK, BLOCK)
            else:
                place = pl.multiple_of(step * BLOCK, BLOCK)
            keys = k_ref[pl.ds(place, BLOCK), :]
            raw = nt(keys, query)
            if masked:
                position = row + block * BLOCK
                allowed = position >= low
                if near:
                    allowed = allowed & (position <= high)
                    raw = raw + bias_ref[0]
                else:
                    raw = raw + bias_ref[jnp.minimum(step, 2)]
                raw = jnp.where(four(allowed), raw, NEGATIVE)
            prob = jnp.exp(raw - log_total)
            grad_prob = nt(v_ref[pl.ds(place, BLOCK), :], grad)
            grad_score = (prob * (grad_prob - delta)).astype(BF16)
            dv_acc[pl.ds(place, BLOCK), :] += nn(prob.astype(BF16), grad)
            dk_acc[pl.ds(place, BLOCK), :] += nn(grad_score, query)
            turned = keys.astype(F32).T.astype(BF16)
            part = jnp.concatenate(
                [nn(turned[:HEAD], grad_score[:, : 2 * BLOCK]), nn(turned[HEAD:], grad_score[:, 2 * BLOCK :])],
                axis=1,
            )
            if start:
                dq_acc[...] = part
            else:
                dq_acc[...] += part
            return grad_score

        grad_score = tile(0, True, True)
        if masked:
            near_ref[0] += grad_score.astype(F32)
            last = mine - first

            @pl.when(last >= 1)
            def _():
                near_ref[1] += tile(1, False, False).astype(F32)

            def advance(step, carry):
                wide = tile(step, False, False).astype(F32)
                far_ref[...] += jnp.sum(wide.reshape(BLOCK // 8, 8, 4 * BLOCK), axis=0)
                return carry

            lax.fori_loop(2, last + 1, advance, 0)
        else:

            def advance(step, carry):
                tile(step, False, False)
                return carry

            lax.fori_loop(1, steps, advance, 0)
        dq_ref[rows, :] = unpad_heads(dq_acc[...]).astype(BF16)
    dkv_ref[0] = dk_acc[...].astype(BF16)
    dkv_ref[1] = dv_acc[...].astype(BF16)
    if masked:
        rowid = lax.broadcasted_iota(jnp.int32, (BLOCK, SPAN), 0)
        lane = lax.broadcasted_iota(jnp.int32, (1, SPAN), 1)
        for head in range(4):
            lanes = slice(head * BLOCK, (head + 1) * BLOCK)
            wide = jnp.concatenate(
                [near_ref[0, :, lanes], near_ref[1, :, lanes], jnp.zeros((BLOCK, 2 * BLOCK), F32)], axis=1
            )
            bit = 1
            while bit < BLOCK:
                wide = jnp.where((rowid & bit) != 0, pltpu.roll(wide, SPAN - bit, 1), wide)
                bit = bit * 2
            sums = jnp.sum(wide, axis=0, keepdims=True)
            far = jnp.sum(far_ref[:, lanes])
            dvec_ref[0, head : head + 1, :] = sums + jnp.where(lane == BLOCK, far, 0.0)


def specs_of(rows, length, pairs, groups):
    cols = pl.BlockSpec((rows, 2 * BLOCK), lambda g, *_: (0, g))
    keys = pl.BlockSpec((length, BLOCK), lambda g, *_: (0, g))
    values = pl.BlockSpec((length, BLOCK), lambda g, *_: (0, groups + g))
    outs = pl.BlockSpec((1, pairs, HEAD, 4 * BLOCK), lambda g, *_: (g, 0, 0, 0))
    logs = pl.BlockSpec((1, pairs, 8, 4 * BLOCK), lambda g, *_: (g, 0, 0, 0))
    vecs = pl.BlockSpec((1, 4, SPAN), lambda g, *_: (g, 0, 0))
    lims = pl.BlockSpec((pairs, BLOCK), lambda g, *_: (0, 0))
    return cols, keys, values, outs, logs, vecs, lims


def attend(query, keys_values, table, extra, masked):
    rows, width = query.shape
    length = keys_values.shape[0]
    groups = width // (4 * HEAD)
    pairs = rows // BLOCK
    cols, kspec, vspec, outs, logs, vecs, lims = specs_of(rows, length, pairs, groups)
    scratch = [pltpu.VMEM((HEAD, 4 * BLOCK), F32)]
    if masked:
        scratch = [pltpu.VMEM((3, BLOCK, 4 * BLOCK), F32)] + scratch
    return pl.pallas_call(
        functools.partial(forward_kernel, masked),
        grid_spec=pltpu.PrefetchScalarGridSpec(
            num_scalar_prefetch=1,
            grid=(groups,),
            in_specs=[cols, kspec, vspec] + ([vecs, lims, lims] if masked else []),
            out_specs=[cols, outs, logs],
            scratch_shapes=scratch,
        ),
        out_shape=[
            jax.ShapeDtypeStruct((rows, width), BF16),
            jax.ShapeDtypeStruct((groups, pairs, HEAD, 4 * BLOCK), F32),
            jax.ShapeDtypeStruct((groups, pairs, 8, 4 * BLOCK), F32),
        ],
        cost_estimate=pl.CostEstimate(
            flops=4 * rows * length * width, bytes_accessed=4 * length * width, transcendentals=rows * length * 16
        ),
        name="attend_self" if masked else "attend_cross",
    )(table, query, keys_values, keys_values, *extra)


def attend_back(query, keys_values, grad, outs_in, logs_in, table, extra, masked):
    rows, width = query.shape
    length = keys_values.shape[0]
    groups = width // (4 * HEAD)
    pairs = rows // BLOCK
    cols, kspec, vspec, outs, logs, vecs, lims = specs_of(rows, length, pairs, groups)
    scratch = [pltpu.VMEM((length, BLOCK), F32), pltpu.VMEM((length, BLOCK), F32), pltpu.VMEM((HEAD, 4 * BLOCK), F32)]
    out_specs = [cols, pl.BlockSpec((2, length, BLOCK), lambda g, *_: (0, 0, g))]
    out_shape = [
        jax.ShapeDtypeStruct((rows, width), BF16),
        jax.ShapeDtypeStruct((2, length, width // 2), BF16),
    ]
    if masked:
        scratch = [pltpu.VMEM((3, BLOCK, 4 * BLOCK), F32)] + scratch
        scratch += [pltpu.VMEM((2, BLOCK, 4 * BLOCK), F32), pltpu.VMEM((8, 4 * BLOCK), F32)]
        out_specs = out_specs + [vecs]
        out_shape = out_shape + [jax.ShapeDtypeStruct((groups, 4, SPAN), F32)]
    return pl.pallas_call(
        functools.partial(backward_kernel, masked),
        grid_spec=pltpu.PrefetchScalarGridSpec(
            num_scalar_prefetch=1,
            grid=(groups,),
            in_specs=[cols, kspec, vspec, cols, outs, logs] + ([vecs, lims, lims] if masked else []),
            out_specs=out_specs,
            scratch_shapes=scratch,
        ),
        out_shape=out_shape,
        cost_estimate=pl.CostEstimate(
            flops=10 * rows * length * width, bytes_accessed=8 * length * width, transcendentals=rows * length * 16
        ),
        name="attend_self_back" if masked else "attend_cross_back",
    )(table, query, keys_values, keys_values, grad, outs_in, logs_in, *extra)


def offset_index(half):
    place = jnp.arange(SPAN, dtype=jnp.int32)
    behind = jnp.where(place >= 2 * BLOCK, place - SPAN, place)
    return behind, jnp.clip(half - behind, 0, 2 * half - 1)


D = 1024
HEADS = 16
KV_HEADS = 8
BUCKETS = 32
EPS = 1e-06
CTX = ("line", "core")


def tn(left, right):
    return lax.dot_general(left, right, (((0,), (0,)), ((), ())), preferred_element_type=F32)


def norm_rows(values, gain):
    scale = lax.rsqrt(jnp.mean(values * values, axis=-1, keepdims=True) + EPS)
    normed = values * scale
    return normed, scale, (normed * gain).astype(BF16)


def norm_back(grad_out, normed, scale, gain):
    grad_gain = jnp.sum(grad_out * normed, axis=0)
    inner = grad_out * gain
    grad_in = scale * (inner - normed * jnp.mean(inner * normed, axis=-1, keepdims=True))
    return grad_in, grad_gain


def gelu_tanh(value):
    return jax.nn.gelu(value, approximate=True)


def partners(size, bit):
    return [(index, index ^ bit) for index in range(size)]


def sum_everywhere(value):
    for axis in ("core", "line", "fsdp"):
        size = lax.axis_size(axis)
        bit = 1
        while bit < size:
            value = value + lax.ppermute(value, axis, partners(size, bit))
            bit = bit * 2
    return value


def half_rows(part):
    half = part.shape[0] // 2
    return lax.dynamic_slice_in_dim(part, lax.axis_index("core") * half, half, axis=0)


def fetch(*parts):
    joined = parts[0] if len(parts) == 1 else jnp.concatenate(parts, axis=1)
    return lax.all_gather(half_rows(joined), ("fsdp", "core"), axis=0, tiled=True)


def swap(value):
    return lax.ppermute(value, "core", [(0, 1), (1, 0)])


def my_columns(value, other=False):
    half = value.shape[1] // 2
    core = lax.axis_index("core")
    core = 1 - core if other else core
    return lax.dynamic_slice_in_dim(value, core * half, half, axis=1)


def weight_grad(hidden, hidden_swapped, *grads):
    mine = jnp.concatenate([my_columns(item) for item in grads], axis=1)
    other = swap(jnp.concatenate([my_columns(item, True) for item in grads], axis=1))
    both_hidden = jnp.concatenate([hidden, hidden_swapped], axis=0)
    both_grad = jnp.concatenate([mine, other], axis=0)
    return tn(both_hidden, both_grad).astype(BF16)


def reduce_grad(partial, widths):
    shard = lax.psum_scatter(partial, "fsdp", scatter_dimension=0, tiled=True)
    piece = lax.psum_scatter(shard, "line", scatter_dimension=0, tiled=True)
    whole = lax.all_gather(piece, CTX, axis=0, tiled=False)
    lines = lax.axis_size("line")
    whole = whole.reshape(lines, 2, piece.shape[0], piece.shape[1])
    rows = lines * piece.shape[0]
    outs = []
    start = 0
    for width in widths:
        part = whole[..., start : start + width // 2]
        outs.append(part.transpose(0, 2, 1, 3).reshape(rows, width).astype(F32))
        start = start + width // 2
    return outs


def body(
    inputs, encoder, teacher, valid_mask, doc_ids, block_order, buckets,
    gain_self, w_query, w_key, w_value, w_out, gain_cross, c_query, c_key, c_value, c_out,
    gain_ffn, w_gate, w_up, w_down, bias_table,
):
    rows, width = inputs.shape[1:]
    lines = lax.axis_size("line")
    shards = lax.axis_size("fsdp")
    contexts = 2 * lines
    length = rows * contexts
    pair = rows // BLOCK
    token_total = length * shards
    key_width = KV_HEADS * HEAD
    context = lax.axis_index("line") * 2 + lax.axis_index("core")
    fsdp = lax.axis_index("fsdp")

    mask_rows = valid_mask.reshape(rows).astype(F32)
    count = sum_everywhere(jnp.broadcast_to(jnp.sum(mask_rows), (8, 128)))[0, 0]
    count = jnp.maximum(count, 1.0)

    small = jnp.concatenate([gain_self, gain_cross, gain_ffn, bias_table.reshape(-1)])
    share = gain_self.shape[0]
    small = lax.all_gather(small, "fsdp", axis=0, tiled=False)
    gains = [
        small[:, index * share : (index + 1) * share].reshape(D).astype(F32) for index in range(3)
    ]
    gain_one, gain_two, gain_three = gains
    table_whole = small[:, 3 * share :].reshape(BUCKETS, HEADS)

    wqkv = fetch(w_query, w_key, w_value)
    wo = fetch(w_out)
    wcq = fetch(c_query)
    wckv = fetch(c_key, c_value)
    wco = fetch(c_out)
    wgu = fetch(w_gate, w_up)
    wd = fetch(w_down)
    hidden_ff = w_gate.shape[1]

    query_blocks = lax.dynamic_slice_in_dim(block_order, context * pair, pair)
    slots = jnp.arange(contexts * pair, dtype=jnp.int32)
    inverse = jnp.sum(jnp.where(block_order[None, :] == slots[:, None], slots[None, :], 0), axis=1)
    docs = doc_ids.reshape(length)
    query_docs = jnp.stack(
        [lax.dynamic_slice_in_dim(docs, query_blocks[index] * BLOCK, BLOCK) for index in range(pair)]
    )
    low = jnp.sum((docs[None, None, :] < query_docs[:, :, None]).astype(jnp.int32), axis=-1)
    high = jnp.sum((docs[None, None, :] <= query_docs[:, :, None]).astype(jnp.int32), axis=-1) - 1
    place_table = jnp.concatenate([query_blocks, low[:, 0] // BLOCK, inverse]).astype(jnp.int32)
    behind, index_of = offset_index(length)
    bucket_match = (jnp.take(buckets, index_of)[None, :] == jnp.arange(BUCKETS, dtype=jnp.int32)[:, None])
    vectors = tn(table_whole, bucket_match.astype(BF16)).reshape(HEADS // 4, 4, SPAN)
    extra = (vectors, low, high)

    flat_in = inputs.reshape(rows, width).astype(F32)
    normed_one, scale_one, hidden_one = norm_rows(flat_in, gain_one)
    packed = nn(hidden_one, wqkv).astype(BF16)
    query = packed[:, :D]
    pairs_whole = lax.all_gather(packed[:, D:], CTX, axis=0, tiled=True)
    attention, outs_one, logs_one = attend(query, pairs_whole, place_table, extra, True)
    mid_one = flat_in + nn(attention, wo)

    encoder_rows = encoder.reshape(encoder.shape[1], width)
    encoder_pairs = nn(encoder_rows, wckv).astype(BF16)
    encoder_whole = lax.all_gather(encoder_pairs, CTX, axis=0, tiled=True)

    normed_two, scale_two, hidden_two = norm_rows(mid_one, gain_two)
    cross_q = nn(hidden_two, wcq).astype(BF16)
    cross, outs_two, logs_two = attend(cross_q, encoder_whole, place_table, (), False)
    mid_two = mid_one + nn(cross, wco)
    normed_three, scale_three, hidden_three = norm_rows(mid_two, gain_three)
    gate = nn(hidden_three, wgu[:, :hidden_ff])
    up = nn(hidden_three, wgu[:, hidden_ff:])
    active, gelu_pull = jax.vjp(gelu_tanh, gate)
    mixed = (active * up).astype(BF16)
    result = mid_two + nn(mixed, wd)
    layer_out = result.astype(BF16)
    diff = result - teacher.reshape(rows, width).astype(F32)
    squared_local = jnp.sum(mask_rows[:, None] * diff * diff)
    grad_result = token_total / count * mask_rows[:, None] * diff

    e_three = grad_result.astype(BF16)
    grad_mixed = nt(e_three, wd)
    (gelu_slope,) = gelu_pull(grad_mixed * up)
    grad_gate = gelu_slope.astype(BF16)
    grad_up = (grad_mixed * active).astype(BF16)
    (grad_down,) = reduce_grad(weight_grad(mixed, swap(mixed), e_three), (D,))
    grad_gate_weight, grad_up_weight = reduce_grad(
        weight_grad(hidden_three, swap(hidden_three), grad_gate, grad_up), (hidden_ff, hidden_ff)
    )
    grad_hidden_three = nt(grad_gate, wgu[:, :hidden_ff]) + nt(grad_up, wgu[:, hidden_ff:])
    grad_norm_three, grad_gain_three = norm_back(grad_hidden_three, normed_three, scale_three, gain_three)
    grad_mid_two = grad_result + grad_norm_three

    e_two = grad_mid_two.astype(BF16)
    (grad_cross_out,) = reduce_grad(weight_grad(cross, swap(cross), e_two), (D,))
    grad_cross = nt(e_two, wco).astype(BF16)
    grad_cross_q, encoder_grad = attend_back(
        cross_q, encoder_whole, grad_cross, outs_two, logs_two, place_table, (), False
    )
    encoder_mine = lax.psum_scatter(encoder_grad, CTX, scatter_dimension=1, tiled=True)
    encoder_mine = jnp.concatenate([encoder_mine[0], encoder_mine[1]], axis=1)
    grad_encoder = nt(encoder_mine, wckv)
    grad_cross_key, grad_cross_value = reduce_grad(
        weight_grad(
            encoder_rows, swap(encoder_rows), encoder_mine[:, :key_width], encoder_mine[:, key_width:]
        ),
        (key_width, key_width),
    )
    (grad_cross_query,) = reduce_grad(weight_grad(hidden_two, swap(hidden_two), grad_cross_q), (D,))
    grad_norm_two, grad_gain_two = norm_back(nt(grad_cross_q, wcq), normed_two, scale_two, gain_two)
    grad_mid_one = grad_mid_two + grad_norm_two

    e_one = grad_mid_one.astype(BF16)
    (grad_out_weight,) = reduce_grad(weight_grad(attention, swap(attention), e_one), (D,))
    grad_attention = nt(e_one, wo).astype(BF16)
    grad_query, grad_pairs, grad_vectors = attend_back(
        query, pairs_whole, grad_attention, outs_one, logs_one, place_table, extra, True
    )
    mine = lax.psum_scatter(grad_pairs, CTX, scatter_dimension=1, tiled=True)
    grad_packed = jnp.concatenate([grad_query, mine[0], mine[1]], axis=1)
    grad_query_weight, grad_key_weight, grad_value_weight = reduce_grad(
        weight_grad(hidden_one, swap(hidden_one), grad_query, mine[0], mine[1]), (D, key_width, key_width)
    )
    grad_norm_one, grad_gain_one = norm_back(nt(grad_packed, wqkv), normed_one, scale_one, gain_one)
    grad_inputs = grad_mid_one + grad_norm_one

    grad_table = lax.dot_general(
        bucket_match.astype(F32) * ((behind >= 1 - BLOCK) & (behind < 2 * BLOCK)).astype(F32)[None, :],
        grad_vectors.reshape(HEADS, SPAN),
        (((1,), (1,)), ((), ())),
        precision=lax.Precision.HIGHEST,
        preferred_element_type=F32,
    )
    sums = jnp.concatenate(
        [
            grad_gain_one,
            grad_gain_two,
            grad_gain_three,
            grad_table.reshape(-1),
            jnp.broadcast_to(squared_local, (512,)),
        ]
    )
    sums = sum_everywhere(sums.reshape(-1, 128)).reshape(-1)
    loss = sums[3 * D + 512] / (D * count)

    def shard_of(offset, amount):
        return lax.dynamic_slice_in_dim(sums, offset + fsdp * (amount // shards), amount // shards)

    return (
        layer_out.reshape(1, rows, width),
        loss,
        grad_inputs.reshape(1, rows, width),
        grad_encoder.reshape(1, encoder.shape[1], width),
        shard_of(0, D),
        grad_query_weight,
        grad_key_weight,
        grad_value_weight,
        grad_out_weight,
        shard_of(D, D),
        grad_cross_query,
        grad_cross_key,
        grad_cross_value,
        grad_cross_out,
        shard_of(2 * D, D),
        grad_gate_weight,
        grad_up_weight,
        grad_down,
        shard_of(3 * D, 512).reshape(BUCKETS // shards, HEADS),
    )


def solution(mesh):
    shape = mesh.devices.shape
    fine = Mesh(mesh.devices.reshape(shape[0] // 2, 2, shape[1]), ("line", "core", "fsdp"))
    tokens = P("fsdp", CTX, None)
    matrix = P("fsdp", None)
    vector = P("fsdp")
    weights = (vector, matrix, matrix, matrix, matrix, vector, matrix, matrix, matrix, matrix, vector)
    weights = weights + (matrix, matrix, matrix, matrix)
    in_specs = (tokens, tokens, tokens, P("fsdp", CTX), matrix, P(), P()) + weights
    out_specs = (tokens, P(), tokens, tokens) + weights
    return jax.shard_map(body, mesh=fine, in_specs=in_specs, out_specs=out_specs, check_vma=False)
```

time: 3670 us -> 1070 us (0.29); the launches traced: 3630 us -> 1070 us
  local copies, waits for them, and re-layouts: 2060 us -> 54.1 us
  waiting for transfers between devices: 1000 us -> 724 us
  matrix products: 263 us -> 75.4 us
  other arithmetic: 131 us -> 21.9 us
  Pallas kernels: 0 us -> 79.8 us
  loops' own time: 75.2 us -> 0 us
    unnamed x22 -> x28, waiting for transfers between devices: 837 us -> 1.12 us
    reshape x74 -> x5, local copies, waits for them, and re-layouts: 645 us -> 0.94 us  [the longest x1 0.68 us: body(): shard_of(3 * D, 512).reshape(BUCKETS // shards, HEADS)]
    reduce_scatter x1 -> x16, waiting for transfers between devices: 0.01 us -> 423 us  [the longest x7 269 us: reduce_grad(): shard = lax.psum_scatter(partial, 'fsdp', scatter_dimension=0, tiled=True)]
    transpose x48 -> x0, local copies, waits for them, and re-layouts: 278 us -> none  [the longest x32 192 us: tile_bias(): grid.transpose(2, 0, 3, 1, 4)]
    rev x8 -> x0, local copies, waits for them, and re-layouts: 258 us -> none  [diagonal_sums(): flipped = jnp.flip(grid, axis=-2)]
    slice x66 -> x8, local copies, waits for them, and re-layouts: 229 us -> 6.25 us  [the longest x1 1.9 us: body(): grad_packed = jnp.concatenate([grad_query, mine[0], mine[1]], axis=1)]
    another operation x33 -> x0, local copies, waits for them, and re-layouts: 215 us -> none  [the longest x32 215 us: toeplitz(): tiled = jnp.tile(padded, (1,) * len(lead) + (block,))]
    dot_general x97 -> x25, matrix products: 263 us -> 75.4 us  [the longest x8 30.1 us: nn(): return jnp.dot(left, right, preferred_element_type=F32)]
  transfers between devices with their start and end apart: 18 -> 52, of which waited for: 10 -> 42; matrix products, arithmetic and copies ran while one was open for 60% -> 10% of each run, Pallas kernels for 0% -> 3%
where the time goes in v1:
time: 1070 us
  waiting for transfers between devices  724 us (68%)
  Pallas kernels  79.8 us (7%)
  matrix products  75.4 us (7%)
  blocking collectives  75.1 us (7%)
  local copies, waits for them, and re-layouts  54.1 us (5%)
  other arithmetic  21.9 us (2%)
  between operations  19.5 us (2%)
  starting transfers between devices  18.3 us (2%)
    reduce_scatter x7, waiting for transfers between devices, reduce_grad(): shard = lax.psum_scatter(partial, 'fsdp', scatter_dimension=0, tiled=True)  269 us
    all_gather x7, waiting for transfers between devices, fetch(): lax.all_gather(half_rows(joined), ('fsdp', 'core'), axis=0, tiled=True)  202 us
    reduce_scatter x7, waiting for transfers between devices, reduce_grad(): piece = lax.psum_scatter(shard, 'line', scatter_dimension=0, tiled=True)  111 us
    all_gather x4, blocking collectives, reduce_grad(): whole = lax.all_gather(piece, CTX, axis=0, tiled=False)  65.5 us
    pallas_call x2, Pallas kernels, attend_back(): pl.pallas_call(functools.partial(backward_kernel, masked), grid_spec=pltp...  45.5 us
    reduce_scatter x1, waiting for transfers between devices, body(): mine = lax.psum_scatter(grad_pairs, CTX, scatter_dimension=1, tiled=True)  43.9 us
    all_gather x3, waiting for transfers between devices, reduce_grad(): whole = lax.all_gather(piece, CTX, axis=0, tiled=False)  38.4 us
    pallas_call x2, Pallas kernels, attend(): pl.pallas_call(functools.partial(forward_kernel, masked), grid_spec=pltpu...  34.3 us
  transfers between devices with their start and end apart: 52, of which 42 were waited for; matrix products, arithmetic and copies ran while one was open for 10% of the time, Pallas kernels for 3%

profile of v1, /device:TPU:0, one launch (start us, length us, event | category | flops | bytes accessed | tf_op | source)
XLA Modules:
  0.0 1068.3 jit_solution(7250922773528288230)
XLA Ops:
  22.6 27.3 %all-gather.22.cloned.1.call-done = bf16[1024,2048]{1,0:T(8,128)(2,1)} async-done(((bf16[128,2048]{1,0:T(8,128)(2,1)}), bf16[1024,2048]{1,0:T(8,128)(2,1)}) %all-gather.22.cloned.1.call-update) | async-done | bytes 4194320 | tf_op jit(solution)/shard_map/all_gather | solution.py:359
  58.1 22.1 %all-gather.30.cloned.1.call-done = bf16[1024,1024]{1,0:T(8,128)(2,1)} async-done(((bf16[128,1024]{1,0:T(8,128)(2,1)}), bf16[1024,1024]{1,0:T(8,128)(2,1)}) %all-gather.30.cloned.1.call-update) | async-done | bytes 2097168 | tf_op jit(solution)/shard_map/all_gather | solution.py:359
  129.4 18.1 %attend_self.1 = (bf16[256,1024]{1,0:T(8,128)(2,1)}, f32[4,2,64,512]{3,2,1,0:T(8,128)}, f32[4,2,8,512]{3,2,1,0:T(8,128)}) custom-call(s32[20]{0:T(128)} %pad_add_fusion.1.table, bf16[256,1024]{1,0:T(8,128)(2,1)} %get-tuple-element.66.refs_0_, bf16[2048,1024]{1,0:T(8,128)(2,1)} %all-gather.24.cloned.1.call-done.refs_1_.refs_2_, ...), custom_call_target="tpu_custom_call" | custom-call | flops 2147483648 | bytes 8388608 | tf_op jit(solution)/shard_map/attend_self/pallas_call | solution.py:248
  161.1 27.3 %all-gather.28.cloned.1.call-done = bf16[1024,1024]{1,0:T(8,128)(2,1)} async-done(((bf16[128,1024]{1,0:T(8,128)(2,1)}), bf16[1024,1024]{1,0:T(8,128)(2,1)}) %all-gather.28.cloned.1.call-update) | async-done | bytes 2097168 | tf_op jit(solution)/shard_map/all_gather | solution.py:359
  191.6 21.2 %all-gather.32.cloned.1.call-done.refs_1_.refs_2_ = bf16[512,1024]{1,0:T(8,128)(2,1)} async-done(((bf16[64,1024]{1,0:T(8,128)(2,1)}), bf16[512,1024]{1,0:T(8,128)(2,1)}) %all-gather.32.cloned.1.call-update) | async-done | bytes 1048592 | tf_op jit(solution)/shard_map/all_gather | solution.py:460
  245.4 67.3 %all-gather.36.cloned.1.call-done = bf16[1024,5632]{1,0:T(8,128)(2,1)} async-done(((bf16[128,5632]{1,0:T(8,128)(2,1)}), bf16[1024,5632]{1,0:T(8,128)(2,1)}) %all-gather.36.cloned.1.call-update) | async-done | bytes 11534352 | tf_op jit(solution)/shard_map/all_gather | solution.py:359
  325.1 33.3 %all-gather.38.cloned.1.call-done = bf16[2816,1024]{1,0:T(8,128)(2,1)} async-done(((bf16[352,1024]{1,0:T(8,128)(2,1)}), bf16[2816,1024]{1,0:T(8,128)(2,1)}) %all-gather.38.cloned.1.call-update) | async-done | bytes 5767184 | tf_op jit(solution)/shard_map/all_gather | solution.py:359
  378.1 16.4 %attend_cross_back.1 = (bf16[256,1024]{1,0:T(8,128)(2,1)}, bf16[2,512,512]{2,1,0:T(8,128)(2,1)}) custom-call(s32[20]{0:T(128)} %pad_add_fusion.1.table, bf16[256,1024]{1,0:T(8,128)(2,1)} %convolution_convert_fusion.10.refs_0_, bf16[512,1024]{1,0:T(8,128)(2,1)} %all-gather.32.cloned.1.call-done.refs_1_.refs_2_, ...), custom_call_target="tpu_custom_call" | custom-call | flops 1342177280 | bytes 4194304 | tf_op jit(solution)/shard_map/attend_cross_back/pallas_call | solution.py:286
  400.8 29.1 %attend_self_back.1 = (bf16[256,1024]{1,0:T(8,128)(2,1)}, bf16[2,2048,512]{2,1,0:T(8,128)(2,1)}, f32[4,4,512]{2,1,0:T(4,128)}) custom-call(s32[20]{0:T(128)} %pad_add_fusion.1.table, bf16[256,1024]{1,0:T(8,128)(2,1)} %get-tuple-element.66.refs_0_, bf16[2048,1024]{1,0:T(8,128)(2,1)} %all-gather.24.cloned.1.call-done.refs_1_.refs_2_, ...), custom_call_target="tpu_custom_call" | custom-call | flops 5368709120 | bytes 16777216 | tf_op jit(solution)/shard_map/attend_self_back/pallas_call | solution.py:286
  440.7 43.9 %reduce-scatter.17.cloned.1.call-done = bf16[2,256,512]{2,1,0:T(8,128)(2,1)} async-done(((bf16[2,2048,512]{2,1,0:T(8,128)(2,1)}), bf16[2,256,512]{2,1,0:T(8,128)(2,1)}) %reduce-scatter.17.cloned.1.call-update) | async-done | bytes 524304 | tf_op jit(solution)/shard_map/reduce_scatter | solution.py:515
  525.3 36.7 %reduce-scatter.45.cloned.1.call-done = bf16[704,512]{1,0:T(8,128)(2,1)} async-done(((bf16[2816,512]{1,0:T(8,128)(2,1)}), bf16[704,512]{1,0:T(8,128)(2,1)}) %reduce-scatter.45.cloned.1.call-update) | async-done | bytes 720912 | tf_op jit(solution)/shard_map/reduce_scatter | solution.py:382
  562.1 38.7 %reduce-scatter.21.cloned.1.call-done = bf16[256,1024]{1,0:T(8,128)(2,1)} async-done(((bf16[1024,1024]{1,0:T(8,128)(2,1)}), bf16[256,1024]{1,0:T(8,128)(2,1)}) %reduce-scatter.21.cloned.1.call-update) | async-done | bytes 524304 | tf_op jit(solution)/shard_map/reduce_scatter | solution.py:382
  600.9 68.4 %reduce-scatter.41.cloned.1.call-done = bf16[256,2816]{1,0:T(8,128)(2,1)} async-done(((bf16[1024,2816]{1,0:T(8,128)(2,1)}), bf16[256,2816]{1,0:T(8,128)(2,1)}) %reduce-scatter.41.cloned.1.call-update) | async-done | bytes 1441808 | tf_op jit(solution)/shard_map/reduce_scatter | solution.py:382
  669.4 31.2 %reduce-scatter.37.cloned.1.call-done = bf16[256,512]{1,0:T(8,128)(2,1)} async-done(((bf16[1024,512]{1,0:T(8,128)(2,1)}), bf16[256,512]{1,0:T(8,128)(2,1)}) %reduce-scatter.37.cloned.1.call-update) | async-done | bytes 262160 | tf_op jit(solution)/shard_map/reduce_scatter | solution.py:382
  700.7 31.2 %reduce-scatter.29.cloned.1.call-done = bf16[256,512]{1,0:T(8,128)(2,1)} async-done(((bf16[1024,512]{1,0:T(8,128)(2,1)}), bf16[256,512]{1,0:T(8,128)(2,1)}) %reduce-scatter.29.cloned.1.call-update) | async-done | bytes 262160 | tf_op jit(solution)/shard_map/reduce_scatter | solution.py:382
  731.9 31.2 %reduce-scatter.25.cloned.1.call-done = bf16[256,512]{1,0:T(8,128)(2,1)} async-done(((bf16[1024,512]{1,0:T(8,128)(2,1)}), bf16[256,512]{1,0:T(8,128)(2,1)}) %reduce-scatter.25.cloned.1.call-update) | async-done | bytes 262160 | tf_op jit(solution)/shard_map/reduce_scatter | solution.py:382
  763.2 31.2 %reduce-scatter.33.cloned.1.call-done = bf16[256,512]{1,0:T(8,128)(2,1)} async-done(((bf16[1024,512]{1,0:T(8,128)(2,1)}), bf16[256,512]{1,0:T(8,128)(2,1)}) %reduce-scatter.33.cloned.1.call-update) | async-done | bytes 262160 | tf_op jit(solution)/shard_map/reduce_scatter | solution.py:382
  794.6 25.2 %reduce-scatter.47.cloned.1.call-done = bf16[176,512]{1,0:T(8,128)(2,1)} async-done(((bf16[704,512]{1,0:T(8,128)(2,1)}), bf16[176,512]{1,0:T(8,128)(2,1)}) %reduce-scatter.47.cloned.1.call-update) | async-done | bytes 180240 | tf_op jit(solution)/shard_map/reduce_scatter | solution.py:383
  819.8 23.0 %reduce-scatter.23.cloned.1.call-done = bf16[64,1024]{1,0:T(8,128)(2,1)} async-done(((bf16[256,1024]{1,0:T(8,128)(2,1)}), bf16[64,1024]{1,0:T(8,128)(2,1)}) %reduce-scatter.23.cloned.1.call-update) | async-done | bytes 131088 | tf_op jit(solution)/shard_map/reduce_scatter | solution.py:383
  845.1 31.7 %reduce-scatter.43.cloned.1.call-done = bf16[64,2816]{1,0:T(8,128)(2,1)} async-done(((bf16[256,2816]{1,0:T(8,128)(2,1)}), bf16[64,2816]{1,0:T(8,128)(2,1)}) %reduce-scatter.43.cloned.1.call-update) | async-done | bytes 360464 | tf_op jit(solution)/shard_map/reduce_scatter | solution.py:383
  876.9 21.0 %reduce-scatter.39.cloned.1.call-done = bf16[64,512]{1,0:T(8,128)(2,1)} async-done(((bf16[256,512]{1,0:T(8,128)(2,1)}), bf16[64,512]{1,0:T(8,128)(2,1)}) %reduce-scatter.39.cloned.1.call-update) | async-done | bytes 65552 | tf_op jit(solution)/shard_map/reduce_scatter | solution.py:383
  939.2 16.5 %all-gather.2 = bf16[512,512]{1,0:T(8,128)(2,1)S(1)} all-gather(bf16[64,512]{1,0:T(8,128)(2,1)} %reduce-scatter.27.cloned.1.call-done), channel_id=4, replica_groups=mesh['line'=4,'core'=2,'fsdp'=4] {'line','core'}, dimensions={0}, use_global_device_ids=true | all-gather | bytes 589824 | tf_op jit(solution)/shard_map/all_gather | solution.py:384
  967.0 17.3 %all-gather.4 = bf16[512,512]{1,0:T(8,128)(2,1)S(1)} all-gather(bf16[64,512]{1,0:T(8,128)(2,1)} %reduce-scatter.35.cloned.1.call-done), channel_id=6, replica_groups=mesh['line'=4,'core'=2,'fsdp'=4] {'line','core'}, dimensions={0}, use_global_device_ids=true | all-gather | bytes 589824 | tf_op jit(solution)/shard_map/all_gather | solution.py:384
  1018.2 31.4 %all-gather.42.cloned.1.call-done = bf16[512,2816]{1,0:T(8,128)(2,1)} async-done(((bf16[64,2816]{1,0:T(8,128)(2,1)}), bf16[512,2816]{1,0:T(8,128)(2,1)}) %all-gather.42.cloned.1.call-update) | async-done | bytes 2883600 | tf_op jit(solution)/shard_map/all_gather | solution.py:384
  (373 shorter events, 307.9 us)
Async XLA Ops:
  11.1 118.3 %all-gather.24.cloned.1.call-start = ((), (), s32[]{:S(2)}) async-start(), calls=%async_computation.17 | async-start | bytes 4718592 | tf_op jit(solution)/shard_map/all_gather | solution.py:454
  56.3 132.2 %all-gather.28.cloned.1.call-start = ((), (), s32[]{:S(2)}) async-start(), calls=%async_computation.19 | async-start | bytes 2359296 | tf_op jit(solution)/shard_map/all_gather | solution.py:359
  58.0 154.8 %all-gather.32.cloned.1.call-start = ((), (), s32[]{:S(2)}) async-start(), calls=%async_computation.21 | async-start | bytes 1179648 | tf_op jit(solution)/shard_map/all_gather | solution.py:460
  82.9 159.8 %all-gather.34.cloned.1.call-start = ((), (), s32[]{:S(2)}) async-start(), calls=%async_computation.22 | async-start | bytes 2359296 | tf_op jit(solution)/shard_map/all_gather | solution.py:359
  84.6 228.1 %all-gather.36.cloned.1.call-start = ((), (), s32[]{:S(2)}) async-start(), calls=%async_computation.23 | async-start | bytes 12976128 | tf_op jit(solution)/shard_map/all_gather | solution.py:359
  87.1 271.3 %all-gather.38.cloned.1.call-start = ((), (), s32[]{:S(2)}) async-start(), calls=%async_computation.24 | async-start | bytes 6488064 | tf_op jit(solution)/shard_map/all_gather | solution.py:359
  88.1 396.6 %reduce-scatter.17.cloned.1.call-start = ((), (), s32[]{:S(2)}) async-start(), calls=%async_computation.25 | async-start | bytes 4718592 | tf_op jit(solution)/shard_map/reduce_scatter | solution.py:515
  430.6 131.4 %reduce-scatter.45.cloned.1.call-start = ((), (), s32[]{:S(2)}) async-start(), calls=%async_computation.39 | async-start | bytes 3604480 | tf_op jit(solution)/shard_map/reduce_scatter | solution.py:382
  439.5 161.3 %reduce-scatter.21.cloned.1.call-start = ((), (), s32[]{:S(2)}) async-start(), calls=%async_computation.27 | async-start | bytes 2621440 | tf_op jit(solution)/shard_map/reduce_scatter | solution.py:382
  491.3 178.0 %reduce-scatter.41.cloned.1.call-start = ((), (), s32[]{:S(2)}) async-start(), calls=%async_computation.37 | async-start | bytes 7208960 | tf_op jit(solution)/shard_map/reduce_scatter | solution.py:382
  507.9 192.7 %reduce-scatter.37.cloned.1.call-start = ((), (), s32[]{:S(2)}) async-start(), calls=%async_computation.35 | async-start | bytes 1310720 | tf_op jit(solution)/shard_map/reduce_scatter | solution.py:382
  513.0 218.9 %reduce-scatter.29.cloned.1.call-start = ((), (), s32[]{:S(2)}) async-start(), calls=%async_computation.31 | async-start | bytes 1310720 | tf_op jit(solution)/shard_map/reduce_scatter | solution.py:382
  517.1 246.1 %reduce-scatter.25.cloned.1.call-start = ((), (), s32[]{:S(2)}) async-start(), calls=%async_computation.29 | async-start | bytes 1310720 | tf_op jit(solution)/shard_map/reduce_scatter | solution.py:382
  521.3 273.2 %reduce-scatter.33.cloned.1.call-start = ((), (), s32[]{:S(2)}) async-start(), calls=%async_computation.33 | async-start | bytes 1310720 | tf_op jit(solution)/shard_map/reduce_scatter | solution.py:382
  525.3 294.5 %reduce-scatter.47.cloned.1.call-start = ((), (), s32[]{:S(2)}) async-start(), calls=%async_computation.40 | async-start | bytes 901120 | tf_op jit(solution)/shard_map/reduce_scatter | solution.py:383
  562.0 280.8 %reduce-scatter.23.cloned.1.call-start = ((), (), s32[]{:S(2)}) async-start(), calls=%async_computation.28 | async-start | bytes 655360 | tf_op jit(solution)/shard_map/reduce_scatter | solution.py:383
  600.8 276.0 %reduce-scatter.43.cloned.1.call-start = ((), (), s32[]{:S(2)}) async-start(), calls=%async_computation.38 | async-start | bytes 1802240 | tf_op jit(solution)/shard_map/reduce_scatter | solution.py:383
  669.3 228.6 %reduce-scatter.39.cloned.1.call-start = ((), (), s32[]{:S(2)}) async-start(), calls=%async_computation.36 | async-start | bytes 327680 | tf_op jit(solution)/shard_map/reduce_scatter | solution.py:383
  700.6 217.7 %reduce-scatter.31.cloned.1.call-start = ((), (), s32[]{:S(2)}) async-start(), calls=%async_computation.32 | async-start | bytes 327680 | tf_op jit(solution)/shard_map/reduce_scatter | solution.py:383
  731.9 207.3 %reduce-scatter.27.cloned.1.call-start = ((), (), s32[]{:S(2)}) async-start(), calls=%async_computation.30 | async-start | bytes 327680 | tf_op jit(solution)/shard_map/reduce_scatter | solution.py:383
  763.2 203.8 %reduce-scatter.35.cloned.1.call-start = ((), (), s32[]{:S(2)}) async-start(), calls=%async_computation.34 | async-start | bytes 327680 | tf_op jit(solution)/shard_map/reduce_scatter | solution.py:383
  794.5 204.6 %all-gather.44.cloned.1.call-start = ((), (), s32[]{:S(2)}) async-start(), calls=%async_computation.43 | async-start | bytes 1622016 | tf_op jit(solution)/shard_map/all_gather | solution.py:384
  819.8 192.5 %all-gather.40.cloned.1.call-start = ((), (), s32[]{:S(2)}) async-start(), calls=%async_computation.41 | async-start | bytes 1179648 | tf_op jit(solution)/shard_map/all_gather | solution.py:384
  842.8 206.7 %all-gather.42.cloned.1.call-start = ((), (), s32[]{:S(2)}) async-start(), calls=%async_computation.42 | async-start | bytes 3244032 | tf_op jit(solution)/shard_map/all_gather | solution.py:384
  (85 other events, 2323.0 us)
Sparse Core Ops, SparseCore 0:
  10.5 39.2 all-gather.21
  52.3 27.7 all-gather.29
  82.3 47.0 all-gather.23
  131.7 26.6 all-gather.25
  160.7 27.7 all-gather.27
  190.5 22.2 all-gather.31
  215.2 27.3 all-gather.33
  245.1 67.5 all-gather.35
  315.2 43.1 all-gather.37
  430.0 54.5 reduce-scatter.16
  487.5 31.0 reduce-scatter.18
  522.1 39.8 reduce-scatter.44
  565.5 35.1 reduce-scatter.20
  603.6 65.6 reduce-scatter.40
  672.6 27.9 reduce-scatter.36
  703.9 27.9 reduce-scatter.28
  735.2 27.9 reduce-scatter.24
  766.5 27.9 reduce-scatter.32
  796.8 22.9 reduce-scatter.46
  821.9 20.8 reduce-scatter.22
  845.1 31.6 reduce-scatter.42
  962.0 26.7 all-gather.43
  990.2 22.0 all-gather.39
  1014.0 35.5 all-gather.41
  (4 shorter events, 74.3 us)

commit v2 on v1

--- a/solution.py
+++ b/solution.py
@@ -339,59 +339,158 @@
     return [(index, index ^ bit) for index in range(size)]
 
 
+def bits_of(size):
+    return [1 << place for place in range(size.bit_length() - 1)]
+
+
+def cross(value, axis, bit):
+    return lax.ppermute(value, axis, partners(lax.axis_size(axis), bit))
+
+
+def swap(value):
+    return cross(value, "core", 1)
+
+
+def after(value, *earlier):
+    return lax.optimization_barrier((value,) + earlier)[0]
+
+
 def sum_everywhere(value):
     for axis in ("core", "line", "fsdp"):
-        size = lax.axis_size(axis)
-        bit = 1
-        while bit < size:
-            value = value + lax.ppermute(value, axis, partners(size, bit))
-            bit = bit * 2
+        for bit in bits_of(lax.axis_size(axis)):
+            value = value + cross(value, axis, bit)
     return value
 
 
-def half_rows(part):
-    half = part.shape[0] // 2
-    return lax.dynamic_slice_in_dim(part, lax.axis_index("core") * half, half, axis=0)
-
-
-def fetch(*parts):
-    joined = parts[0] if len(parts) == 1 else jnp.concatenate(parts, axis=1)
-    return lax.all_gather(half_rows(joined), ("fsdp", "core"), axis=0, tiled=True)
-
-
-def swap(value):
-    return lax.ppermute(value, "core", [(0, 1), (1, 0)])
-
-
-def my_columns(value, other=False):
+def add(left, right):
+    return (left.astype(F32) + right.astype(F32)).astype(BF16)
+
+
+def blank(shape):
+    return pl.pallas_call(
+        lambda out_ref: None,
+        out_shape=jax.ShapeDtypeStruct(shape, BF16),
+        out_specs=pl.BlockSpec(memory_space=pl.ANY),
+        name="blank",
+    )()
+
+
+def spread(have, axis, bits):
+    for bit in bits:
+        have = have + [(mask ^ bit, cross(piece, axis, bit)) for mask, piece in have]
+    return have
+
+
+def gather_small(value):
+    size = lax.axis_size("fsdp")
+    me = lax.axis_index("fsdp")
+    whole = jnp.zeros((size, value.shape[0]), value.dtype)
+    for mask, piece in spread([(0, value)], "fsdp", bits_of(size)):
+        whole = lax.dynamic_update_slice(whole, piece[None], (me ^ mask, 0))
+    return whole
+
+
+def columns_of(value, core):
     half = value.shape[1] // 2
+    return lax.dynamic_slice_in_dim(value, core * half, half, axis=1)
+
+
+def gather_weights(parts, earlier):
+    size = lax.axis_size("fsdp")
+    me = lax.axis_index("fsdp")
     core = lax.axis_index("core")
-    core = 1 - core if other else core
-    return lax.dynamic_slice_in_dim(value, core * half, half, axis=1)
+    mine = jnp.concatenate([columns_of(part, core) for part in parts], axis=1)
+    mine = after(mine, *earlier)
+    rows, width = mine.shape
+    bits = bits_of(size)
+    half = rows // 2
+    whole = lax.dynamic_update_slice(blank((size * rows, width)), mine, (me * rows, 0))
+    first = []
+    for stream in range(2):
+        order = bits if stream == 0 else bits[::-1]
+        have = spread([(0, mine[stream * half : (stream + 1) * half])], "fsdp", order)
+        first.append(have[1][1])
+        for mask, piece in have[1:]:
+            start = (me ^ mask) * rows + stream * half
+            whole = lax.dynamic_update_slice(whole, piece, (start, 0))
+    other = swap(whole)
+    return whole, other, first
+
+
+def by_core(mine, other):
+    first = lax.axis_index("core") == 0
+    return jnp.where(first, mine, other), jnp.where(first, other, mine)
 
 
 def weight_grad(hidden, hidden_swapped, *grads):
-    mine = jnp.concatenate([my_columns(item) for item in grads], axis=1)
-    other = swap(jnp.concatenate([my_columns(item, True) for item in grads], axis=1))
+    core = lax.axis_index("core")
+    mine = jnp.concatenate([columns_of(item, core) for item in grads], axis=1)
+    other = swap(jnp.concatenate([columns_of(item, 1 - core) for item in grads], axis=1))
     both_hidden = jnp.concatenate([hidden, hidden_swapped], axis=0)
     both_grad = jnp.concatenate([mine, other], axis=0)
     return tn(both_hidden, both_grad).astype(BF16)
 
 
+def halve(value, axis, bit, place):
+    mine = (lax.axis_index(axis) // bit) % 2
+    keep = lax.dynamic_index_in_dim(value, mine, place, keepdims=False)
+    send = lax.dynamic_index_in_dim(value, 1 - mine, place, keepdims=False)
+    return add(keep, cross(send, axis, bit))
+
+
 def reduce_grad(partial, widths):
-    shard = lax.psum_scatter(partial, "fsdp", scatter_dimension=0, tiled=True)
-    piece = lax.psum_scatter(shard, "line", scatter_dimension=0, tiled=True)
-    whole = lax.all_gather(piece, CTX, axis=0, tiled=False)
+    size = lax.axis_size("fsdp")
     lines = lax.axis_size("line")
-    whole = whole.reshape(lines, 2, piece.shape[0], piece.shape[1])
-    rows = lines * piece.shape[0]
+    rows = partial.shape[0] // size
+    width = partial.shape[1]
+    bits = bits_of(size)
+    folded = partial.reshape([2] * len(bits) + [2, rows // 2, width])
+    sums = []
+    for stream in range(2):
+        order = bits if stream == 0 else bits[::-1]
+        value = lax.index_in_dim(folded, stream, len(bits), keepdims=False)
+        left = bits[::-1]
+        for bit in order:
+            place = left.index(bit)
+            value = halve(value, "fsdp", bit, place)
+            left = [item for item in left if item != bit]
+        sums.append(value)
+    shard = jnp.stack(sums)
+    line_bits = bits_of(lines)
+    value = shard.reshape([2] * len(line_bits) + [rows // lines, width])
+    for bit in line_bits:
+        value = halve(value, "line", bit, value.ndim - 3)
+    have = spread([(0, value)], "line", line_bits[::-1])
+    have = [piece for _, piece in sorted(have, key=lambda item: item[0])]
+    mine = jnp.stack(have)
+    other = swap(mine)
+    me = lax.axis_index("line")
     outs = []
     start = 0
-    for width in widths:
-        part = whole[..., start : start + width // 2]
-        outs.append(part.transpose(0, 2, 1, 3).reshape(rows, width).astype(F32))
-        start = start + width // 2
+    for wide in widths:
+        part = slice(start, start + wide // 2)
+        both = jnp.concatenate(by_core(mine[..., part], other[..., part]), axis=2)
+        ordered = [lax.dynamic_index_in_dim(both, me ^ index, 0, keepdims=False) for index in range(lines)]
+        outs.append(jnp.concatenate(ordered, axis=0).astype(F32))
+        start = start + wide // 2
     return outs
+
+
+def gather_context(value):
+    have = spread([(0, value)], "line", bits_of(lax.axis_size("line"))[::-1])
+    have = [piece for _, piece in sorted(have, key=lambda item: item[0])]
+    return jnp.concatenate(have + [swap(piece) for piece in have], axis=0)
+
+
+def reduce_context(value):
+    lines = lax.axis_size("line")
+    two, total, width = value.shape
+    value = value.reshape(two, 2, lines, total // (2 * lines), width)
+    value = add(value[:, 0], swap(value[:, 1]))
+    for bit in bits_of(lines):
+        value = value.reshape(two, value.shape[1] // 2, 2, value.shape[2], width)
+        value = add(value[:, :, 0], cross(value[:, :, 1], "line", bit))
+    return value[:, 0]
 
 
 def body(
@@ -416,25 +515,37 @@
 
     small = jnp.concatenate([gain_self, gain_cross, gain_ffn, bias_table.reshape(-1)])
     share = gain_self.shape[0]
-    small = lax.all_gather(small, "fsdp", axis=0, tiled=False)
-    gains = [
+    small = gather_small(small)
+    gain_one, gain_two, gain_three = [
         small[:, index * share : (index + 1) * share].reshape(D).astype(F32) for index in range(3)
     ]
-    gain_one, gain_two, gain_three = gains
     table_whole = small[:, 3 * share :].reshape(BUCKETS, HEADS)
 
-    wqkv = fetch(w_query, w_key, w_value)
-    wo = fetch(w_out)
-    wcq = fetch(c_query)
-    wckv = fetch(c_key, c_value)
-    wco = fetch(c_out)
-    wgu = fetch(w_gate, w_up)
-    wd = fetch(w_down)
+    joint = jnp.concatenate
+    qkv_mine, qkv_other, first = gather_weights((joint([w_query, w_key, w_value], axis=1),), ())
+    mid_mine, mid_other, first = gather_weights((w_out, c_query, joint([c_key, c_value], axis=1), c_out), first)
+    gu_mine, gu_other, first = gather_weights((joint([w_gate, w_up], axis=1),), first)
+    wd_mine, wd_other, first = gather_weights((w_down,), first)
+    halves = D // 2
+    wo, wcq, wckv, wco = [
+        (mid_mine[:, index * halves : (index + 1) * halves], mid_other[:, index * halves : (index + 1) * halves])
+        for index in range(4)
+    ]
+    core = lax.axis_index("core")
     hidden_ff = w_gate.shape[1]
+
+    def times(left, weight):
+        return joint(by_core(nn(left, weight[0]), nn(left, weight[1])), axis=1)
+
+    def times_back(grad, weight):
+        return nt(columns_of(grad, core), weight[0]) + nt(columns_of(grad, 1 - core), weight[1])
 
     query_blocks = lax.dynamic_slice_in_dim(block_order, context * pair, pair)
     slots = jnp.arange(contexts * pair, dtype=jnp.int32)
-    inverse = jnp.sum(jnp.where(block_order[None, :] == slots[:, None], slots[None, :], 0), axis=1)
+    owner = slots // pair
+    near = ((owner % 2) ^ core) * lines + ((owner // 2) ^ lax.axis_index("line"))
+    slots_near = near * pair + slots % pair
+    inverse = jnp.sum(jnp.where(block_order[None, :] == slots[:, None], slots_near[None, :], 0), axis=1)
     docs = doc_ids.reshape(length)
     query_docs = jnp.stack(
         [lax.dynamic_slice_in_dim(docs, query_blocks[index] * BLOCK, BLOCK) for index in range(pair)]
@@ -449,33 +560,31 @@
 
     flat_in = inputs.reshape(rows, width).astype(F32)
     normed_one, scale_one, hidden_one = norm_rows(flat_in, gain_one)
-    packed = nn(hidden_one, wqkv).astype(BF16)
-    query = packed[:, :D]
-    pairs_whole = lax.all_gather(packed[:, D:], CTX, axis=0, tiled=True)
+    query, pairs = by_core(nn(hidden_one, qkv_mine).astype(BF16), nn(hidden_one, qkv_other).astype(BF16))
+    pairs_whole = gather_context(pairs)
     attention, outs_one, logs_one = attend(query, pairs_whole, place_table, extra, True)
-    mid_one = flat_in + nn(attention, wo)
+    mid_one = flat_in + times(attention, wo)
 
     encoder_rows = encoder.reshape(encoder.shape[1], width)
-    encoder_pairs = nn(encoder_rows, wckv).astype(BF16)
-    encoder_whole = lax.all_gather(encoder_pairs, CTX, axis=0, tiled=True)
+    encoder_pairs = times(encoder_rows, wckv).astype(BF16)
+    encoder_whole = gather_context(encoder_pairs)
 
     normed_two, scale_two, hidden_two = norm_rows(mid_one, gain_two)
-    cross_q = nn(hidden_two, wcq).astype(BF16)
-    cross, outs_two, logs_two = attend(cross_q, encoder_whole, place_table, (), False)
-    mid_two = mid_one + nn(cross, wco)
+    cross_q = times(hidden_two, wcq).astype(BF16)
+    crossed, outs_two, logs_two = attend(cross_q, encoder_whole, place_table, (), False)
+    mid_two = mid_one + times(crossed, wco)
     normed_three, scale_three, hidden_three = norm_rows(mid_two, gain_three)
-    gate = nn(hidden_three, wgu[:, :hidden_ff])
-    up = nn(hidden_three, wgu[:, hidden_ff:])
+    gate, up = by_core(nn(hidden_three, gu_mine), nn(hidden_three, gu_other))
     active, gelu_pull = jax.vjp(gelu_tanh, gate)
     mixed = (active * up).astype(BF16)
-    result = mid_two + nn(mixed, wd)
+    result = mid_two + times(mixed, (wd_mine, wd_other))
     layer_out = result.astype(BF16)
     diff = result - teacher.reshape(rows, width).astype(F32)
     squared_local = jnp.sum(mask_rows[:, None] * diff * diff)
     grad_result = token_total / count * mask_rows[:, None] * diff
 
     e_three = grad_result.astype(BF16)
-    grad_mixed = nt(e_three, wd)
+    grad_mixed = times_back(e_three, (wd_mine, wd_other))
     (gelu_slope,) = gelu_pull(grad_mixed * up)
     grad_gate = gelu_slope.astype(BF16)
     grad_up = (grad_mixed * active).astype(BF16)
@@ -483,19 +592,19 @@
     grad_gate_weight, grad_up_weight = reduce_grad(
         weight_grad(hidden_three, swap(hidden_three), grad_gate, grad_up), (hidden_ff, hidden_ff)
     )
-    grad_hidden_three = nt(grad_gate, wgu[:, :hidden_ff]) + nt(grad_up, wgu[:, hidden_ff:])
+    grad_hidden_three = times_back(joint([grad_gate, grad_up], axis=1), (gu_mine, gu_other))
     grad_norm_three, grad_gain_three = norm_back(grad_hidden_three, normed_three, scale_three, gain_three)
     grad_mid_two = grad_result + grad_norm_three
 
     e_two = grad_mid_two.astype(BF16)
-    (grad_cross_out,) = reduce_grad(weight_grad(cross, swap(cross), e_two), (D,))
-    grad_cross = nt(e_two, wco).astype(BF16)
+    (grad_cross_out,) = reduce_grad(weight_grad(crossed, swap(crossed), e_two), (D,))
+    grad_cross = times_back(e_two, wco).astype(BF16)
     grad_cross_q, encoder_grad = attend_back(
         cross_q, encoder_whole, grad_cross, outs_two, logs_two, place_table, (), False
     )
-    encoder_mine = lax.psum_scatter(encoder_grad, CTX, scatter_dimension=1, tiled=True)
+    encoder_mine = reduce_context(encoder_grad)
     encoder_mine = jnp.concatenate([encoder_mine[0], encoder_mine[1]], axis=1)
-    grad_encoder = nt(encoder_mine, wckv)
+    grad_encoder = times_back(encoder_mine, wckv)
     grad_cross_key, grad_cross_value = reduce_grad(
         weight_grad(
             encoder_rows, swap(encoder_rows), encoder_mine[:, :key_width], encoder_mine[:, key_width:]
@@ -503,21 +612,21 @@
         (key_width, key_width),
     )
     (grad_cross_query,) = reduce_grad(weight_grad(hidden_two, swap(hidden_two), grad_cross_q), (D,))
-    grad_norm_two, grad_gain_two = norm_back(nt(grad_cross_q, wcq), normed_two, scale_two, gain_two)
+    grad_norm_two, grad_gain_two = norm_back(times_back(grad_cross_q, wcq), normed_two, scale_two, gain_two)
     grad_mid_one = grad_mid_two + grad_norm_two
 
     e_one = grad_mid_one.astype(BF16)
     (grad_out_weight,) = reduce_grad(weight_grad(attention, swap(attention), e_one), (D,))
-    grad_attention = nt(e_one, wo).astype(BF16)
+    grad_attention = times_back(e_one, wo).astype(BF16)
     grad_query, grad_pairs, grad_vectors = attend_back(
         query, pairs_whole, grad_attention, outs_one, logs_one, place_table, extra, True
     )
-    mine = lax.psum_scatter(grad_pairs, CTX, scatter_dimension=1, tiled=True)
+    mine = reduce_context(grad_pairs)
     grad_packed = jnp.concatenate([grad_query, mine[0], mine[1]], axis=1)
     grad_query_weight, grad_key_weight, grad_value_weight = reduce_grad(
         weight_grad(hidden_one, swap(hidden_one), grad_query, mine[0], mine[1]), (D, key_width, key_width)
     )
-    grad_norm_one, grad_gain_one = norm_back(nt(grad_packed, wqkv), normed_one, scale_one, gain_one)
+    grad_norm_one, grad_gain_one = norm_back(times_back(grad_packed, (qkv_mine, qkv_other)), normed_one, scale_one, gain_one)
     grad_inputs = grad_mid_one + grad_norm_one
 
     grad_table = lax.dot_general(

time: 1070 us -> 787 us (0.74)
  waiting for transfers between devices: 724 us -> 349 us
  starting transfers between devices: 18.3 us -> 160 us
  blocking collectives: 75.1 us -> 0 us
  other arithmetic: 21.9 us -> 49.1 us
  matrix products: 75.4 us -> 90.3 us
  between operations: 19.5 us -> 7.65 us
    reduce_scatter x16 -> x0, waiting for transfers between devices: 423 us -> none  [the longest x7 269 us: reduce_grad(): shard = lax.psum_scatter(partial, 'fsdp', scatter_dimension=0, tiled=True)]
    ppermute x24 -> x145, waiting for transfers between devices: 26.1 us -> 349 us  [cross(): return lax.ppermute(value, axis, partners(lax.axis_size(axis), bit))]
    all_gather x12 -> x0, waiting for transfers between devices: 274 us -> none  [the longest x7 202 us: fetch(): lax.all_gather(half_rows(joined), ('fsdp', 'core'), axis=0, tiled=True)]
    ppermute x24 -> x145, starting transfers between devices: 16.1 us -> 160 us  [cross(): return lax.ppermute(value, axis, partners(lax.axis_size(axis), bit))]
    all_gather x5 -> x0, blocking collectives: 75.1 us -> none  [the longest x4 65.5 us: reduce_grad(): whole = lax.all_gather(piece, CTX, axis=0, tiled=False)]
    dynamic_update_slice x0 -> x32, local copies, waits for them, and re-layouts: none -> 21.4 us  [the longest x24 17.3 us: gather_weights(): whole = lax.dynamic_update_slice(whole, piece, (start, 0))]
    dot_general x8 -> x14, matrix products: 21.1 us -> 36.3 us  [nt(): lax.dot_general(left, right, (((1,), (1,)), ((), ())), preferred_element_...]
    convert_element_type x8 -> x59, other arithmetic: 6 us -> 19.7 us  [the longest x11 13.3 us: reduce_grad(): outs.append(jnp.concatenate(ordered, axis=0).astype(F32))]
  transfers between devices with their start and end apart: 52 -> 145, of which waited for: 42 -> 63; matrix products, arithmetic and copies ran while one was open for 10% -> 24% of each run, Pallas kernels for 3% -> 9%
where the time goes in v2:
time: 787 us; the launch traced here: 788 us
  waiting for transfers between devices  349 us (44%)
  starting transfers between devices  160 us (20%)
  matrix products  90.3 us (11%)
  Pallas kernels  70.5 us (9%)
  local copies, waits for them, and re-layouts  61.7 us (8%)
  other arithmetic  49.1 us (6%)
    ppermute x145, waiting for transfers between devices, cross(): return lax.ppermute(value, axis, partners(lax.axis_size(axis), bit))  349 us
    ppermute x145, starting transfers between devices, cross(): return lax.ppermute(value, axis, partners(lax.axis_size(axis), bit))  160 us
    pallas_call x2, Pallas kernels, attend_back(): pl.pallas_call(functools.partial(backward_kernel, masked), grid_spec=pltp...  40.6 us
    dot_general x14, matrix products, nt(): lax.dot_general(left, right, (((1,), (1,)), ((), ())), preferred_element_...  36.3 us
    dot_general x14, matrix products, nn(): return jnp.dot(left, right, preferred_element_type=F32)  34.2 us
    pallas_call x2, Pallas kernels, attend(): pl.pallas_call(functools.partial(forward_kernel, masked), grid_spec=pltpu...  29.9 us
    dot_general x8, matrix products, tn(): lax.dot_general(left, right, (((0,), (0,)), ((), ())), preferred_element_...  19.6 us
    dynamic_update_slice x24, local copies, waits for them, and re-layouts, gather_weights(): whole = lax.dynamic_update_slice(whole, piece, (start, 0))  17.3 us
  transfers between devices with their start and end apart: 145, of which 63 were waited for; matrix products, arithmetic and copies ran while one was open for 24% of the time, Pallas kernels for 9%

profile of v2, /device:TPU:0, one launch (start us, length us, event | category | flops | bytes accessed | tf_op | source)
XLA Modules:
  0.0 787.8 jit_solution(3566465046835498788)
XLA Ops:
  65.1 14.5 %collective-permute-done.5 = bf16[128,1024]{1,0:T(8,128)(2,1)S(1)} collective-permute-done((bf16[128,1024]{1,0:T(8,128)(2,1)}, bf16[128,1024]{1,0:T(8,128)(2,1)S(1)}, u32[]{:S(2)}, u32[]{:S(2)}) %collective-permute-start.5) | collective-permute-done | bytes 262176 | tf_op jit(solution)/shard_map/ppermute | solution.py:347
  93.7 9.3 %collective-permute-done.19 = bf16[128,2048]{1,0:T(8,128)(2,1)S(1)} collective-permute-done((bf16[128,2048]{1,0:T(8,128)(2,1)S(1)}, bf16[128,2048]{1,0:T(8,128)(2,1)S(1)}, u32[]{:S(2)}, u32[]{:S(2)}) %collective-permute-start.19) | collective-permute-done | bytes 524320 | tf_op jit(solution)/shard_map/ppermute | solution.py:347
  106.6 13.6 %collective-permute-done.22 = bf16[128,2048]{1,0:T(8,128)(2,1)S(1)} collective-permute-done((bf16[128,2048]{1,0:T(8,128)(2,1)S(1)}, bf16[128,2048]{1,0:T(8,128)(2,1)S(1)}, u32[]{:S(2)}, u32[]{:S(2)}) %collective-permute-start.22) | collective-permute-done | bytes 524320 | tf_op jit(solution)/shard_map/ppermute | solution.py:347
  123.4 10.5 %collective-permute-done.32 = bf16[128,2816]{1,0:T(8,128)(2,1)S(1)} collective-permute-done((bf16[128,2816]{1,0:T(8,128)(2,1)S(1)}, bf16[128,2816]{1,0:T(8,128)(2,1)S(1)}, u32[]{:S(2)}, u32[]{:S(2)}) %collective-permute-start.32) | collective-permute-done | bytes 720928 | tf_op jit(solution)/shard_map/ppermute | solution.py:347
  142.9 14.2 %collective-permute-done.33 = bf16[128,2816]{1,0:T(8,128)(2,1)S(1)} collective-permute-done((bf16[128,2816]{1,0:T(8,128)(2,1)S(1)}, bf16[128,2816]{1,0:T(8,128)(2,1)S(1)}, u32[]{:S(2)}, u32[]{:S(2)}) %collective-permute-start.33) | collective-permute-done | bytes 720928 | tf_op jit(solution)/shard_map/ppermute | solution.py:347
  178.5 10.7 %collective-permute-done.11 = bf16[256,1024]{1,0:T(8,128)(2,1)S(1)} collective-permute-done((bf16[256,1024]{1,0:T(8,128)(2,1)S(1)}, bf16[256,1024]{1,0:T(8,128)(2,1)S(1)}, u32[]{:S(2)}, u32[]{:S(2)}) %collective-permute-start.11) | collective-permute-done | bytes 524320 | tf_op jit(solution)/shard_map/ppermute | solution.py:347
  191.5 8.8 %collective-permute-done.10 = bf16[256,1024]{1,0:T(8,128)(2,1)S(1)} collective-permute-done((bf16[256,1024]{1,0:T(8,128)(2,1)S(1)}, bf16[256,1024]{1,0:T(8,128)(2,1)S(1)}, u32[]{:S(2)}, u32[]{:S(2)}) %collective-permute-start.10) | collective-permute-done | bytes 524320 | tf_op jit(solution)/shard_map/ppermute | solution.py:347
  212.2 13.7 %attend_self.1 = (bf16[256,1024]{1,0:T(8,128)(2,1)}, f32[4,2,64,512]{3,2,1,0:T(8,128)}, f32[4,2,8,512]{3,2,1,0:T(8,128)}) custom-call(s32[20]{0:T(128)} %pad_add_fusion.1.table, bf16[256,1024]{1,0:T(8,128)(2,1)} %get-tuple-element.124.refs_0_, bf16[2048,1024]{1,0:T(8,128)(2,1)} %copy-done.59, bf16[2048,1024]{1,0:T(8,128)(2,1)} %copy-done.59, ...), custom_call_target="tpu_custom_call" | custom-call | flops 2147483648 | bytes 8388608 | tf_op jit(solution)/shard_map/attend_self/pallas_call | solution.py:248
  256.7 16.2 %attend_cross.1 = (bf16[256,1024]{1,0:T(8,128)(2,1)}, f32[4,2,64,512]{3,2,1,0:T(8,128)}, f32[4,2,8,512]{3,2,1,0:T(8,128)}) custom-call(s32[20]{0:T(128)} %pad_add_fusion.1.table, bf16[256,1024]{1,0:T(8,128)(2,1)} %pad_maximum_fusion.5.refs_0_, bf16[512,1024]{1,0:T(8,128)(2,1)} %constant_dynamic-update-slice_fusion.36.refs_1_.refs_2_, ...), custom_call_target="tpu_custom_call" | custom-call | flops 536870912 | bytes 2097152 | tf_op jit(solution)/shard_map/attend_cross/pallas_call | solution.py:248
  320.8 16.4 %attend_cross_back.1 = (bf16[256,1024]{1,0:T(8,128)(2,1)}, bf16[2,512,512]{2,1,0:T(8,128)(2,1)}) custom-call(s32[20]{0:T(128)} %pad_add_fusion.1.table, bf16[256,1024]{1,0:T(8,128)(2,1)} %pad_maximum_fusion.5.refs_0_, bf16[512,1024]{1,0:T(8,128)(2,1)} %constant_dynamic-update-slice_fusion.36.refs_1_.refs_2_, ...), custom_call_target="tpu_custom_call" | custom-call | flops 1342177280 | bytes 4194304 | tf_op jit(solution)/shard_map/attend_cross_back/pallas_call | solution.py:286
  348.7 24.2 %attend_self_back.1 = (bf16[256,1024]{1,0:T(8,128)(2,1)}, bf16[2,2048,512]{2,1,0:T(8,128)(2,1)}, f32[4,4,512]{2,1,0:T(4,128)}) custom-call(s32[20]{0:T(128)} %pad_add_fusion.1.table, bf16[256,1024]{1,0:T(8,128)(2,1)} %get-tuple-element.124.refs_0_, bf16[2048,1024]{1,0:T(8,128)(2,1)} %copy-done.59, bf16[2048,1024]{1,0:T(8,128)(2,1)} %copy-done.59, ...), custom_call_target="tpu_custom_call" | custom-call | flops 5368709120 | bytes 16777216 | tf_op jit(solution)/shard_map/attend_self_back/pallas_call | solution.py:286
  389.7 10.6 %collective-permute-start.75 = (bf16[2,128,512]{2,1,0:T(8,128)(2,1)S(1)}, bf16[2,128,512]{2,1,0:T(8,128)(2,1)S(1)}, u32[]{:S(2)}, u32[]{:S(2)}) collective-permute-start(bf16[2,128,512]{2,1,0:T(8,128)(2,1)S(1)} %dynamic-slice_bitcast_fusion.18), channel_id=1, source_target_pairs={{0,1},{1,0},{2,3},{3,2},{4,5},{5,4},{6,7},{7,6},{8,9},{9,8},{10,11... | collective-permute-start | bytes 786440 | tf_op jit(solution)/shard_map/ppermute | solution.py:347
  415.0 13.0 %collective-permute-start.59 = (bf16[2,2,64,512]{3,2,1,0:T(8,128)(2,1)S(1)}, bf16[2,2,64,512]{3,2,1,0:T(8,128)(2,1)S(1)}, u32[]{:S(2)}, u32[]{:S(2)}) collective-permute-start(bf16[2,2,64,512]{3,2,1,0:T(8,128)(2,1)S(1)} %slice_bitcast_fusion.6), channel_id=1, source_target_pairs={{0,8},{8,0},{16,24},{24,16},{1,9},{9,1},{17,25},{25,17},{2,10},{10... | collective-permute-start | bytes 786440 | tf_op jit(solution)/shard_map/ppermute | solution.py:347
  522.0 7.9 %convolution_convert_fusion = bf16[1024,2816]{1,0:T(8,128)(2,1)S(1)} fusion(bf16[256,2816]{1,0:T(8,128)(2,1)S(1)} %collective-permute-done.122, bf16[256,1408]{1,0:T(8,128)(2,1)S(1)} %copy-done.38, bf16[256,1408]{1,0:T(8,128)(2,1)S(1)} %copy-done.39, bf16[256,1024]{1,0:T(8,128)(2,1)S(1)} %collective-permute-done.121, bf16[256,1024]{1,0:T(8,128)(2,1)S(1)} %copy-done.45), kind=kOutput, calls=%fused_computation.1 | convolution fusion | flops 2966421504 | bytes 9699328 | tf_op jit(solution)/shard_map/dot_general | solution.py:318
  552.8 32.6 %collective-permute-done.135 = bf16[2,352,512]{2,1,0:T(8,128)(2,1)S(1)} collective-permute-done((bf16[2,352,512]{2,1,0:T(8,128)(2,1)S(1)}, bf16[2,352,512]{2,1,0:T(8,128)(2,1)S(1)}, u32[]{:S(2)}, u32[]{:S(2)}) %collective-permute-start.135) | collective-permute-done | bytes 720928 | tf_op jit(solution)/shard_map/ppermute | solution.py:347
  604.8 23.8 %collective-permute-done.139 = bf16[2,176,512]{2,1,0:T(8,128)(2,1)S(1)} collective-permute-done((bf16[2,176,512]{2,1,0:T(8,128)(2,1)S(1)}, bf16[2,176,512]{2,1,0:T(8,128)(2,1)S(1)}, u32[]{:S(2)}, u32[]{:S(2)}) %collective-permute-start.139) | collective-permute-done | bytes 360480 | tf_op jit(solution)/shard_map/ppermute | solution.py:347
  631.7 8.7 %collective-permute-done.140 = bf16[176,512]{1,0:T(8,128)(2,1)S(1)} collective-permute-done((bf16[176,512]{1,0:T(8,128)(2,1)S(1)}, bf16[176,512]{1,0:T(8,128)(2,1)S(1)}, u32[]{:S(2)}, u32[]{:S(2)}) %collective-permute-start.140) | collective-permute-done | bytes 180256 | tf_op jit(solution)/shard_map/ppermute | solution.py:347
  643.1 12.7 %collective-permute-done.142 = bf16[176,512]{1,0:T(8,128)(2,1)S(1)} collective-permute-done((bf16[176,512]{1,0:T(8,128)(2,1)S(1)}, bf16[176,512]{1,0:T(8,128)(2,1)S(1)}, u32[]{:S(2)}, u32[]{:S(2)}) %collective-permute-start.142) | collective-permute-done | bytes 180256 | tf_op jit(solution)/shard_map/ppermute | solution.py:347
  663.5 8.2 %collective-permute-done.52 = bf16[2,1,256,512]{3,2,1,0:T(8,128)(2,1)S(1)} collective-permute-done((bf16[2,1,256,512]{3,2,1,0:T(8,128)(2,1)S(1)}, bf16[2,1,256,512]{3,2,1,0:T(8,128)(2,1)S(1)}, u32[]{:S(2)}, u32[]{:S(2)}) %collective-permute-start.52) | collective-permute-done | bytes 524320 | tf_op jit(solution)/shard_map/ppermute | solution.py:347
  680.7 13.8 %collective-permute-done.55 = f32[32,128]{1,0:T(8,128)S(1)} collective-permute-done((f32[32,128]{1,0:T(8,128)S(1)}, f32[32,128]{1,0:T(8,128)S(1)}, u32[]{:S(2)}, u32[]{:S(2)}) %collective-permute-start.55) | collective-permute-done | bytes 16416 | tf_op jit(solution)/shard_map/ppermute | solution.py:347
  701.9 9.9 %collective-permute-done.63 = bf16[2,128,1024]{2,1,0:T(8,128)(2,1)S(1)} collective-permute-done((bf16[2,128,1024]{2,1,0:T(8,128)(2,1)S(1)}, bf16[2,128,1024]{2,1,0:T(8,128)(2,1)S(1)}, u32[]{:S(2)}, u32[]{:S(2)}) %collective-permute-start.63) | collective-permute-done | bytes 524320 | tf_op jit(solution)/shard_map/ppermute | solution.py:347
  731.9 7.6 collective-permute-done.128
  739.7 7.5 collective-permute-done.68
  759.8 13.8 %collective-permute-done.69 = bf16[64,1024]{1,0:T(8,128)(2,1)S(1)} collective-permute-done((bf16[64,1024]{1,0:T(8,128)(2,1)S(1)}, bf16[64,1024]{1,0:T(8,128)(2,1)S(1)}, u32[]{:S(2)}, u32[]{:S(2)}) %collective-permute-start.69) | collective-permute-done | bytes 131104 | tf_op jit(solution)/shard_map/ppermute | solution.py:347
  (729 shorter events, 458.0 us)
Async XLA Ops:
  10.9 46.6 %collective-permute-start.3 = (bf16[128,1024]{1,0:T(8,128)(2,1)}, bf16[128,1024]{1,0:T(8,128)(2,1)}, u32[]{:S(2)}, u32[]{:S(2)}) collective-permute-start(bf16[128,1024]{1,0:T(8,128)(2,1)} %get-tuple-element.170), channel_id=1, source_target_pairs={{0,1},{1,0},{2,3},{3,2},{4,5},{5,4},{6,7},{7,6},{8,9},{9,8},{10,11... | collective-permute-start | bytes 786440 | tf_op jit(solution)/shard_map/ppermute | solution.py:347
  11.5 51.8 %collective-permute-start.4 = (bf16[128,1024]{1,0:T(8,128)(2,1)}, bf16[128,1024]{1,0:T(8,128)(2,1)}, u32[]{:S(2)}, u32[]{:S(2)}) collective-permute-start(bf16[128,1024]{1,0:T(8,128)(2,1)} %get-tuple-element.170), channel_id=1, source_target_pairs={{0,2},{1,3},{2,0},{3,1},{4,6},{5,7},{6,4},{7,5},{8,10},{9,11},{10,... | collective-permute-start | bytes 786440 | tf_op jit(solution)/shard_map/ppermute | solution.py:347
  37.7 42.6 %collective-permute-start.7 = (bf16[128,1024]{1,0:T(8,128)(2,1)}, bf16[128,1024]{1,0:T(8,128)(2,1)S(1)}, u32[]{:S(2)}, u32[]{:S(2)}) collective-permute-start(bf16[128,1024]{1,0:T(8,128)(2,1)} %get-tuple-element.169), channel_id=1, source_target_pairs={{0,1},{1,0},{2,3},{3,2},{4,5},{5,4},{6,7},{7,6},{8,9},{9,8},{10,11... | collective-permute-start | bytes 786440 | tf_op jit(solution)/shard_map/ppermute | solution.py:347
  59.2 32.1 %collective-permute-start.18 = (bf16[128,2048]{1,0:T(8,128)(2,1)S(1)}, bf16[128,2048]{1,0:T(8,128)(2,1)S(1)}, u32[]{:S(2)}, u32[]{:S(2)}) collective-permute-start(bf16[128,2048]{1,0:T(8,128)(2,1)S(1)} %get-tuple-element.123), channel_id=1, source_target_pairs={{0,2},{1,3},{2,0},{3,1},{4,6},{5,7},{6,4},{7,5},{8,10},{9,11},{10,... | collective-permute-start | bytes 1572872 | tf_op jit(solution)/shard_map/ppermute | solution.py:347
  88.0 71.5 %collective-permute-start.9 = (bf16[1024,1024]{1,0:T(8,128)(2,1)S(1)}, bf16[1024,1024]{1,0:T(8,128)(2,1)S(1)}, u32[]{:S(2)}, u32[]{:S(2)}) collective-permute-start(bf16[1024,1024]{1,0:T(8,128)(2,1)S(1)} %constant_dynamic-update-slice_fusion.21), channel_id=1, source_target_pairs={{0,4},{4,0},{1,5},{5,1},{2,6},{6,2},{3,7},{7,3},{8,12},{12,8},{9,1... | collective-permute-start | bytes 6291464 | tf_op jit(solution)/shard_map/ppermute | solution.py:347
  121.1 104.8 %collective-permute-start.23 = (bf16[1024,2048]{1,0:T(8,128)(2,1)}, bf16[1024,2048]{1,0:T(8,128)(2,1)}, u32[]{:S(2)}, u32[]{:S(2)}) collective-permute-start(bf16[1024,2048]{1,0:T(8,128)(2,1)} %constant_dynamic-update-slice_fusion.14), channel_id=1, source_target_pairs={{0,4},{4,0},{1,5},{5,1},{2,6},{6,2},{3,7},{7,3},{8,12},{12,8},{9,1... | collective-permute-start | bytes 12582920 | tf_op jit(solution)/shard_map/ppermute | solution.py:347
  208.3 273.3 %collective-permute-start.97 = (bf16[64,1024]{1,0:T(8,128)(2,1)}, bf16[64,1024]{1,0:T(8,128)(2,1)}, u32[]{:S(2)}, u32[]{:S(2)}) collective-permute-start(bf16[64,1024]{1,0:T(8,128)(2,1)} %bitcast.10), channel_id=1, source_target_pairs={{0,4},{4,0},{1,5},{5,1},{2,6},{6,2},{3,7},{7,3},{8,12},{12,8},{9,1... | collective-permute-start | bytes 393224 | tf_op jit(solution)/shard_map/ppermute | solution.py:347
  208.9 487.4 %collective-permute-start.61 = (bf16[256,1024]{1,0:T(8,128)(2,1)}, bf16[256,1024]{1,0:T(8,128)(2,1)}, u32[]{:S(2)}, u32[]{:S(2)}) collective-permute-start(bf16[256,1024]{1,0:T(8,128)(2,1)} %fusion.44), channel_id=1, source_target_pairs={{0,4},{4,0},{1,5},{5,1},{2,6},{6,2},{3,7},{7,3},{8,12},{12,8},{9,1... | collective-permute-start | bytes 1572872 | tf_op jit(solution)/shard_map/ppermute | solution.py:347
  209.0 73.2 %collective-permute-start.37 = (bf16[1024,2816]{1,0:T(8,128)(2,1)}, bf16[1024,2816]{1,0:T(8,128)(2,1)}, u32[]{:S(2)}, u32[]{:S(2)}) collective-permute-start(bf16[1024,2816]{1,0:T(8,128)(2,1)} %constant_dynamic-update-slice_fusion.7), channel_id=1, source_target_pairs={{0,4},{4,0},{1,5},{5,1},{2,6},{6,2},{3,7},{7,3},{8,12},{12,8},{9,1... | collective-permute-start | bytes 17301512 | tf_op jit(solution)/shard_map/ppermute | solution.py:347
  254.9 33.0 %collective-permute-start.44 = (bf16[2816,512]{1,0:T(8,128)(2,1)}, bf16[2816,512]{1,0:T(8,128)(2,1)}, u32[]{:S(2)}, u32[]{:S(2)}) collective-permute-start(bf16[2816,512]{1,0:T(8,128)(2,1)} %constant_dynamic-update-slice_fusion), channel_id=1, source_target_pairs={{0,4},{4,0},{1,5},{5,1},{2,6},{6,2},{3,7},{7,3},{8,12},{12,8},{9,1... | collective-permute-start | bytes 8650760 | tf_op jit(solution)/shard_map/ppermute | solution.py:347
  256.0 123.3 %collective-permute-start.73 = (bf16[256,1024]{1,0:T(8,128)(2,1)}, bf16[256,1024]{1,0:T(8,128)(2,1)}, u32[]{:S(2)}, u32[]{:S(2)}) collective-permute-start(bf16[256,1024]{1,0:T(8,128)(2,1)} %get-tuple-element.33), channel_id=1, source_target_pairs={{0,4},{4,0},{1,5},{5,1},{2,6},{6,2},{3,7},{7,3},{8,12},{12,8},{9,1... | collective-permute-start | bytes 1572872 | tf_op jit(solution)/shard_map/ppermute | solution.py:347
  282.3 104.7 %collective-permute-start.85 = (bf16[256,1024]{1,0:T(8,128)(2,1)}, bf16[256,1024]{1,0:T(8,128)(2,1)}, u32[]{:S(2)}, u32[]{:S(2)}) collective-permute-start(bf16[256,1024]{1,0:T(8,128)(2,1)} %multiply_convert_fusion.3), channel_id=1, source_target_pairs={{0,4},{4,0},{1,5},{5,1},{2,6},{6,2},{3,7},{7,3},{8,12},{12,8},{9,1... | collective-permute-start | bytes 1572872 | tf_op jit(solution)/shard_map/ppermute | solution.py:347
  344.2 40.6 %collective-permute-start.74 = (bf16[256,512]{1,0:T(8,128)(2,1)}, bf16[256,512]{1,0:T(8,128)(2,1)}, u32[]{:S(2)}, u32[]{:S(2)}) collective-permute-start(bf16[256,512]{1,0:T(8,128)(2,1)} %get-tuple-element.160), channel_id=1, source_target_pairs={{0,4},{4,0},{1,5},{5,1},{2,6},{6,2},{3,7},{7,3},{8,12},{12,8},{9,1... | collective-permute-start | bytes 786440 | tf_op jit(solution)/shard_map/ppermute | solution.py:347
  415.0 36.7 %collective-permute-start.59 = (bf16[2,2,64,512]{3,2,1,0:T(8,128)(2,1)S(1)}, bf16[2,2,64,512]{3,2,1,0:T(8,128)(2,1)S(1)}, u32[]{:S(2)}, u32[]{:S(2)}) collective-permute-start(bf16[2,2,64,512]{3,2,1,0:T(8,128)(2,1)S(1)} %slice_bitcast_fusion.6), channel_id=1, source_target_pairs={{0,8},{8,0},{16,24},{24,16},{1,9},{9,1},{17,25},{25,17},{2,10},{10... | collective-permute-start | bytes 786440 | tf_op jit(solution)/shard_map/ppermute | solution.py:347
  486.1 35.3 %collective-permute-start.121 = (bf16[256,1024]{1,0:T(8,128)(2,1)S(1)}, bf16[256,1024]{1,0:T(8,128)(2,1)S(1)}, u32[]{:S(2)}, u32[]{:S(2)}) collective-permute-start(bf16[256,1024]{1,0:T(8,128)(2,1)S(1)} %copy-done.45), channel_id=1, source_target_pairs={{0,4},{4,0},{1,5},{5,1},{2,6},{6,2},{3,7},{7,3},{8,12},{12,8},{9,1... | collective-permute-start | bytes 1572872 | tf_op jit(solution)/shard_map/ppermute | solution.py:347
  492.9 46.8 %collective-permute-start.133 = (bf16[256,2816]{1,0:T(8,128)(2,1)S(1)}, bf16[256,2816]{1,0:T(8,128)(2,1)S(1)}, u32[]{:S(2)}, u32[]{:S(2)}) collective-permute-start(bf16[256,2816]{1,0:T(8,128)(2,1)S(1)} %copy-done.24), channel_id=1, source_target_pairs={{0,4},{4,0},{1,5},{5,1},{2,6},{6,2},{3,7},{7,3},{8,12},{12,8},{9,1... | collective-permute-start | bytes 4325384 | tf_op jit(solution)/shard_map/ppermute | solution.py:347
  537.9 65.1 %collective-permute-start.123 = (bf16[2,128,2816]{2,1,0:T(8,128)(2,1)S(1)}, bf16[2,128,2816]{2,1,0:T(8,128)(2,1)S(1)}, u32[]{:S(2)}, u32[]{:S(2)}) collective-permute-start(bf16[2,128,2816]{2,1,0:T(8,128)(2,1)S(1)} %dynamic-slice_bitcast_fusion.1), channel_id=1, source_target_pairs={{0,1},{1,0},{2,3},{3,2},{4,5},{5,4},{6,7},{7,6},{8,9},{9,8},{10,11... | collective-permute-start | bytes 4325384 | tf_op jit(solution)/shard_map/ppermute | solution.py:347
  544.6 85.9 %collective-permute-start.125 = (bf16[2,128,2816]{2,1,0:T(8,128)(2,1)S(1)}, bf16[2,128,2816]{2,1,0:T(8,128)(2,1)S(1)}, u32[]{:S(2)}, u32[]{:S(2)}) collective-permute-start(bf16[2,128,2816]{2,1,0:T(8,128)(2,1)S(1)} %dynamic-slice_bitcast_fusion), channel_id=1, source_target_pairs={{0,2},{1,3},{2,0},{3,1},{4,6},{5,7},{6,4},{7,5},{8,10},{9,11},{10,... | collective-permute-start | bytes 4325384 | tf_op jit(solution)/shard_map/ppermute | solution.py:347
  547.6 37.8 %collective-permute-start.135 = (bf16[2,352,512]{2,1,0:T(8,128)(2,1)S(1)}, bf16[2,352,512]{2,1,0:T(8,128)(2,1)S(1)}, u32[]{:S(2)}, u32[]{:S(2)}) collective-permute-start(bf16[2,352,512]{2,1,0:T(8,128)(2,1)S(1)} %dynamic-slice_bitcast_fusion.3), channel_id=1, source_target_pairs={{0,1},{1,0},{2,3},{3,2},{4,5},{5,4},{6,7},{7,6},{8,9},{9,8},{10,11... | collective-permute-start | bytes 2162696 | tf_op jit(solution)/shard_map/ppermute | solution.py:347
  550.9 43.6 %collective-permute-start.137 = (bf16[2,352,512]{2,1,0:T(8,128)(2,1)S(1)}, bf16[2,352,512]{2,1,0:T(8,128)(2,1)S(1)}, u32[]{:S(2)}, u32[]{:S(2)}) collective-permute-start(bf16[2,352,512]{2,1,0:T(8,128)(2,1)S(1)} %dynamic-slice_bitcast_fusion.2), channel_id=1, source_target_pairs={{0,2},{1,3},{2,0},{3,1},{4,6},{5,7},{6,4},{7,5},{8,10},{9,11},{10,... | collective-permute-start | bytes 2162696 | tf_op jit(solution)/shard_map/ppermute | solution.py:347
  598.7 41.8 %collective-permute-start.51 = (bf16[2,2,256,512]{3,2,0,1:T(8,128)(2,1)S(1)}, bf16[2,2,256,512]{3,2,0,1:T(8,128)(2,1)S(1)}, u32[]{:S(2)}, u32[]{:S(2)}) collective-permute-start(bf16[2,2,256,512]{3,2,0,1:T(8,128)(2,1)S(1)} %bitcast.660), channel_id=1, source_target_pairs={{0,8},{8,0},{16,24},{24,16},{1,9},{9,1},{17,25},{25,17},{2,10},{10... | collective-permute-start | bytes 3145736 | tf_op jit(solution)/shard_map/ppermute | solution.py:347
  603.4 59.6 %collective-permute-start.124 = (bf16[128,2816]{1,0:T(8,128)(2,1)S(1)}, bf16[128,2816]{1,0:T(8,128)(2,1)S(1)}, u32[]{:S(2)}, u32[]{:S(2)}) collective-permute-start(bf16[128,2816]{1,0:T(8,128)(2,1)S(1)} %dynamic-slice_bitcast_fusion.5), channel_id=1, source_target_pairs={{0,2},{1,3},{2,0},{3,1},{4,6},{5,7},{6,4},{7,5},{8,10},{9,11},{10,... | collective-permute-start | bytes 2162696 | tf_op jit(solution)/shard_map/ppermute | solution.py:347
  630.9 32.3 %collective-permute-start.126 = (bf16[128,2816]{1,0:T(8,128)(2,1)S(1)}, bf16[128,2816]{1,0:T(8,128)(2,1)S(1)}, u32[]{:S(2)}, u32[]{:S(2)}) collective-permute-start(bf16[128,2816]{1,0:T(8,128)(2,1)S(1)} %dynamic-slice_bitcast_fusion.4), channel_id=1, source_target_pairs={{0,1},{1,0},{2,3},{3,2},{4,5},{5,4},{6,7},{7,6},{8,9},{9,8},{10,11... | collective-permute-start | bytes 2162696 | tf_op jit(solution)/shard_map/ppermute | solution.py:347
  662.9 95.7 %collective-permute-start.144 = (bf16[4,176,512]{2,1,0:T(8,128)(2,1)S(1)}, bf16[4,176,512]{2,1,0:T(8,128)(2,1)}, u32[]{:S(2)}, u32[]{:S(2)}) collective-permute-start(bf16[4,176,512]{2,1,0:T(8,128)(2,1)S(1)} %pad_maximum_fusion.4), channel_id=1, source_target_pairs={{0,4},{4,0},{1,5},{5,1},{2,6},{6,2},{3,7},{7,3},{8,12},{12,8},{9,1... | collective-permute-start | bytes 2162696 | tf_op jit(solution)/shard_map/ppermute | solution.py:347
  (183 other events, 2042.1 us)

commit v3 on v2

--- a/solution.py
+++ b/solution.py
@@ -351,17 +351,6 @@
     return cross(value, "core", 1)
 
 
-def after(value, *earlier):
-    return lax.optimization_barrier((value,) + earlier)[0]
-
-
-def sum_everywhere(value):
-    for axis in ("core", "line", "fsdp"):
-        for bit in bits_of(lax.axis_size(axis)):
-            value = value + cross(value, axis, bit)
-    return value
-
-
 def add(left, right):
     return (left.astype(F32) + right.astype(F32)).astype(BF16)
 
@@ -375,17 +364,54 @@
     )()
 
 
-def spread(have, axis, bits):
-    for bit in bits:
-        have = have + [(mask ^ bit, cross(piece, axis, bit)) for mask, piece in have]
-    return have
-
-
-def gather_small(value):
+class Lane:
+    def __init__(self, steps):
+        self.steps = steps
+        self.result = None
+        self.pending = next(steps)
+
+    def push(self, arrived):
+        try:
+            self.pending = self.steps.send(arrived)
+        except StopIteration as end:
+            self.pending, self.result = None, end.value
+
+    def take(self):
+        while self.pending is not None:
+            tick([self], ())
+        return self.result
+
+
+def tick(lanes, live):
+    active = [lane for lane in lanes if lane.pending is not None]
+    live, arrived = lax.optimization_barrier((live, [lane.pending for lane in active]))
+    for lane, value in zip(active, arrived):
+        lane.push(value)
+    return live
+
+
+def swap_steps(*values):
+    got = yield [swap(value) for value in values]
+    return got
+
+
+def sum_steps(value):
+    for axis in ("core", "line", "fsdp"):
+        for bit in bits_of(lax.axis_size(axis)):
+            (got,) = yield [cross(value, axis, bit)]
+            value = value + got
+    return value
+
+
+def small_steps(value):
     size = lax.axis_size("fsdp")
     me = lax.axis_index("fsdp")
+    have = [(0, value)]
+    for bit in bits_of(size):
+        got = yield [cross(piece, "fsdp", bit) for _, piece in have]
+        have = have + [(mask ^ bit, piece) for (mask, _), piece in zip(have, got)]
     whole = jnp.zeros((size, value.shape[0]), value.dtype)
-    for mask, piece in spread([(0, value)], "fsdp", bits_of(size)):
+    for mask, piece in have:
         whole = lax.dynamic_update_slice(whole, piece[None], (me ^ mask, 0))
     return whole
 
@@ -395,26 +421,29 @@
     return lax.dynamic_slice_in_dim(value, core * half, half, axis=1)
 
 
-def gather_weights(parts, earlier):
+def half_columns(parts):
+    core = lax.axis_index("core")
+    return jnp.concatenate([columns_of(part, core) for part in parts], axis=1)
+
+
+def gather_steps(mine):
     size = lax.axis_size("fsdp")
     me = lax.axis_index("fsdp")
-    core = lax.axis_index("core")
-    mine = jnp.concatenate([columns_of(part, core) for part in parts], axis=1)
-    mine = after(mine, *earlier)
     rows, width = mine.shape
     bits = bits_of(size)
     half = rows // 2
+    streams = [[(0, mine[stream * half : (stream + 1) * half])] for stream in range(2)]
     whole = lax.dynamic_update_slice(blank((size * rows, width)), mine, (me * rows, 0))
-    first = []
-    for stream in range(2):
-        order = bits if stream == 0 else bits[::-1]
-        have = spread([(0, mine[stream * half : (stream + 1) * half])], "fsdp", order)
-        first.append(have[1][1])
-        for mask, piece in have[1:]:
-            start = (me ^ mask) * rows + stream * half
-            whole = lax.dynamic_update_slice(whole, piece, (start, 0))
-    other = swap(whole)
-    return whole, other, first
+    for step in range(len(bits)):
+        chosen = [(bits if stream == 0 else bits[::-1])[step] for stream in range(2)]
+        got = yield [[cross(piece, "fsdp", chosen[stream]) for _, piece in streams[stream]] for stream in range(2)]
+        for stream in range(2):
+            fresh = [(mask ^ chosen[stream], piece) for (mask, _), piece in zip(streams[stream], got[stream])]
+            streams[stream] = streams[stream] + fresh
+            for mask, piece in fresh:
+                whole = lax.dynamic_update_slice(whole, piece, ((me ^ mask) * rows + stream * half, 0))
+    whole, other = yield whole, swap(whole)
+    return whole, other
 
 
 def by_core(mine, other):
@@ -422,48 +451,55 @@
     return jnp.where(first, mine, other), jnp.where(first, other, mine)
 
 
-def weight_grad(hidden, hidden_swapped, *grads):
+def grad_halves(*grads):
     core = lax.axis_index("core")
     mine = jnp.concatenate([columns_of(item, core) for item in grads], axis=1)
-    other = swap(jnp.concatenate([columns_of(item, 1 - core) for item in grads], axis=1))
+    return mine, jnp.concatenate([columns_of(item, 1 - core) for item in grads], axis=1)
+
+
+def weight_grad(hidden, hidden_swapped, mine, arrived):
     both_hidden = jnp.concatenate([hidden, hidden_swapped], axis=0)
-    both_grad = jnp.concatenate([mine, other], axis=0)
+    both_grad = jnp.concatenate([mine, arrived], axis=0)
     return tn(both_hidden, both_grad).astype(BF16)
 
 
-def halve(value, axis, bit, place):
+def split(value, axis, bit, place):
     mine = (lax.axis_index(axis) // bit) % 2
     keep = lax.dynamic_index_in_dim(value, mine, place, keepdims=False)
-    send = lax.dynamic_index_in_dim(value, 1 - mine, place, keepdims=False)
-    return add(keep, cross(send, axis, bit))
-
-
-def reduce_grad(partial, widths):
+    return keep, lax.dynamic_index_in_dim(value, 1 - mine, place, keepdims=False)
+
+
+def reduce_steps(partial, widths):
     size = lax.axis_size("fsdp")
     lines = lax.axis_size("line")
     rows = partial.shape[0] // size
     width = partial.shape[1]
     bits = bits_of(size)
     folded = partial.reshape([2] * len(bits) + [2, rows // 2, width])
-    sums = []
-    for stream in range(2):
-        order = bits if stream == 0 else bits[::-1]
-        value = lax.index_in_dim(folded, stream, len(bits), keepdims=False)
-        left = bits[::-1]
-        for bit in order:
-            place = left.index(bit)
-            value = halve(value, "fsdp", bit, place)
-            left = [item for item in left if item != bit]
-        sums.append(value)
-    shard = jnp.stack(sums)
+    values = [lax.index_in_dim(folded, stream, len(bits), keepdims=False) for stream in range(2)]
+    left = [bits[::-1], bits[::-1]]
+    for step in range(len(bits)):
+        chosen = [(bits if stream == 0 else bits[::-1])[step] for stream in range(2)]
+        parts = [
+            split(values[stream], "fsdp", chosen[stream], left[stream].index(chosen[stream])) for stream in range(2)
+        ]
+        got = yield [cross(parts[stream][1], "fsdp", chosen[stream]) for stream in range(2)]
+        values = [add(parts[stream][0], got[stream]) for stream in range(2)]
+        left = [[item for item in left[stream] if item != chosen[stream]] for stream in range(2)]
+    shard = jnp.stack(values)
     line_bits = bits_of(lines)
     value = shard.reshape([2] * len(line_bits) + [rows // lines, width])
     for bit in line_bits:
-        value = halve(value, "line", bit, value.ndim - 3)
-    have = spread([(0, value)], "line", line_bits[::-1])
+        keep, send = split(value, "line", bit, value.ndim - 3)
+        (got,) = yield [cross(send, "line", bit)]
+        value = add(keep, got)
+    have = [(0, value)]
+    for bit in line_bits[::-1]:
+        got = yield [cross(piece, "line", bit) for _, piece in have]
+        have = have + [(mask ^ bit, piece) for (mask, _), piece in zip(have, got)]
     have = [piece for _, piece in sorted(have, key=lambda item: item[0])]
     mine = jnp.stack(have)
-    other = swap(mine)
+    (other,) = yield [swap(mine)]
     me = lax.axis_index("line")
     outs = []
     start = 0
@@ -476,20 +512,26 @@
     return outs
 
 
-def gather_context(value):
-    have = spread([(0, value)], "line", bits_of(lax.axis_size("line"))[::-1])
-    have = [piece for _, piece in sorted(have, key=lambda item: item[0])]
-    return jnp.concatenate(have + [swap(piece) for piece in have], axis=0)
-
-
-def reduce_context(value):
+def gather_context_steps(value):
+    have = [(0, value)]
+    for bit in bits_of(lax.axis_size("line"))[::-1]:
+        got = yield [cross(piece, "line", bit) for _, piece in have]
+        have = have + [(mask ^ bit, piece) for (mask, _), piece in zip(have, got)]
+    mine = jnp.concatenate([piece for _, piece in sorted(have, key=lambda item: item[0])], axis=0)
+    (other,) = yield [swap(mine)]
+    return jnp.concatenate([mine, other], axis=0)
+
+
+def reduce_context_steps(value):
     lines = lax.axis_size("line")
     two, total, width = value.shape
     value = value.reshape(two, 2, lines, total // (2 * lines), width)
-    value = add(value[:, 0], swap(value[:, 1]))
+    (got,) = yield [swap(value[:, 1])]
+    value = add(value[:, 0], got)
     for bit in bits_of(lines):
         value = value.reshape(two, value.shape[1] // 2, 2, value.shape[2], width)
-        value = add(value[:, :, 0], cross(value[:, :, 1], "line", bit))
+        (got,) = yield [cross(value[:, :, 1], "line", bit)]
+        value = add(value[:, :, 0], got)
     return value[:, 0]
 
 
@@ -509,36 +551,27 @@
     context = lax.axis_index("line") * 2 + lax.axis_index("core")
     fsdp = lax.axis_index("fsdp")
 
-    mask_rows = valid_mask.reshape(rows).astype(F32)
-    count = sum_everywhere(jnp.broadcast_to(jnp.sum(mask_rows), (8, 128)))[0, 0]
-    count = jnp.maximum(count, 1.0)
-
-    small = jnp.concatenate([gain_self, gain_cross, gain_ffn, bias_table.reshape(-1)])
-    share = gain_self.shape[0]
-    small = gather_small(small)
-    gain_one, gain_two, gain_three = [
-        small[:, index * share : (index + 1) * share].reshape(D).astype(F32) for index in range(3)
-    ]
-    table_whole = small[:, 3 * share :].reshape(BUCKETS, HEADS)
-
-    joint = jnp.concatenate
-    qkv_mine, qkv_other, first = gather_weights((joint([w_query, w_key, w_value], axis=1),), ())
-    mid_mine, mid_other, first = gather_weights((w_out, c_query, joint([c_key, c_value], axis=1), c_out), first)
-    gu_mine, gu_other, first = gather_weights((joint([w_gate, w_up], axis=1),), first)
-    wd_mine, wd_other, first = gather_weights((w_down,), first)
-    halves = D // 2
-    wo, wcq, wckv, wco = [
-        (mid_mine[:, index * halves : (index + 1) * halves], mid_other[:, index * halves : (index + 1) * halves])
-        for index in range(4)
-    ]
     core = lax.axis_index("core")
     hidden_ff = w_gate.shape[1]
+    joint = jnp.concatenate
+    halves = D // 2
+    share = gain_self.shape[0]
 
     def times(left, weight):
         return joint(by_core(nn(left, weight[0]), nn(left, weight[1])), axis=1)
 
     def times_back(grad, weight):
         return nt(columns_of(grad, core), weight[0]) + nt(columns_of(grad, 1 - core), weight[1])
+
+    lane_qkv = Lane(gather_steps(half_columns([joint([w_query, w_key, w_value], axis=1)])))
+    lane_small = Lane(small_steps(joint([gain_self, gain_cross, gain_ffn, bias_table.reshape(-1)])))
+    mask_rows = valid_mask.reshape(rows).astype(F32)
+    lane_count = Lane(sum_steps(jnp.broadcast_to(jnp.sum(mask_rows), (8, 128))))
+    mid_shard = half_columns([w_out, c_query, joint([c_key, c_value], axis=1), c_out])
+    mid_shard = tick([lane_qkv, lane_small], mid_shard)
+
+    gu_shard = half_columns([joint([w_gate, w_up], axis=1)])
+    wd_shard = half_columns([w_down])
 
     query_blocks = lax.dynamic_slice_in_dim(block_order, context * pair, pair)
     slots = jnp.arange(contexts * pair, dtype=jnp.int32)
@@ -555,28 +588,80 @@
     place_table = jnp.concatenate([query_blocks, low[:, 0] // BLOCK, inverse]).astype(jnp.int32)
     behind, index_of = offset_index(length)
     bucket_match = (jnp.take(buckets, index_of)[None, :] == jnp.arange(BUCKETS, dtype=jnp.int32)[:, None])
+
+    gu_shard, wd_shard, low, high, place_table, bucket_match = tick(
+        [lane_qkv, lane_small, lane_count], (gu_shard, wd_shard, low, high, place_table, bucket_match)
+    )
+
+    small = lane_small.take()
+    gain_one, gain_two, gain_three = [
+        small[:, index * share : (index + 1) * share].reshape(D).astype(F32) for index in range(3)
+    ]
+    table_whole = small[:, 3 * share :].reshape(BUCKETS, HEADS)
     vectors = tn(table_whole, bucket_match.astype(BF16)).reshape(HEADS // 4, 4, SPAN)
-    extra = (vectors, low, high)
-
     flat_in = inputs.reshape(rows, width).astype(F32)
     normed_one, scale_one, hidden_one = norm_rows(flat_in, gain_one)
+    hidden_one, vectors = tick([lane_qkv, lane_count], (hidden_one, vectors))
+    extra = (vectors, low, high)
+
+    qkv_mine, qkv_other = lane_qkv.take()
+    lane_mid = Lane(gather_steps(mid_shard))
     query, pairs = by_core(nn(hidden_one, qkv_mine).astype(BF16), nn(hidden_one, qkv_other).astype(BF16))
-    pairs_whole = gather_context(pairs)
-    attention, outs_one, logs_one = attend(query, pairs_whole, place_table, extra, True)
-    mid_one = flat_in + times(attention, wo)
-
+    query, pairs = tick([lane_count], (query, pairs))
+
+    lane_keys = Lane(gather_context_steps(pairs))
+    gu_shard = tick([lane_keys, lane_mid, lane_count], gu_shard)
+    lane_hidden_one = Lane(swap_steps(hidden_one))
+    wd_shard = tick([lane_keys, lane_mid, lane_count, lane_hidden_one], wd_shard)
+    lane_gu = Lane(gather_steps(gu_shard))
+    tick([lane_keys, lane_mid], ())
+    mid_mine, mid_other = lane_mid.take()
+    wo, wcq, wckv, wco = [
+        (mid_mine[:, index * halves : (index + 1) * halves], mid_other[:, index * halves : (index + 1) * halves])
+        for index in range(4)
+    ]
     encoder_rows = encoder.reshape(encoder.shape[1], width)
     encoder_pairs = times(encoder_rows, wckv).astype(BF16)
-    encoder_whole = gather_context(encoder_pairs)
-
+    pairs_whole, encoder_pairs = tick([], (lane_keys.take(), encoder_pairs))
+
+    lane_encoder = Lane(gather_context_steps(encoder_pairs))
+    lane_encoder_rows = Lane(swap_steps(encoder_rows))
+    attention, outs_one, logs_one = attend(query, pairs_whole, place_table, extra, True)
+    attention, outs_one, logs_one = tick([lane_gu, lane_encoder, lane_encoder_rows], (attention, outs_one, logs_one))
+
+    lane_attention = Lane(swap_steps(attention))
+    mid_one = flat_in + times(attention, wo)
     normed_two, scale_two, hidden_two = norm_rows(mid_one, gain_two)
     cross_q = times(hidden_two, wcq).astype(BF16)
+    mid_one, normed_two, hidden_two, cross_q, scale_two = tick(
+        [lane_encoder, lane_attention], (mid_one, normed_two, hidden_two, cross_q, scale_two)
+    )
+    tick([lane_encoder], ())
+    encoder_whole = lane_encoder.take()
+
+    lane_hidden_two = Lane(swap_steps(hidden_two))
     crossed, outs_two, logs_two = attend(cross_q, encoder_whole, place_table, (), False)
+    crossed, outs_two, logs_two = tick([lane_gu, lane_hidden_two], (crossed, outs_two, logs_two))
+
+    lane_wd = Lane(gather_steps(wd_shard))
+    lane_crossed = Lane(swap_steps(crossed))
     mid_two = mid_one + times(crossed, wco)
     normed_three, scale_three, hidden_three = norm_rows(mid_two, gain_three)
+    mid_two, normed_three, hidden_three, scale_three = tick(
+        [lane_gu, lane_wd, lane_crossed], (mid_two, normed_three, hidden_three, scale_three)
+    )
+
+    gu_mine, gu_other = lane_gu.take()
+    lane_hidden_three = Lane(swap_steps(hidden_three))
     gate, up = by_core(nn(hidden_three, gu_mine), nn(hidden_three, gu_other))
     active, gelu_pull = jax.vjp(gelu_tanh, gate)
     mixed = (active * up).astype(BF16)
+    mixed, gate, up, active = tick([lane_wd, lane_hidden_three], (mixed, gate, up, active))
+    lane_mixed = Lane(swap_steps(mixed))
+    tick([lane_wd, lane_mixed], ())
+
+    wd_mine, wd_other = lane_wd.take()
+    count = jnp.maximum(lane_count.take()[0, 0], 1.0)
     result = mid_two + times(mixed, (wd_mine, wd_other))
     layer_out = result.astype(BF16)
     diff = result - teacher.reshape(rows, width).astype(F32)
@@ -584,49 +669,92 @@
     grad_result = token_total / count * mask_rows[:, None] * diff
 
     e_three = grad_result.astype(BF16)
+    down_mine, down_away = grad_halves(e_three)
+    grad_result, e_three, down_mine, down_away, squared_local, layer_out = tick(
+        [], (grad_result, e_three, down_mine, down_away, squared_local, layer_out)
+    )
+    lane_down = Lane(swap_steps(down_away))
     grad_mixed = times_back(e_three, (wd_mine, wd_other))
     (gelu_slope,) = gelu_pull(grad_mixed * up)
     grad_gate = gelu_slope.astype(BF16)
     grad_up = (grad_mixed * active).astype(BF16)
-    (grad_down,) = reduce_grad(weight_grad(mixed, swap(mixed), e_three), (D,))
-    grad_gate_weight, grad_up_weight = reduce_grad(
-        weight_grad(hidden_three, swap(hidden_three), grad_gate, grad_up), (hidden_ff, hidden_ff)
-    )
+    wide_mine, wide_away = grad_halves(grad_gate, grad_up)
+    grad_gate, grad_up, wide_mine, wide_away = tick([lane_down], (grad_gate, grad_up, wide_mine, wide_away))
+
+    lane_wide = Lane(swap_steps(wide_away))
+    partial_down = weight_grad(mixed, lane_mixed.take()[0], down_mine, lane_down.take()[0])
+    partial_down = tick([lane_wide], partial_down)
+
+    lane_down = Lane(reduce_steps(partial_down, (D,)))
+    partial_wide = weight_grad(hidden_three, lane_hidden_three.take()[0], wide_mine, lane_wide.take()[0])
     grad_hidden_three = times_back(joint([grad_gate, grad_up], axis=1), (gu_mine, gu_other))
+    partial_wide, grad_hidden_three = tick([lane_down], (partial_wide, grad_hidden_three))
+
+    lane_wide = Lane(reduce_steps(partial_wide, (hidden_ff, hidden_ff)))
     grad_norm_three, grad_gain_three = norm_back(grad_hidden_three, normed_three, scale_three, gain_three)
     grad_mid_two = grad_result + grad_norm_three
 
     e_two = grad_mid_two.astype(BF16)
-    (grad_cross_out,) = reduce_grad(weight_grad(crossed, swap(crossed), e_two), (D,))
     grad_cross = times_back(e_two, wco).astype(BF16)
     grad_cross_q, encoder_grad = attend_back(
         cross_q, encoder_whole, grad_cross, outs_two, logs_two, place_table, (), False
     )
-    encoder_mine = reduce_context(encoder_grad)
-    encoder_mine = jnp.concatenate([encoder_mine[0], encoder_mine[1]], axis=1)
-    grad_encoder = times_back(encoder_mine, wckv)
-    grad_cross_key, grad_cross_value = reduce_grad(
-        weight_grad(
-            encoder_rows, swap(encoder_rows), encoder_mine[:, :key_width], encoder_mine[:, key_width:]
-        ),
-        (key_width, key_width),
-    )
-    (grad_cross_query,) = reduce_grad(weight_grad(hidden_two, swap(hidden_two), grad_cross_q), (D,))
+    out_mine, out_away = grad_halves(e_two, grad_cross_q)
+    grad_mid_two, grad_cross_q, encoder_grad, out_mine, out_away = tick(
+        [lane_down, lane_wide], (grad_mid_two, grad_cross_q, encoder_grad, out_mine, out_away)
+    )
+
+    lane_encoder = Lane(reduce_context_steps(encoder_grad))
+    lane_out = Lane(swap_steps(out_away))
     grad_norm_two, grad_gain_two = norm_back(times_back(grad_cross_q, wcq), normed_two, scale_two, gain_two)
     grad_mid_one = grad_mid_two + grad_norm_two
 
     e_one = grad_mid_one.astype(BF16)
-    (grad_out_weight,) = reduce_grad(weight_grad(attention, swap(attention), e_one), (D,))
+    one_mine, one_away = grad_halves(e_one)
     grad_attention = times_back(e_one, wo).astype(BF16)
+    grad_mid_one, one_mine, one_away, grad_attention = tick(
+        [lane_down, lane_encoder, lane_out], (grad_mid_one, one_mine, one_away, grad_attention)
+    )
+    lane_one = Lane(swap_steps(one_away))
     grad_query, grad_pairs, grad_vectors = attend_back(
         query, pairs_whole, grad_attention, outs_one, logs_one, place_table, extra, True
     )
-    mine = reduce_context(grad_pairs)
-    grad_packed = jnp.concatenate([grad_query, mine[0], mine[1]], axis=1)
-    grad_query_weight, grad_key_weight, grad_value_weight = reduce_grad(
-        weight_grad(hidden_one, swap(hidden_one), grad_query, mine[0], mine[1]), (D, key_width, key_width)
-    )
-    grad_norm_one, grad_gain_one = norm_back(times_back(grad_packed, (qkv_mine, qkv_other)), normed_one, scale_one, gain_one)
+    grad_query, grad_pairs, grad_vectors = tick(
+        [lane_down, lane_wide, lane_encoder, lane_one], (grad_query, grad_pairs, grad_vectors)
+    )
+
+    lane_pairs = Lane(reduce_context_steps(grad_pairs))
+    arrived = lane_out.take()[0]
+    partial_out = weight_grad(crossed, lane_crossed.take()[0], out_mine[:, :halves], arrived[:, :halves])
+    partial_query = weight_grad(hidden_two, lane_hidden_two.take()[0], out_mine[:, halves:], arrived[:, halves:])
+    partial_one = weight_grad(attention, lane_attention.take()[0], one_mine, lane_one.take()[0])
+    partial_mid = joint([partial_out, partial_query, partial_one], axis=1)
+    partial_mid = tick([lane_pairs, lane_wide, lane_encoder], partial_mid)
+
+    lane_mid = Lane(reduce_steps(partial_mid, (D, D, D)))
+    encoder_mine = joint([lane_encoder.take()[0], lane_encoder.take()[1]], axis=1)
+    grad_encoder = times_back(encoder_mine, wckv)
+    keys_mine, keys_away = grad_halves(encoder_mine[:, :key_width], encoder_mine[:, key_width:])
+    grad_encoder, keys_mine, keys_away = tick([lane_pairs, lane_mid, lane_wide], (grad_encoder, keys_mine, keys_away))
+
+    lane_keys = Lane(swap_steps(keys_away))
+    tick([lane_pairs, lane_mid, lane_keys], ())
+    mine = lane_pairs.take()
+    last_mine, last_away = grad_halves(grad_query, mine[0], mine[1])
+    last_mine, last_away = tick([], (last_mine, last_away))
+
+    lane_last = Lane(swap_steps(last_away))
+    partial_keys = weight_grad(encoder_rows, lane_encoder_rows.take()[0], keys_mine, lane_keys.take()[0])
+    partial_keys = tick([lane_last], partial_keys)
+    partial_last = weight_grad(hidden_one, lane_hidden_one.take()[0], last_mine, lane_last.take()[0])
+    partial_last = joint([partial_last, partial_keys], axis=1)
+    partial_last = tick([lane_wide, lane_down], partial_last)
+
+    lane_last = Lane(reduce_steps(partial_last, (D, key_width, key_width, key_width, key_width)))
+    grad_packed = joint([grad_query, mine[0], mine[1]], axis=1)
+    grad_norm_one, grad_gain_one = norm_back(
+        times_back(grad_packed, (qkv_mine, qkv_other)), normed_one, scale_one, gain_one
+    )
     grad_inputs = grad_mid_one + grad_norm_one
 
     grad_table = lax.dot_general(
@@ -645,7 +773,16 @@
             jnp.broadcast_to(squared_local, (512,)),
         ]
     )
-    sums = sum_everywhere(sums.reshape(-1, 128)).reshape(-1)
+    sums, grad_inputs = tick([lane_last, lane_wide, lane_mid, lane_down], (sums.reshape(-1, 128), grad_inputs))
+    lane_sums = Lane(sum_steps(sums))
+    lanes = [lane_last, lane_wide, lane_mid, lane_down, lane_sums]
+    while any(lane.pending is not None for lane in lanes):
+        tick(lanes, ())
+    sums = lane_sums.take().reshape(-1)
+    (grad_down,) = lane_down.take()
+    grad_gate_weight, grad_up_weight = lane_wide.take()
+    grad_cross_out, grad_cross_query, grad_out_weight = lane_mid.take()
+    grad_query_weight, grad_key_weight, grad_value_weight, grad_cross_key, grad_cross_value = lane_last.take()
     loss = sums[3 * D + 512] / (D * count)
 
     def shard_of(offset, amount):

time: 787 us -> 696 us (0.88)
  waiting for transfers between devices: 349 us -> 151 us
  local copies, waits for them, and re-layouts: 61.7 us -> 161 us
  other arithmetic: 49.1 us -> 87.6 us
  starting transfers between devices: 160 us -> 122 us
    ppermute x145 -> x108, waiting for transfers between devices: 349 us -> 151 us  [cross(): return lax.ppermute(value, axis, partners(lax.axis_size(axis), bit))]
    ppermute x145 -> x108, starting transfers between devices: 160 us -> 122 us  [cross(): return lax.ppermute(value, axis, partners(lax.axis_size(axis), bit))]
    unnamed x147 -> x242, local copies, waits for them, and re-layouts: 13.3 us -> 47.9 us
    convert_element_type x46 -> x28, other arithmetic: 5.01 us -> 24.4 us  [add(): return (left.astype(F32) + right.astype(F32)).astype(BF16)]
    dynamic_slice x0 -> x4, local copies, waits for them, and re-layouts: none -> 18.6 us  [split(): keep = lax.dynamic_index_in_dim(value, mine, place, keepdims=False)]
    slice x16 -> x15, local copies, waits for them, and re-layouts: 3.09 us -> 19.3 us  [the longest x4 11.4 us: reduce_steps(): lax.index_in_dim(folded, stream, len(bits), keepdims=False)]
    dynamic_update_slice x32 -> x31, local copies, waits for them, and re-layouts: 21.4 us -> 35.8 us  [the longest x24 32.3 us: gather_steps(): lax.dynamic_update_slice(whole, piece, ((me ^ mask) * rows + stream * hal...]
    reshape x0 -> x2, local copies, waits for them, and re-layouts: none -> 9.35 us  [reduce_steps(): folded = partial.reshape([2] * len(bits) + [2, rows // 2, width])]
  transfers between devices with their start and end apart: 145 -> 108, of which waited for: 63 -> 32; matrix products, arithmetic and copies ran while one was open for 24% -> 40% of each run, Pallas kernels for 9% -> 10%
where the time goes in v3:
time: 696 us; the launch traced here: 693 us
  local copies, waits for them, and re-layouts  161 us (23%)
  waiting for transfers between devices  151 us (22%)
  starting transfers between devices  122 us (18%)
  matrix products  93.3 us (13%)
  other arithmetic  87.6 us (13%)
  Pallas kernels  70.5 us (10%)
  between operations  7.19 us (1%)
    ppermute x108, waiting for transfers between devices, cross(): return lax.ppermute(value, axis, partners(lax.axis_size(axis), bit))  151 us
    ppermute x108, starting transfers between devices, cross(): return lax.ppermute(value, axis, partners(lax.axis_size(axis), bit))  122 us
    unnamed x242, local copies, waits for them, and re-layouts  47.9 us
    pallas_call x2, Pallas kernels, attend_back(): pl.pallas_call(functools.partial(backward_kernel, masked), grid_spec=pltp...  40.6 us
    dot_general x14, matrix products, nt(): lax.dot_general(left, right, (((1,), (1,)), ((), ())), preferred_element_...  36.8 us
    dot_general x14, matrix products, nn(): return jnp.dot(left, right, preferred_element_type=F32)  36.7 us
    dynamic_update_slice x24, local copies, waits for them, and re-layouts, gather_steps(): lax.dynamic_update_slice(whole, piece, ((me ^ mask) * rows + stream * hal...  32.3 us
    pallas_call x2, Pallas kernels, attend(): pl.pallas_call(functools.partial(forward_kernel, masked), grid_spec=pltpu...  29.9 us
  transfers between devices with their start and end apart: 108, of which 32 were waited for; matrix products, arithmetic and copies ran while one was open for 40% of the time, Pallas kernels for 10%

profile of v3, /device:TPU:0, one launch (start us, length us, event | category | flops | bytes accessed | tf_op | source)
XLA Modules:
  0.0 692.8 jit_solution(5064319620461233948)
XLA Ops:
  62.4 10.6 %collective-permute-done.16 = f32[8,128]{1,0:T(8,128)S(1)} collective-permute-done((f32[8,128]{1,0:T(8,128)S(1)}, f32[8,128]{1,0:T(8,128)S(1)}, u32[]{:S(2)}, u32[]{:S(2)}) %collective-permute-start.16) | collective-permute-done | bytes 4128 | tf_op jit(solution)/shard_map/ppermute | solution.py:347
  74.4 10.5 %collective-permute-done.13 = bf16[256,1024]{1,0:T(8,128)(2,1)} collective-permute-done((bf16[256,1024]{1,0:T(8,128)(2,1)}, bf16[256,1024]{1,0:T(8,128)(2,1)}, u32[]{:S(2)}, u32[]{:S(2)}) %collective-permute-start.13) | collective-permute-done | bytes 524320 | tf_op jit(solution)/shard_map/ppermute | solution.py:347
  98.1 8.1 %collective-permute-done.18 = bf16[256,1024]{1,0:T(8,128)(2,1)S(1)} collective-permute-done((bf16[256,1024]{1,0:T(8,128)(2,1)}, bf16[256,1024]{1,0:T(8,128)(2,1)S(1)}, u32[]{:S(2)}, u32[]{:S(2)}) %collective-permute-start.18) | collective-permute-done | bytes 524320 | tf_op jit(solution)/shard_map/ppermute | solution.py:347
  132.0 13.5 %attend_self.1 = (bf16[256,1024]{1,0:T(8,128)(2,1)}, f32[4,2,64,512]{3,2,1,0:T(8,128)}, f32[4,2,8,512]{3,2,1,0:T(8,128)}) custom-call(s32[20]{0:T(128)} %pad_add_fusion.1.table, bf16[256,1024]{1,0:T(8,128)(2,1)} %get-tuple-element.234.refs_0_, bf16[2048,1024]{1,0:T(8,128)(2,1)} %constant_dynamic-update-slice_fusion.28.refs_1_.refs_2_, ...), custom_call_target="tpu_custom_call" | custom-call | flops 2147483648 | bytes 8388608 | tf_op jit(solution)/shard_map/attend_self/pallas_call | solution.py:248
  149.8 13.2 %collective-permute-start.31 = (bf16[64,1024]{1,0:T(8,128)(2,1)S(1)}, bf16[64,1024]{1,0:T(8,128)(2,1)S(1)}, u32[]{:S(2)}, u32[]{:S(2)}) collective-permute-start(bf16[64,1024]{1,0:T(8,128)(2,1)S(1)} %pad_maximum_fusion.17), channel_id=1, source_target_pairs={{0,8},{8,0},{16,24},{24,16},{1,9},{9,1},{17,25},{25,17},{2,10},{10... | collective-permute-start | bytes 393224 | tf_op jit(solution)/shard_map/ppermute | solution.py:347
  185.2 16.4 %attend_cross.1 = (bf16[256,1024]{1,0:T(8,128)(2,1)}, f32[4,2,64,512]{3,2,1,0:T(8,128)}, f32[4,2,8,512]{3,2,1,0:T(8,128)}) custom-call(s32[20]{0:T(128)} %pad_add_fusion.1.table, bf16[256,1024]{1,0:T(8,128)(2,1)} %pad_maximum_fusion.11.refs_0_, bf16[512,1024]{1,0:T(8,128)(2,1)} %constant_dynamic-update-slice_fusion.33.refs_1_.refs_2_, ...), custom_call_target="tpu_custom_call" | custom-call | flops 536870912 | bytes 2097152 | tf_op jit(solution)/shard_map/attend_cross/pallas_call | solution.py:248
  220.4 7.5 %collective-permute-done.42 = bf16[352,512]{1,0:T(8,128)(2,1)S(1)} collective-permute-done((bf16[352,512]{1,0:T(8,128)(2,1)S(1)}, bf16[352,512]{1,0:T(8,128)(2,1)S(1)}, u32[]{:S(2)}, u32[]{:S(2)}) %collective-permute-start.42) | collective-permute-done | bytes 360480 | tf_op jit(solution)/shard_map/ppermute | solution.py:347
  234.6 6.3 multiply_multiply_fusion.2
  268.4 5.4 multiply_convert_fusion
  294.4 8.5 %collective-permute-done.53 = bf16[2,352,512]{2,1,0:T(8,128)(2,1)S(1)} collective-permute-done((bf16[2,352,512]{2,1,0:T(8,128)(2,1)S(1)}, bf16[2,352,512]{2,1,0:T(8,128)(2,1)S(1)}, u32[]{:S(2)}, u32[]{:S(2)}) %collective-permute-start.53) | collective-permute-done | bytes 720928 | tf_op jit(solution)/shard_map/ppermute | solution.py:347
  319.8 16.6 %attend_cross_back.1 = (bf16[256,1024]{1,0:T(8,128)(2,1)}, bf16[2,512,512]{2,1,0:T(8,128)(2,1)}) custom-call(s32[20]{0:T(128)} %pad_add_fusion.1.table, bf16[256,1024]{1,0:T(8,128)(2,1)} %pad_maximum_fusion.11.refs_0_, bf16[512,1024]{1,0:T(8,128)(2,1)} %constant_dynamic-update-slice_fusion.33.refs_1_.refs_2_, ...), custom_call_target="tpu_custom_call" | custom-call | flops 1342177280 | bytes 4194304 | tf_op jit(solution)/shard_map/attend_cross_back/pallas_call | solution.py:286
  337.9 10.3 %collective-permute-done.57 = bf16[2,128,2816]{2,1,0:T(8,128)(2,1)} collective-permute-done((bf16[2,128,2816]{2,1,0:T(8,128)(2,1)}, bf16[2,128,2816]{2,1,0:T(8,128)(2,1)}, u32[]{:S(2)}, u32[]{:S(2)}) %collective-permute-start.57) | collective-permute-done | bytes 1441824 | tf_op jit(solution)/shard_map/ppermute | solution.py:347
  371.8 24.0 %attend_self_back.1 = (bf16[256,1024]{1,0:T(8,128)(2,1)}, bf16[2,2048,512]{2,1,0:T(8,128)(2,1)}, f32[4,4,512]{2,1,0:T(4,128)}) custom-call(s32[20]{0:T(128)} %pad_add_fusion.1.table, bf16[256,1024]{1,0:T(8,128)(2,1)} %get-tuple-element.234.refs_0_, bf16[2048,1024]{1,0:T(8,128)(2,1)} %constant_dynamic-update-slice_fusion.28.refs_1_.refs_2_, ...), custom_call_target="tpu_custom_call" | custom-call | flops 5368709120 | bytes 16777216 | tf_op jit(solution)/shard_map/attend_self_back/pallas_call | solution.py:286
  403.2 9.1 %collective-permute-start.67 = (bf16[2,4,256,512]{3,2,1,0:T(8,128)(2,1)}, bf16[2,4,256,512]{3,2,1,0:T(8,128)(2,1)S(1)}, u32[]{:S(2)}, u32[]{:S(2)}) collective-permute-start(bf16[2,4,256,512]{3,2,1,0:T(8,128)(2,1)} %slice_bitcast_fusion), channel_id=1, source_target_pairs={{0,4},{4,0},{1,5},{5,1},{2,6},{6,2},{3,7},{7,3},{8,12},{12,8},{9,1... | collective-permute-start | bytes 6291464 | tf_op jit(solution)/shard_map/ppermute | solution.py:347
  429.4 6.5 collective-permute-done.69
  435.8 5.5 collective-permute-done.68
  449.6 5.4 fusion.303
  463.9 7.8 %collective-permute-start.71 = (bf16[2,128,1536]{2,1,0:T(8,128)(2,1)}, bf16[2,128,1536]{2,1,0:T(8,128)(2,1)}, u32[]{:S(2)}, u32[]{:S(2)}) collective-permute-start(bf16[2,128,1536]{2,1,0:T(8,128)(2,1)} %bitcast.458), channel_id=1, source_target_pairs={{0,1},{1,0},{2,3},{3,2},{4,5},{5,4},{6,7},{7,6},{8,9},{9,8},{10,11... | collective-permute-start | bytes 2359304 | tf_op jit(solution)/shard_map/ppermute | solution.py:347
  523.0 15.8 %collective-permute-done.74 = bf16[2,1,256,512]{3,2,1,0:T(8,128)(2,1)S(1)} collective-permute-done((bf16[2,1,256,512]{3,2,1,0:T(8,128)(2,1)S(1)}, bf16[2,1,256,512]{3,2,1,0:T(8,128)(2,1)S(1)}, u32[]{:S(2)}, u32[]{:S(2)}) %collective-permute-start.74) | collective-permute-done | bytes 524320 | tf_op jit(solution)/shard_map/ppermute | solution.py:347
  573.7 6.0 constant_dynamic-slice_fusion
  620.2 9.6 %collective-permute-done.91 = bf16[64,1536]{1,0:T(8,128)(2,1)S(1)} collective-permute-done((bf16[64,1536]{1,0:T(8,128)(2,1)S(1)}, bf16[64,1536]{1,0:T(8,128)(2,1)S(1)}, u32[]{:S(2)}, u32[]{:S(2)}) %collective-permute-start.91) | collective-permute-done | bytes 196640 | tf_op jit(solution)/shard_map/ppermute | solution.py:347
  642.6 7.3 %collective-permute-done.96 = f32[32,128]{1,0:T(8,128)S(1)} collective-permute-done((f32[32,128]{1,0:T(8,128)S(1)}, f32[32,128]{1,0:T(8,128)S(1)}, u32[]{:S(2)}, u32[]{:S(2)}) %collective-permute-start.96) | collective-permute-done | bytes 16416 | tf_op jit(solution)/shard_map/ppermute | solution.py:347
  654.4 6.3 collective-permute-done.100
  666.5 6.8 collective-permute-done.101
  (721 shorter events, 448.7 us)
Async XLA Ops:
  3.9 30.6 %collective-permute-start = (bf16[128,1024]{1,0:T(8,128)(2,1)}, bf16[128,1024]{1,0:T(8,128)(2,1)}, u32[]{:S(2)}, u32[]{:S(2)}) collective-permute-start(bf16[128,1024]{1,0:T(8,128)(2,1)} %get-tuple-element.536), channel_id=1, source_target_pairs={{0,2},{1,3},{2,0},{3,1},{4,6},{5,7},{6,4},{7,5},{8,10},{9,11},{10,... | collective-permute-start | bytes 786440 | tf_op jit(solution)/shard_map/ppermute | solution.py:347
  115.2 30.2 %collective-permute-start.30 = (bf16[64,1024]{1,0:T(8,128)(2,1)S(1)}, bf16[64,1024]{1,0:T(8,128)(2,1)S(1)}, u32[]{:S(2)}, u32[]{:S(2)}) collective-permute-start(bf16[64,1024]{1,0:T(8,128)(2,1)S(1)} %bitcast.473), channel_id=1, source_target_pairs={{0,4},{4,0},{1,5},{5,1},{2,6},{6,2},{3,7},{7,3},{8,12},{12,8},{9,1... | collective-permute-start | bytes 393224 | tf_op jit(solution)/shard_map/ppermute | solution.py:347
  119.0 30.7 %collective-permute-start.27 = (bf16[128,2816]{1,0:T(8,128)(2,1)}, bf16[128,2816]{1,0:T(8,128)(2,1)S(1)}, u32[]{:S(2)}, u32[]{:S(2)}) collective-permute-start(bf16[128,2816]{1,0:T(8,128)(2,1)} %get-tuple-element.486), channel_id=1, source_target_pairs={{0,1},{1,0},{2,3},{3,2},{4,5},{5,4},{6,7},{7,6},{8,9},{9,8},{10,11... | collective-permute-start | bytes 2162696 | tf_op jit(solution)/shard_map/ppermute | solution.py:347
  119.9 81.7 %collective-permute-start.35 = (bf16[128,2816]{1,0:T(8,128)(2,1)}, bf16[128,2816]{1,0:T(8,128)(2,1)}, u32[]{:S(2)}, u32[]{:S(2)}) collective-permute-start(bf16[128,2816]{1,0:T(8,128)(2,1)} %get-tuple-element.486), channel_id=1, source_target_pairs={{0,2},{1,3},{2,0},{3,1},{4,6},{5,7},{6,4},{7,5},{8,10},{9,11},{10,... | collective-permute-start | bytes 2162696 | tf_op jit(solution)/shard_map/ppermute | solution.py:347
  124.9 38.1 %collective-permute-start.28 = (bf16[128,2816]{1,0:T(8,128)(2,1)}, bf16[128,2816]{1,0:T(8,128)(2,1)}, u32[]{:S(2)}, u32[]{:S(2)}) collective-permute-start(bf16[128,2816]{1,0:T(8,128)(2,1)} %get-tuple-element.485), channel_id=1, source_target_pairs={{0,2},{1,3},{2,0},{3,1},{4,6},{5,7},{6,4},{7,5},{8,10},{9,11},{10,... | collective-permute-start | bytes 2162696 | tf_op jit(solution)/shard_map/ppermute | solution.py:347
  131.7 31.3 %collective-permute-start.29 = (bf16[64,1024]{1,0:T(8,128)(2,1)S(1)}, bf16[64,1024]{1,0:T(8,128)(2,1)S(1)}, u32[]{:S(2)}, u32[]{:S(2)}) collective-permute-start(bf16[64,1024]{1,0:T(8,128)(2,1)S(1)} %pad_maximum_fusion.17), channel_id=1, source_target_pairs={{0,16},{8,24},{16,0},{24,8},{1,17},{9,25},{17,1},{25,9},{2,18},{10... | collective-permute-start | bytes 393224 | tf_op jit(solution)/shard_map/ppermute | solution.py:347
  145.5 56.2 %collective-permute-start.37 = (bf16[128,2816]{1,0:T(8,128)(2,1)}, bf16[128,2816]{1,0:T(8,128)(2,1)}, u32[]{:S(2)}, u32[]{:S(2)}) collective-permute-start(bf16[128,2816]{1,0:T(8,128)(2,1)} %get-tuple-element.485), channel_id=1, source_target_pairs={{0,1},{1,0},{2,3},{3,2},{4,5},{5,4},{6,7},{7,6},{8,9},{9,8},{10,11... | collective-permute-start | bytes 2162696 | tf_op jit(solution)/shard_map/ppermute | solution.py:347
  209.9 35.6 %collective-permute-start.44 = (bf16[352,512]{1,0:T(8,128)(2,1)S(1)}, bf16[352,512]{1,0:T(8,128)(2,1)S(1)}, u32[]{:S(2)}, u32[]{:S(2)}) collective-permute-start(bf16[352,512]{1,0:T(8,128)(2,1)S(1)} %get-tuple-element.498), channel_id=1, source_target_pairs={{0,2},{1,3},{2,0},{3,1},{4,6},{5,7},{6,4},{7,5},{8,10},{9,11},{10,... | collective-permute-start | bytes 1081352 | tf_op jit(solution)/shard_map/ppermute | solution.py:347
  306.3 31.5 %collective-permute-start.55 = (bf16[352,512]{1,0:T(8,128)(2,1)}, bf16[352,512]{1,0:T(8,128)(2,1)}, u32[]{:S(2)}, u32[]{:S(2)}) collective-permute-start(bf16[352,512]{1,0:T(8,128)(2,1)} %dynamic-slice_bitcast_fusion.12), channel_id=1, source_target_pairs={{0,2},{1,3},{2,0},{3,1},{4,6},{5,7},{6,4},{7,5},{8,10},{9,11},{10,... | collective-permute-start | bytes 1081352 | tf_op jit(solution)/shard_map/ppermute | solution.py:347
  309.7 38.5 %collective-permute-start.57 = (bf16[2,128,2816]{2,1,0:T(8,128)(2,1)}, bf16[2,128,2816]{2,1,0:T(8,128)(2,1)}, u32[]{:S(2)}, u32[]{:S(2)}) collective-permute-start(bf16[2,128,2816]{2,1,0:T(8,128)(2,1)} %dynamic-slice_bitcast_fusion.1), channel_id=1, source_target_pairs={{0,1},{1,0},{2,3},{3,2},{4,5},{5,4},{6,7},{7,6},{8,9},{9,8},{10,11... | collective-permute-start | bytes 4325384 | tf_op jit(solution)/shard_map/ppermute | solution.py:347
  312.6 35.6 %collective-permute-start.58 = (bf16[2,128,2816]{2,1,0:T(8,128)(2,1)}, bf16[2,128,2816]{2,1,0:T(8,128)(2,1)}, u32[]{:S(2)}, u32[]{:S(2)}) collective-permute-start(bf16[2,128,2816]{2,1,0:T(8,128)(2,1)} %dynamic-slice_bitcast_fusion), channel_id=1, source_target_pairs={{0,2},{1,3},{2,0},{3,1},{4,6},{5,7},{6,4},{7,5},{8,10},{9,11},{10,... | collective-permute-start | bytes 4325384 | tf_op jit(solution)/shard_map/ppermute | solution.py:347
  361.4 39.4 %collective-permute-start.63 = (bf16[128,2816]{1,0:T(8,128)(2,1)}, bf16[128,2816]{1,0:T(8,128)(2,1)}, u32[]{:S(2)}, u32[]{:S(2)}) collective-permute-start(bf16[128,2816]{1,0:T(8,128)(2,1)} %dynamic-slice_bitcast_fusion.3), channel_id=1, source_target_pairs={{0,2},{1,3},{2,0},{3,1},{4,6},{5,7},{6,4},{7,5},{8,10},{9,11},{10,... | collective-permute-start | bytes 2162696 | tf_op jit(solution)/shard_map/ppermute | solution.py:347
  364.9 35.8 %collective-permute-start.64 = (bf16[128,2816]{1,0:T(8,128)(2,1)S(1)}, bf16[128,2816]{1,0:T(8,128)(2,1)S(1)}, u32[]{:S(2)}, u32[]{:S(2)}) collective-permute-start(bf16[128,2816]{1,0:T(8,128)(2,1)S(1)} %dynamic-slice_bitcast_fusion.2), channel_id=1, source_target_pairs={{0,1},{1,0},{2,3},{3,2},{4,5},{5,4},{6,7},{7,6},{8,9},{9,8},{10,11... | collective-permute-start | bytes 2162696 | tf_op jit(solution)/shard_map/ppermute | solution.py:347
  368.4 32.4 %collective-permute-start.62 = (bf16[176,512]{1,0:T(8,128)(2,1)}, bf16[176,512]{1,0:T(8,128)(2,1)}, u32[]{:S(2)}, u32[]{:S(2)}) collective-permute-start(bf16[176,512]{1,0:T(8,128)(2,1)} %dynamic-slice_bitcast_fusion.15), channel_id=1, source_target_pairs={{0,16},{8,24},{16,0},{24,8},{1,17},{9,25},{17,1},{25,9},{2,18},{10... | collective-permute-start | bytes 540680 | tf_op jit(solution)/shard_map/ppermute | solution.py:347
  369.6 31.2 %collective-permute-start.65 = (bf16[2,2,64,512]{3,2,1,0:T(8,128)(2,1)}, bf16[2,2,64,512]{3,2,1,0:T(8,128)(2,1)}, u32[]{:S(2)}, u32[]{:S(2)}) collective-permute-start(bf16[2,2,64,512]{3,2,1,0:T(8,128)(2,1)} %slice_bitcast_fusion.7), channel_id=1, source_target_pairs={{0,8},{8,0},{16,24},{24,16},{1,9},{9,1},{17,25},{25,17},{2,10},{10... | collective-permute-start | bytes 786440 | tf_op jit(solution)/shard_map/ppermute | solution.py:347
  403.2 38.1 %collective-permute-start.67 = (bf16[2,4,256,512]{3,2,1,0:T(8,128)(2,1)}, bf16[2,4,256,512]{3,2,1,0:T(8,128)(2,1)S(1)}, u32[]{:S(2)}, u32[]{:S(2)}) collective-permute-start(bf16[2,4,256,512]{3,2,1,0:T(8,128)(2,1)} %slice_bitcast_fusion), channel_id=1, source_target_pairs={{0,4},{4,0},{1,5},{5,1},{2,6},{6,2},{3,7},{7,3},{8,12},{12,8},{9,1... | collective-permute-start | bytes 6291464 | tf_op jit(solution)/shard_map/ppermute | solution.py:347
  424.2 130.4 %collective-permute-start.80 = (bf16[176,512]{1,0:T(8,128)(2,1)}, bf16[176,512]{1,0:T(8,128)(2,1)}, u32[]{:S(2)}, u32[]{:S(2)}) collective-permute-start(bf16[176,512]{1,0:T(8,128)(2,1)} %fusion.168), channel_id=1, source_target_pairs={{0,16},{8,24},{16,0},{24,8},{1,17},{9,25},{17,1},{25,9},{2,18},{10... | collective-permute-start | bytes 540680 | tf_op jit(solution)/shard_map/ppermute | solution.py:347
  444.9 59.7 %collective-permute-start.70 = (bf16[2,2,256,512]{3,2,0,1:T(8,128)(2,1)}, bf16[2,2,256,512]{3,2,0,1:T(8,128)(2,1)}, u32[]{:S(2)}, u32[]{:S(2)}) collective-permute-start(bf16[2,2,256,512]{3,2,0,1:T(8,128)(2,1)} %bitcast.429), channel_id=1, source_target_pairs={{0,8},{8,0},{16,24},{24,16},{1,9},{9,1},{17,25},{25,17},{2,10},{10... | collective-permute-start | bytes 3145736 | tf_op jit(solution)/shard_map/ppermute | solution.py:347
  463.9 40.8 %collective-permute-start.71 = (bf16[2,128,1536]{2,1,0:T(8,128)(2,1)}, bf16[2,128,1536]{2,1,0:T(8,128)(2,1)}, u32[]{:S(2)}, u32[]{:S(2)}) collective-permute-start(bf16[2,128,1536]{2,1,0:T(8,128)(2,1)} %bitcast.458), channel_id=1, source_target_pairs={{0,1},{1,0},{2,3},{3,2},{4,5},{5,4},{6,7},{7,6},{8,9},{9,8},{10,11... | collective-permute-start | bytes 2359304 | tf_op jit(solution)/shard_map/ppermute | solution.py:347
  506.3 32.5 %collective-permute-start.74 = (bf16[2,1,256,512]{3,2,1,0:T(8,128)(2,1)S(1)}, bf16[2,1,256,512]{3,2,1,0:T(8,128)(2,1)S(1)}, u32[]{:S(2)}, u32[]{:S(2)}) collective-permute-start(bf16[2,1,256,512]{3,2,1,0:T(8,128)(2,1)S(1)} %slice_bitcast_fusion.2), channel_id=1, source_target_pairs={{0,16},{8,24},{16,0},{24,8},{1,17},{9,25},{17,1},{25,9},{2,18},{10... | collective-permute-start | bytes 1572872 | tf_op jit(solution)/shard_map/ppermute | solution.py:347
  513.0 75.5 %collective-permute-start.86 = (bf16[176,512]{1,0:T(8,128)(2,1)}, bf16[176,512]{1,0:T(8,128)(2,1)}, u32[]{:S(2)}, u32[]{:S(2)}) collective-permute-start(bf16[176,512]{1,0:T(8,128)(2,1)} %fusion.168), channel_id=1, source_target_pairs={{0,8},{8,0},{16,24},{24,16},{1,9},{9,1},{17,25},{25,17},{2,10},{10... | collective-permute-start | bytes 540680 | tf_op jit(solution)/shard_map/ppermute | solution.py:347
  518.6 36.0 %collective-permute-start.79 = (bf16[64,2816]{1,0:T(8,128)(2,1)}, bf16[64,2816]{1,0:T(8,128)(2,1)}, u32[]{:S(2)}, u32[]{:S(2)}) collective-permute-start(bf16[64,2816]{1,0:T(8,128)(2,1)} %fusion.108), channel_id=1, source_target_pairs={{0,16},{8,24},{16,0},{24,8},{1,17},{9,25},{17,1},{25,9},{2,18},{10... | collective-permute-start | bytes 1081352 | tf_op jit(solution)/shard_map/ppermute | solution.py:347
  521.4 69.2 %collective-permute-start.83 = (bf16[64,2816]{1,0:T(8,128)(2,1)}, bf16[64,2816]{1,0:T(8,128)(2,1)}, u32[]{:S(2)}, u32[]{:S(2)}) collective-permute-start(bf16[64,2816]{1,0:T(8,128)(2,1)} %fusion.108), channel_id=1, source_target_pairs={{0,8},{8,0},{16,24},{24,16},{1,9},{9,1},{17,25},{25,17},{2,10},{10... | collective-permute-start | bytes 1081352 | tf_op jit(solution)/shard_map/ppermute | solution.py:347
  546.4 52.9 %collective-permute-start.85 = (bf16[2,64,1536]{2,1,0:T(8,128)(2,1)}, bf16[2,64,1536]{2,1,0:T(8,128)(2,1)}, u32[]{:S(2)}, u32[]{:S(2)}) collective-permute-start(bf16[2,64,1536]{2,1,0:T(8,128)(2,1)} %fusion.137), channel_id=1, source_target_pairs={{0,8},{8,0},{16,24},{24,16},{1,9},{9,1},{17,25},{25,17},{2,10},{10... | collective-permute-start | bytes 1179656 | tf_op jit(solution)/shard_map/ppermute | solution.py:347
  (191 other events, 2010.1 us)

commit v4 on v3

--- a/solution.py
+++ b/solution.py
@@ -225,13 +225,13 @@
             dvec_ref[0, head : head + 1, :] = sums + jnp.where(lane == BLOCK, far, 0.0)
 
 
-def specs_of(rows, length, pairs, groups):
-    cols = pl.BlockSpec((rows, 2 * BLOCK), lambda g, *_: (0, g))
-    keys = pl.BlockSpec((length, BLOCK), lambda g, *_: (0, g))
-    values = pl.BlockSpec((length, BLOCK), lambda g, *_: (0, groups + g))
-    outs = pl.BlockSpec((1, pairs, HEAD, 4 * BLOCK), lambda g, *_: (g, 0, 0, 0))
-    logs = pl.BlockSpec((1, pairs, 8, 4 * BLOCK), lambda g, *_: (g, 0, 0, 0))
-    vecs = pl.BlockSpec((1, 4, SPAN), lambda g, *_: (g, 0, 0))
+def specs_of(rows, length, pairs, groups, first=0):
+    cols = pl.BlockSpec((rows, 2 * BLOCK), lambda g, *_: (0, g + first))
+    keys = pl.BlockSpec((length, BLOCK), lambda g, *_: (0, g + first))
+    values = pl.BlockSpec((length, BLOCK), lambda g, *_: (0, groups + g + first))
+    outs = pl.BlockSpec((1, pairs, HEAD, 4 * BLOCK), lambda g, *_: (g + first, 0, 0, 0))
+    logs = pl.BlockSpec((1, pairs, 8, 4 * BLOCK), lambda g, *_: (g + first, 0, 0, 0))
+    vecs = pl.BlockSpec((1, 4, SPAN), lambda g, *_: (g + first, 0, 0))
     lims = pl.BlockSpec((pairs, BLOCK), lambda g, *_: (0, 0))
     return cols, keys, values, outs, logs, vecs, lims
 
@@ -266,35 +266,37 @@
     )(table, query, keys_values, keys_values, *extra)
 
 
-def attend_back(query, keys_values, grad, outs_in, logs_in, table, extra, masked):
+def attend_back(query, keys_values, grad, outs_in, logs_in, table, extra, masked, part=0, parts=1):
     rows, width = query.shape
     length = keys_values.shape[0]
     groups = width // (4 * HEAD)
     pairs = rows // BLOCK
-    cols, kspec, vspec, outs, logs, vecs, lims = specs_of(rows, length, pairs, groups)
+    count = groups // parts
+    cols, kspec, vspec, outs, logs, vecs, lims = specs_of(rows, length, pairs, groups, part * count)
     scratch = [pltpu.VMEM((length, BLOCK), F32), pltpu.VMEM((length, BLOCK), F32), pltpu.VMEM((HEAD, 4 * BLOCK), F32)]
-    out_specs = [cols, pl.BlockSpec((2, length, BLOCK), lambda g, *_: (0, 0, g))]
+    out_specs = [pl.BlockSpec((rows, 2 * BLOCK), lambda g, *_: (0, g)), pl.BlockSpec((2, length, BLOCK), lambda g, *_: (0, 0, g))]
     out_shape = [
-        jax.ShapeDtypeStruct((rows, width), BF16),
-        jax.ShapeDtypeStruct((2, length, width // 2), BF16),
+        jax.ShapeDtypeStruct((rows, width // parts), BF16),
+        jax.ShapeDtypeStruct((2, length, width // 2 // parts), BF16),
     ]
     if masked:
         scratch = [pltpu.VMEM((3, BLOCK, 4 * BLOCK), F32)] + scratch
         scratch += [pltpu.VMEM((2, BLOCK, 4 * BLOCK), F32), pltpu.VMEM((8, 4 * BLOCK), F32)]
-        out_specs = out_specs + [vecs]
-        out_shape = out_shape + [jax.ShapeDtypeStruct((groups, 4, SPAN), F32)]
+        out_specs = out_specs + [pl.BlockSpec((1, 4, SPAN), lambda g, *_: (g, 0, 0))]
+        out_shape = out_shape + [jax.ShapeDtypeStruct((count, 4, SPAN), F32)]
     return pl.pallas_call(
         functools.partial(backward_kernel, masked),
         grid_spec=pltpu.PrefetchScalarGridSpec(
             num_scalar_prefetch=1,
-            grid=(groups,),
+            grid=(count,),
             in_specs=[cols, kspec, vspec, cols, outs, logs] + ([vecs, lims, lims] if masked else []),
             out_specs=out_specs,
             scratch_shapes=scratch,
         ),
         out_shape=out_shape,
         cost_estimate=pl.CostEstimate(
-            flops=10 * rows * length * width, bytes_accessed=8 * length * width, transcendentals=rows * length * 16
+            flops=10 * rows * length * width // parts, bytes_accessed=8 * length * width // parts,
+            transcendentals=rows * length * 16 // parts
         ),
         name="attend_self_back" if masked else "attend_cross_back",
     )(table, query, keys_values, keys_values, grad, outs_in, logs_in, *extra)
@@ -355,13 +357,29 @@
     return (left.astype(F32) + right.astype(F32)).astype(BF16)
 
 
-def blank(shape):
+def place_kernel(spots, rows, me_ref, *refs):
+    pieces, whole_ref, sems = refs[: len(spots)], refs[len(spots)], refs[len(spots) + 1]
+    copies = []
+    for index, (mask, offset) in enumerate(spots):
+        count = pieces[index].shape[0]
+        start = pl.multiple_of((me_ref[0] ^ mask) * rows + offset, count)
+        copies.append(pltpu.make_async_copy(pieces[index], whole_ref.at[pl.ds(start, count), :], sems.at[index]))
+    for copy in copies:
+        copy.start()
+    for copy in copies:
+        copy.wait()
+
+
+def place(me, pieces, spots, size, rows):
+    anywhere = pl.BlockSpec(memory_space=pl.ANY)
     return pl.pallas_call(
-        lambda out_ref: None,
-        out_shape=jax.ShapeDtypeStruct(shape, BF16),
-        out_specs=pl.BlockSpec(memory_space=pl.ANY),
-        name="blank",
-    )()
+        functools.partial(place_kernel, spots, rows),
+        in_specs=[pl.BlockSpec(memory_space=pltpu.SMEM)] + [anywhere] * len(pieces),
+        out_specs=anywhere,
+        out_shape=jax.ShapeDtypeStruct((size * rows, pieces[0].shape[1]), BF16),
+        scratch_shapes=[pltpu.SemaphoreType.DMA((len(pieces),))],
+        name="place",
+    )(me.reshape(1), *pieces)
 
 
 class Lane:
@@ -375,6 +393,11 @@
             self.pending = self.steps.send(arrived)
         except StopIteration as end:
             self.pending, self.result = None, end.value
+
+    def take(self):
+        while self.pending is not None:
+            tick([self], ())
+        return self.result
 
     def take(self):
         while self.pending is not None:
@@ -433,15 +456,15 @@
     bits = bits_of(size)
     half = rows // 2
     streams = [[(0, mine[stream * half : (stream + 1) * half])] for stream in range(2)]
-    whole = lax.dynamic_update_slice(blank((size * rows, width)), mine, (me * rows, 0))
     for step in range(len(bits)):
         chosen = [(bits if stream == 0 else bits[::-1])[step] for stream in range(2)]
         got = yield [[cross(piece, "fsdp", chosen[stream]) for _, piece in streams[stream]] for stream in range(2)]
         for stream in range(2):
             fresh = [(mask ^ chosen[stream], piece) for (mask, _), piece in zip(streams[stream], got[stream])]
             streams[stream] = streams[stream] + fresh
-            for mask, piece in fresh:
-                whole = lax.dynamic_update_slice(whole, piece, ((me ^ mask) * rows + stream * half, 0))
+    spots = [(0, 0)] + [(mask, stream * half) for stream in range(2) for mask, _ in streams[stream][1:]]
+    pieces = [mine] + [piece for stream in range(2) for _, piece in streams[stream][1:]]
+    whole = place(me, pieces, spots, size, rows)
     whole, other = yield whole, swap(whole)
     return whole, other
 
@@ -469,26 +492,28 @@
     return keep, lax.dynamic_index_in_dim(value, 1 - mine, place, keepdims=False)
 
 
-def reduce_steps(partial, widths):
+def reduce_steps(partials, widths):
     size = lax.axis_size("fsdp")
     lines = lax.axis_size("line")
-    rows = partial.shape[0] // size
-    width = partial.shape[1]
+    rows = partials[0].shape[0] // size
+    width = partials[0].shape[1]
+    many = len(partials)
     bits = bits_of(size)
-    folded = partial.reshape([2] * len(bits) + [2, rows // 2, width])
-    values = [lax.index_in_dim(folded, stream, len(bits), keepdims=False) for stream in range(2)]
+    folded = jnp.stack(partials).reshape([many] + [2] * len(bits) + [2, rows // 2, width])
+    values = [lax.index_in_dim(folded, stream, 1 + len(bits), keepdims=False) for stream in range(2)]
     left = [bits[::-1], bits[::-1]]
     for step in range(len(bits)):
         chosen = [(bits if stream == 0 else bits[::-1])[step] for stream in range(2)]
         parts = [
-            split(values[stream], "fsdp", chosen[stream], left[stream].index(chosen[stream])) for stream in range(2)
+            split(values[stream], "fsdp", chosen[stream], 1 + left[stream].index(chosen[stream]))
+            for stream in range(2)
         ]
         got = yield [cross(parts[stream][1], "fsdp", chosen[stream]) for stream in range(2)]
         values = [add(parts[stream][0], got[stream]) for stream in range(2)]
         left = [[item for item in left[stream] if item != chosen[stream]] for stream in range(2)]
-    shard = jnp.stack(values)
+    shard = jnp.stack(values, axis=1)
     line_bits = bits_of(lines)
-    value = shard.reshape([2] * len(line_bits) + [rows // lines, width])
+    value = shard.reshape([many] + [2] * len(line_bits) + [rows // lines, width])
     for bit in line_bits:
         keep, send = split(value, "line", bit, value.ndim - 3)
         (got,) = yield [cross(send, "line", bit)]
@@ -502,13 +527,14 @@
     (other,) = yield [swap(mine)]
     me = lax.axis_index("line")
     outs = []
-    start = 0
-    for wide in widths:
-        part = slice(start, start + wide // 2)
-        both = jnp.concatenate(by_core(mine[..., part], other[..., part]), axis=2)
-        ordered = [lax.dynamic_index_in_dim(both, me ^ index, 0, keepdims=False) for index in range(lines)]
-        outs.append(jnp.concatenate(ordered, axis=0).astype(F32))
-        start = start + wide // 2
+    for index in range(many):
+        start = 0
+        for wide in widths[index]:
+            part = slice(start, start + wide // 2)
+            both = jnp.concatenate(by_core(mine[:, index, :, part], other[:, index, :, part]), axis=2)
+            ordered = [lax.dynamic_index_in_dim(both, me ^ entry, 0, keepdims=False) for entry in range(lines)]
+            outs.append(jnp.concatenate(ordered, axis=0).astype(F32))
+            start = start + wide // 2
     return outs
 
 
@@ -566,7 +592,6 @@
     lane_qkv = Lane(gather_steps(half_columns([joint([w_query, w_key, w_value], axis=1)])))
     lane_small = Lane(small_steps(joint([gain_self, gain_cross, gain_ffn, bias_table.reshape(-1)])))
     mask_rows = valid_mask.reshape(rows).astype(F32)
-    lane_count = Lane(sum_steps(jnp.broadcast_to(jnp.sum(mask_rows), (8, 128))))
     mid_shard = half_columns([w_out, c_query, joint([c_key, c_value], axis=1), c_out])
     mid_shard = tick([lane_qkv, lane_small], mid_shard)
 
@@ -590,7 +615,7 @@
     bucket_match = (jnp.take(buckets, index_of)[None, :] == jnp.arange(BUCKETS, dtype=jnp.int32)[:, None])
 
     gu_shard, wd_shard, low, high, place_table, bucket_match = tick(
-        [lane_qkv, lane_small, lane_count], (gu_shard, wd_shard, low, high, place_table, bucket_match)
+        [lane_qkv, lane_small], (gu_shard, wd_shard, low, high, place_table, bucket_match)
     )
 
     small = lane_small.take()
@@ -601,18 +626,18 @@
     vectors = tn(table_whole, bucket_match.astype(BF16)).reshape(HEADS // 4, 4, SPAN)
     flat_in = inputs.reshape(rows, width).astype(F32)
     normed_one, scale_one, hidden_one = norm_rows(flat_in, gain_one)
-    hidden_one, vectors = tick([lane_qkv, lane_count], (hidden_one, vectors))
+    hidden_one, vectors = tick([lane_qkv], (hidden_one, vectors))
     extra = (vectors, low, high)
 
     qkv_mine, qkv_other = lane_qkv.take()
     lane_mid = Lane(gather_steps(mid_shard))
     query, pairs = by_core(nn(hidden_one, qkv_mine).astype(BF16), nn(hidden_one, qkv_other).astype(BF16))
-    query, pairs = tick([lane_count], (query, pairs))
+    query, pairs = tick([], (query, pairs))
 
     lane_keys = Lane(gather_context_steps(pairs))
-    gu_shard = tick([lane_keys, lane_mid, lane_count], gu_shard)
+    gu_shard = tick([lane_keys, lane_mid], gu_shard)
     lane_hidden_one = Lane(swap_steps(hidden_one))
-    wd_shard = tick([lane_keys, lane_mid, lane_count, lane_hidden_one], wd_shard)
+    wd_shard = tick([lane_keys, lane_mid, lane_hidden_one], wd_shard)
     lane_gu = Lane(gather_steps(gu_shard))
     tick([lane_keys, lane_mid], ())
     mid_mine, mid_other = lane_mid.take()
@@ -626,29 +651,30 @@
 
     lane_encoder = Lane(gather_context_steps(encoder_pairs))
     lane_encoder_rows = Lane(swap_steps(encoder_rows))
+    lane_count = Lane(sum_steps(jnp.broadcast_to(jnp.sum(mask_rows), (8, 128))))
     attention, outs_one, logs_one = attend(query, pairs_whole, place_table, extra, True)
-    attention, outs_one, logs_one = tick([lane_gu, lane_encoder, lane_encoder_rows], (attention, outs_one, logs_one))
+    attention, outs_one, logs_one = tick([lane_gu, lane_encoder, lane_encoder_rows, lane_count], (attention, outs_one, logs_one))
 
     lane_attention = Lane(swap_steps(attention))
     mid_one = flat_in + times(attention, wo)
     normed_two, scale_two, hidden_two = norm_rows(mid_one, gain_two)
     cross_q = times(hidden_two, wcq).astype(BF16)
     mid_one, normed_two, hidden_two, cross_q, scale_two = tick(
-        [lane_encoder, lane_attention], (mid_one, normed_two, hidden_two, cross_q, scale_two)
-    )
-    tick([lane_encoder], ())
+        [lane_encoder, lane_attention, lane_count], (mid_one, normed_two, hidden_two, cross_q, scale_two)
+    )
+    tick([lane_encoder, lane_count], ())
     encoder_whole = lane_encoder.take()
 
     lane_hidden_two = Lane(swap_steps(hidden_two))
     crossed, outs_two, logs_two = attend(cross_q, encoder_whole, place_table, (), False)
-    crossed, outs_two, logs_two = tick([lane_gu, lane_hidden_two], (crossed, outs_two, logs_two))
+    crossed, outs_two, logs_two = tick([lane_gu, lane_hidden_two, lane_count], (crossed, outs_two, logs_two))
 
     lane_wd = Lane(gather_steps(wd_shard))
     lane_crossed = Lane(swap_steps(crossed))
     mid_two = mid_one + times(crossed, wco)
     normed_three, scale_three, hidden_three = norm_rows(mid_two, gain_three)
     mid_two, normed_three, hidden_three, scale_three = tick(
-        [lane_gu, lane_wd, lane_crossed], (mid_two, normed_three, hidden_three, scale_three)
+        [lane_gu, lane_wd, lane_crossed, lane_count], (mid_two, normed_three, hidden_three, scale_three)
     )
 
     gu_mine, gu_other = lane_gu.take()
@@ -685,12 +711,12 @@
     partial_down = weight_grad(mixed, lane_mixed.take()[0], down_mine, lane_down.take()[0])
     partial_down = tick([lane_wide], partial_down)
 
-    lane_down = Lane(reduce_steps(partial_down, (D,)))
+    lane_down = Lane(reduce_steps([partial_down], [(D,)]))
     partial_wide = weight_grad(hidden_three, lane_hidden_three.take()[0], wide_mine, lane_wide.take()[0])
     grad_hidden_three = times_back(joint([grad_gate, grad_up], axis=1), (gu_mine, gu_other))
     partial_wide, grad_hidden_three = tick([lane_down], (partial_wide, grad_hidden_three))
 
-    lane_wide = Lane(reduce_steps(partial_wide, (hidden_ff, hidden_ff)))
+    lane_wide = Lane(reduce_steps([partial_wide], [(hidden_ff, hidden_ff)]))
     grad_norm_three, grad_gain_three = norm_back(grad_hidden_three, normed_three, scale_three, gain_three)
     grad_mid_two = grad_result + grad_norm_three
 
@@ -716,41 +742,59 @@
         [lane_down, lane_encoder, lane_out], (grad_mid_one, one_mine, one_away, grad_attention)
     )
     lane_one = Lane(swap_steps(one_away))
-    grad_query, grad_pairs, grad_vectors = attend_back(
-        query, pairs_whole, grad_attention, outs_one, logs_one, place_table, extra, True
-    )
-    grad_query, grad_pairs, grad_vectors = tick(
-        [lane_down, lane_wide, lane_encoder, lane_one], (grad_query, grad_pairs, grad_vectors)
-    )
-
-    lane_pairs = Lane(reduce_context_steps(grad_pairs))
+
+    def attend_part(part):
+        return attend_back(
+            query, pairs_whole, grad_attention, outs_one, logs_one, place_table, extra, True, part, 2
+        )
+
+    query_first, pairs_first, vectors_first = attend_part(0)
+    query_first, pairs_first, vectors_first, grad_attention = tick(
+        [lane_down, lane_wide, lane_encoder, lane_one], (query_first, pairs_first, vectors_first, grad_attention)
+    )
+    lane_first = Lane(reduce_context_steps(pairs_first))
+    query_second, pairs_second, vectors_second = attend_part(1)
+    grad_query = joint([query_first, query_second], axis=1)
+    grad_vectors = joint([vectors_first, vectors_second], axis=0)
+    query_mine, query_away = grad_halves(grad_query)
+    pairs_second, grad_query, grad_vectors, query_mine, query_away = tick(
+        [lane_down, lane_wide, lane_encoder, lane_first],
+        (pairs_second, grad_query, grad_vectors, query_mine, query_away),
+    )
+
+    lane_second = Lane(reduce_context_steps(pairs_second))
+    lane_query = Lane(swap_steps(query_away))
     arrived = lane_out.take()[0]
     partial_out = weight_grad(crossed, lane_crossed.take()[0], out_mine[:, :halves], arrived[:, :halves])
-    partial_query = weight_grad(hidden_two, lane_hidden_two.take()[0], out_mine[:, halves:], arrived[:, halves:])
+    partial_cross = weight_grad(hidden_two, lane_hidden_two.take()[0], out_mine[:, halves:], arrived[:, halves:])
     partial_one = weight_grad(attention, lane_attention.take()[0], one_mine, lane_one.take()[0])
-    partial_mid = joint([partial_out, partial_query, partial_one], axis=1)
-    partial_mid = tick([lane_pairs, lane_wide, lane_encoder], partial_mid)
-
-    lane_mid = Lane(reduce_steps(partial_mid, (D, D, D)))
-    encoder_mine = joint([lane_encoder.take()[0], lane_encoder.take()[1]], axis=1)
+    encoder_got = lane_encoder.take()
+    encoder_mine = joint([encoder_got[0], encoder_got[1]], axis=1)
+    keys_mine, keys_away = grad_halves(encoder_mine[:, :key_width], encoder_mine[:, key_width:])
+    partial_out, partial_cross, partial_one, encoder_mine, keys_mine, keys_away = tick(
+        [lane_first, lane_second, lane_down, lane_query],
+        (partial_out, partial_cross, partial_one, encoder_mine, keys_mine, keys_away),
+    )
+
+    lane_keys = Lane(swap_steps(keys_away))
+    partial_query = weight_grad(hidden_one, lane_hidden_one.take()[0], query_mine, lane_query.take()[0])
+    lane_mid = Lane(reduce_steps([partial_out, partial_cross, partial_one, partial_query], [(D,)] * 4))
     grad_encoder = times_back(encoder_mine, wckv)
-    keys_mine, keys_away = grad_halves(encoder_mine[:, :key_width], encoder_mine[:, key_width:])
-    grad_encoder, keys_mine, keys_away = tick([lane_pairs, lane_mid, lane_wide], (grad_encoder, keys_mine, keys_away))
-
-    lane_keys = Lane(swap_steps(keys_away))
-    tick([lane_pairs, lane_mid, lane_keys], ())
-    mine = lane_pairs.take()
-    last_mine, last_away = grad_halves(grad_query, mine[0], mine[1])
-    last_mine, last_away = tick([], (last_mine, last_away))
+    grad_encoder = tick([lane_first, lane_second, lane_down, lane_wide, lane_keys], grad_encoder)
+
+    partial_keys = weight_grad(encoder_rows, lane_encoder_rows.take()[0], keys_mine, lane_keys.take()[0])
+    partial_keys = tick([lane_second, lane_mid], partial_keys)
+    pairs_first, pairs_second = lane_first.take(), lane_second.take()
+    mine = [joint([pairs_first[index], pairs_second[index]], axis=1) for index in range(2)]
+    last_mine, last_away = grad_halves(mine[0], mine[1])
+    mine, last_mine, last_away = tick([], (mine, last_mine, last_away))
 
     lane_last = Lane(swap_steps(last_away))
-    partial_keys = weight_grad(encoder_rows, lane_encoder_rows.take()[0], keys_mine, lane_keys.take()[0])
-    partial_keys = tick([lane_last], partial_keys)
+    tick([lane_last], ())
     partial_last = weight_grad(hidden_one, lane_hidden_one.take()[0], last_mine, lane_last.take()[0])
-    partial_last = joint([partial_last, partial_keys], axis=1)
-    partial_last = tick([lane_wide, lane_down], partial_last)
-
-    lane_last = Lane(reduce_steps(partial_last, (D, key_width, key_width, key_width, key_width)))
+    partial_last = tick([lane_mid, lane_wide], partial_last)
+
+    lane_last = Lane(reduce_steps([partial_last, partial_keys], [(key_width, key_width)] * 2))
     grad_packed = joint([grad_query, mine[0], mine[1]], axis=1)
     grad_norm_one, grad_gain_one = norm_back(
         times_back(grad_packed, (qkv_mine, qkv_other)), normed_one, scale_one, gain_one
@@ -781,8 +825,8 @@
     sums = lane_sums.take().reshape(-1)
     (grad_down,) = lane_down.take()
     grad_gate_weight, grad_up_weight = lane_wide.take()
-    grad_cross_out, grad_cross_query, grad_out_weight = lane_mid.take()
-    grad_query_weight, grad_key_weight, grad_value_weight, grad_cross_key, grad_cross_value = lane_last.take()
+    grad_cross_out, grad_cross_query, grad_out_weight, grad_query_weight = lane_mid.take()
+    grad_key_weight, grad_value_weight, grad_cross_key, grad_cross_value = lane_last.take()
     loss = sums[3 * D + 512] / (D * count)
 
     def shard_of(offset, amount):

time: 696 us -> 1060 us (1.52)
  Pallas kernels: 70.5 us -> 541 us
  local copies, waits for them, and re-layouts: 161 us -> 57.1 us
  waiting for transfers between devices: 151 us -> 203 us
  other arithmetic: 87.6 us -> 63.9 us
  matrix products: 93.3 us -> 77.4 us
    pallas_call x4, Pallas kernels: 0.01 us -> 457 us  [place(): pl.pallas_call(functools.partial(place_kernel, spots, rows), in_specs=[pl...]
    ppermute x108 -> x112, waiting for transfers between devices: 151 us -> 203 us  [cross(): return lax.ppermute(value, axis, partners(lax.axis_size(axis), bit))]
    dynamic_update_slice x27 -> x0, local copies, waits for them, and re-layouts: 35.4 us -> none  [the longest x24 32.3 us: gather_steps(): lax.dynamic_update_slice(whole, piece, ((me ^ mask) * rows + stream * hal...]
    unnamed x242 -> x249, local copies, waits for them, and re-layouts: 47.9 us -> 16.4 us
    dynamic_slice x4 -> x0, local copies, waits for them, and re-layouts: 18.6 us -> none  [split(): keep = lax.dynamic_index_in_dim(value, mine, place, keepdims=False)]
    pallas_call x2 -> x3, Pallas kernels: 40.6 us -> 49 us  [attend_back(): pl.pallas_call(functools.partial(backward_kernel, masked), grid_spec=pltp...]
    convert_element_type x28 -> x30, other arithmetic: 24.4 us -> 16.9 us  [add(): return (left.astype(F32) + right.astype(F32)).astype(BF16)]
    ppermute x108 -> x112, starting transfers between devices: 122 us -> 116 us  [cross(): return lax.ppermute(value, axis, partners(lax.axis_size(axis), bit))]
  transfers between devices with their start and end apart: 108 -> 112, of which waited for: 32 -> 37; matrix products, arithmetic and copies ran while one was open for 40% -> 15% of each run, Pallas kernels for 10% -> 8%
where the time goes in v4:
time: 1060 us; the launch traced here: 1070 us
  Pallas kernels  541 us (51%)
  waiting for transfers between devices  203 us (19%)
  starting transfers between devices  116 us (11%)
  matrix products  77.4 us (7%)
  other arithmetic  63.9 us (6%)
  local copies, waits for them, and re-layouts  57.1 us (5%)
    pallas_call x4, Pallas kernels, place(): pl.pallas_call(functools.partial(place_kernel, spots, rows), in_specs=[pl...  457 us
    ppermute x112, waiting for transfers between devices, cross(): return lax.ppermute(value, axis, partners(lax.axis_size(axis), bit))  203 us
    ppermute x112, starting transfers between devices, cross(): return lax.ppermute(value, axis, partners(lax.axis_size(axis), bit))  116 us
    pallas_call x3, Pallas kernels, attend_back(): pl.pallas_call(functools.partial(backward_kernel, masked), grid_spec=pltp...  49 us
    pallas_call x2, Pallas kernels, attend(): pl.pallas_call(functools.partial(forward_kernel, masked), grid_spec=pltpu...  34.5 us
    dot_general x14, matrix products, nn(): return jnp.dot(left, right, preferred_element_type=F32)  28.5 us
    dot_general x14, matrix products, nt(): lax.dot_general(left, right, (((1,), (1,)), ((), ())), preferred_element_...  27.5 us
  transfers between devices with their start and end apart: 112, of which 37 were waited for; matrix products, arithmetic and copies ran while one was open for 15% of the time, Pallas kernels for 8%

profile of v4, /device:TPU:0, one launch (start us, length us, event | category | flops | bytes accessed | tf_op | source)
XLA Modules:
  0.0 1066.2 jit_solution(10933447208128227450)
XLA Ops:
  38.0 64.7 %place.4 = bf16[1024,1024]{1,0:T(8,128)(2,1)} custom-call(s32[1]{0:T(128)} %bitcast.9.me_ref, bf16[256,1024]{1,0:T(8,128)(2,1)} %copy-done.20, bf16[128,1024]{1,0:T(8,128)(2,1)} %collective-permute-done.1.refs_1_, bf16[128,1024]{1,0:T(8,128)(2,1)} %collective-permute-done.refs_2_, bf16[128,1024]{1,0:T(8,128)(2,1)} %copy-done.70, ...), custom_call_target="tpu_custom_call" | custom-call | tf_op jit(solution)/shard_map/place/pallas_call | solution.py:375
  120.5 19.4 %collective-permute-done.11 = bf16[256,1024]{1,0:T(8,128)(2,1)S(1)} collective-permute-done((bf16[256,1024]{1,0:T(8,128)(2,1)S(1)}, bf16[256,1024]{1,0:T(8,128)(2,1)S(1)}, u32[]{:S(2)}, u32[]{:S(2)}) %collective-permute-start.11) | collective-permute-done | bytes 524320 | tf_op jit(solution)/shard_map/ppermute | solution.py:349
  143.4 10.2 collective-permute-done.14
  155.3 128.2 %place.5 = bf16[1024,2048]{1,0:T(8,128)(2,1)} custom-call(s32[1]{0:T(128)} %bitcast.9.me_ref, bf16[256,2048]{1,0:T(8,128)(2,1)} %pad_maximum_fusion.5.refs_0_, bf16[128,2048]{1,0:T(8,128)(2,1)} %collective-permute-done.12.refs_1_, bf16[128,2048]{1,0:T(8,128)(2,1)} %copy-done.57, bf16[128,2048]{1,0:T(8,128)(2,1)} %copy-done.59, ...), custom_call_target="tpu_custom_call" | custom-call | tf_op jit(solution)/shard_map/place/pallas_call | solution.py:375
  302.5 18.1 %attend_self.1 = (bf16[256,1024]{1,0:T(8,128)(2,1)}, f32[4,2,64,512]{3,2,1,0:T(8,128)}, f32[4,2,8,512]{3,2,1,0:T(8,128)}) custom-call(s32[20]{0:T(128)} %pad_add_fusion.1.table, bf16[256,1024]{1,0:T(8,128)(2,1)} %get-tuple-element.240.refs_0_, bf16[2048,1024]{1,0:T(8,128)(2,1)} %constant_dynamic-update-slice_fusion.refs_1_.refs_2_, ...), custom_call_target="tpu_custom_call" | custom-call | flops 2147483648 | bytes 8388608 | tf_op jit(solution)/shard_map/attend_self/pallas_call | solution.py:248
  320.6 14.7 %collective-permute-start.27 = (bf16[64,1024]{1,0:T(8,128)(2,1)S(1)}, bf16[64,1024]{1,0:T(8,128)(2,1)S(1)}, u32[]{:S(2)}, u32[]{:S(2)}) collective-permute-start(bf16[64,1024]{1,0:T(8,128)(2,1)S(1)} %pad_maximum_fusion.17), channel_id=1, source_target_pairs={{0,8},{8,0},{16,24},{24,16},{1,9},{9,1},{17,25},{25,17},{2,10},{10... | collective-permute-start | bytes 393224 | tf_op jit(solution)/shard_map/ppermute | solution.py:349
  355.3 12.3 %collective-permute-done.33.refs_2_ = bf16[128,2816]{1,0:T(8,128)(2,1)} collective-permute-done((bf16[128,2816]{1,0:T(8,128)(2,1)}, bf16[128,2816]{1,0:T(8,128)(2,1)}, u32[]{:S(2)}, u32[]{:S(2)}) %collective-permute-start.33) | collective-permute-done | bytes 720928 | tf_op jit(solution)/shard_map/ppermute | solution.py:349
  367.6 16.4 %attend_cross.1 = (bf16[256,1024]{1,0:T(8,128)(2,1)}, f32[4,2,64,512]{3,2,1,0:T(8,128)}, f32[4,2,8,512]{3,2,1,0:T(8,128)}) custom-call(s32[20]{0:T(128)} %pad_add_fusion.1.table, bf16[256,1024]{1,0:T(8,128)(2,1)} %pad_maximum_fusion.8.refs_0_, bf16[512,1024]{1,0:T(8,128)(2,1)} %copy-done.86, bf16[512,1024]{1,0:T(8,128)(2,1)} %copy-done.86), custom_call_target="tpu_custom_call" | custom-call | flops 536870912 | bytes 2097152 | tf_op jit(solution)/shard_map/attend_cross/pallas_call | solution.py:248
  384.0 175.9 %place.6 = bf16[1024,2816]{1,0:T(8,128)(2,1)} custom-call(s32[1]{0:T(128)} %bitcast.9.me_ref, bf16[256,2816]{1,0:T(8,128)(2,1)} %copy-done.5, bf16[128,2816]{1,0:T(8,128)(2,1)} %collective-permute-done.22.refs_1_, bf16[128,2816]{1,0:T(8,128)(2,1)} %collective-permute-done.33.refs_2_, bf16[128,2816]{1,0:T(8,128)(2,1)} %collective-permute-done.34.refs_3_, ...), custom_call_target="tpu_custom_call" | custom-call | tf_op jit(solution)/shard_map/place/pallas_call | solution.py:375
  592.1 88.5 %place.7 = bf16[2816,512]{1,0:T(8,128)(2,1)} custom-call(s32[1]{0:T(128)} %bitcast.9.me_ref, bf16[704,512]{1,0:T(8,128)(2,1)} %constant_dynamic-slice_fusion.23.refs_0_, bf16[352,512]{1,0:T(8,128)(2,1)} %copy-done.61, bf16[352,512]{1,0:T(8,128)(2,1)} %copy-done.63, bf16[352,512]{1,0:T(8,128)(2,1)} %copy-done.65, bf16[352,512]{1,0:T(8,128)(2,1)} %copy-done.62, ...), custom_call_target="tpu_custom_call" | custom-call | tf_op jit(solution)/shard_map/place/pallas_call | solution.py:375
  717.9 10.9 %collective-permute-done.53 = bf16[1,2,352,512]{3,2,1,0:T(8,128)(2,1)S(1)} collective-permute-done((bf16[1,2,352,512]{3,2,1,0:T(8,128)(2,1)S(1)}, bf16[1,2,352,512]{3,2,1,0:T(8,128)(2,1)S(1)}, u32[]{:S(2)}, u32[]{:S(2)}) %collective-permute-start.53) | collective-permute-done | bytes 720928 | tf_op jit(solution)/shard_map/ppermute | solution.py:349
  744.2 16.6 %attend_cross_back.1 = (bf16[256,1024]{1,0:T(8,128)(2,1)}, bf16[2,512,512]{2,1,0:T(8,128)(2,1)}) custom-call(s32[20]{0:T(128)} %pad_add_fusion.1.table, bf16[256,1024]{1,0:T(8,128)(2,1)} %pad_maximum_fusion.8.refs_0_, bf16[512,1024]{1,0:T(8,128)(2,1)} %copy-done.86, bf16[512,1024]{1,0:T(8,128)(2,1)} %copy-done.86, bf16[256,1024]{1,0:T(8,128)(2,1)} %fusion.36.refs_3_, ...), custom_call_target="tpu_custom_call" | custom-call | flops 1342177280 | bytes 4194304 | tf_op jit(solution)/shard_map/attend_cross_back/pallas_call | solution.py:287
  762.2 11.6 %collective-permute-done.57 = bf16[1,2,128,2816]{3,2,1,0:T(8,128)(2,1)} collective-permute-done((bf16[1,2,128,2816]{3,2,1,0:T(8,128)(2,1)}, bf16[1,2,128,2816]{3,2,1,0:T(8,128)(2,1)}, u32[]{:S(2)}, u32[]{:S(2)}) %collective-permute-start.57) | collective-permute-done | bytes 1441824 | tf_op jit(solution)/shard_map/ppermute | solution.py:349
  800.5 16.1 %attend_self_back.2 = (bf16[256,512]{1,0:T(8,128)(2,1)}, bf16[2,2048,256]{2,1,0:T(8,128)(2,1)}, f32[2,4,512]{2,1,0:T(4,128)}) custom-call(s32[20]{0:T(128)} %pad_add_fusion.1.table, bf16[256,1024]{1,0:T(8,128)(2,1)} %get-tuple-element.240.refs_0_, bf16[2048,1024]{1,0:T(8,128)(2,1)} %constant_dynamic-update-slice_fusion.refs_1_.refs_2_, ...), custom_call_target="tpu_custom_call" | custom-call | flops 2684354560 | bytes 8388608 | tf_op jit(solution)/shard_map/attend_self_back/pallas_call | solution.py:287
  824.9 8.1 collective-permute-start.73
  841.5 16.4 %attend_self_back.3 = (bf16[256,512]{1,0:T(8,128)(2,1)}, bf16[2,2048,256]{2,1,0:T(8,128)(2,1)}, f32[2,4,512]{2,1,0:T(4,128)}) custom-call(s32[20]{0:T(128)} %pad_add_fusion.1.table, bf16[256,1024]{1,0:T(8,128)(2,1)} %get-tuple-element.240.refs_0_, bf16[2048,1024]{1,0:T(8,128)(2,1)} %constant_dynamic-update-slice_fusion.refs_1_.refs_2_, ...), custom_call_target="tpu_custom_call" | custom-call | flops 2684354560 | bytes 8388608 | tf_op jit(solution)/shard_map/attend_self_back/pallas_call | solution.py:287
  868.2 8.4 collective-permute-start.74
  882.1 12.4 %collective-permute-done.71 = bf16[2,2,256,256]{3,2,0,1:T(8,128)(2,1)S(1)} collective-permute-done((bf16[2,2,256,256]{3,2,0,1:T(8,128)(2,1)}, bf16[2,2,256,256]{3,2,0,1:T(8,128)(2,1)S(1)}, u32[]{:S(2)}, u32[]{:S(2)}) %collective-permute-start.71) | collective-permute-done | bytes 524320 | tf_op jit(solution)/shard_map/ppermute | solution.py:349
  913.0 6.1 collective-permute-done.77
  925.9 22.2 %collective-permute-done.81 = bf16[2,1,256,256]{3,2,1,0:T(8,128)(2,1)S(1)} collective-permute-done((bf16[2,1,256,256]{3,2,1,0:T(8,128)(2,1)S(1)}, bf16[2,1,256,256]{3,2,1,0:T(8,128)(2,1)S(1)}, u32[]{:S(2)}, u32[]{:S(2)}) %collective-permute-start.81) | collective-permute-done | bytes 262176 | tf_op jit(solution)/shard_map/ppermute | solution.py:349
  954.5 12.5 %collective-permute-done.85 = bf16[4,128,512]{2,1,0:T(8,128)(2,1)S(1)} collective-permute-done((bf16[4,128,512]{2,1,0:T(8,128)(2,1)S(1)}, bf16[4,128,512]{2,1,0:T(8,128)(2,1)S(1)}, u32[]{:S(2)}, u32[]{:S(2)}) %collective-permute-start.85) | collective-permute-done | bytes 524320 | tf_op jit(solution)/shard_map/ppermute | solution.py:349
  974.2 16.6 %collective-permute-done.91 = bf16[1,64,2816]{2,1,0:T(8,128)(2,1)S(1)} collective-permute-done((bf16[1,64,2816]{2,1,0:T(8,128)(2,1)S(1)}, bf16[1,64,2816]{2,1,0:T(8,128)(2,1)S(1)}, u32[]{:S(2)}, u32[]{:S(2)}) %collective-permute-start.91) | collective-permute-done | bytes 360480 | tf_op jit(solution)/shard_map/ppermute | solution.py:349
  1000.6 7.7 collective-permute-done.96
  1013.2 15.1 %collective-permute-done.100 = f32[32,128]{1,0:T(8,128)S(1)} collective-permute-done((f32[32,128]{1,0:T(8,128)S(1)}, f32[32,128]{1,0:T(8,128)S(1)}, u32[]{:S(2)}, u32[]{:S(2)}) %collective-permute-start.100) | collective-permute-done | bytes 16416 | tf_op jit(solution)/shard_map/ppermute | solution.py:349
  (722 shorter events, 329.7 us)
Async XLA Ops:
  3.8 31.1 %collective-permute-start = (bf16[128,1024]{1,0:T(8,128)(2,1)}, bf16[128,1024]{1,0:T(8,128)(2,1)}, u32[]{:S(2)}, u32[]{:S(2)}) collective-permute-start(bf16[128,1024]{1,0:T(8,128)(2,1)} %get-tuple-element.558), channel_id=1, source_target_pairs={{0,2},{1,3},{2,0},{3,1},{4,6},{5,7},{6,4},{7,5},{8,10},{9,11},{10,... | collective-permute-start | bytes 786440 | tf_op jit(solution)/shard_map/ppermute | solution.py:349
  285.5 49.7 %collective-permute-start.25 = (bf16[64,1024]{1,0:T(8,128)(2,1)S(1)}, bf16[64,1024]{1,0:T(8,128)(2,1)}, u32[]{:S(2)}, u32[]{:S(2)}) collective-permute-start(bf16[64,1024]{1,0:T(8,128)(2,1)S(1)} %bitcast.600), channel_id=1, source_target_pairs={{0,4},{4,0},{1,5},{5,1},{2,6},{6,2},{3,7},{7,3},{8,12},{12,8},{9,1... | collective-permute-start | bytes 393224 | tf_op jit(solution)/shard_map/ppermute | solution.py:349
  286.9 33.7 %collective-permute-start.26 = (f32[8,128]{1,0:T(8,128)S(1)}, f32[8,128]{1,0:T(8,128)}, u32[]{:S(2)}, u32[]{:S(2)}) collective-permute-start(f32[8,128]{1,0:T(8,128)S(1)} %broadcast_in_dim.32), channel_id=1, source_target_pairs={{0,4},{4,0},{1,5},{5,1},{2,6},{6,2},{3,7},{7,3},{8,12},{12,8},{9,1... | collective-permute-start | bytes 12296 | tf_op jit(solution)/shard_map/ppermute | solution.py:349
  290.0 45.3 %collective-permute-start.22 = (bf16[128,2816]{1,0:T(8,128)(2,1)}, bf16[128,2816]{1,0:T(8,128)(2,1)}, u32[]{:S(2)}, u32[]{:S(2)}) collective-permute-start(bf16[128,2816]{1,0:T(8,128)(2,1)} %get-tuple-element.500), channel_id=1, source_target_pairs={{0,1},{1,0},{2,3},{3,2},{4,5},{5,4},{6,7},{7,6},{8,9},{9,8},{10,11... | collective-permute-start | bytes 2162696 | tf_op jit(solution)/shard_map/ppermute | solution.py:349
  293.9 41.3 %collective-permute-start.23 = (bf16[128,2816]{1,0:T(8,128)(2,1)}, bf16[128,2816]{1,0:T(8,128)(2,1)}, u32[]{:S(2)}, u32[]{:S(2)}) collective-permute-start(bf16[128,2816]{1,0:T(8,128)(2,1)} %get-tuple-element.499), channel_id=1, source_target_pairs={{0,2},{1,3},{2,0},{3,1},{4,6},{5,7},{6,4},{7,5},{8,10},{9,11},{10,... | collective-permute-start | bytes 2162696 | tf_op jit(solution)/shard_map/ppermute | solution.py:349
  299.5 35.8 %collective-permute-start.24 = (bf16[64,1024]{1,0:T(8,128)(2,1)S(1)}, bf16[64,1024]{1,0:T(8,128)(2,1)S(1)}, u32[]{:S(2)}, u32[]{:S(2)}) collective-permute-start(bf16[64,1024]{1,0:T(8,128)(2,1)S(1)} %pad_maximum_fusion.17), channel_id=1, source_target_pairs={{0,16},{8,24},{16,0},{24,8},{1,17},{9,25},{17,1},{25,9},{2,18},{10... | collective-permute-start | bytes 393224 | tf_op jit(solution)/shard_map/ppermute | solution.py:349
  320.6 26.7 %collective-permute-start.27 = (bf16[64,1024]{1,0:T(8,128)(2,1)S(1)}, bf16[64,1024]{1,0:T(8,128)(2,1)S(1)}, u32[]{:S(2)}, u32[]{:S(2)}) collective-permute-start(bf16[64,1024]{1,0:T(8,128)(2,1)S(1)} %pad_maximum_fusion.17), channel_id=1, source_target_pairs={{0,8},{8,0},{16,24},{24,16},{1,9},{9,1},{17,25},{25,17},{2,10},{10... | collective-permute-start | bytes 393224 | tf_op jit(solution)/shard_map/ppermute | solution.py:349
  349.6 34.4 %collective-permute-start.35 = (bf16[128,2816]{1,0:T(8,128)(2,1)}, bf16[128,2816]{1,0:T(8,128)(2,1)}, u32[]{:S(2)}, u32[]{:S(2)}) collective-permute-start(bf16[128,2816]{1,0:T(8,128)(2,1)} %get-tuple-element.499), channel_id=1, source_target_pairs={{0,1},{1,0},{2,3},{3,2},{4,5},{5,4},{6,7},{7,6},{8,9},{9,8},{10,11... | collective-permute-start | bytes 2162696 | tf_op jit(solution)/shard_map/ppermute | solution.py:349
  349.6 34.4 %collective-permute-start.34 = (bf16[128,2816]{1,0:T(8,128)(2,1)}, bf16[128,2816]{1,0:T(8,128)(2,1)}, u32[]{:S(2)}, u32[]{:S(2)}) collective-permute-start(bf16[128,2816]{1,0:T(8,128)(2,1)} %collective-permute-done.22.refs_1_), channel_id=1, source_target_pairs={{0,2},{1,3},{2,0},{3,1},{4,6},{5,7},{6,4},{7,5},{8,10},{9,11},{10,... | collective-permute-start | bytes 2162696 | tf_op jit(solution)/shard_map/ppermute | solution.py:349
  354.1 29.9 %collective-permute-start.36 = (bf16[128,2816]{1,0:T(8,128)(2,1)}, bf16[128,2816]{1,0:T(8,128)(2,1)}, u32[]{:S(2)}, u32[]{:S(2)}) collective-permute-start(bf16[128,2816]{1,0:T(8,128)(2,1)} %collective-permute-done.23.refs_4_), channel_id=1, source_target_pairs={{0,1},{1,0},{2,3},{3,2},{4,5},{5,4},{6,7},{7,6},{8,9},{9,8},{10,11... | collective-permute-start | bytes 2162696 | tf_op jit(solution)/shard_map/ppermute | solution.py:349
  354.1 29.9 %collective-permute-start.37 = (bf16[256,1024]{1,0:T(8,128)(2,1)S(1)}, bf16[256,1024]{1,0:T(8,128)(2,1)}, u32[]{:S(2)}, u32[]{:S(2)}) collective-permute-start(bf16[256,1024]{1,0:T(8,128)(2,1)S(1)} %get-tuple-element.280), channel_id=1, source_target_pairs={{0,4},{4,0},{1,5},{5,1},{2,6},{6,2},{3,7},{7,3},{8,12},{12,8},{9,1... | collective-permute-start | bytes 1572872 | tf_op jit(solution)/shard_map/ppermute | solution.py:349
  730.4 31.8 %collective-permute-start.55 = (bf16[1,352,512]{2,1,0:T(8,128)(2,1)S(1)}, bf16[1,352,512]{2,1,0:T(8,128)(2,1)}, u32[]{:S(2)}, u32[]{:S(2)}) collective-permute-start(bf16[1,352,512]{2,1,0:T(8,128)(2,1)S(1)} %dynamic-slice_bitcast_fusion.13), channel_id=1, source_target_pairs={{0,2},{1,3},{2,0},{3,1},{4,6},{5,7},{6,4},{7,5},{8,10},{9,11},{10,... | collective-permute-start | bytes 1081352 | tf_op jit(solution)/shard_map/ppermute | solution.py:349
  733.2 29.0 %collective-permute-start.56 = (bf16[1,352,512]{2,1,0:T(8,128)(2,1)}, bf16[1,352,512]{2,1,0:T(8,128)(2,1)}, u32[]{:S(2)}, u32[]{:S(2)}) collective-permute-start(bf16[1,352,512]{2,1,0:T(8,128)(2,1)} %dynamic-slice_bitcast_fusion.12), channel_id=1, source_target_pairs={{0,1},{1,0},{2,3},{3,2},{4,5},{5,4},{6,7},{7,6},{8,9},{9,8},{10,11... | collective-permute-start | bytes 1081352 | tf_op jit(solution)/shard_map/ppermute | solution.py:349
  735.5 38.3 %collective-permute-start.57 = (bf16[1,2,128,2816]{3,2,1,0:T(8,128)(2,1)}, bf16[1,2,128,2816]{3,2,1,0:T(8,128)(2,1)}, u32[]{:S(2)}, u32[]{:S(2)}) collective-permute-start(bf16[1,2,128,2816]{3,2,1,0:T(8,128)(2,1)} %dynamic-slice_bitcast_fusion.1), channel_id=1, source_target_pairs={{0,1},{1,0},{2,3},{3,2},{4,5},{5,4},{6,7},{7,6},{8,9},{9,8},{10,11... | collective-permute-start | bytes 4325384 | tf_op jit(solution)/shard_map/ppermute | solution.py:349
  738.1 35.7 %collective-permute-start.58 = (bf16[1,2,128,2816]{3,2,1,0:T(8,128)(2,1)}, bf16[1,2,128,2816]{3,2,1,0:T(8,128)(2,1)}, u32[]{:S(2)}, u32[]{:S(2)}) collective-permute-start(bf16[1,2,128,2816]{3,2,1,0:T(8,128)(2,1)} %dynamic-slice_bitcast_fusion), channel_id=1, source_target_pairs={{0,2},{1,3},{2,0},{3,1},{4,6},{5,7},{6,4},{7,5},{8,10},{9,11},{10,... | collective-permute-start | bytes 4325384 | tf_op jit(solution)/shard_map/ppermute | solution.py:349
  788.7 34.0 %collective-permute-start.63 = (bf16[1,128,2816]{2,1,0:T(8,128)(2,1)}, bf16[1,128,2816]{2,1,0:T(8,128)(2,1)}, u32[]{:S(2)}, u32[]{:S(2)}) collective-permute-start(bf16[1,128,2816]{2,1,0:T(8,128)(2,1)} %dynamic-slice_bitcast_fusion.5), channel_id=1, source_target_pairs={{0,2},{1,3},{2,0},{3,1},{4,6},{5,7},{6,4},{7,5},{8,10},{9,11},{10,... | collective-permute-start | bytes 2162696 | tf_op jit(solution)/shard_map/ppermute | solution.py:349
  791.8 30.9 %collective-permute-start.64 = (bf16[1,128,2816]{2,1,0:T(8,128)(2,1)}, bf16[1,128,2816]{2,1,0:T(8,128)(2,1)}, u32[]{:S(2)}, u32[]{:S(2)}) collective-permute-start(bf16[1,128,2816]{2,1,0:T(8,128)(2,1)} %dynamic-slice_bitcast_fusion.4), channel_id=1, source_target_pairs={{0,1},{1,0},{2,3},{3,2},{4,5},{5,4},{6,7},{7,6},{8,9},{9,8},{10,11... | collective-permute-start | bytes 2162696 | tf_op jit(solution)/shard_map/ppermute | solution.py:349
  824.5 39.1 %collective-permute-start.67 = (bf16[1,176,512]{2,1,0:T(8,128)(2,1)}, bf16[1,176,512]{2,1,0:T(8,128)(2,1)}, u32[]{:S(2)}, u32[]{:S(2)}) collective-permute-start(bf16[1,176,512]{2,1,0:T(8,128)(2,1)} %fusion.172), channel_id=1, source_target_pairs={{0,16},{8,24},{16,0},{24,8},{1,17},{9,25},{17,1},{25,9},{2,18},{10... | collective-permute-start | bytes 540680 | tf_op jit(solution)/shard_map/ppermute | solution.py:349
  824.9 57.0 %collective-permute-start.73 = (bf16[1,176,512]{2,1,0:T(8,128)(2,1)}, bf16[1,176,512]{2,1,0:T(8,128)(2,1)}, u32[]{:S(2)}, u32[]{:S(2)}) collective-permute-start(bf16[1,176,512]{2,1,0:T(8,128)(2,1)} %fusion.172), channel_id=1, source_target_pairs={{0,8},{8,0},{16,24},{24,16},{1,9},{9,1},{17,25},{25,17},{2,10},{10... | collective-permute-start | bytes 540680 | tf_op jit(solution)/shard_map/ppermute | solution.py:349
  836.7 26.9 %collective-permute-start.68 = (bf16[1,2,64,2816]{3,2,1,0:T(8,128)(2,1)}, bf16[1,2,64,2816]{3,2,1,0:T(8,128)(2,1)}, u32[]{:S(2)}, u32[]{:S(2)}) collective-permute-start(bf16[1,2,64,2816]{3,2,1,0:T(8,128)(2,1)} %fusion.99), channel_id=1, source_target_pairs={{0,8},{8,0},{16,24},{24,16},{1,9},{9,1},{17,25},{25,17},{2,10},{10... | collective-permute-start | bytes 2162696 | tf_op jit(solution)/shard_map/ppermute | solution.py:349
  907.2 40.8 %collective-permute-start.82 = (bf16[4,2,128,512]{3,2,1,0:T(8,128)(2,1)S(1)}, bf16[4,2,128,512]{3,2,1,0:T(8,128)(2,1)S(1)}, u32[]{:S(2)}, u32[]{:S(2)}) collective-permute-start(bf16[4,2,128,512]{3,2,1,0:T(8,128)(2,1)S(1)} %dynamic-slice_bitcast_fusion.3), channel_id=1, source_target_pairs={{0,1},{1,0},{2,3},{3,2},{4,5},{5,4},{6,7},{7,6},{8,9},{9,8},{10,11... | collective-permute-start | bytes 3145736 | tf_op jit(solution)/shard_map/ppermute | solution.py:349
  907.3 40.7 %collective-permute-start.83 = (bf16[4,2,128,512]{3,2,1,0:T(8,128)(2,1)S(1)}, bf16[4,2,128,512]{3,2,1,0:T(8,128)(2,1)S(1)}, u32[]{:S(2)}, u32[]{:S(2)}) collective-permute-start(bf16[4,2,128,512]{3,2,1,0:T(8,128)(2,1)S(1)} %dynamic-slice_bitcast_fusion.2), channel_id=1, source_target_pairs={{0,2},{1,3},{2,0},{3,1},{4,6},{5,7},{6,4},{7,5},{8,10},{9,11},{10,... | collective-permute-start | bytes 3145736 | tf_op jit(solution)/shard_map/ppermute | solution.py:349
  919.2 35.3 %collective-permute-start.87 = (bf16[1,64,2816]{2,1,0:T(8,128)(2,1)S(1)}, bf16[1,64,2816]{2,1,0:T(8,128)(2,1)S(1)}, u32[]{:S(2)}, u32[]{:S(2)}) collective-permute-start(bf16[1,64,2816]{2,1,0:T(8,128)(2,1)S(1)} %fusion.100), channel_id=1, source_target_pairs={{0,16},{8,24},{16,0},{24,8},{1,17},{9,25},{17,1},{25,9},{2,18},{10... | collective-permute-start | bytes 1081352 | tf_op jit(solution)/shard_map/ppermute | solution.py:349
  920.4 53.8 %collective-permute-start.90 = (bf16[1,64,2816]{2,1,0:T(8,128)(2,1)S(1)}, bf16[1,64,2816]{2,1,0:T(8,128)(2,1)S(1)}, u32[]{:S(2)}, u32[]{:S(2)}) collective-permute-start(bf16[1,64,2816]{2,1,0:T(8,128)(2,1)S(1)} %fusion.100), channel_id=1, source_target_pairs={{0,8},{8,0},{16,24},{24,16},{1,9},{9,1},{17,25},{25,17},{2,10},{10... | collective-permute-start | bytes 1081352 | tf_op jit(solution)/shard_map/ppermute | solution.py:349
  (200 other events, 2705.1 us)

commit v5 on v4

--- a/solution.py
+++ b/solution.py
@@ -374,7 +374,7 @@
     anywhere = pl.BlockSpec(memory_space=pl.ANY)
     return pl.pallas_call(
         functools.partial(place_kernel, spots, rows),
-        in_specs=[pl.BlockSpec(memory_space=pltpu.SMEM)] + [anywhere] * len(pieces),
+        in_specs=[pl.BlockSpec(memory_space=pltpu.SMEM)] + [pl.BlockSpec(memory_space=pltpu.VMEM)] * len(pieces),
         out_specs=anywhere,
         out_shape=jax.ShapeDtypeStruct((size * rows, pieces[0].shape[1]), BF16),
         scratch_shapes=[pltpu.SemaphoreType.DMA((len(pieces),))],

time: 1060 us -> 617 us (0.58); the launches traced: 1070 us -> 612 us
  Pallas kernels: 541 us -> 98.8 us
    pallas_call x4, Pallas kernels: 457 us -> 15.6 us  [place(): pl.pallas_call(functools.partial(place_kernel, spots, rows), in_specs=[pl...]
  transfers between devices with their start and end apart: 112 -> 112, of which waited for: 37 -> 35; matrix products, arithmetic and copies ran while one was open for 15% -> 26% of each run, Pallas kernels for 8% -> 14%
where the time goes in v5:
time: 617 us; the launch traced here: 612 us
  waiting for transfers between devices  194 us (31%)
  starting transfers between devices  114 us (18%)
  Pallas kernels  98.8 us (16%)
  matrix products  77.4 us (13%)
  other arithmetic  63.9 us (10%)
  local copies, waits for them, and re-layouts  57 us (9%)
  between operations  7.45 us (1%)
    ppermute x112, waiting for transfers between devices, cross(): return lax.ppermute(value, axis, partners(lax.axis_size(axis), bit))  194 us
    ppermute x112, starting transfers between devices, cross(): return lax.ppermute(value, axis, partners(lax.axis_size(axis), bit))  114 us
    pallas_call x3, Pallas kernels, attend_back(): pl.pallas_call(functools.partial(backward_kernel, masked), grid_spec=pltp...  48.7 us
    pallas_call x2, Pallas kernels, attend(): pl.pallas_call(functools.partial(forward_kernel, masked), grid_spec=pltpu...  34.5 us
    dot_general x14, matrix products, nn(): return jnp.dot(left, right, preferred_element_type=F32)  28.5 us
    dot_general x14, matrix products, nt(): lax.dot_general(left, right, (((1,), (1,)), ((), ())), preferred_element_...  27.5 us
    dot_general x9, matrix products, tn(): lax.dot_general(left, right, (((0,), (0,)), ((), ())), preferred_element_...  20.5 us
    convert_element_type x30, other arithmetic, add(): return (left.astype(F32) + right.astype(F32)).astype(BF16)  16.9 us
  transfers between devices with their start and end apart: 112, of which 35 were waited for; matrix products, arithmetic and copies ran while one was open for 26% of the time, Pallas kernels for 14%

profile of v5, /device:TPU:0, one launch (start us, length us, event | category | flops | bytes accessed | tf_op | source)
XLA Modules:
  0.0 611.7 jit_solution(7044158780114824270)
XLA Ops:
  58.6 19.4 %collective-permute-done.11 = bf16[256,1024]{1,0:T(8,128)(2,1)S(1)} collective-permute-done((bf16[256,1024]{1,0:T(8,128)(2,1)S(1)}, bf16[256,1024]{1,0:T(8,128)(2,1)S(1)}, u32[]{:S(2)}, u32[]{:S(2)}) %collective-permute-start.11) | collective-permute-done | bytes 524320 | tf_op jit(solution)/shard_map/ppermute | solution.py:349
  81.6 10.2 %collective-permute-done.14 = bf16[256,1024]{1,0:T(8,128)(2,1)S(1)} collective-permute-done((bf16[256,1024]{1,0:T(8,128)(2,1)S(1)}, bf16[256,1024]{1,0:T(8,128)(2,1)S(1)}, u32[]{:S(2)}, u32[]{:S(2)}) %collective-permute-start.14) | collective-permute-done | bytes 524320 | tf_op jit(solution)/shard_map/ppermute | solution.py:349
  93.4 4.2 place.5
  116.6 18.1 %attend_self.1 = (bf16[256,1024]{1,0:T(8,128)(2,1)}, f32[4,2,64,512]{3,2,1,0:T(8,128)}, f32[4,2,8,512]{3,2,1,0:T(8,128)}) custom-call(s32[20]{0:T(128)} %pad_add_fusion.1.table, bf16[256,1024]{1,0:T(8,128)(2,1)} %get-tuple-element.240.refs_0_, bf16[2048,1024]{1,0:T(8,128)(2,1)} %constant_dynamic-update-slice_fusion.refs_1_.refs_2_, ...), custom_call_target="tpu_custom_call" | custom-call | flops 2147483648 | bytes 8388608 | tf_op jit(solution)/shard_map/attend_self/pallas_call | solution.py:248
  152.2 4.4 collective-permute-start.35
  161.5 7.8 %collective-permute-done.33.refs_2_ = bf16[128,2816]{1,0:T(8,128)(2,1)} collective-permute-done((bf16[128,2816]{1,0:T(8,128)(2,1)}, bf16[128,2816]{1,0:T(8,128)(2,1)}, u32[]{:S(2)}, u32[]{:S(2)}) %collective-permute-start.33) | collective-permute-done | bytes 720928 | tf_op jit(solution)/shard_map/ppermute | solution.py:349
  171.9 16.4 %attend_cross.1 = (bf16[256,1024]{1,0:T(8,128)(2,1)}, f32[4,2,64,512]{3,2,1,0:T(8,128)}, f32[4,2,8,512]{3,2,1,0:T(8,128)}) custom-call(s32[20]{0:T(128)} %pad_add_fusion.1.table, bf16[256,1024]{1,0:T(8,128)(2,1)} %pad_maximum_fusion.8.refs_0_, bf16[512,1024]{1,0:T(8,128)(2,1)} %copy-done.86, bf16[512,1024]{1,0:T(8,128)(2,1)} %copy-done.86), custom_call_target="tpu_custom_call" | custom-call | flops 536870912 | bytes 2097152 | tf_op jit(solution)/shard_map/attend_cross/pallas_call | solution.py:248
  188.6 5.2 place.6
  266.5 11.2 %collective-permute-done.53 = bf16[1,2,352,512]{3,2,1,0:T(8,128)(2,1)S(1)} collective-permute-done((bf16[1,2,352,512]{3,2,1,0:T(8,128)(2,1)S(1)}, bf16[1,2,352,512]{3,2,1,0:T(8,128)(2,1)S(1)}, u32[]{:S(2)}, u32[]{:S(2)}) %collective-permute-start.53) | collective-permute-done | bytes 720928 | tf_op jit(solution)/shard_map/ppermute | solution.py:349
  293.1 16.6 %attend_cross_back.1 = (bf16[256,1024]{1,0:T(8,128)(2,1)}, bf16[2,512,512]{2,1,0:T(8,128)(2,1)}) custom-call(s32[20]{0:T(128)} %pad_add_fusion.1.table, bf16[256,1024]{1,0:T(8,128)(2,1)} %pad_maximum_fusion.8.refs_0_, bf16[512,1024]{1,0:T(8,128)(2,1)} %copy-done.86, bf16[512,1024]{1,0:T(8,128)(2,1)} %copy-done.86, bf16[256,1024]{1,0:T(8,128)(2,1)} %fusion.36.refs_3_, ...), custom_call_target="tpu_custom_call" | custom-call | flops 1342177280 | bytes 4194304 | tf_op jit(solution)/shard_map/attend_cross_back/pallas_call | solution.py:287
  311.1 11.2 %collective-permute-done.57 = bf16[1,2,128,2816]{3,2,1,0:T(8,128)(2,1)} collective-permute-done((bf16[1,2,128,2816]{3,2,1,0:T(8,128)(2,1)}, bf16[1,2,128,2816]{3,2,1,0:T(8,128)(2,1)}, u32[]{:S(2)}, u32[]{:S(2)}) %collective-permute-start.57) | collective-permute-done | bytes 1441824 | tf_op jit(solution)/shard_map/ppermute | solution.py:349
  348.8 15.9 %attend_self_back.2 = (bf16[256,512]{1,0:T(8,128)(2,1)}, bf16[2,2048,256]{2,1,0:T(8,128)(2,1)}, f32[2,4,512]{2,1,0:T(4,128)}) custom-call(s32[20]{0:T(128)} %pad_add_fusion.1.table, bf16[256,1024]{1,0:T(8,128)(2,1)} %get-tuple-element.240.refs_0_, bf16[2048,1024]{1,0:T(8,128)(2,1)} %constant_dynamic-update-slice_fusion.refs_1_.refs_2_, ...), custom_call_target="tpu_custom_call" | custom-call | flops 2684354560 | bytes 8388608 | tf_op jit(solution)/shard_map/attend_self_back/pallas_call | solution.py:287
  383.1 16.2 %attend_self_back.3 = (bf16[256,512]{1,0:T(8,128)(2,1)}, bf16[2,2048,256]{2,1,0:T(8,128)(2,1)}, f32[2,4,512]{2,1,0:T(4,128)}) custom-call(s32[20]{0:T(128)} %pad_add_fusion.1.table, bf16[256,1024]{1,0:T(8,128)(2,1)} %get-tuple-element.240.refs_0_, bf16[2048,1024]{1,0:T(8,128)(2,1)} %constant_dynamic-update-slice_fusion.refs_1_.refs_2_, ...), custom_call_target="tpu_custom_call" | custom-call | flops 2684354560 | bytes 8388608 | tf_op jit(solution)/shard_map/attend_self_back/pallas_call | solution.py:287
  416.9 18.1 %collective-permute-done.71 = bf16[2,2,256,256]{3,2,0,1:T(8,128)(2,1)S(1)} collective-permute-done((bf16[2,2,256,256]{3,2,0,1:T(8,128)(2,1)}, bf16[2,2,256,256]{3,2,0,1:T(8,128)(2,1)S(1)}, u32[]{:S(2)}, u32[]{:S(2)}) %collective-permute-start.71) | collective-permute-done | bytes 524320 | tf_op jit(solution)/shard_map/ppermute | solution.py:349
  450.4 4.4 collective-permute-start.83
  454.8 5.1 collective-permute-done.77
  465.9 22.6 %collective-permute-done.81 = bf16[2,1,256,256]{3,2,1,0:T(8,128)(2,1)S(1)} collective-permute-done((bf16[2,1,256,256]{3,2,1,0:T(8,128)(2,1)S(1)}, bf16[2,1,256,256]{3,2,1,0:T(8,128)(2,1)S(1)}, u32[]{:S(2)}, u32[]{:S(2)}) %collective-permute-start.81) | collective-permute-done | bytes 262176 | tf_op jit(solution)/shard_map/ppermute | solution.py:349
  495.7 4.9 collective-permute-start.86
  501.5 6.5 %collective-permute-done.85 = bf16[4,128,512]{2,1,0:T(8,128)(2,1)S(1)} collective-permute-done((bf16[4,128,512]{2,1,0:T(8,128)(2,1)S(1)}, bf16[4,128,512]{2,1,0:T(8,128)(2,1)S(1)}, u32[]{:S(2)}, u32[]{:S(2)}) %collective-permute-start.85) | collective-permute-done | bytes 524320 | tf_op jit(solution)/shard_map/ppermute | solution.py:349
  507.9 5.0 collective-permute-done.86
  519.7 16.6 %collective-permute-done.91 = bf16[1,64,2816]{2,1,0:T(8,128)(2,1)S(1)} collective-permute-done((bf16[1,64,2816]{2,1,0:T(8,128)(2,1)S(1)}, bf16[1,64,2816]{2,1,0:T(8,128)(2,1)S(1)}, u32[]{:S(2)}, u32[]{:S(2)}) %collective-permute-start.91) | collective-permute-done | bytes 360480 | tf_op jit(solution)/shard_map/ppermute | solution.py:349
  547.0 6.8 %collective-permute-done.96 = bf16[4,64,512]{2,1,0:T(8,128)(2,1)S(1)} collective-permute-done((bf16[4,64,512]{2,1,0:T(8,128)(2,1)S(1)}, bf16[4,64,512]{2,1,0:T(8,128)(2,1)S(1)}, u32[]{:S(2)}, u32[]{:S(2)}) %collective-permute-start.96) | collective-permute-done | bytes 262176 | tf_op jit(solution)/shard_map/ppermute | solution.py:349
  558.8 15.1 %collective-permute-done.100 = f32[32,128]{1,0:T(8,128)S(1)} collective-permute-done((f32[32,128]{1,0:T(8,128)S(1)}, f32[32,128]{1,0:T(8,128)S(1)}, u32[]{:S(2)}, u32[]{:S(2)}) %collective-permute-start.100) | collective-permute-done | bytes 16416 | tf_op jit(solution)/shard_map/ppermute | solution.py:349
  577.3 5.6 collective-permute-done.104
  (722 shorter events, 336.7 us)
Async XLA Ops:
  3.8 31.1 %collective-permute-start = (bf16[128,1024]{1,0:T(8,128)(2,1)}, bf16[128,1024]{1,0:T(8,128)(2,1)}, u32[]{:S(2)}, u32[]{:S(2)}) collective-permute-start(bf16[128,1024]{1,0:T(8,128)(2,1)} %get-tuple-element.558), channel_id=1, source_target_pairs={{0,2},{1,3},{2,0},{3,1},{4,6},{5,7},{6,4},{7,5},{8,10},{9,11},{10,... | collective-permute-start | bytes 786440 | tf_op jit(solution)/shard_map/ppermute | solution.py:349
  8.8 26.1 %collective-permute-start.5 = (bf16[128,1024]{1,0:T(8,128)(2,1)}, bf16[128,1024]{1,0:T(8,128)(2,1)}, u32[]{:S(2)}, u32[]{:S(2)}) collective-permute-start(bf16[128,1024]{1,0:T(8,128)(2,1)} %get-tuple-element.557), channel_id=1, source_target_pairs={{0,1},{1,0},{2,3},{3,2},{4,5},{5,4},{6,7},{7,6},{8,9},{9,8},{10,11... | collective-permute-start | bytes 786440 | tf_op jit(solution)/shard_map/ppermute | solution.py:349
  99.7 37.3 %collective-permute-start.25 = (bf16[64,1024]{1,0:T(8,128)(2,1)S(1)}, bf16[64,1024]{1,0:T(8,128)(2,1)}, u32[]{:S(2)}, u32[]{:S(2)}) collective-permute-start(bf16[64,1024]{1,0:T(8,128)(2,1)S(1)} %bitcast.600), channel_id=1, source_target_pairs={{0,4},{4,0},{1,5},{5,1},{2,6},{6,2},{3,7},{7,3},{8,12},{12,8},{9,1... | collective-permute-start | bytes 393224 | tf_op jit(solution)/shard_map/ppermute | solution.py:349
  101.1 33.7 %collective-permute-start.26 = (f32[8,128]{1,0:T(8,128)S(1)}, f32[8,128]{1,0:T(8,128)}, u32[]{:S(2)}, u32[]{:S(2)}) collective-permute-start(f32[8,128]{1,0:T(8,128)S(1)} %broadcast_in_dim.32), channel_id=1, source_target_pairs={{0,4},{4,0},{1,5},{5,1},{2,6},{6,2},{3,7},{7,3},{8,12},{12,8},{9,1... | collective-permute-start | bytes 12296 | tf_op jit(solution)/shard_map/ppermute | solution.py:349
  104.2 32.9 %collective-permute-start.22 = (bf16[128,2816]{1,0:T(8,128)(2,1)}, bf16[128,2816]{1,0:T(8,128)(2,1)}, u32[]{:S(2)}, u32[]{:S(2)}) collective-permute-start(bf16[128,2816]{1,0:T(8,128)(2,1)} %get-tuple-element.500), channel_id=1, source_target_pairs={{0,1},{1,0},{2,3},{3,2},{4,5},{5,4},{6,7},{7,6},{8,9},{9,8},{10,11... | collective-permute-start | bytes 2162696 | tf_op jit(solution)/shard_map/ppermute | solution.py:349
  108.1 28.9 %collective-permute-start.23 = (bf16[128,2816]{1,0:T(8,128)(2,1)}, bf16[128,2816]{1,0:T(8,128)(2,1)}, u32[]{:S(2)}, u32[]{:S(2)}) collective-permute-start(bf16[128,2816]{1,0:T(8,128)(2,1)} %get-tuple-element.499), channel_id=1, source_target_pairs={{0,2},{1,3},{2,0},{3,1},{4,6},{5,7},{6,4},{7,5},{8,10},{9,11},{10,... | collective-permute-start | bytes 2162696 | tf_op jit(solution)/shard_map/ppermute | solution.py:349
  152.2 36.1 %collective-permute-start.35 = (bf16[128,2816]{1,0:T(8,128)(2,1)}, bf16[128,2816]{1,0:T(8,128)(2,1)}, u32[]{:S(2)}, u32[]{:S(2)}) collective-permute-start(bf16[128,2816]{1,0:T(8,128)(2,1)} %get-tuple-element.499), channel_id=1, source_target_pairs={{0,1},{1,0},{2,3},{3,2},{4,5},{5,4},{6,7},{7,6},{8,9},{9,8},{10,11... | collective-permute-start | bytes 2162696 | tf_op jit(solution)/shard_map/ppermute | solution.py:349
  156.6 31.7 %collective-permute-start.34 = (bf16[128,2816]{1,0:T(8,128)(2,1)}, bf16[128,2816]{1,0:T(8,128)(2,1)}, u32[]{:S(2)}, u32[]{:S(2)}) collective-permute-start(bf16[128,2816]{1,0:T(8,128)(2,1)} %collective-permute-done.22.refs_1_), channel_id=1, source_target_pairs={{0,2},{1,3},{2,0},{3,1},{4,6},{5,7},{6,4},{7,5},{8,10},{9,11},{10,... | collective-permute-start | bytes 2162696 | tf_op jit(solution)/shard_map/ppermute | solution.py:349
  156.7 31.9 %collective-permute-start.36 = (bf16[128,2816]{1,0:T(8,128)(2,1)}, bf16[128,2816]{1,0:T(8,128)(2,1)}, u32[]{:S(2)}, u32[]{:S(2)}) collective-permute-start(bf16[128,2816]{1,0:T(8,128)(2,1)} %collective-permute-done.23.refs_4_), channel_id=1, source_target_pairs={{0,1},{1,0},{2,3},{3,2},{4,5},{5,4},{6,7},{7,6},{8,9},{9,8},{10,11... | collective-permute-start | bytes 2162696 | tf_op jit(solution)/shard_map/ppermute | solution.py:349
  160.4 28.2 %collective-permute-start.37 = (bf16[256,1024]{1,0:T(8,128)(2,1)S(1)}, bf16[256,1024]{1,0:T(8,128)(2,1)}, u32[]{:S(2)}, u32[]{:S(2)}) collective-permute-start(bf16[256,1024]{1,0:T(8,128)(2,1)S(1)} %get-tuple-element.280), channel_id=1, source_target_pairs={{0,4},{4,0},{1,5},{5,1},{2,6},{6,2},{3,7},{7,3},{8,12},{12,8},{9,1... | collective-permute-start | bytes 1572872 | tf_op jit(solution)/shard_map/ppermute | solution.py:349
  279.0 32.1 %collective-permute-start.55 = (bf16[1,352,512]{2,1,0:T(8,128)(2,1)S(1)}, bf16[1,352,512]{2,1,0:T(8,128)(2,1)}, u32[]{:S(2)}, u32[]{:S(2)}) collective-permute-start(bf16[1,352,512]{2,1,0:T(8,128)(2,1)S(1)} %dynamic-slice_bitcast_fusion.13), channel_id=1, source_target_pairs={{0,2},{1,3},{2,0},{3,1},{4,6},{5,7},{6,4},{7,5},{8,10},{9,11},{10,... | collective-permute-start | bytes 1081352 | tf_op jit(solution)/shard_map/ppermute | solution.py:349
  281.8 29.3 %collective-permute-start.56 = (bf16[1,352,512]{2,1,0:T(8,128)(2,1)}, bf16[1,352,512]{2,1,0:T(8,128)(2,1)}, u32[]{:S(2)}, u32[]{:S(2)}) collective-permute-start(bf16[1,352,512]{2,1,0:T(8,128)(2,1)} %dynamic-slice_bitcast_fusion.12), channel_id=1, source_target_pairs={{0,1},{1,0},{2,3},{3,2},{4,5},{5,4},{6,7},{7,6},{8,9},{9,8},{10,11... | collective-permute-start | bytes 1081352 | tf_op jit(solution)/shard_map/ppermute | solution.py:349
  283.9 38.5 %collective-permute-start.57 = (bf16[1,2,128,2816]{3,2,1,0:T(8,128)(2,1)}, bf16[1,2,128,2816]{3,2,1,0:T(8,128)(2,1)}, u32[]{:S(2)}, u32[]{:S(2)}) collective-permute-start(bf16[1,2,128,2816]{3,2,1,0:T(8,128)(2,1)} %dynamic-slice_bitcast_fusion.1), channel_id=1, source_target_pairs={{0,1},{1,0},{2,3},{3,2},{4,5},{5,4},{6,7},{7,6},{8,9},{9,8},{10,11... | collective-permute-start | bytes 4325384 | tf_op jit(solution)/shard_map/ppermute | solution.py:349
  286.7 35.7 %collective-permute-start.58 = (bf16[1,2,128,2816]{3,2,1,0:T(8,128)(2,1)}, bf16[1,2,128,2816]{3,2,1,0:T(8,128)(2,1)}, u32[]{:S(2)}, u32[]{:S(2)}) collective-permute-start(bf16[1,2,128,2816]{3,2,1,0:T(8,128)(2,1)} %dynamic-slice_bitcast_fusion), channel_id=1, source_target_pairs={{0,2},{1,3},{2,0},{3,1},{4,6},{5,7},{6,4},{7,5},{8,10},{9,11},{10,... | collective-permute-start | bytes 4325384 | tf_op jit(solution)/shard_map/ppermute | solution.py:349
  336.9 33.9 %collective-permute-start.63 = (bf16[1,128,2816]{2,1,0:T(8,128)(2,1)}, bf16[1,128,2816]{2,1,0:T(8,128)(2,1)}, u32[]{:S(2)}, u32[]{:S(2)}) collective-permute-start(bf16[1,128,2816]{2,1,0:T(8,128)(2,1)} %dynamic-slice_bitcast_fusion.5), channel_id=1, source_target_pairs={{0,2},{1,3},{2,0},{3,1},{4,6},{5,7},{6,4},{7,5},{8,10},{9,11},{10,... | collective-permute-start | bytes 2162696 | tf_op jit(solution)/shard_map/ppermute | solution.py:349
  340.5 30.3 %collective-permute-start.64 = (bf16[1,128,2816]{2,1,0:T(8,128)(2,1)}, bf16[1,128,2816]{2,1,0:T(8,128)(2,1)}, u32[]{:S(2)}, u32[]{:S(2)}) collective-permute-start(bf16[1,128,2816]{2,1,0:T(8,128)(2,1)} %dynamic-slice_bitcast_fusion.4), channel_id=1, source_target_pairs={{0,1},{1,0},{2,3},{3,2},{4,5},{5,4},{6,7},{7,6},{8,9},{9,8},{10,11... | collective-permute-start | bytes 2162696 | tf_op jit(solution)/shard_map/ppermute | solution.py:349
  372.6 32.5 %collective-permute-start.67 = (bf16[1,176,512]{2,1,0:T(8,128)(2,1)}, bf16[1,176,512]{2,1,0:T(8,128)(2,1)}, u32[]{:S(2)}, u32[]{:S(2)}) collective-permute-start(bf16[1,176,512]{2,1,0:T(8,128)(2,1)} %fusion.172), channel_id=1, source_target_pairs={{0,16},{8,24},{16,0},{24,8},{1,17},{9,25},{17,1},{25,9},{2,18},{10... | collective-permute-start | bytes 540680 | tf_op jit(solution)/shard_map/ppermute | solution.py:349
  372.9 43.8 %collective-permute-start.73 = (bf16[1,176,512]{2,1,0:T(8,128)(2,1)}, bf16[1,176,512]{2,1,0:T(8,128)(2,1)}, u32[]{:S(2)}, u32[]{:S(2)}) collective-permute-start(bf16[1,176,512]{2,1,0:T(8,128)(2,1)} %fusion.172), channel_id=1, source_target_pairs={{0,8},{8,0},{16,24},{24,16},{1,9},{9,1},{17,25},{25,17},{2,10},{10... | collective-permute-start | bytes 540680 | tf_op jit(solution)/shard_map/ppermute | solution.py:349
  378.5 26.5 %collective-permute-start.68 = (bf16[1,2,64,2816]{3,2,1,0:T(8,128)(2,1)}, bf16[1,2,64,2816]{3,2,1,0:T(8,128)(2,1)}, u32[]{:S(2)}, u32[]{:S(2)}) collective-permute-start(bf16[1,2,64,2816]{3,2,1,0:T(8,128)(2,1)} %fusion.99), channel_id=1, source_target_pairs={{0,8},{8,0},{16,24},{24,16},{1,9},{9,1},{17,25},{25,17},{2,10},{10... | collective-permute-start | bytes 2162696 | tf_op jit(solution)/shard_map/ppermute | solution.py:349
  416.8 31.3 %collective-permute-start.79 = (bf16[1,64,2816]{2,1,0:T(8,128)(2,1)}, bf16[1,64,2816]{2,1,0:T(8,128)(2,1)S(1)}, u32[]{:S(2)}, u32[]{:S(2)}) collective-permute-start(bf16[1,64,2816]{2,1,0:T(8,128)(2,1)} %dynamic-slice_bitcast_fusion.11), channel_id=1, source_target_pairs={{0,16},{8,24},{16,0},{24,8},{1,17},{9,25},{17,1},{25,9},{2,18},{10... | collective-permute-start | bytes 1081352 | tf_op jit(solution)/shard_map/ppermute | solution.py:349
  448.1 40.4 %collective-permute-start.82 = (bf16[4,2,128,512]{3,2,1,0:T(8,128)(2,1)S(1)}, bf16[4,2,128,512]{3,2,1,0:T(8,128)(2,1)S(1)}, u32[]{:S(2)}, u32[]{:S(2)}) collective-permute-start(bf16[4,2,128,512]{3,2,1,0:T(8,128)(2,1)S(1)} %dynamic-slice_bitcast_fusion.3), channel_id=1, source_target_pairs={{0,1},{1,0},{2,3},{3,2},{4,5},{5,4},{6,7},{7,6},{8,9},{9,8},{10,11... | collective-permute-start | bytes 3145736 | tf_op jit(solution)/shard_map/ppermute | solution.py:349
  450.4 38.1 %collective-permute-start.83 = (bf16[4,2,128,512]{3,2,1,0:T(8,128)(2,1)S(1)}, bf16[4,2,128,512]{3,2,1,0:T(8,128)(2,1)S(1)}, u32[]{:S(2)}, u32[]{:S(2)}) collective-permute-start(bf16[4,2,128,512]{3,2,1,0:T(8,128)(2,1)S(1)} %dynamic-slice_bitcast_fusion.2), channel_id=1, source_target_pairs={{0,2},{1,3},{2,0},{3,1},{4,6},{5,7},{6,4},{7,5},{8,10},{9,11},{10,... | collective-permute-start | bytes 3145736 | tf_op jit(solution)/shard_map/ppermute | solution.py:349
  459.9 41.5 %collective-permute-start.87 = (bf16[1,64,2816]{2,1,0:T(8,128)(2,1)S(1)}, bf16[1,64,2816]{2,1,0:T(8,128)(2,1)S(1)}, u32[]{:S(2)}, u32[]{:S(2)}) collective-permute-start(bf16[1,64,2816]{2,1,0:T(8,128)(2,1)S(1)} %fusion.100), channel_id=1, source_target_pairs={{0,16},{8,24},{16,0},{24,8},{1,17},{9,25},{17,1},{25,9},{2,18},{10... | collective-permute-start | bytes 1081352 | tf_op jit(solution)/shard_map/ppermute | solution.py:349
  460.4 59.3 %collective-permute-start.90 = (bf16[1,64,2816]{2,1,0:T(8,128)(2,1)S(1)}, bf16[1,64,2816]{2,1,0:T(8,128)(2,1)S(1)}, u32[]{:S(2)}, u32[]{:S(2)}) collective-permute-start(bf16[1,64,2816]{2,1,0:T(8,128)(2,1)S(1)} %fusion.100), channel_id=1, source_target_pairs={{0,8},{8,0},{16,24},{24,16},{1,9},{9,1},{17,25},{25,17},{2,10},{10... | collective-permute-start | bytes 1081352 | tf_op jit(solution)/shard_map/ppermute | solution.py:349
  (200 other events, 2015.8 us)

commit v6 on v5

--- a/solution.py
+++ b/solution.py
@@ -419,11 +419,18 @@
 
 
 def sum_steps(value):
-    for axis in ("core", "line", "fsdp"):
+    for axis in ("core", "fsdp", "line"):
         for bit in bits_of(lax.axis_size(axis)):
             (got,) = yield [cross(value, axis, bit)]
             value = value + got
     return value
+
+
+def count_steps(value):
+    (got,) = yield [swap(value)]
+    value = value + got
+    got = yield [cross(value, "line", mask) for mask in range(1, lax.axis_size("line"))]
+    return value + sum(got)
 
 
 def small_steps(value):
@@ -589,14 +596,37 @@
     def times_back(grad, weight):
         return nt(columns_of(grad, core), weight[0]) + nt(columns_of(grad, 1 - core), weight[1])
 
+    mask_rows = valid_mask.reshape(rows).astype(F32)
+    assert rows <= 256
+    local_count = jnp.broadcast_to(jnp.sum(mask_rows), (128,)).astype(BF16)
     lane_qkv = Lane(gather_steps(half_columns([joint([w_query, w_key, w_value], axis=1)])))
-    lane_small = Lane(small_steps(joint([gain_self, gain_cross, gain_ffn, bias_table.reshape(-1)])))
-    mask_rows = valid_mask.reshape(rows).astype(F32)
-    mid_shard = half_columns([w_out, c_query, joint([c_key, c_value], axis=1), c_out])
+    lane_small = Lane(small_steps(joint([gain_self, gain_cross, gain_ffn, bias_table.reshape(-1), local_count])))
+    mid_parts = tick([lane_qkv, lane_small], (w_out, c_query, c_key, c_value, c_out))
+
+    mid_shard = half_columns([mid_parts[0], mid_parts[1], joint(mid_parts[2:4], axis=1), mid_parts[4]])
     mid_shard = tick([lane_qkv, lane_small], mid_shard)
 
-    gu_shard = half_columns([joint([w_gate, w_up], axis=1)])
-    wd_shard = half_columns([w_down])
+    small = lane_small.take()
+    gain_one, gain_two, gain_three = [
+        small[:, index * share : (index + 1) * share].reshape(D).astype(F32) for index in range(3)
+    ]
+    table_whole = small[:, 3 * share : -128].reshape(BUCKETS, HEADS)
+    lane_count = Lane(count_steps(jnp.broadcast_to(jnp.sum(small[:, -128:].astype(F32), axis=0), (8, 128))))
+    flat_in = inputs.reshape(rows, width).astype(F32)
+    normed_one, scale_one, hidden_one = norm_rows(flat_in, gain_one)
+    hidden_one = tick([lane_qkv, lane_count], hidden_one)
+
+    qkv_mine, qkv_other = lane_qkv.take()
+    lane_mid = Lane(gather_steps(mid_shard))
+    query, pairs = by_core(nn(hidden_one, qkv_mine).astype(BF16), nn(hidden_one, qkv_other).astype(BF16))
+    query, pairs, late = tick(
+        [lane_mid, lane_count], (query, pairs, (w_gate, w_up, w_down, doc_ids, block_order, buckets, table_whole))
+    )
+    gate_part, up_part, down_part, doc_ids, block_order, buckets, table_whole = late
+
+    lane_keys = Lane(gather_context_steps(pairs))
+    gu_shard = half_columns([joint([gate_part, up_part], axis=1)])
+    wd_shard = half_columns([down_part])
 
     query_blocks = lax.dynamic_slice_in_dim(block_order, context * pair, pair)
     slots = jnp.arange(contexts * pair, dtype=jnp.int32)
@@ -614,32 +644,15 @@
     behind, index_of = offset_index(length)
     bucket_match = (jnp.take(buckets, index_of)[None, :] == jnp.arange(BUCKETS, dtype=jnp.int32)[:, None])
 
-    gu_shard, wd_shard, low, high, place_table, bucket_match = tick(
-        [lane_qkv, lane_small], (gu_shard, wd_shard, low, high, place_table, bucket_match)
-    )
-
-    small = lane_small.take()
-    gain_one, gain_two, gain_three = [
-        small[:, index * share : (index + 1) * share].reshape(D).astype(F32) for index in range(3)
-    ]
-    table_whole = small[:, 3 * share :].reshape(BUCKETS, HEADS)
     vectors = tn(table_whole, bucket_match.astype(BF16)).reshape(HEADS // 4, 4, SPAN)
-    flat_in = inputs.reshape(rows, width).astype(F32)
-    normed_one, scale_one, hidden_one = norm_rows(flat_in, gain_one)
-    hidden_one, vectors = tick([lane_qkv], (hidden_one, vectors))
+    gu_shard, wd_shard, low, high, place_table, bucket_match, vectors = tick(
+        [lane_keys, lane_mid], (gu_shard, wd_shard, low, high, place_table, bucket_match, vectors)
+    )
     extra = (vectors, low, high)
 
-    qkv_mine, qkv_other = lane_qkv.take()
-    lane_mid = Lane(gather_steps(mid_shard))
-    query, pairs = by_core(nn(hidden_one, qkv_mine).astype(BF16), nn(hidden_one, qkv_other).astype(BF16))
-    query, pairs = tick([], (query, pairs))
-
-    lane_keys = Lane(gather_context_steps(pairs))
-    gu_shard = tick([lane_keys, lane_mid], gu_shard)
+    lane_gu = Lane(gather_steps(gu_shard))
     lane_hidden_one = Lane(swap_steps(hidden_one))
-    wd_shard = tick([lane_keys, lane_mid, lane_hidden_one], wd_shard)
-    lane_gu = Lane(gather_steps(gu_shard))
-    tick([lane_keys, lane_mid], ())
+    tick([lane_keys, lane_mid, lane_hidden_one], ())
     mid_mine, mid_other = lane_mid.take()
     wo, wcq, wckv, wco = [
         (mid_mine[:, index * halves : (index + 1) * halves], mid_other[:, index * halves : (index + 1) * halves])
@@ -647,34 +660,36 @@
     ]
     encoder_rows = encoder.reshape(encoder.shape[1], width)
     encoder_pairs = times(encoder_rows, wckv).astype(BF16)
-    pairs_whole, encoder_pairs = tick([], (lane_keys.take(), encoder_pairs))
+    encoder_pairs = tick([lane_keys, lane_gu], encoder_pairs)
+    pairs_whole = lane_keys.take()
 
     lane_encoder = Lane(gather_context_steps(encoder_pairs))
     lane_encoder_rows = Lane(swap_steps(encoder_rows))
-    lane_count = Lane(sum_steps(jnp.broadcast_to(jnp.sum(mask_rows), (8, 128))))
     attention, outs_one, logs_one = attend(query, pairs_whole, place_table, extra, True)
-    attention, outs_one, logs_one = tick([lane_gu, lane_encoder, lane_encoder_rows, lane_count], (attention, outs_one, logs_one))
+    attention, outs_one, logs_one, wd_shard = tick(
+        [lane_encoder, lane_encoder_rows], (attention, outs_one, logs_one, wd_shard)
+    )
 
     lane_attention = Lane(swap_steps(attention))
+    lane_wd = Lane(gather_steps(wd_shard))
     mid_one = flat_in + times(attention, wo)
     normed_two, scale_two, hidden_two = norm_rows(mid_one, gain_two)
     cross_q = times(hidden_two, wcq).astype(BF16)
     mid_one, normed_two, hidden_two, cross_q, scale_two = tick(
-        [lane_encoder, lane_attention, lane_count], (mid_one, normed_two, hidden_two, cross_q, scale_two)
-    )
-    tick([lane_encoder, lane_count], ())
+        [lane_encoder, lane_attention, lane_gu], (mid_one, normed_two, hidden_two, cross_q, scale_two)
+    )
+    tick([lane_encoder, lane_wd], ())
     encoder_whole = lane_encoder.take()
 
     lane_hidden_two = Lane(swap_steps(hidden_two))
     crossed, outs_two, logs_two = attend(cross_q, encoder_whole, place_table, (), False)
-    crossed, outs_two, logs_two = tick([lane_gu, lane_hidden_two, lane_count], (crossed, outs_two, logs_two))
-
-    lane_wd = Lane(gather_steps(wd_shard))
+    crossed, outs_two, logs_two = tick([lane_gu, lane_wd, lane_hidden_two], (crossed, outs_two, logs_two))
+
     lane_crossed = Lane(swap_steps(crossed))
     mid_two = mid_one + times(crossed, wco)
     normed_three, scale_three, hidden_three = norm_rows(mid_two, gain_three)
     mid_two, normed_three, hidden_three, scale_three = tick(
-        [lane_gu, lane_wd, lane_crossed, lane_count], (mid_two, normed_three, hidden_three, scale_three)
+        [lane_wd, lane_crossed], (mid_two, normed_three, hidden_three, scale_three)
     )
 
     gu_mine, gu_other = lane_gu.take()
@@ -682,9 +697,8 @@
     gate, up = by_core(nn(hidden_three, gu_mine), nn(hidden_three, gu_other))
     active, gelu_pull = jax.vjp(gelu_tanh, gate)
     mixed = (active * up).astype(BF16)
-    mixed, gate, up, active = tick([lane_wd, lane_hidden_three], (mixed, gate, up, active))
+    mixed, gate, up, active = tick([lane_hidden_three], (mixed, gate, up, active))
     lane_mixed = Lane(swap_steps(mixed))
-    tick([lane_wd, lane_mixed], ())
 
     wd_mine, wd_other = lane_wd.take()
     count = jnp.maximum(lane_count.take()[0, 0], 1.0)
@@ -697,7 +711,7 @@
     e_three = grad_result.astype(BF16)
     down_mine, down_away = grad_halves(e_three)
     grad_result, e_three, down_mine, down_away, squared_local, layer_out = tick(
-        [], (grad_result, e_three, down_mine, down_away, squared_local, layer_out)
+        [lane_mixed], (grad_result, e_three, down_mine, down_away, squared_local, layer_out)
     )
     lane_down = Lane(swap_steps(down_away))
     grad_mixed = times_back(e_three, (wd_mine, wd_other))
@@ -739,7 +753,7 @@
     one_mine, one_away = grad_halves(e_one)
     grad_attention = times_back(e_one, wo).astype(BF16)
     grad_mid_one, one_mine, one_away, grad_attention = tick(
-        [lane_down, lane_encoder, lane_out], (grad_mid_one, one_mine, one_away, grad_attention)
+        [lane_down, lane_wide, lane_encoder, lane_out], (grad_mid_one, one_mine, one_away, grad_attention)
     )
     lane_one = Lane(swap_steps(one_away))
 
@@ -772,7 +786,7 @@
     encoder_mine = joint([encoder_got[0], encoder_got[1]], axis=1)
     keys_mine, keys_away = grad_halves(encoder_mine[:, :key_width], encoder_mine[:, key_width:])
     partial_out, partial_cross, partial_one, encoder_mine, keys_mine, keys_away = tick(
-        [lane_first, lane_second, lane_down, lane_query],
+        [lane_first, lane_second, lane_down, lane_wide, lane_query],
         (partial_out, partial_cross, partial_one, encoder_mine, keys_mine, keys_away),
     )
 
@@ -780,10 +794,10 @@
     partial_query = weight_grad(hidden_one, lane_hidden_one.take()[0], query_mine, lane_query.take()[0])
     lane_mid = Lane(reduce_steps([partial_out, partial_cross, partial_one, partial_query], [(D,)] * 4))
     grad_encoder = times_back(encoder_mine, wckv)
-    grad_encoder = tick([lane_first, lane_second, lane_down, lane_wide, lane_keys], grad_encoder)
+    grad_encoder = tick([lane_first, lane_second, lane_down, lane_keys], grad_encoder)
 
     partial_keys = weight_grad(encoder_rows, lane_encoder_rows.take()[0], keys_mine, lane_keys.take()[0])
-    partial_keys = tick([lane_second, lane_mid], partial_keys)
+    partial_keys = tick([lane_second, lane_mid, lane_wide], partial_keys)
     pairs_first, pairs_second = lane_first.take(), lane_second.take()
     mine = [joint([pairs_first[index], pairs_second[index]], axis=1) for index in range(2)]
     last_mine, last_away = grad_halves(mine[0], mine[1])

time: 617 us -> 632 us (1.024)
  waiting for transfers between devices: 194 us -> 217 us
    ppermute x112 -> x111, waiting for transfers between devices: 194 us -> 217 us  [cross(): return lax.ppermute(value, axis, partners(lax.axis_size(axis), bit))]
    ppermute x112 -> x111, starting transfers between devices: 114 us -> 110 us  [cross(): return lax.ppermute(value, axis, partners(lax.axis_size(axis), bit))]
    unnamed x249 -> x206, local copies, waits for them, and re-layouts: 16.3 us -> 17 us
  transfers between devices with their start and end apart: 112 -> 111, of which waited for: 35 -> 40; matrix products, arithmetic and copies ran while one was open for 26% -> 27% of each run, Pallas kernels for 14% -> 13%
where the time goes in v6:
time: 632 us; the launch traced here: 628 us
  waiting for transfers between devices  217 us (34%)
  starting transfers between devices  110 us (17%)
  Pallas kernels  99 us (16%)
  matrix products  75.2 us (12%)
  other arithmetic  65.8 us (10%)
  local copies, waits for them, and re-layouts  53.7 us (8%)
  between operations  7.49 us (1%)
    ppermute x111, waiting for transfers between devices, cross(): return lax.ppermute(value, axis, partners(lax.axis_size(axis), bit))  217 us
    ppermute x111, starting transfers between devices, cross(): return lax.ppermute(value, axis, partners(lax.axis_size(axis), bit))  110 us
    pallas_call x3, Pallas kernels, attend_back(): pl.pallas_call(functools.partial(backward_kernel, masked), grid_spec=pltp...  48.9 us
    pallas_call x2, Pallas kernels, attend(): pl.pallas_call(functools.partial(forward_kernel, masked), grid_spec=pltpu...  34.5 us
    dot_general x14, matrix products, nn(): return jnp.dot(left, right, preferred_element_type=F32)  28.6 us
    dot_general x14, matrix products, nt(): lax.dot_general(left, right, (((1,), (1,)), ((), ())), preferred_element_...  28.6 us
    dot_general x9, matrix products, tn(): lax.dot_general(left, right, (((0,), (0,)), ((), ())), preferred_element_...  17.2 us
    unnamed x206, local copies, waits for them, and re-layouts  17 us
  transfers between devices with their start and end apart: 111, of which 40 were waited for; matrix products, arithmetic and copies ran while one was open for 27% of the time, Pallas kernels for 13%

profile of v6, /device:TPU:0, one launch (start us, length us, event | category | flops | bytes accessed | tf_op | source)
XLA Modules:
  0.0 628.4 jit_solution(6387809595288633448)
XLA Ops:
  68.9 16.3 %collective-permute-done.16 = bf16[256,1024]{1,0:T(8,128)(2,1)} collective-permute-done((bf16[256,1024]{1,0:T(8,128)(2,1)S(1)}, bf16[256,1024]{1,0:T(8,128)(2,1)}, u32[]{:S(2)}, u32[]{:S(2)}) %collective-permute-start.16) | collective-permute-done | bytes 524320 | tf_op jit(solution)/shard_map/ppermute | solution.py:349
  92.1 5.6 collective-permute-done.24
  97.7 7.2 %collective-permute-done.21 = bf16[256,1024]{1,0:T(8,128)(2,1)S(1)} collective-permute-done((bf16[256,1024]{1,0:T(8,128)(2,1)S(1)}, bf16[256,1024]{1,0:T(8,128)(2,1)S(1)}, u32[]{:S(2)}, u32[]{:S(2)}) %collective-permute-start.21) | collective-permute-done | bytes 524320 | tf_op jit(solution)/shard_map/ppermute | solution.py:349
  104.8 10.3 %collective-permute-done.22 = bf16[256,1024]{1,0:T(8,128)(2,1)S(1)} collective-permute-done((bf16[256,1024]{1,0:T(8,128)(2,1)}, bf16[256,1024]{1,0:T(8,128)(2,1)S(1)}, u32[]{:S(2)}, u32[]{:S(2)}) %collective-permute-start.22) | collective-permute-done | bytes 524320 | tf_op jit(solution)/shard_map/ppermute | solution.py:349
  127.4 10.4 %collective-permute-done.26.refs_1_ = bf16[128,2816]{1,0:T(8,128)(2,1)} collective-permute-done((bf16[128,2816]{1,0:T(8,128)(2,1)}, bf16[128,2816]{1,0:T(8,128)(2,1)}, u32[]{:S(2)}, u32[]{:S(2)}) %collective-permute-start.26) | collective-permute-done | bytes 720928 | tf_op jit(solution)/shard_map/ppermute | solution.py:349
  138.4 15.2 %collective-permute-done.27.refs_4_ = bf16[128,2816]{1,0:T(8,128)(2,1)} collective-permute-done((bf16[128,2816]{1,0:T(8,128)(2,1)}, bf16[128,2816]{1,0:T(8,128)(2,1)}, u32[]{:S(2)}, u32[]{:S(2)}) %collective-permute-start.27) | collective-permute-done | bytes 720928 | tf_op jit(solution)/shard_map/ppermute | solution.py:349
  158.6 18.1 %attend_self.1 = (bf16[256,1024]{1,0:T(8,128)(2,1)}, f32[4,2,64,512]{3,2,1,0:T(8,128)}, f32[4,2,8,512]{3,2,1,0:T(8,128)}) custom-call(s32[20]{0:T(128)} %pad_add_fusion.1.table, bf16[256,1024]{1,0:T(8,128)(2,1)} %get-tuple-element.268.refs_0_, bf16[2048,1024]{1,0:T(8,128)(2,1)} %constant_dynamic-update-slice_fusion.refs_1_.refs_2_, ...), custom_call_target="tpu_custom_call" | custom-call | flops 2147483648 | bytes 8388608 | tf_op jit(solution)/shard_map/attend_self/pallas_call | solution.py:248
  183.7 7.2 %collective-permute-start.30 = (bf16[64,1024]{1,0:T(8,128)(2,1)S(1)}, bf16[64,1024]{1,0:T(8,128)(2,1)S(1)}, u32[]{:S(2)}, u32[]{:S(2)}) collective-permute-start(bf16[64,1024]{1,0:T(8,128)(2,1)S(1)} %pad_maximum_fusion.17), channel_id=1, source_target_pairs={{0,8},{8,0},{16,24},{24,16},{1,9},{9,1},{17,25},{25,17},{2,10},{10... | collective-permute-start | bytes 393224 | tf_op jit(solution)/shard_map/ppermute | solution.py:349
  211.1 5.9 collective-permute-done.38.refs_1_
  223.1 5.2 collective-permute-done.41.refs_2_
  230.8 16.4 %attend_cross.1 = (bf16[256,1024]{1,0:T(8,128)(2,1)}, f32[4,2,64,512]{3,2,1,0:T(8,128)}, f32[4,2,8,512]{3,2,1,0:T(8,128)}) custom-call(s32[20]{0:T(128)} %pad_add_fusion.1.table, bf16[256,1024]{1,0:T(8,128)(2,1)} %pad_maximum_fusion.8.refs_0_, bf16[512,1024]{1,0:T(8,128)(2,1)} %constant_dynamic-update-slice_fusion.5.refs_1_.refs_2_, ...), custom_call_target="tpu_custom_call" | custom-call | flops 536870912 | bytes 2097152 | tf_op jit(solution)/shard_map/attend_cross/pallas_call | solution.py:248
  300.7 9.8 %collective-permute-done.53 = bf16[1,2,352,512]{3,2,1,0:T(8,128)(2,1)S(1)} collective-permute-done((bf16[1,2,352,512]{3,2,1,0:T(8,128)(2,1)S(1)}, bf16[1,2,352,512]{3,2,1,0:T(8,128)(2,1)S(1)}, u32[]{:S(2)}, u32[]{:S(2)}) %collective-permute-start.53) | collective-permute-done | bytes 720928 | tf_op jit(solution)/shard_map/ppermute | solution.py:349
  326.5 16.6 %attend_cross_back.1 = (bf16[256,1024]{1,0:T(8,128)(2,1)}, bf16[2,512,512]{2,1,0:T(8,128)(2,1)}) custom-call(s32[20]{0:T(128)} %pad_add_fusion.1.table, bf16[256,1024]{1,0:T(8,128)(2,1)} %pad_maximum_fusion.8.refs_0_, bf16[512,1024]{1,0:T(8,128)(2,1)} %constant_dynamic-update-slice_fusion.5.refs_1_.refs_2_, ...), custom_call_target="tpu_custom_call" | custom-call | flops 1342177280 | bytes 4194304 | tf_op jit(solution)/shard_map/attend_cross_back/pallas_call | solution.py:287
  344.5 10.0 %collective-permute-done.54 = bf16[1,352,512]{2,1,0:T(8,128)(2,1)} collective-permute-done((bf16[1,352,512]{2,1,0:T(8,128)(2,1)}, bf16[1,352,512]{2,1,0:T(8,128)(2,1)}, u32[]{:S(2)}, u32[]{:S(2)}) %collective-permute-start.54) | collective-permute-done | bytes 360480 | tf_op jit(solution)/shard_map/ppermute | solution.py:349
  382.9 16.0 %attend_self_back.2 = (bf16[256,512]{1,0:T(8,128)(2,1)}, bf16[2,2048,256]{2,1,0:T(8,128)(2,1)}, f32[2,4,512]{2,1,0:T(4,128)}) custom-call(s32[20]{0:T(128)} %pad_add_fusion.1.table, bf16[256,1024]{1,0:T(8,128)(2,1)} %get-tuple-element.268.refs_0_, bf16[2048,1024]{1,0:T(8,128)(2,1)} %constant_dynamic-update-slice_fusion.refs_1_.refs_2_, ...), custom_call_target="tpu_custom_call" | custom-call | flops 2684354560 | bytes 8388608 | tf_op jit(solution)/shard_map/attend_self_back/pallas_call | solution.py:287
  421.8 16.3 %attend_self_back.3 = (bf16[256,512]{1,0:T(8,128)(2,1)}, bf16[2,2048,256]{2,1,0:T(8,128)(2,1)}, f32[2,4,512]{2,1,0:T(4,128)}) custom-call(s32[20]{0:T(128)} %pad_add_fusion.1.table, bf16[256,1024]{1,0:T(8,128)(2,1)} %get-tuple-element.268.refs_0_, bf16[2048,1024]{1,0:T(8,128)(2,1)} %constant_dynamic-update-slice_fusion.refs_1_.refs_2_, ...), custom_call_target="tpu_custom_call" | custom-call | flops 2684354560 | bytes 8388608 | tf_op jit(solution)/shard_map/attend_self_back/pallas_call | solution.py:287
  455.6 19.0 %collective-permute-done.74 = bf16[1,176,512]{2,1,0:T(8,128)(2,1)S(1)} collective-permute-done((bf16[1,176,512]{2,1,0:T(8,128)(2,1)}, bf16[1,176,512]{2,1,0:T(8,128)(2,1)S(1)}, u32[]{:S(2)}, u32[]{:S(2)}) %collective-permute-start.74) | collective-permute-done | bytes 180256 | tf_op jit(solution)/shard_map/ppermute | solution.py:349
  490.0 10.5 %collective-permute-done.77 = bf16[2,1,256,256]{3,2,1,0:T(8,128)(2,1)S(1)} collective-permute-done((bf16[2,1,256,256]{3,2,1,0:T(8,128)(2,1)S(1)}, bf16[2,1,256,256]{3,2,1,0:T(8,128)(2,1)S(1)}, u32[]{:S(2)}, u32[]{:S(2)}) %collective-permute-start.77) | collective-permute-done | bytes 262176 | tf_op jit(solution)/shard_map/ppermute | solution.py:349
  508.0 10.7 %collective-permute-done.85 = bf16[1,64,2816]{2,1,0:T(8,128)(2,1)S(1)} collective-permute-done((bf16[1,64,2816]{2,1,0:T(8,128)(2,1)}, bf16[1,64,2816]{2,1,0:T(8,128)(2,1)S(1)}, u32[]{:S(2)}, u32[]{:S(2)}) %collective-permute-start.85) | collective-permute-done | bytes 360480 | tf_op jit(solution)/shard_map/ppermute | solution.py:349
  518.7 7.0 %collective-permute-done.82 = bf16[4,2,128,512]{3,2,1,0:T(8,128)(2,1)S(1)} collective-permute-done((bf16[4,2,128,512]{3,2,1,0:T(8,128)(2,1)S(1)}, bf16[4,2,128,512]{3,2,1,0:T(8,128)(2,1)S(1)}, u32[]{:S(2)}, u32[]{:S(2)}) %collective-permute-start.82) | collective-permute-done | bytes 1048608 | tf_op jit(solution)/shard_map/ppermute | solution.py:349
  535.8 6.4 %collective-permute-done.88 = bf16[4,128,512]{2,1,0:T(8,128)(2,1)S(1)} collective-permute-done((bf16[4,128,512]{2,1,0:T(8,128)(2,1)S(1)}, bf16[4,128,512]{2,1,0:T(8,128)(2,1)S(1)}, u32[]{:S(2)}, u32[]{:S(2)}) %collective-permute-start.88) | collective-permute-done | bytes 524320 | tf_op jit(solution)/shard_map/ppermute | solution.py:349
  547.0 9.8 %collective-permute-done.92 = bf16[4,2,64,512]{3,2,0,1:T(8,128)(2,1)S(1)} collective-permute-done((bf16[4,2,64,512]{3,2,0,1:T(8,128)(2,1)S(1)}, bf16[4,2,64,512]{3,2,0,1:T(8,128)(2,1)S(1)}, u32[]{:S(2)}, u32[]{:S(2)}) %collective-permute-start.92) | collective-permute-done | bytes 524320 | tf_op jit(solution)/shard_map/ppermute | solution.py:349
  565.4 6.8 %collective-permute-done.95 = bf16[4,64,512]{2,1,0:T(8,128)(2,1)S(1)} collective-permute-done((bf16[4,64,512]{2,1,0:T(8,128)(2,1)S(1)}, bf16[4,64,512]{2,1,0:T(8,128)(2,1)S(1)}, u32[]{:S(2)}, u32[]{:S(2)}) %collective-permute-start.95) | collective-permute-done | bytes 262176 | tf_op jit(solution)/shard_map/ppermute | solution.py:349
  580.4 6.0 collective-permute-done.98
  (674 shorter events, 358.3 us)
Async XLA Ops:
  89.5 25.7 %collective-permute-start.23 = (bf16[1024,2048]{1,0:T(8,128)(2,1)}, bf16[1024,2048]{1,0:T(8,128)(2,1)S(1)}, u32[]{:S(2)}, u32[]{:S(2)}) collective-permute-start(bf16[1024,2048]{1,0:T(8,128)(2,1)} %place.5), channel_id=1, source_target_pairs={{0,4},{4,0},{1,5},{5,1},{2,6},{6,2},{3,7},{7,3},{8,12},{12,8},{9,1... | collective-permute-start | bytes 12582920 | tf_op jit(solution)/shard_map/ppermute | solution.py:349
  116.8 36.8 %collective-permute-start.25 = (bf16[1024,1024]{1,0:T(8,128)(2,1)S(1)}, bf16[1024,1024]{1,0:T(8,128)(2,1)S(1)}, u32[]{:S(2)}, u32[]{:S(2)}) collective-permute-start(bf16[1024,1024]{1,0:T(8,128)(2,1)S(1)} %pad_maximum_fusion.1), channel_id=1, source_target_pairs={{0,4},{4,0},{1,5},{5,1},{2,6},{6,2},{3,7},{7,3},{8,12},{12,8},{9,1... | collective-permute-start | bytes 6291464 | tf_op jit(solution)/shard_map/ppermute | solution.py:349
  116.9 59.9 %collective-permute-start.29 = (bf16[64,1024]{1,0:T(8,128)(2,1)S(1)}, bf16[64,1024]{1,0:T(8,128)(2,1)S(1)}, u32[]{:S(2)}, u32[]{:S(2)}) collective-permute-start(bf16[64,1024]{1,0:T(8,128)(2,1)S(1)} %bitcast.593), channel_id=1, source_target_pairs={{0,4},{4,0},{1,5},{5,1},{2,6},{6,2},{3,7},{7,3},{8,12},{12,8},{9,1... | collective-permute-start | bytes 393224 | tf_op jit(solution)/shard_map/ppermute | solution.py:349
  120.0 63.7 %collective-permute-start.33 = (bf16[128,2816]{1,0:T(8,128)(2,1)}, bf16[128,2816]{1,0:T(8,128)(2,1)}, u32[]{:S(2)}, u32[]{:S(2)}) collective-permute-start(bf16[128,2816]{1,0:T(8,128)(2,1)} %get-tuple-element.518), channel_id=1, source_target_pairs={{0,2},{1,3},{2,0},{3,1},{4,6},{5,7},{6,4},{7,5},{8,10},{9,11},{10,... | collective-permute-start | bytes 2162696 | tf_op jit(solution)/shard_map/ppermute | solution.py:349
  121.1 32.4 %collective-permute-start.27 = (bf16[128,2816]{1,0:T(8,128)(2,1)}, bf16[128,2816]{1,0:T(8,128)(2,1)}, u32[]{:S(2)}, u32[]{:S(2)}) collective-permute-start(bf16[128,2816]{1,0:T(8,128)(2,1)} %get-tuple-element.517), channel_id=1, source_target_pairs={{0,2},{1,3},{2,0},{3,1},{4,6},{5,7},{6,4},{7,5},{8,10},{9,11},{10,... | collective-permute-start | bytes 2162696 | tf_op jit(solution)/shard_map/ppermute | solution.py:349
  137.8 53.0 %collective-permute-start.35 = (bf16[128,2816]{1,0:T(8,128)(2,1)}, bf16[128,2816]{1,0:T(8,128)(2,1)}, u32[]{:S(2)}, u32[]{:S(2)}) collective-permute-start(bf16[128,2816]{1,0:T(8,128)(2,1)} %get-tuple-element.517), channel_id=1, source_target_pairs={{0,1},{1,0},{2,3},{3,2},{4,5},{5,4},{6,7},{7,6},{8,9},{9,8},{10,11... | collective-permute-start | bytes 2162696 | tf_op jit(solution)/shard_map/ppermute | solution.py:349
  155.9 42.8 %collective-permute-start.34 = (bf16[128,2816]{1,0:T(8,128)(2,1)}, bf16[128,2816]{1,0:T(8,128)(2,1)}, u32[]{:S(2)}, u32[]{:S(2)}) collective-permute-start(bf16[128,2816]{1,0:T(8,128)(2,1)} %collective-permute-done.26.refs_1_), channel_id=1, source_target_pairs={{0,2},{1,3},{2,0},{3,1},{4,6},{5,7},{6,4},{7,5},{8,10},{9,11},{10,... | collective-permute-start | bytes 2162696 | tf_op jit(solution)/shard_map/ppermute | solution.py:349
  203.9 43.4 %collective-permute-start.40 = (bf16[1024,2816]{1,0:T(8,128)(2,1)}, bf16[1024,2816]{1,0:T(8,128)(2,1)}, u32[]{:S(2)}, u32[]{:S(2)}) collective-permute-start(bf16[1024,2816]{1,0:T(8,128)(2,1)} %place.6), channel_id=1, source_target_pairs={{0,4},{4,0},{1,5},{5,1},{2,6},{6,2},{3,7},{7,3},{8,12},{12,8},{9,1... | collective-permute-start | bytes 17301512 | tf_op jit(solution)/shard_map/ppermute | solution.py:349
  217.0 30.2 %collective-permute-start.45 = (bf16[256,1024]{1,0:T(8,128)(2,1)}, bf16[256,1024]{1,0:T(8,128)(2,1)}, u32[]{:S(2)}, u32[]{:S(2)}) collective-permute-start(bf16[256,1024]{1,0:T(8,128)(2,1)} %copy-done.36), channel_id=1, source_target_pairs={{0,4},{4,0},{1,5},{5,1},{2,6},{6,2},{3,7},{7,3},{8,12},{12,8},{9,1... | collective-permute-start | bytes 1572872 | tf_op jit(solution)/shard_map/ppermute | solution.py:349
  220.7 26.6 %collective-permute-start.43 = (bf16[352,512]{1,0:T(8,128)(2,1)}, bf16[352,512]{1,0:T(8,128)(2,1)}, u32[]{:S(2)}, u32[]{:S(2)}) collective-permute-start(bf16[352,512]{1,0:T(8,128)(2,1)} %get-tuple-element.541), channel_id=1, source_target_pairs={{0,1},{1,0},{2,3},{3,2},{4,5},{5,4},{6,7},{7,6},{8,9},{9,8},{10,11... | collective-permute-start | bytes 1081352 | tf_op jit(solution)/shard_map/ppermute | solution.py:349
  221.0 26.2 %collective-permute-start.42 = (bf16[352,512]{1,0:T(8,128)(2,1)}, bf16[352,512]{1,0:T(8,128)(2,1)}, u32[]{:S(2)}, u32[]{:S(2)}) collective-permute-start(bf16[352,512]{1,0:T(8,128)(2,1)} %collective-permute-done.38.refs_1_), channel_id=1, source_target_pairs={{0,2},{1,3},{2,0},{3,1},{4,6},{5,7},{6,4},{7,5},{8,10},{9,11},{10,... | collective-permute-start | bytes 1081352 | tf_op jit(solution)/shard_map/ppermute | solution.py:349
  313.7 40.8 %collective-permute-start.57 = (bf16[1,2,128,2816]{3,2,1,0:T(8,128)(2,1)}, bf16[1,2,128,2816]{3,2,1,0:T(8,128)(2,1)}, u32[]{:S(2)}, u32[]{:S(2)}) collective-permute-start(bf16[1,2,128,2816]{3,2,1,0:T(8,128)(2,1)} %dynamic-slice_bitcast_fusion), channel_id=1, source_target_pairs={{0,2},{1,3},{2,0},{3,1},{4,6},{5,7},{6,4},{7,5},{8,10},{9,11},{10,... | collective-permute-start | bytes 4325384 | tf_op jit(solution)/shard_map/ppermute | solution.py:349
  315.6 28.9 %collective-permute-start.55 = (bf16[1,352,512]{2,1,0:T(8,128)(2,1)}, bf16[1,352,512]{2,1,0:T(8,128)(2,1)}, u32[]{:S(2)}, u32[]{:S(2)}) collective-permute-start(bf16[1,352,512]{2,1,0:T(8,128)(2,1)} %dynamic-slice_bitcast_fusion.12), channel_id=1, source_target_pairs={{0,1},{1,0},{2,3},{3,2},{4,5},{5,4},{6,7},{7,6},{8,9},{9,8},{10,11... | collective-permute-start | bytes 1081352 | tf_op jit(solution)/shard_map/ppermute | solution.py:349
  317.7 38.7 %collective-permute-start.56 = (bf16[1,2,128,2816]{3,2,1,0:T(8,128)(2,1)}, bf16[1,2,128,2816]{3,2,1,0:T(8,128)(2,1)}, u32[]{:S(2)}, u32[]{:S(2)}) collective-permute-start(bf16[1,2,128,2816]{3,2,1,0:T(8,128)(2,1)} %dynamic-slice_bitcast_fusion.1), channel_id=1, source_target_pairs={{0,1},{1,0},{2,3},{3,2},{4,5},{5,4},{6,7},{7,6},{8,9},{9,8},{10,11... | collective-permute-start | bytes 4325384 | tf_op jit(solution)/shard_map/ppermute | solution.py:349
  319.9 34.6 %collective-permute-start.54 = (bf16[1,352,512]{2,1,0:T(8,128)(2,1)}, bf16[1,352,512]{2,1,0:T(8,128)(2,1)}, u32[]{:S(2)}, u32[]{:S(2)}) collective-permute-start(bf16[1,352,512]{2,1,0:T(8,128)(2,1)} %dynamic-slice_bitcast_fusion.13), channel_id=1, source_target_pairs={{0,2},{1,3},{2,0},{3,1},{4,6},{5,7},{6,4},{7,5},{8,10},{9,11},{10,... | collective-permute-start | bytes 1081352 | tf_op jit(solution)/shard_map/ppermute | solution.py:349
  378.0 26.0 %collective-permute-start.65 = (bf16[2,2,64,512]{3,2,1,0:T(8,128)(2,1)}, bf16[2,2,64,512]{3,2,1,0:T(8,128)(2,1)S(1)}, u32[]{:S(2)}, u32[]{:S(2)}) collective-permute-start(bf16[2,2,64,512]{3,2,1,0:T(8,128)(2,1)} %slice_bitcast_fusion.11), channel_id=1, source_target_pairs={{0,8},{8,0},{16,24},{24,16},{1,9},{9,1},{17,25},{25,17},{2,10},{10... | collective-permute-start | bytes 786440 | tf_op jit(solution)/shard_map/ppermute | solution.py:349
  405.7 36.2 %collective-permute-start.67 = (bf16[1,176,512]{2,1,0:T(8,128)(2,1)S(1)}, bf16[1,176,512]{2,1,0:T(8,128)(2,1)}, u32[]{:S(2)}, u32[]{:S(2)}) collective-permute-start(bf16[1,176,512]{2,1,0:T(8,128)(2,1)S(1)} %fusion.172), channel_id=1, source_target_pairs={{0,16},{8,24},{16,0},{24,8},{1,17},{9,25},{17,1},{25,9},{2,18},{10... | collective-permute-start | bytes 540680 | tf_op jit(solution)/shard_map/ppermute | solution.py:349
  407.3 47.0 %collective-permute-start.73 = (bf16[1,176,512]{2,1,0:T(8,128)(2,1)S(1)}, bf16[1,176,512]{2,1,0:T(8,128)(2,1)}, u32[]{:S(2)}, u32[]{:S(2)}) collective-permute-start(bf16[1,176,512]{2,1,0:T(8,128)(2,1)S(1)} %fusion.172), channel_id=1, source_target_pairs={{0,8},{8,0},{16,24},{24,16},{1,9},{9,1},{17,25},{25,17},{2,10},{10... | collective-permute-start | bytes 540680 | tf_op jit(solution)/shard_map/ppermute | solution.py:349
  412.7 29.1 %collective-permute-start.69 = (bf16[2,1,64,512]{3,2,0,1:T(8,128)(2,1)}, bf16[2,1,64,512]{3,2,0,1:T(8,128)(2,1)S(1)}, u32[]{:S(2)}, u32[]{:S(2)}) collective-permute-start(bf16[2,1,64,512]{3,2,0,1:T(8,128)(2,1)} %slice_bitcast_fusion.17), channel_id=1, source_target_pairs={{0,16},{8,24},{16,0},{24,8},{1,17},{9,25},{17,1},{25,9},{2,18},{10... | collective-permute-start | bytes 393224 | tf_op jit(solution)/shard_map/ppermute | solution.py:349
  443.9 30.6 %collective-permute-start.75 = (bf16[1,64,2816]{2,1,0:T(8,128)(2,1)}, bf16[1,64,2816]{2,1,0:T(8,128)(2,1)}, u32[]{:S(2)}, u32[]{:S(2)}) collective-permute-start(bf16[1,64,2816]{2,1,0:T(8,128)(2,1)} %fusion.100), channel_id=1, source_target_pairs={{0,16},{8,24},{16,0},{24,8},{1,17},{9,25},{17,1},{25,9},{2,18},{10... | collective-permute-start | bytes 1081352 | tf_op jit(solution)/shard_map/ppermute | solution.py:349
  446.6 28.0 %collective-permute-start.71 = (bf16[2,2,256,256]{3,2,0,1:T(8,128)(2,1)}, bf16[2,2,256,256]{3,2,0,1:T(8,128)(2,1)}, u32[]{:S(2)}, u32[]{:S(2)}) collective-permute-start(bf16[2,2,256,256]{3,2,0,1:T(8,128)(2,1)} %bitcast.536), channel_id=1, source_target_pairs={{0,8},{8,0},{16,24},{24,16},{1,9},{9,1},{17,25},{25,17},{2,10},{10... | collective-permute-start | bytes 1572872 | tf_op jit(solution)/shard_map/ppermute | solution.py:349
  474.6 33.4 %collective-permute-start.84 = (bf16[1,64,2816]{2,1,0:T(8,128)(2,1)}, bf16[1,64,2816]{2,1,0:T(8,128)(2,1)S(1)}, u32[]{:S(2)}, u32[]{:S(2)}) collective-permute-start(bf16[1,64,2816]{2,1,0:T(8,128)(2,1)} %fusion.100), channel_id=1, source_target_pairs={{0,8},{8,0},{16,24},{24,16},{1,9},{9,1},{17,25},{25,17},{2,10},{10... | collective-permute-start | bytes 1081352 | tf_op jit(solution)/shard_map/ppermute | solution.py:349
  476.1 26.6 %collective-permute-start.79 = (bf16[4,1,176,512]{3,2,0,1:T(8,128)(2,1)S(1)}, bf16[4,1,176,512]{3,2,0,1:T(8,128)(2,1)S(1)}, u32[]{:S(2)}, u32[]{:S(2)}) collective-permute-start(bf16[4,1,176,512]{3,2,0,1:T(8,128)(2,1)S(1)} %pad_maximum_fusion.7), channel_id=1, source_target_pairs={{0,4},{4,0},{1,5},{5,1},{2,6},{6,2},{3,7},{7,3},{8,12},{12,8},{9,1... | collective-permute-start | bytes 2162696 | tf_op jit(solution)/shard_map/ppermute | solution.py:349
  489.4 29.2 %collective-permute-start.83 = (bf16[4,2,128,512]{3,2,1,0:T(8,128)(2,1)S(1)}, bf16[4,2,128,512]{3,2,1,0:T(8,128)(2,1)S(1)}, u32[]{:S(2)}, u32[]{:S(2)}) collective-permute-start(bf16[4,2,128,512]{3,2,1,0:T(8,128)(2,1)S(1)} %dynamic-slice_bitcast_fusion.2), channel_id=1, source_target_pairs={{0,2},{1,3},{2,0},{3,1},{4,6},{5,7},{6,4},{7,5},{8,10},{9,11},{10,... | collective-permute-start | bytes 3145736 | tf_op jit(solution)/shard_map/ppermute | solution.py:349
  (177 other events, 1793.5 us)

commit v7 on v6

--- a/solution.py
+++ b/solution.py
@@ -456,7 +456,7 @@
     return jnp.concatenate([columns_of(part, core) for part in parts], axis=1)
 
 
-def gather_steps(mine):
+def gather_steps(mine, fine=False):
     size = lax.axis_size("fsdp")
     me = lax.axis_index("fsdp")
     rows, width = mine.shape
@@ -465,7 +465,14 @@
     streams = [[(0, mine[stream * half : (stream + 1) * half])] for stream in range(2)]
     for step in range(len(bits)):
         chosen = [(bits if stream == 0 else bits[::-1])[step] for stream in range(2)]
-        got = yield [[cross(piece, "fsdp", chosen[stream]) for _, piece in streams[stream]] for stream in range(2)]
+        have = len(streams[0])
+        got = [[], []]
+        for spot in range(have) if fine else [slice(0, have)]:
+            spot = spot if isinstance(spot, slice) else slice(spot, spot + 1)
+            arrived = yield [
+                [cross(piece, "fsdp", chosen[stream]) for _, piece in streams[stream][spot]] for stream in range(2)
+            ]
+            got = [got[stream] + arrived[stream] for stream in range(2)]
         for stream in range(2):
             fresh = [(mask ^ chosen[stream], piece) for (mask, _), piece in zip(streams[stream], got[stream])]
             streams[stream] = streams[stream] + fresh
@@ -525,32 +532,39 @@
         keep, send = split(value, "line", bit, value.ndim - 3)
         (got,) = yield [cross(send, "line", bit)]
         value = add(keep, got)
-    have = [(0, value)]
+    mine = value[None]
     for bit in line_bits[::-1]:
-        got = yield [cross(piece, "line", bit) for _, piece in have]
-        have = have + [(mask ^ bit, piece) for (mask, _), piece in zip(have, got)]
-    have = [piece for _, piece in sorted(have, key=lambda item: item[0])]
-    mine = jnp.stack(have)
+        (got,) = yield [cross(mine, "line", bit)]
+        mine = jnp.concatenate([mine, got], axis=0)
     (other,) = yield [swap(mine)]
     me = lax.axis_index("line")
+
+    def spot(entry):
+        mask = me ^ entry
+        return sum(((mask // bit) % 2) * (lines // (2 * bit)) for bit in line_bits)
+
     outs = []
     for index in range(many):
         start = 0
         for wide in widths[index]:
             part = slice(start, start + wide // 2)
             both = jnp.concatenate(by_core(mine[:, index, :, part], other[:, index, :, part]), axis=2)
-            ordered = [lax.dynamic_index_in_dim(both, me ^ entry, 0, keepdims=False) for entry in range(lines)]
+            ordered = [lax.dynamic_index_in_dim(both, spot(entry), 0, keepdims=False) for entry in range(lines)]
             outs.append(jnp.concatenate(ordered, axis=0).astype(F32))
             start = start + wide // 2
     return outs
 
 
 def gather_context_steps(value):
-    have = [(0, value)]
+    rows = value.shape[0]
+    mine = value
+    masks = [0]
     for bit in bits_of(lax.axis_size("line"))[::-1]:
-        got = yield [cross(piece, "line", bit) for _, piece in have]
-        have = have + [(mask ^ bit, piece) for (mask, _), piece in zip(have, got)]
-    mine = jnp.concatenate([piece for _, piece in sorted(have, key=lambda item: item[0])], axis=0)
+        (got,) = yield [cross(mine, "line", bit)]
+        mine = jnp.concatenate([mine, got], axis=0)
+        masks = masks + [mask ^ bit for mask in masks]
+    order = [masks.index(mask) for mask in range(len(masks))]
+    mine = jnp.concatenate([mine[at * rows : (at + 1) * rows] for at in order], axis=0)
     (other,) = yield [swap(mine)]
     return jnp.concatenate([mine, other], axis=0)
 
@@ -650,9 +664,8 @@
     )
     extra = (vectors, low, high)
 
-    lane_gu = Lane(gather_steps(gu_shard))
-    lane_hidden_one = Lane(swap_steps(hidden_one))
-    tick([lane_keys, lane_mid, lane_hidden_one], ())
+    lane_gu = Lane(gather_steps(gu_shard, True))
+    tick([lane_keys, lane_mid, lane_gu], ())
     mid_mine, mid_other = lane_mid.take()
     wo, wcq, wckv, wco = [
         (mid_mine[:, index * halves : (index + 1) * halves], mid_other[:, index * halves : (index + 1) * halves])
@@ -660,25 +673,26 @@
     ]
     encoder_rows = encoder.reshape(encoder.shape[1], width)
     encoder_pairs = times(encoder_rows, wckv).astype(BF16)
-    encoder_pairs = tick([lane_keys, lane_gu], encoder_pairs)
+    encoder_pairs, wd_shard = tick([lane_keys], (encoder_pairs, wd_shard))
     pairs_whole = lane_keys.take()
 
     lane_encoder = Lane(gather_context_steps(encoder_pairs))
     lane_encoder_rows = Lane(swap_steps(encoder_rows))
+    lane_wd = Lane(gather_steps(wd_shard))
+    lane_hidden_one = Lane(swap_steps(hidden_one))
     attention, outs_one, logs_one = attend(query, pairs_whole, place_table, extra, True)
-    attention, outs_one, logs_one, wd_shard = tick(
-        [lane_encoder, lane_encoder_rows], (attention, outs_one, logs_one, wd_shard)
+    attention, outs_one, logs_one = tick(
+        [lane_encoder, lane_encoder_rows, lane_gu, lane_wd, lane_hidden_one], (attention, outs_one, logs_one)
     )
 
     lane_attention = Lane(swap_steps(attention))
-    lane_wd = Lane(gather_steps(wd_shard))
     mid_one = flat_in + times(attention, wo)
     normed_two, scale_two, hidden_two = norm_rows(mid_one, gain_two)
     cross_q = times(hidden_two, wcq).astype(BF16)
     mid_one, normed_two, hidden_two, cross_q, scale_two = tick(
         [lane_encoder, lane_attention, lane_gu], (mid_one, normed_two, hidden_two, cross_q, scale_two)
     )
-    tick([lane_encoder, lane_wd], ())
+    tick([lane_encoder], ())
     encoder_whole = lane_encoder.take()
 
     lane_hidden_two = Lane(swap_steps(hidden_two))

time: 632 us -> 593 us (0.938)
  waiting for transfers between devices: 217 us -> 189 us
  starting transfers between devices: 110 us -> 97.2 us
    ppermute x111 -> x105, waiting for transfers between devices: 217 us -> 189 us  [cross(): return lax.ppermute(value, axis, partners(lax.axis_size(axis), bit))]
    ppermute x111 -> x105, starting transfers between devices: 110 us -> 97.2 us  [cross(): return lax.ppermute(value, axis, partners(lax.axis_size(axis), bit))]
    convert_element_type x30 -> x26, other arithmetic: 16.8 us -> 14.3 us  [add(): return (left.astype(F32) + right.astype(F32)).astype(BF16)]
    unnamed x206 -> x230, local copies, waits for them, and re-layouts: 17 us -> 17.2 us
  transfers between devices with their start and end apart: 111 -> 105, of which waited for: 40 -> 43; matrix products, arithmetic and copies ran while one was open for 27% -> 28% of each run, Pallas kernels for 13% -> 14%
where the time goes in v7:
time: 593 us; the launch traced here: 592 us
  waiting for transfers between devices  189 us (32%)
  Pallas kernels  99.2 us (17%)
  starting transfers between devices  97.2 us (16%)
  matrix products  76.1 us (13%)
  other arithmetic  65.6 us (11%)
  local copies, waits for them, and re-layouts  56.4 us (10%)
  between operations  7.65 us (1%)
    ppermute x105, waiting for transfers between devices, cross(): return lax.ppermute(value, axis, partners(lax.axis_size(axis), bit))  189 us
    ppermute x105, starting transfers between devices, cross(): return lax.ppermute(value, axis, partners(lax.axis_size(axis), bit))  97.2 us
    pallas_call x3, Pallas kernels, attend_back(): pl.pallas_call(functools.partial(backward_kernel, masked), grid_spec=pltp...  49.1 us
    pallas_call x2, Pallas kernels, attend(): pl.pallas_call(functools.partial(forward_kernel, masked), grid_spec=pltpu...  34.5 us
    dot_general x14, matrix products, nn(): return jnp.dot(left, right, preferred_element_type=F32)  28.8 us
    dot_general x14, matrix products, nt(): lax.dot_general(left, right, (((1,), (1,)), ((), ())), preferred_element_...  28.6 us
    dot_general x9, matrix products, tn(): lax.dot_general(left, right, (((0,), (0,)), ((), ())), preferred_element_...  17.3 us
    unnamed x230, local copies, waits for them, and re-layouts  17.2 us
  transfers between devices with their start and end apart: 105, of which 43 were waited for; matrix products, arithmetic and copies ran while one was open for 28% of the time, Pallas kernels for 14%

profile of v7, /device:TPU:0, one launch (start us, length us, event | category | flops | bytes accessed | tf_op | source)
XLA Modules:
  0.0 591.6 jit_solution(12500118798470447579)
XLA Ops:
  65.5 17.0 %collective-permute-done.16 = bf16[256,1024]{1,0:T(8,128)(2,1)} collective-permute-done((bf16[256,1024]{1,0:T(8,128)(2,1)S(1)}, bf16[256,1024]{1,0:T(8,128)(2,1)}, u32[]{:S(2)}, u32[]{:S(2)}) %collective-permute-start.16) | collective-permute-done | bytes 524320 | tf_op jit(solution)/shard_map/ppermute | solution.py:349
  92.3 16.0 %collective-permute-done.23.refs_1_ = bf16[128,2816]{1,0:T(8,128)(2,1)} collective-permute-done((bf16[128,2816]{1,0:T(8,128)(2,1)}, bf16[128,2816]{1,0:T(8,128)(2,1)}, u32[]{:S(2)}, u32[]{:S(2)}) %collective-permute-start.23) | collective-permute-done | bytes 720928 | tf_op jit(solution)/shard_map/ppermute | solution.py:349
  108.6 4.9 collective-permute-done.21
  130.9 18.1 %attend_self.1 = (bf16[256,1024]{1,0:T(8,128)(2,1)}, f32[4,2,64,512]{3,2,1,0:T(8,128)}, f32[4,2,8,512]{3,2,1,0:T(8,128)}) custom-call(s32[20]{0:T(128)} %pad_add_fusion.1.table, bf16[256,1024]{1,0:T(8,128)(2,1)} %get-tuple-element.261.refs_0_, bf16[2048,1024]{1,0:T(8,128)(2,1)} %constant_dynamic-update-slice_fusion.refs_1_.refs_2_, ...), custom_call_target="tpu_custom_call" | custom-call | flops 2147483648 | bytes 8388608 | tf_op jit(solution)/shard_map/attend_self/pallas_call | solution.py:248
  169.6 5.1 place.6
  181.9 6.9 %collective-permute-done.39.refs_2_ = bf16[352,512]{1,0:T(8,128)(2,1)S(1)} collective-permute-done((bf16[352,512]{1,0:T(8,128)(2,1)}, bf16[352,512]{1,0:T(8,128)(2,1)S(1)}, u32[]{:S(2)}, u32[]{:S(2)}) %collective-permute-start.39) | collective-permute-done | bytes 360480 | tf_op jit(solution)/shard_map/ppermute | solution.py:349
  194.2 16.4 %attend_cross.1 = (bf16[256,1024]{1,0:T(8,128)(2,1)}, f32[4,2,64,512]{3,2,1,0:T(8,128)}, f32[4,2,8,512]{3,2,1,0:T(8,128)}) custom-call(s32[20]{0:T(128)} %pad_add_fusion.1.table, bf16[256,1024]{1,0:T(8,128)(2,1)} %pad_maximum_fusion.10.refs_0_, bf16[512,1024]{1,0:T(8,128)(2,1)} %constant_dynamic-update-slice_fusion.5.refs_1_.refs_2_, ...), custom_call_target="tpu_custom_call" | custom-call | flops 536870912 | bytes 2097152 | tf_op jit(solution)/shard_map/attend_cross/pallas_call | solution.py:248
  221.8 4.7 fusion.334
  241.2 4.7 multiply_convert_fusion
  249.9 4.3 fusion.29
  258.4 4.8 convolution_convert_fusion
  263.2 10.6 %collective-permute-done.51 = bf16[1,2,352,512]{3,2,1,0:T(8,128)(2,1)S(1)} collective-permute-done((bf16[1,2,352,512]{3,2,1,0:T(8,128)(2,1)S(1)}, bf16[1,2,352,512]{3,2,1,0:T(8,128)(2,1)S(1)}, u32[]{:S(2)}, u32[]{:S(2)}) %collective-permute-start.51) | collective-permute-done | bytes 720928 | tf_op jit(solution)/shard_map/ppermute | solution.py:349
  289.2 16.6 %attend_cross_back.1 = (bf16[256,1024]{1,0:T(8,128)(2,1)}, bf16[2,512,512]{2,1,0:T(8,128)(2,1)}) custom-call(s32[20]{0:T(128)} %pad_add_fusion.1.table, bf16[256,1024]{1,0:T(8,128)(2,1)} %pad_maximum_fusion.10.refs_0_, bf16[512,1024]{1,0:T(8,128)(2,1)} %constant_dynamic-update-slice_fusion.5.refs_1_.refs_2_, ...), custom_call_target="tpu_custom_call" | custom-call | flops 1342177280 | bytes 4194304 | tf_op jit(solution)/shard_map/attend_cross_back/pallas_call | solution.py:287
  307.2 10.0 %collective-permute-done.52 = bf16[1,352,512]{2,1,0:T(8,128)(2,1)} collective-permute-done((bf16[1,352,512]{2,1,0:T(8,128)(2,1)}, bf16[1,352,512]{2,1,0:T(8,128)(2,1)}, u32[]{:S(2)}, u32[]{:S(2)}) %collective-permute-start.52) | collective-permute-done | bytes 360480 | tf_op jit(solution)/shard_map/ppermute | solution.py:349
  346.1 16.1 %attend_self_back.2 = (bf16[256,512]{1,0:T(8,128)(2,1)}, bf16[2,2048,256]{2,1,0:T(8,128)(2,1)}, f32[2,4,512]{2,1,0:T(4,128)}) custom-call(s32[20]{0:T(128)} %pad_add_fusion.1.table, bf16[256,1024]{1,0:T(8,128)(2,1)} %get-tuple-element.261.refs_0_, bf16[2048,1024]{1,0:T(8,128)(2,1)} %constant_dynamic-update-slice_fusion.refs_1_.refs_2_, ...), custom_call_target="tpu_custom_call" | custom-call | flops 2684354560 | bytes 8388608 | tf_op jit(solution)/shard_map/attend_self_back/pallas_call | solution.py:287
  379.3 16.4 %attend_self_back.3 = (bf16[256,512]{1,0:T(8,128)(2,1)}, bf16[2,2048,256]{2,1,0:T(8,128)(2,1)}, f32[2,4,512]{2,1,0:T(4,128)}) custom-call(s32[20]{0:T(128)} %pad_add_fusion.1.table, bf16[256,1024]{1,0:T(8,128)(2,1)} %get-tuple-element.261.refs_0_, bf16[2048,1024]{1,0:T(8,128)(2,1)} %constant_dynamic-update-slice_fusion.refs_1_.refs_2_, ...), custom_call_target="tpu_custom_call" | custom-call | flops 2684354560 | bytes 8388608 | tf_op jit(solution)/shard_map/attend_self_back/pallas_call | solution.py:287
  424.3 10.1 %collective-permute-done.69 = bf16[2,2,256,256]{3,2,0,1:T(8,128)(2,1)} collective-permute-done((bf16[2,2,256,256]{3,2,0,1:T(8,128)(2,1)}, bf16[2,2,256,256]{3,2,0,1:T(8,128)(2,1)}, u32[]{:S(2)}, u32[]{:S(2)}) %collective-permute-start.69) | collective-permute-done | bytes 524320 | tf_op jit(solution)/shard_map/ppermute | solution.py:349
  466.0 12.6 %collective-permute-done.81 = bf16[2,1,64,2816]{3,2,0,1:T(8,128)(2,1)S(1)} collective-permute-done((bf16[2,1,64,2816]{3,2,0,1:T(8,128)(2,1)S(1)}, bf16[2,1,64,2816]{3,2,0,1:T(8,128)(2,1)S(1)}, u32[]{:S(2)}, u32[]{:S(2)}) %collective-permute-start.81) | collective-permute-done | bytes 720928 | tf_op jit(solution)/shard_map/ppermute | solution.py:349
  492.4 5.5 collective-permute-done.84
  500.4 5.2 collective-permute-start.88
  509.0 8.2 %collective-permute-done.88 = bf16[4,2,64,512]{3,2,0,1:T(8,128)(2,1)S(1)} collective-permute-done((bf16[4,2,64,512]{3,2,0,1:T(8,128)(2,1)S(1)}, bf16[4,2,64,512]{3,2,0,1:T(8,128)(2,1)S(1)}, u32[]{:S(2)}, u32[]{:S(2)}) %collective-permute-start.88) | collective-permute-done | bytes 524320 | tf_op jit(solution)/shard_map/ppermute | solution.py:349
  522.8 10.1 %collective-permute-done.91 = bf16[4,64,512]{2,1,0:T(8,128)(2,1)S(1)} collective-permute-done((bf16[4,64,512]{2,1,0:T(8,128)(2,1)S(1)}, bf16[4,64,512]{2,1,0:T(8,128)(2,1)S(1)}, u32[]{:S(2)}, u32[]{:S(2)}) %collective-permute-start.91) | collective-permute-done | bytes 262176 | tf_op jit(solution)/shard_map/ppermute | solution.py:349
  538.1 6.8 %collective-permute-done.94 = bf16[1,4,64,512]{3,2,0,1:T(8,128)(2,1)S(1)} collective-permute-done((bf16[1,4,64,512]{3,2,0,1:T(8,128)(2,1)S(1)}, bf16[1,4,64,512]{3,2,0,1:T(8,128)(2,1)S(1)}, u32[]{:S(2)}, u32[]{:S(2)}) %collective-permute-start.94) | collective-permute-done | bytes 262176 | tf_op jit(solution)/shard_map/ppermute | solution.py:349
  552.5 8.4 %collective-permute-done.96 = bf16[2,64,512]{2,1,0:T(8,128)(2,1)S(1)} collective-permute-done((bf16[2,64,512]{2,1,0:T(8,128)(2,1)S(1)}, bf16[2,64,512]{2,1,0:T(8,128)(2,1)S(1)}, u32[]{:S(2)}, u32[]{:S(2)}) %collective-permute-start.96) | collective-permute-done | bytes 131104 | tf_op jit(solution)/shard_map/ppermute | solution.py:349
  (694 shorter events, 344.4 us)
Async XLA Ops:
  57.7 24.8 %collective-permute-start.16 = (bf16[256,1024]{1,0:T(8,128)(2,1)S(1)}, bf16[256,1024]{1,0:T(8,128)(2,1)}, u32[]{:S(2)}, u32[]{:S(2)}) collective-permute-start(bf16[256,1024]{1,0:T(8,128)(2,1)S(1)} %get-tuple-element.257), channel_id=1, source_target_pairs={{0,16},{8,24},{16,0},{24,8},{1,17},{9,25},{17,1},{25,9},{2,18},{10... | collective-permute-start | bytes 1572872 | tf_op jit(solution)/shard_map/ppermute | solution.py:349
  86.7 26.8 %collective-permute-start.22 = (bf16[1024,2048]{1,0:T(8,128)(2,1)}, bf16[1024,2048]{1,0:T(8,128)(2,1)S(1)}, u32[]{:S(2)}, u32[]{:S(2)}) collective-permute-start(bf16[1024,2048]{1,0:T(8,128)(2,1)} %place.5), channel_id=1, source_target_pairs={{0,4},{4,0},{1,5},{5,1},{2,6},{6,2},{3,7},{7,3},{8,12},{12,8},{9,1... | collective-permute-start | bytes 12582920 | tf_op jit(solution)/shard_map/ppermute | solution.py:349
  87.9 25.6 %collective-permute-start.21 = (bf16[512,1024]{1,0:T(8,128)(2,1)S(1)}, bf16[512,1024]{1,0:T(8,128)(2,1)S(1)}, u32[]{:S(2)}, u32[]{:S(2)}) collective-permute-start(bf16[512,1024]{1,0:T(8,128)(2,1)S(1)} %pad_maximum_fusion.6), channel_id=1, source_target_pairs={{0,8},{8,0},{16,24},{24,16},{1,9},{9,1},{17,25},{25,17},{2,10},{10... | collective-permute-start | bytes 3145736 | tf_op jit(solution)/shard_map/ppermute | solution.py:349
  117.5 31.5 %collective-permute-start.28 = (bf16[128,2816]{1,0:T(8,128)(2,1)}, bf16[128,2816]{1,0:T(8,128)(2,1)S(1)}, u32[]{:S(2)}, u32[]{:S(2)}) collective-permute-start(bf16[128,2816]{1,0:T(8,128)(2,1)} %get-tuple-element.504), channel_id=1, source_target_pairs={{0,2},{1,3},{2,0},{3,1},{4,6},{5,7},{6,4},{7,5},{8,10},{9,11},{10,... | collective-permute-start | bytes 2162696 | tf_op jit(solution)/shard_map/ppermute | solution.py:349
  118.0 31.6 %collective-permute-start.29 = (bf16[128,2816]{1,0:T(8,128)(2,1)}, bf16[128,2816]{1,0:T(8,128)(2,1)}, u32[]{:S(2)}, u32[]{:S(2)}) collective-permute-start(bf16[128,2816]{1,0:T(8,128)(2,1)} %get-tuple-element.503), channel_id=1, source_target_pairs={{0,1},{1,0},{2,3},{3,2},{4,5},{5,4},{6,7},{7,6},{8,9},{9,8},{10,11... | collective-permute-start | bytes 2162696 | tf_op jit(solution)/shard_map/ppermute | solution.py:349
  124.7 28.2 %collective-permute-start.30 = (bf16[352,512]{1,0:T(8,128)(2,1)}, bf16[352,512]{1,0:T(8,128)(2,1)S(1)}, u32[]{:S(2)}, u32[]{:S(2)}) collective-permute-start(bf16[352,512]{1,0:T(8,128)(2,1)} %get-tuple-element.531), channel_id=1, source_target_pairs={{0,1},{1,0},{2,3},{3,2},{4,5},{5,4},{6,7},{7,6},{8,9},{9,8},{10,11... | collective-permute-start | bytes 1081352 | tf_op jit(solution)/shard_map/ppermute | solution.py:349
  125.6 27.4 %collective-permute-start.31 = (bf16[352,512]{1,0:T(8,128)(2,1)}, bf16[352,512]{1,0:T(8,128)(2,1)S(1)}, u32[]{:S(2)}, u32[]{:S(2)}) collective-permute-start(bf16[352,512]{1,0:T(8,128)(2,1)} %get-tuple-element.530), channel_id=1, source_target_pairs={{0,2},{1,3},{2,0},{3,1},{4,6},{5,7},{6,4},{7,5},{8,10},{9,11},{10,... | collective-permute-start | bytes 1081352 | tf_op jit(solution)/shard_map/ppermute | solution.py:349
  174.8 35.9 %collective-permute-start.38 = (bf16[1024,2816]{1,0:T(8,128)(2,1)}, bf16[1024,2816]{1,0:T(8,128)(2,1)}, u32[]{:S(2)}, u32[]{:S(2)}) collective-permute-start(bf16[1024,2816]{1,0:T(8,128)(2,1)} %place.6), channel_id=1, source_target_pairs={{0,4},{4,0},{1,5},{5,1},{2,6},{6,2},{3,7},{7,3},{8,12},{12,8},{9,1... | collective-permute-start | bytes 17301512 | tf_op jit(solution)/shard_map/ppermute | solution.py:349
  179.5 31.1 %collective-permute-start.43 = (bf16[256,1024]{1,0:T(8,128)(2,1)S(1)}, bf16[256,1024]{1,0:T(8,128)(2,1)}, u32[]{:S(2)}, u32[]{:S(2)}) collective-permute-start(bf16[256,1024]{1,0:T(8,128)(2,1)S(1)} %get-tuple-element.297), channel_id=1, source_target_pairs={{0,4},{4,0},{1,5},{5,1},{2,6},{6,2},{3,7},{7,3},{8,12},{12,8},{9,1... | collective-permute-start | bytes 1572872 | tf_op jit(solution)/shard_map/ppermute | solution.py:349
  179.5 31.1 %collective-permute-start.41 = (bf16[352,512]{1,0:T(8,128)(2,1)}, bf16[352,512]{1,0:T(8,128)(2,1)}, u32[]{:S(2)}, u32[]{:S(2)}) collective-permute-start(bf16[352,512]{1,0:T(8,128)(2,1)} %get-tuple-element.530), channel_id=1, source_target_pairs={{0,1},{1,0},{2,3},{3,2},{4,5},{5,4},{6,7},{7,6},{8,9},{9,8},{10,11... | collective-permute-start | bytes 1081352 | tf_op jit(solution)/shard_map/ppermute | solution.py:349
  276.5 40.7 %collective-permute-start.55 = (bf16[1,2,128,2816]{3,2,1,0:T(8,128)(2,1)}, bf16[1,2,128,2816]{3,2,1,0:T(8,128)(2,1)}, u32[]{:S(2)}, u32[]{:S(2)}) collective-permute-start(bf16[1,2,128,2816]{3,2,1,0:T(8,128)(2,1)} %dynamic-slice_bitcast_fusion), channel_id=1, source_target_pairs={{0,2},{1,3},{2,0},{3,1},{4,6},{5,7},{6,4},{7,5},{8,10},{9,11},{10,... | collective-permute-start | bytes 4325384 | tf_op jit(solution)/shard_map/ppermute | solution.py:349
  278.5 28.7 %collective-permute-start.53 = (bf16[1,352,512]{2,1,0:T(8,128)(2,1)}, bf16[1,352,512]{2,1,0:T(8,128)(2,1)}, u32[]{:S(2)}, u32[]{:S(2)}) collective-permute-start(bf16[1,352,512]{2,1,0:T(8,128)(2,1)} %dynamic-slice_bitcast_fusion.12), channel_id=1, source_target_pairs={{0,1},{1,0},{2,3},{3,2},{4,5},{5,4},{6,7},{7,6},{8,9},{9,8},{10,11... | collective-permute-start | bytes 1081352 | tf_op jit(solution)/shard_map/ppermute | solution.py:349
  280.1 39.0 %collective-permute-start.54 = (bf16[1,2,128,2816]{3,2,1,0:T(8,128)(2,1)}, bf16[1,2,128,2816]{3,2,1,0:T(8,128)(2,1)}, u32[]{:S(2)}, u32[]{:S(2)}) collective-permute-start(bf16[1,2,128,2816]{3,2,1,0:T(8,128)(2,1)} %dynamic-slice_bitcast_fusion.1), channel_id=1, source_target_pairs={{0,1},{1,0},{2,3},{3,2},{4,5},{5,4},{6,7},{7,6},{8,9},{9,8},{10,11... | collective-permute-start | bytes 4325384 | tf_op jit(solution)/shard_map/ppermute | solution.py:349
  282.8 34.4 %collective-permute-start.52 = (bf16[1,352,512]{2,1,0:T(8,128)(2,1)}, bf16[1,352,512]{2,1,0:T(8,128)(2,1)}, u32[]{:S(2)}, u32[]{:S(2)}) collective-permute-start(bf16[1,352,512]{2,1,0:T(8,128)(2,1)} %dynamic-slice_bitcast_fusion.13), channel_id=1, source_target_pairs={{0,2},{1,3},{2,0},{3,1},{4,6},{5,7},{6,4},{7,5},{8,10},{9,11},{10,... | collective-permute-start | bytes 1081352 | tf_op jit(solution)/shard_map/ppermute | solution.py:349
  340.8 26.5 %collective-permute-start.63 = (bf16[2,2,64,512]{3,2,1,0:T(8,128)(2,1)}, bf16[2,2,64,512]{3,2,1,0:T(8,128)(2,1)}, u32[]{:S(2)}, u32[]{:S(2)}) collective-permute-start(bf16[2,2,64,512]{3,2,1,0:T(8,128)(2,1)} %slice_bitcast_fusion.11), channel_id=1, source_target_pairs={{0,8},{8,0},{16,24},{24,16},{1,9},{9,1},{17,25},{25,17},{2,10},{10... | collective-permute-start | bytes 786440 | tf_op jit(solution)/shard_map/ppermute | solution.py:349
  341.4 25.8 %collective-permute-start.62 = (bf16[1,2,64,2816]{3,2,1,0:T(8,128)(2,1)S(1)}, bf16[1,2,64,2816]{3,2,1,0:T(8,128)(2,1)}, u32[]{:S(2)}, u32[]{:S(2)}) collective-permute-start(bf16[1,2,64,2816]{3,2,1,0:T(8,128)(2,1)S(1)} %fusion.99), channel_id=1, source_target_pairs={{0,8},{8,0},{16,24},{24,16},{1,9},{9,1},{17,25},{25,17},{2,10},{10... | collective-permute-start | bytes 2162696 | tf_op jit(solution)/shard_map/ppermute | solution.py:349
  369.2 30.3 %collective-permute-start.67 = (bf16[2,1,64,512]{3,2,0,1:T(8,128)(2,1)}, bf16[2,1,64,512]{3,2,0,1:T(8,128)(2,1)S(1)}, u32[]{:S(2)}, u32[]{:S(2)}) collective-permute-start(bf16[2,1,64,512]{3,2,0,1:T(8,128)(2,1)} %slice_bitcast_fusion.17), channel_id=1, source_target_pairs={{0,16},{8,24},{16,0},{24,8},{1,17},{9,25},{17,1},{25,9},{2,18},{10... | collective-permute-start | bytes 393224 | tf_op jit(solution)/shard_map/ppermute | solution.py:349
  371.4 30.5 %collective-permute-start.66 = (bf16[1,64,2816]{2,1,0:T(8,128)(2,1)}, bf16[1,64,2816]{2,1,0:T(8,128)(2,1)}, u32[]{:S(2)}, u32[]{:S(2)}) collective-permute-start(bf16[1,64,2816]{2,1,0:T(8,128)(2,1)} %dynamic-slice_bitcast_fusion.11), channel_id=1, source_target_pairs={{0,16},{8,24},{16,0},{24,8},{1,17},{9,25},{17,1},{25,9},{2,18},{10... | collective-permute-start | bytes 1081352 | tf_op jit(solution)/shard_map/ppermute | solution.py:349
  375.2 26.6 %collective-permute-start.68 = (bf16[2,4,256,256]{3,2,1,0:T(8,128)(2,1)}, bf16[2,4,256,256]{3,2,1,0:T(8,128)(2,1)S(1)}, u32[]{:S(2)}, u32[]{:S(2)}) collective-permute-start(bf16[2,4,256,256]{3,2,1,0:T(8,128)(2,1)} %slice_bitcast_fusion.3), channel_id=1, source_target_pairs={{0,4},{4,0},{1,5},{5,1},{2,6},{6,2},{3,7},{7,3},{8,12},{12,8},{9,1... | collective-permute-start | bytes 3145736 | tf_op jit(solution)/shard_map/ppermute | solution.py:349
  376.2 25.6 %collective-permute-start.65 = (bf16[1,1,176,512]{3,2,0,1:T(8,128)(2,1)S(1)}, bf16[1,1,176,512]{3,2,0,1:T(8,128)(2,1)S(1)}, u32[]{:S(2)}, u32[]{:S(2)}) collective-permute-start(bf16[1,1,176,512]{3,2,0,1:T(8,128)(2,1)S(1)} %fusion.191), channel_id=1, source_target_pairs={{0,16},{8,24},{16,0},{24,8},{1,17},{9,25},{17,1},{25,9},{2,18},{10... | collective-permute-start | bytes 540680 | tf_op jit(solution)/shard_map/ppermute | solution.py:349
  409.6 24.9 %collective-permute-start.69 = (bf16[2,2,256,256]{3,2,0,1:T(8,128)(2,1)}, bf16[2,2,256,256]{3,2,0,1:T(8,128)(2,1)}, u32[]{:S(2)}, u32[]{:S(2)}) collective-permute-start(bf16[2,2,256,256]{3,2,0,1:T(8,128)(2,1)} %bitcast.504), channel_id=1, source_target_pairs={{0,8},{8,0},{16,24},{24,16},{1,9},{9,1},{17,25},{25,17},{2,10},{10... | collective-permute-start | bytes 1572872 | tf_op jit(solution)/shard_map/ppermute | solution.py:349
  442.8 35.8 %collective-permute-start.81 = (bf16[2,1,64,2816]{3,2,0,1:T(8,128)(2,1)S(1)}, bf16[2,1,64,2816]{3,2,0,1:T(8,128)(2,1)S(1)}, u32[]{:S(2)}, u32[]{:S(2)}) collective-permute-start(bf16[2,1,64,2816]{3,2,0,1:T(8,128)(2,1)S(1)} %pad_maximum_fusion.9), channel_id=1, source_target_pairs={{0,8},{8,0},{16,24},{24,16},{1,9},{9,1},{17,25},{25,17},{2,10},{10... | collective-permute-start | bytes 2162696 | tf_op jit(solution)/shard_map/ppermute | solution.py:349
  450.4 28.2 %collective-permute-start.80 = (bf16[4,2,128,512]{3,2,1,0:T(8,128)(2,1)S(1)}, bf16[4,2,128,512]{3,2,1,0:T(8,128)(2,1)S(1)}, u32[]{:S(2)}, u32[]{:S(2)}) collective-permute-start(bf16[4,2,128,512]{3,2,1,0:T(8,128)(2,1)S(1)} %dynamic-slice_bitcast_fusion.2), channel_id=1, source_target_pairs={{0,2},{1,3},{2,0},{3,1},{4,6},{5,7},{6,4},{7,5},{8,10},{9,11},{10,... | collective-permute-start | bytes 3145736 | tf_op jit(solution)/shard_map/ppermute | solution.py:349
  455.5 26.0 %collective-permute-start.79 = (bf16[4,2,128,512]{3,2,1,0:T(8,128)(2,1)S(1)}, bf16[4,2,128,512]{3,2,1,0:T(8,128)(2,1)S(1)}, u32[]{:S(2)}, u32[]{:S(2)}) collective-permute-start(bf16[4,2,128,512]{3,2,1,0:T(8,128)(2,1)S(1)} %dynamic-slice_bitcast_fusion.3), channel_id=1, source_target_pairs={{0,1},{1,0},{2,3},{3,2},{4,5},{5,4},{6,7},{7,6},{8,9},{9,8},{10,11... | collective-permute-start | bytes 3145736 | tf_op jit(solution)/shard_map/ppermute | solution.py:349
  (184 other events, 1840.9 us)

commit v8 on v7

--- a/solution.py
+++ b/solution.py
@@ -618,7 +618,8 @@
     mid_parts = tick([lane_qkv, lane_small], (w_out, c_query, c_key, c_value, c_out))
 
     mid_shard = half_columns([mid_parts[0], mid_parts[1], joint(mid_parts[2:4], axis=1), mid_parts[4]])
-    mid_shard = tick([lane_qkv, lane_small], mid_shard)
+    mid_shard, late = tick([lane_qkv, lane_small], (mid_shard, (w_gate, w_up, doc_ids, block_order, buckets)))
+    w_gate, w_up, doc_ids, block_order, buckets = late
 
     small = lane_small.take()
     gain_one, gain_two, gain_three = [
@@ -628,19 +629,7 @@
     lane_count = Lane(count_steps(jnp.broadcast_to(jnp.sum(small[:, -128:].astype(F32), axis=0), (8, 128))))
     flat_in = inputs.reshape(rows, width).astype(F32)
     normed_one, scale_one, hidden_one = norm_rows(flat_in, gain_one)
-    hidden_one = tick([lane_qkv, lane_count], hidden_one)
-
-    qkv_mine, qkv_other = lane_qkv.take()
-    lane_mid = Lane(gather_steps(mid_shard))
-    query, pairs = by_core(nn(hidden_one, qkv_mine).astype(BF16), nn(hidden_one, qkv_other).astype(BF16))
-    query, pairs, late = tick(
-        [lane_mid, lane_count], (query, pairs, (w_gate, w_up, w_down, doc_ids, block_order, buckets, table_whole))
-    )
-    gate_part, up_part, down_part, doc_ids, block_order, buckets, table_whole = late
-
-    lane_keys = Lane(gather_context_steps(pairs))
-    gu_shard = half_columns([joint([gate_part, up_part], axis=1)])
-    wd_shard = half_columns([down_part])
+    gu_shard = half_columns([joint([w_gate, w_up], axis=1)])
 
     query_blocks = lax.dynamic_slice_in_dim(block_order, context * pair, pair)
     slots = jnp.arange(contexts * pair, dtype=jnp.int32)
@@ -659,10 +648,19 @@
     bucket_match = (jnp.take(buckets, index_of)[None, :] == jnp.arange(BUCKETS, dtype=jnp.int32)[:, None])
 
     vectors = tn(table_whole, bucket_match.astype(BF16)).reshape(HEADS // 4, 4, SPAN)
-    gu_shard, wd_shard, low, high, place_table, bucket_match, vectors = tick(
-        [lane_keys, lane_mid], (gu_shard, wd_shard, low, high, place_table, bucket_match, vectors)
+    hidden_one, gu_shard, low, high, place_table, bucket_match, vectors = tick(
+        [lane_qkv, lane_count], (hidden_one, gu_shard, low, high, place_table, bucket_match, vectors)
     )
     extra = (vectors, low, high)
+
+    qkv_mine, qkv_other = lane_qkv.take()
+    lane_mid = Lane(gather_steps(mid_shard))
+    query, pairs = by_core(nn(hidden_one, qkv_mine).astype(BF16), nn(hidden_one, qkv_other).astype(BF16))
+    query, pairs, w_down = tick([lane_mid, lane_count], (query, pairs, w_down))
+
+    lane_keys = Lane(gather_context_steps(pairs))
+    wd_shard = half_columns([w_down])
+    wd_shard = tick([lane_keys, lane_mid], wd_shard)
 
     lane_gu = Lane(gather_steps(gu_shard, True))
     tick([lane_keys, lane_mid, lane_gu], ())
@@ -682,7 +680,7 @@
     lane_hidden_one = Lane(swap_steps(hidden_one))
     attention, outs_one, logs_one = attend(query, pairs_whole, place_table, extra, True)
     attention, outs_one, logs_one = tick(
-        [lane_encoder, lane_encoder_rows, lane_gu, lane_wd, lane_hidden_one], (attention, outs_one, logs_one)
+        [lane_encoder, lane_encoder_rows, lane_gu, lane_hidden_one], (attention, outs_one, logs_one)
     )
 
     lane_attention = Lane(swap_steps(attention))
@@ -690,7 +688,7 @@
     normed_two, scale_two, hidden_two = norm_rows(mid_one, gain_two)
     cross_q = times(hidden_two, wcq).astype(BF16)
     mid_one, normed_two, hidden_two, cross_q, scale_two = tick(
-        [lane_encoder, lane_attention, lane_gu], (mid_one, normed_two, hidden_two, cross_q, scale_two)
+        [lane_encoder, lane_attention, lane_gu, lane_wd], (mid_one, normed_two, hidden_two, cross_q, scale_two)
     )
     tick([lane_encoder], ())
     encoder_whole = lane_encoder.take()
@@ -811,7 +809,7 @@
     grad_encoder = tick([lane_first, lane_second, lane_down, lane_keys], grad_encoder)
 
     partial_keys = weight_grad(encoder_rows, lane_encoder_rows.take()[0], keys_mine, lane_keys.take()[0])
-    partial_keys = tick([lane_second, lane_mid, lane_wide], partial_keys)
+    partial_keys = tick([lane_second, lane_mid], partial_keys)
     pairs_first, pairs_second = lane_first.take(), lane_second.take()
     mine = [joint([pairs_first[index], pairs_second[index]], axis=1) for index in range(2)]
     last_mine, last_away = grad_halves(mine[0], mine[1])

time: 593 us -> 609 us (1.027)
  starting transfers between devices: 97.2 us -> 108 us
  local copies, waits for them, and re-layouts: 56.4 us -> 64.3 us
    ppermute x105, starting transfers between devices: 97.2 us -> 108 us  [cross(): return lax.ppermute(value, axis, partners(lax.axis_size(axis), bit))]
    unnamed x230 -> x242, local copies, waits for them, and re-layouts: 17.2 us -> 19.8 us
  transfers between devices with their start and end apart: 105 -> 105, of which waited for: 43 -> 41; matrix products, arithmetic and copies ran while one was open for 28% -> 28% of each run, Pallas kernels for 14% -> 14%
where the time goes in v8:
time: 609 us
  waiting for transfers between devices  190 us (31%)
  starting transfers between devices  108 us (18%)
  Pallas kernels  99.2 us (16%)
  matrix products  75 us (12%)
  other arithmetic  64.5 us (11%)
  local copies, waits for them, and re-layouts  64.3 us (11%)
  between operations  7.7 us (1%)
    ppermute x105, waiting for transfers between devices, cross(): return lax.ppermute(value, axis, partners(lax.axis_size(axis), bit))  190 us
    ppermute x105, starting transfers between devices, cross(): return lax.ppermute(value, axis, partners(lax.axis_size(axis), bit))  108 us
    pallas_call x3, Pallas kernels, attend_back(): pl.pallas_call(functools.partial(backward_kernel, masked), grid_spec=pltp...  49 us
    pallas_call x2, Pallas kernels, attend(): pl.pallas_call(functools.partial(forward_kernel, masked), grid_spec=pltpu...  34.5 us
    dot_general x14, matrix products, nt(): lax.dot_general(left, right, (((1,), (1,)), ((), ())), preferred_element_...  28.6 us
    dot_general x14, matrix products, nn(): return jnp.dot(left, right, preferred_element_type=F32)  27.1 us
    unnamed x242, local copies, waits for them, and re-layouts  19.8 us
    dot_general x9, matrix products, tn(): lax.dot_general(left, right, (((0,), (0,)), ((), ())), preferred_element_...  17.9 us
  transfers between devices with their start and end apart: 105, of which 41 were waited for; matrix products, arithmetic and copies ran while one was open for 28% of the time, Pallas kernels for 14%

profile of v8, /device:TPU:0, one launch (start us, length us, event | category | flops | bytes accessed | tf_op | source)
XLA Modules:
  0.0 608.7 jit_solution(8344330513732943278)
XLA Ops:
  66.9 8.2 %collective-permute-done.17.refs_2_ = bf16[128,2048]{1,0:T(8,128)(2,1)S(1)} collective-permute-done((bf16[128,2048]{1,0:T(8,128)(2,1)}, bf16[128,2048]{1,0:T(8,128)(2,1)S(1)}, u32[]{:S(2)}, u32[]{:S(2)}) %collective-permute-start.17) | collective-permute-done | bytes 524320 | tf_op jit(solution)/shard_map/ppermute | solution.py:349
  75.7 10.1 %collective-permute-done.16 = bf16[256,1024]{1,0:T(8,128)(2,1)S(1)} collective-permute-done((bf16[256,1024]{1,0:T(8,128)(2,1)S(1)}, bf16[256,1024]{1,0:T(8,128)(2,1)S(1)}, u32[]{:S(2)}, u32[]{:S(2)}) %collective-permute-start.16) | collective-permute-done | bytes 524320 | tf_op jit(solution)/shard_map/ppermute | solution.py:349
  96.5 15.4 %collective-permute-done.23.refs_1_ = bf16[128,2816]{1,0:T(8,128)(2,1)} collective-permute-done((bf16[128,2816]{1,0:T(8,128)(2,1)}, bf16[128,2816]{1,0:T(8,128)(2,1)}, u32[]{:S(2)}, u32[]{:S(2)}) %collective-permute-start.23) | collective-permute-done | bytes 720928 | tf_op jit(solution)/shard_map/ppermute | solution.py:349
  130.1 18.1 %attend_self.1 = (bf16[256,1024]{1,0:T(8,128)(2,1)}, f32[4,2,64,512]{3,2,1,0:T(8,128)}, f32[4,2,8,512]{3,2,1,0:T(8,128)}) custom-call(s32[20]{0:T(128)} %pad_add_fusion.1.table, bf16[256,1024]{1,0:T(8,128)(2,1)} %get-tuple-element.255.refs_0_, bf16[2048,1024]{1,0:T(8,128)(2,1)} %constant_dynamic-update-slice_fusion.refs_1_.refs_2_, ...), custom_call_target="tpu_custom_call" | custom-call | flops 2147483648 | bytes 8388608 | tf_op jit(solution)/shard_map/attend_self/pallas_call | solution.py:248
  158.5 7.9 %collective-permute-done.33.refs_3_ = bf16[128,2816]{1,0:T(8,128)(2,1)} collective-permute-done((bf16[128,2816]{1,0:T(8,128)(2,1)}, bf16[128,2816]{1,0:T(8,128)(2,1)}, u32[]{:S(2)}, u32[]{:S(2)}) %collective-permute-start.33) | collective-permute-done | bytes 720928 | tf_op jit(solution)/shard_map/ppermute | solution.py:349
  166.4 10.7 %collective-permute-start.31 = (bf16[128,1024]{1,0:T(8,128)(2,1)S(1)}, bf16[128,1024]{1,0:T(8,128)(2,1)}, u32[]{:S(2)}, u32[]{:S(2)}) collective-permute-start(bf16[128,1024]{1,0:T(8,128)(2,1)S(1)} %pad_maximum_fusion.19), channel_id=1, source_target_pairs={{0,8},{8,0},{16,24},{24,16},{1,9},{9,1},{17,25},{25,17},{2,10},{10... | collective-permute-start | bytes 786440 | tf_op jit(solution)/shard_map/ppermute | solution.py:349
  182.9 5.2 place.6
  194.2 7.5 %collective-permute-done.39.refs_2_ = bf16[352,512]{1,0:T(8,128)(2,1)S(1)} collective-permute-done((bf16[352,512]{1,0:T(8,128)(2,1)}, bf16[352,512]{1,0:T(8,128)(2,1)S(1)}, u32[]{:S(2)}, u32[]{:S(2)}) %collective-permute-start.39) | collective-permute-done | bytes 360480 | tf_op jit(solution)/shard_map/ppermute | solution.py:349
  206.5 16.4 %attend_cross.1 = (bf16[256,1024]{1,0:T(8,128)(2,1)}, f32[4,2,64,512]{3,2,1,0:T(8,128)}, f32[4,2,8,512]{3,2,1,0:T(8,128)}) custom-call(s32[20]{0:T(128)} %pad_add_fusion.1.table, bf16[256,1024]{1,0:T(8,128)(2,1)} %pad_maximum_fusion.10.refs_0_, bf16[512,1024]{1,0:T(8,128)(2,1)} %constant_dynamic-update-slice_fusion.5.refs_1_.refs_2_, ...), custom_call_target="tpu_custom_call" | custom-call | flops 536870912 | bytes 2097152 | tf_op jit(solution)/shard_map/attend_cross/pallas_call | solution.py:248
  277.1 9.9 %collective-permute-done.51 = bf16[1,2,352,512]{3,2,1,0:T(8,128)(2,1)S(1)} collective-permute-done((bf16[1,2,352,512]{3,2,1,0:T(8,128)(2,1)S(1)}, bf16[1,2,352,512]{3,2,1,0:T(8,128)(2,1)S(1)}, u32[]{:S(2)}, u32[]{:S(2)}) %collective-permute-start.51) | collective-permute-done | bytes 720928 | tf_op jit(solution)/shard_map/ppermute | solution.py:349
  302.3 16.6 %attend_cross_back.1 = (bf16[256,1024]{1,0:T(8,128)(2,1)}, bf16[2,512,512]{2,1,0:T(8,128)(2,1)}) custom-call(s32[20]{0:T(128)} %pad_add_fusion.1.table, bf16[256,1024]{1,0:T(8,128)(2,1)} %pad_maximum_fusion.10.refs_0_, bf16[512,1024]{1,0:T(8,128)(2,1)} %constant_dynamic-update-slice_fusion.5.refs_1_.refs_2_, ...), custom_call_target="tpu_custom_call" | custom-call | flops 1342177280 | bytes 4194304 | tf_op jit(solution)/shard_map/attend_cross_back/pallas_call | solution.py:287
  320.3 9.9 %collective-permute-done.52 = bf16[1,352,512]{2,1,0:T(8,128)(2,1)} collective-permute-done((bf16[1,352,512]{2,1,0:T(8,128)(2,1)}, bf16[1,352,512]{2,1,0:T(8,128)(2,1)}, u32[]{:S(2)}, u32[]{:S(2)}) %collective-permute-start.52) | collective-permute-done | bytes 360480 | tf_op jit(solution)/shard_map/ppermute | solution.py:349
  359.9 16.0 %attend_self_back.2 = (bf16[256,512]{1,0:T(8,128)(2,1)}, bf16[2,2048,256]{2,1,0:T(8,128)(2,1)}, f32[2,4,512]{2,1,0:T(4,128)}) custom-call(s32[20]{0:T(128)} %pad_add_fusion.1.table, bf16[256,1024]{1,0:T(8,128)(2,1)} %get-tuple-element.255.refs_0_, bf16[2048,1024]{1,0:T(8,128)(2,1)} %constant_dynamic-update-slice_fusion.refs_1_.refs_2_, ...), custom_call_target="tpu_custom_call" | custom-call | flops 2684354560 | bytes 8388608 | tf_op jit(solution)/shard_map/attend_self_back/pallas_call | solution.py:287
  395.8 16.4 %attend_self_back.3 = (bf16[256,512]{1,0:T(8,128)(2,1)}, bf16[2,2048,256]{2,1,0:T(8,128)(2,1)}, f32[2,4,512]{2,1,0:T(4,128)}) custom-call(s32[20]{0:T(128)} %pad_add_fusion.1.table, bf16[256,1024]{1,0:T(8,128)(2,1)} %get-tuple-element.255.refs_0_, bf16[2048,1024]{1,0:T(8,128)(2,1)} %constant_dynamic-update-slice_fusion.refs_1_.refs_2_, ...), custom_call_target="tpu_custom_call" | custom-call | flops 2684354560 | bytes 8388608 | tf_op jit(solution)/shard_map/attend_self_back/pallas_call | solution.py:287
  438.4 10.7 %collective-permute-done.69 = bf16[2,2,256,256]{3,2,0,1:T(8,128)(2,1)} collective-permute-done((bf16[2,2,256,256]{3,2,0,1:T(8,128)(2,1)}, bf16[2,2,256,256]{3,2,0,1:T(8,128)(2,1)}, u32[]{:S(2)}, u32[]{:S(2)}) %collective-permute-start.69) | collective-permute-done | bytes 524320 | tf_op jit(solution)/shard_map/ppermute | solution.py:349
  464.7 8.5 %collective-permute-start.80 = (bf16[4,2,128,512]{3,2,1,0:T(8,128)(2,1)S(1)}, bf16[4,2,128,512]{3,2,1,0:T(8,128)(2,1)S(1)}, u32[]{:S(2)}, u32[]{:S(2)}) collective-permute-start(bf16[4,2,128,512]{3,2,1,0:T(8,128)(2,1)S(1)} %dynamic-slice_bitcast_fusion.2), channel_id=1, source_target_pairs={{0,2},{1,3},{2,0},{3,1},{4,6},{5,7},{6,4},{7,5},{8,10},{9,11},{10,... | collective-permute-start | bytes 3145736 | tf_op jit(solution)/shard_map/ppermute | solution.py:349
  479.4 11.6 %collective-permute-done.78 = bf16[2,1,256,256]{3,2,1,0:T(8,128)(2,1)S(1)} collective-permute-done((bf16[2,1,256,256]{3,2,1,0:T(8,128)(2,1)S(1)}, bf16[2,1,256,256]{3,2,1,0:T(8,128)(2,1)S(1)}, u32[]{:S(2)}, u32[]{:S(2)}) %collective-permute-start.78) | collective-permute-done | bytes 262176 | tf_op jit(solution)/shard_map/ppermute | solution.py:349
  491.0 5.8 collective-permute-done.80
  506.2 5.9 collective-permute-done.83
  514.8 5.3 collective-permute-start.88
  524.6 8.2 %collective-permute-done.88 = bf16[4,2,64,512]{3,2,0,1:T(8,128)(2,1)S(1)} collective-permute-done((bf16[4,2,64,512]{3,2,0,1:T(8,128)(2,1)S(1)}, bf16[4,2,64,512]{3,2,0,1:T(8,128)(2,1)S(1)}, u32[]{:S(2)}, u32[]{:S(2)}) %collective-permute-start.88) | collective-permute-done | bytes 524320 | tf_op jit(solution)/shard_map/ppermute | solution.py:349
  539.3 10.8 %collective-permute-done.91 = bf16[4,64,512]{2,1,0:T(8,128)(2,1)S(1)} collective-permute-done((bf16[4,64,512]{2,1,0:T(8,128)(2,1)S(1)}, bf16[4,64,512]{2,1,0:T(8,128)(2,1)S(1)}, u32[]{:S(2)}, u32[]{:S(2)}) %collective-permute-start.91) | collective-permute-done | bytes 262176 | tf_op jit(solution)/shard_map/ppermute | solution.py:349
  555.1 6.8 %collective-permute-done.94 = bf16[1,4,64,512]{3,2,0,1:T(8,128)(2,1)S(1)} collective-permute-done((bf16[1,4,64,512]{3,2,0,1:T(8,128)(2,1)S(1)}, bf16[1,4,64,512]{3,2,0,1:T(8,128)(2,1)S(1)}, u32[]{:S(2)}, u32[]{:S(2)}) %collective-permute-start.94) | collective-permute-done | bytes 262176 | tf_op jit(solution)/shard_map/ppermute | solution.py:349
  569.5 8.6 %collective-permute-done.96 = bf16[2,64,512]{2,1,0:T(8,128)(2,1)S(1)} collective-permute-done((bf16[2,64,512]{2,1,0:T(8,128)(2,1)S(1)}, bf16[2,64,512]{2,1,0:T(8,128)(2,1)S(1)}, u32[]{:S(2)}, u32[]{:S(2)}) %collective-permute-start.96) | collective-permute-done | bytes 131104 | tf_op jit(solution)/shard_map/ppermute | solution.py:349
  (706 shorter events, 350.4 us)
Async XLA Ops:
  91.7 25.8 %collective-permute-start.22 = (bf16[1024,2048]{1,0:T(8,128)(2,1)}, bf16[1024,2048]{1,0:T(8,128)(2,1)S(1)}, u32[]{:S(2)}, u32[]{:S(2)}) collective-permute-start(bf16[1024,2048]{1,0:T(8,128)(2,1)} %place.5), channel_id=1, source_target_pairs={{0,4},{4,0},{1,5},{5,1},{2,6},{6,2},{3,7},{7,3},{8,12},{12,8},{9,1... | collective-permute-start | bytes 12582920 | tf_op jit(solution)/shard_map/ppermute | solution.py:349
  118.9 29.3 %collective-permute-start.27 = (bf16[64,1024]{1,0:T(8,128)(2,1)S(1)}, bf16[64,1024]{1,0:T(8,128)(2,1)S(1)}, u32[]{:S(2)}, u32[]{:S(2)}) collective-permute-start(bf16[64,1024]{1,0:T(8,128)(2,1)S(1)} %bitcast.555), channel_id=1, source_target_pairs={{0,4},{4,0},{1,5},{5,1},{2,6},{6,2},{3,7},{7,3},{8,12},{12,8},{9,1... | collective-permute-start | bytes 393224 | tf_op jit(solution)/shard_map/ppermute | solution.py:349
  120.0 28.4 %collective-permute-start.28 = (bf16[128,2816]{1,0:T(8,128)(2,1)}, bf16[128,2816]{1,0:T(8,128)(2,1)S(1)}, u32[]{:S(2)}, u32[]{:S(2)}) collective-permute-start(bf16[128,2816]{1,0:T(8,128)(2,1)} %get-tuple-element.502), channel_id=1, source_target_pairs={{0,2},{1,3},{2,0},{3,1},{4,6},{5,7},{6,4},{7,5},{8,10},{9,11},{10,... | collective-permute-start | bytes 2162696 | tf_op jit(solution)/shard_map/ppermute | solution.py:349
  121.5 28.9 %collective-permute-start.29 = (bf16[128,2816]{1,0:T(8,128)(2,1)}, bf16[128,2816]{1,0:T(8,128)(2,1)}, u32[]{:S(2)}, u32[]{:S(2)}) collective-permute-start(bf16[128,2816]{1,0:T(8,128)(2,1)} %get-tuple-element.501), channel_id=1, source_target_pairs={{0,1},{1,0},{2,3},{3,2},{4,5},{5,4},{6,7},{7,6},{8,9},{9,8},{10,11... | collective-permute-start | bytes 2162696 | tf_op jit(solution)/shard_map/ppermute | solution.py:349
  122.6 25.7 %collective-permute-start.30 = (bf16[256,1024]{1,0:T(8,128)(2,1)S(1)}, bf16[256,1024]{1,0:T(8,128)(2,1)}, u32[]{:S(2)}, u32[]{:S(2)}) collective-permute-start(bf16[256,1024]{1,0:T(8,128)(2,1)S(1)} %copy-done.32), channel_id=1, source_target_pairs={{0,4},{4,0},{1,5},{5,1},{2,6},{6,2},{3,7},{7,3},{8,12},{12,8},{9,1... | collective-permute-start | bytes 1572872 | tf_op jit(solution)/shard_map/ppermute | solution.py:349
  126.3 26.1 %collective-permute-start.26 = (bf16[64,1024]{1,0:T(8,128)(2,1)S(1)}, bf16[64,1024]{1,0:T(8,128)(2,1)S(1)}, u32[]{:S(2)}, u32[]{:S(2)}) collective-permute-start(bf16[64,1024]{1,0:T(8,128)(2,1)S(1)} %pad_maximum_fusion.23), channel_id=1, source_target_pairs={{0,16},{8,24},{16,0},{24,8},{1,17},{9,25},{17,1},{25,9},{2,18},{10... | collective-permute-start | bytes 393224 | tf_op jit(solution)/shard_map/ppermute | solution.py:349
  148.3 31.4 %collective-permute-start.34 = (bf16[128,2816]{1,0:T(8,128)(2,1)}, bf16[128,2816]{1,0:T(8,128)(2,1)}, u32[]{:S(2)}, u32[]{:S(2)}) collective-permute-start(bf16[128,2816]{1,0:T(8,128)(2,1)} %collective-permute-done.24.refs_4_), channel_id=1, source_target_pairs={{0,1},{1,0},{2,3},{3,2},{4,5},{5,4},{6,7},{7,6},{8,9},{9,8},{10,11... | collective-permute-start | bytes 2162696 | tf_op jit(solution)/shard_map/ppermute | solution.py:349
  148.4 31.3 %collective-permute-start.35 = (bf16[352,512]{1,0:T(8,128)(2,1)}, bf16[352,512]{1,0:T(8,128)(2,1)}, u32[]{:S(2)}, u32[]{:S(2)}) collective-permute-start(bf16[352,512]{1,0:T(8,128)(2,1)} %get-tuple-element.529), channel_id=1, source_target_pairs={{0,1},{1,0},{2,3},{3,2},{4,5},{5,4},{6,7},{7,6},{8,9},{9,8},{10,11... | collective-permute-start | bytes 1081352 | tf_op jit(solution)/shard_map/ppermute | solution.py:349
  150.4 29.3 %collective-permute-start.36 = (bf16[352,512]{1,0:T(8,128)(2,1)}, bf16[352,512]{1,0:T(8,128)(2,1)}, u32[]{:S(2)}, u32[]{:S(2)}) collective-permute-start(bf16[352,512]{1,0:T(8,128)(2,1)} %get-tuple-element.528), channel_id=1, source_target_pairs={{0,2},{1,3},{2,0},{3,1},{4,6},{5,7},{6,4},{7,5},{8,10},{9,11},{10,... | collective-permute-start | bytes 1081352 | tf_op jit(solution)/shard_map/ppermute | solution.py:349
  154.2 28.7 %collective-permute-start.32 = (bf16[256,1024]{1,0:T(8,128)(2,1)}, bf16[256,1024]{1,0:T(8,128)(2,1)}, u32[]{:S(2)}, u32[]{:S(2)}) collective-permute-start(bf16[256,1024]{1,0:T(8,128)(2,1)} %get-tuple-element.278), channel_id=1, source_target_pairs={{0,4},{4,0},{1,5},{5,1},{2,6},{6,2},{3,7},{7,3},{8,12},{12,8},{9,1... | collective-permute-start | bytes 1572872 | tf_op jit(solution)/shard_map/ppermute | solution.py:349
  188.1 34.9 %collective-permute-start.38 = (bf16[1024,2816]{1,0:T(8,128)(2,1)}, bf16[1024,2816]{1,0:T(8,128)(2,1)}, u32[]{:S(2)}, u32[]{:S(2)}) collective-permute-start(bf16[1024,2816]{1,0:T(8,128)(2,1)} %place.6), channel_id=1, source_target_pairs={{0,4},{4,0},{1,5},{5,1},{2,6},{6,2},{3,7},{7,3},{8,12},{12,8},{9,1... | collective-permute-start | bytes 17301512 | tf_op jit(solution)/shard_map/ppermute | solution.py:349
  192.7 30.3 %collective-permute-start.43 = (bf16[256,1024]{1,0:T(8,128)(2,1)}, bf16[256,1024]{1,0:T(8,128)(2,1)}, u32[]{:S(2)}, u32[]{:S(2)}) collective-permute-start(bf16[256,1024]{1,0:T(8,128)(2,1)} %copy-done.50), channel_id=1, source_target_pairs={{0,4},{4,0},{1,5},{5,1},{2,6},{6,2},{3,7},{7,3},{8,12},{12,8},{9,1... | collective-permute-start | bytes 1572872 | tf_op jit(solution)/shard_map/ppermute | solution.py:349
  192.7 30.3 %collective-permute-start.41 = (bf16[352,512]{1,0:T(8,128)(2,1)}, bf16[352,512]{1,0:T(8,128)(2,1)}, u32[]{:S(2)}, u32[]{:S(2)}) collective-permute-start(bf16[352,512]{1,0:T(8,128)(2,1)} %get-tuple-element.528), channel_id=1, source_target_pairs={{0,1},{1,0},{2,3},{3,2},{4,5},{5,4},{6,7},{7,6},{8,9},{9,8},{10,11... | collective-permute-start | bytes 1081352 | tf_op jit(solution)/shard_map/ppermute | solution.py:349
  289.3 40.8 %collective-permute-start.55 = (bf16[1,2,128,2816]{3,2,1,0:T(8,128)(2,1)}, bf16[1,2,128,2816]{3,2,1,0:T(8,128)(2,1)}, u32[]{:S(2)}, u32[]{:S(2)}) collective-permute-start(bf16[1,2,128,2816]{3,2,1,0:T(8,128)(2,1)} %dynamic-slice_bitcast_fusion), channel_id=1, source_target_pairs={{0,2},{1,3},{2,0},{3,1},{4,6},{5,7},{6,4},{7,5},{8,10},{9,11},{10,... | collective-permute-start | bytes 4325384 | tf_op jit(solution)/shard_map/ppermute | solution.py:349
  291.7 28.6 %collective-permute-start.53 = (bf16[1,352,512]{2,1,0:T(8,128)(2,1)}, bf16[1,352,512]{2,1,0:T(8,128)(2,1)}, u32[]{:S(2)}, u32[]{:S(2)}) collective-permute-start(bf16[1,352,512]{2,1,0:T(8,128)(2,1)} %dynamic-slice_bitcast_fusion.12), channel_id=1, source_target_pairs={{0,1},{1,0},{2,3},{3,2},{4,5},{5,4},{6,7},{7,6},{8,9},{9,8},{10,11... | collective-permute-start | bytes 1081352 | tf_op jit(solution)/shard_map/ppermute | solution.py:349
  294.1 38.1 %collective-permute-start.54 = (bf16[1,2,128,2816]{3,2,1,0:T(8,128)(2,1)}, bf16[1,2,128,2816]{3,2,1,0:T(8,128)(2,1)}, u32[]{:S(2)}, u32[]{:S(2)}) collective-permute-start(bf16[1,2,128,2816]{3,2,1,0:T(8,128)(2,1)} %dynamic-slice_bitcast_fusion.1), channel_id=1, source_target_pairs={{0,1},{1,0},{2,3},{3,2},{4,5},{5,4},{6,7},{7,6},{8,9},{9,8},{10,11... | collective-permute-start | bytes 4325384 | tf_op jit(solution)/shard_map/ppermute | solution.py:349
  296.0 34.1 %collective-permute-start.52 = (bf16[1,352,512]{2,1,0:T(8,128)(2,1)}, bf16[1,352,512]{2,1,0:T(8,128)(2,1)}, u32[]{:S(2)}, u32[]{:S(2)}) collective-permute-start(bf16[1,352,512]{2,1,0:T(8,128)(2,1)} %dynamic-slice_bitcast_fusion.13), channel_id=1, source_target_pairs={{0,2},{1,3},{2,0},{3,1},{4,6},{5,7},{6,4},{7,5},{8,10},{9,11},{10,... | collective-permute-start | bytes 1081352 | tf_op jit(solution)/shard_map/ppermute | solution.py:349
  354.2 26.8 %collective-permute-start.63 = (bf16[2,2,64,512]{3,2,1,0:T(8,128)(2,1)}, bf16[2,2,64,512]{3,2,1,0:T(8,128)(2,1)}, u32[]{:S(2)}, u32[]{:S(2)}) collective-permute-start(bf16[2,2,64,512]{3,2,1,0:T(8,128)(2,1)} %slice_bitcast_fusion.11), channel_id=1, source_target_pairs={{0,8},{8,0},{16,24},{24,16},{1,9},{9,1},{17,25},{25,17},{2,10},{10... | collective-permute-start | bytes 786440 | tf_op jit(solution)/shard_map/ppermute | solution.py:349
  382.9 33.0 %collective-permute-start.67 = (bf16[2,1,64,512]{3,2,0,1:T(8,128)(2,1)}, bf16[2,1,64,512]{3,2,0,1:T(8,128)(2,1)S(1)}, u32[]{:S(2)}, u32[]{:S(2)}) collective-permute-start(bf16[2,1,64,512]{3,2,0,1:T(8,128)(2,1)} %slice_bitcast_fusion.17), channel_id=1, source_target_pairs={{0,16},{8,24},{16,0},{24,8},{1,17},{9,25},{17,1},{25,9},{2,18},{10... | collective-permute-start | bytes 393224 | tf_op jit(solution)/shard_map/ppermute | solution.py:349
  388.0 27.9 %collective-permute-start.66 = (bf16[1,64,2816]{2,1,0:T(8,128)(2,1)}, bf16[1,64,2816]{2,1,0:T(8,128)(2,1)}, u32[]{:S(2)}, u32[]{:S(2)}) collective-permute-start(bf16[1,64,2816]{2,1,0:T(8,128)(2,1)} %dynamic-slice_bitcast_fusion.11), channel_id=1, source_target_pairs={{0,16},{8,24},{16,0},{24,8},{1,17},{9,25},{17,1},{25,9},{2,18},{10... | collective-permute-start | bytes 1081352 | tf_op jit(solution)/shard_map/ppermute | solution.py:349
  389.1 26.8 %collective-permute-start.68 = (bf16[2,4,256,256]{3,2,1,0:T(8,128)(2,1)}, bf16[2,4,256,256]{3,2,1,0:T(8,128)(2,1)S(1)}, u32[]{:S(2)}, u32[]{:S(2)}) collective-permute-start(bf16[2,4,256,256]{3,2,1,0:T(8,128)(2,1)} %slice_bitcast_fusion.3), channel_id=1, source_target_pairs={{0,4},{4,0},{1,5},{5,1},{2,6},{6,2},{3,7},{7,3},{8,12},{12,8},{9,1... | collective-permute-start | bytes 3145736 | tf_op jit(solution)/shard_map/ppermute | solution.py:349
  422.9 26.2 %collective-permute-start.69 = (bf16[2,2,256,256]{3,2,0,1:T(8,128)(2,1)}, bf16[2,2,256,256]{3,2,0,1:T(8,128)(2,1)}, u32[]{:S(2)}, u32[]{:S(2)}) collective-permute-start(bf16[2,2,256,256]{3,2,0,1:T(8,128)(2,1)} %bitcast.509), channel_id=1, source_target_pairs={{0,8},{8,0},{16,24},{24,16},{1,9},{9,1},{17,25},{25,17},{2,10},{10... | collective-permute-start | bytes 1572872 | tf_op jit(solution)/shard_map/ppermute | solution.py:349
  456.8 49.4 %collective-permute-start.84 = (bf16[2,1,64,2816]{3,2,0,1:T(8,128)(2,1)S(1)}, bf16[2,1,64,2816]{3,2,0,1:T(8,128)(2,1)S(1)}, u32[]{:S(2)}, u32[]{:S(2)}) collective-permute-start(bf16[2,1,64,2816]{3,2,0,1:T(8,128)(2,1)S(1)} %pad_maximum_fusion.9), channel_id=1, source_target_pairs={{0,8},{8,0},{16,24},{24,16},{1,9},{9,1},{17,25},{25,17},{2,10},{10... | collective-permute-start | bytes 2162696 | tf_op jit(solution)/shard_map/ppermute | solution.py:349
  464.7 32.1 %collective-permute-start.80 = (bf16[4,2,128,512]{3,2,1,0:T(8,128)(2,1)S(1)}, bf16[4,2,128,512]{3,2,1,0:T(8,128)(2,1)S(1)}, u32[]{:S(2)}, u32[]{:S(2)}) collective-permute-start(bf16[4,2,128,512]{3,2,1,0:T(8,128)(2,1)S(1)} %dynamic-slice_bitcast_fusion.2), channel_id=1, source_target_pairs={{0,2},{1,3},{2,0},{3,1},{4,6},{5,7},{6,4},{7,5},{8,10},{9,11},{10,... | collective-permute-start | bytes 3145736 | tf_op jit(solution)/shard_map/ppermute | solution.py:349
  (190 other events, 2075.5 us)

commit v9 on v7

--- a/solution.py
+++ b/solution.py
@@ -636,12 +636,16 @@
     query, pairs, late = tick(
         [lane_mid, lane_count], (query, pairs, (w_gate, w_up, w_down, doc_ids, block_order, buckets, table_whole))
     )
-    gate_part, up_part, down_part, doc_ids, block_order, buckets, table_whole = late
+    gate_part, up_part, down_part, *late = late
 
     lane_keys = Lane(gather_context_steps(pairs))
     gu_shard = half_columns([joint([gate_part, up_part], axis=1)])
     wd_shard = half_columns([down_part])
 
+    gu_shard, wd_shard, late = tick([lane_keys, lane_mid], (gu_shard, wd_shard, late))
+    doc_ids, block_order, buckets, table_whole = late
+
+    lane_gu = Lane(gather_steps(gu_shard, True))
     query_blocks = lax.dynamic_slice_in_dim(block_order, context * pair, pair)
     slots = jnp.arange(contexts * pair, dtype=jnp.int32)
     owner = slots // pair
@@ -659,13 +663,10 @@
     bucket_match = (jnp.take(buckets, index_of)[None, :] == jnp.arange(BUCKETS, dtype=jnp.int32)[:, None])
 
     vectors = tn(table_whole, bucket_match.astype(BF16)).reshape(HEADS // 4, 4, SPAN)
-    gu_shard, wd_shard, low, high, place_table, bucket_match, vectors = tick(
-        [lane_keys, lane_mid], (gu_shard, wd_shard, low, high, place_table, bucket_match, vectors)
+    low, high, place_table, bucket_match, vectors = tick(
+        [lane_keys, lane_mid, lane_gu], (low, high, place_table, bucket_match, vectors)
     )
     extra = (vectors, low, high)
-
-    lane_gu = Lane(gather_steps(gu_shard, True))
-    tick([lane_keys, lane_mid, lane_gu], ())
     mid_mine, mid_other = lane_mid.take()
     wo, wcq, wckv, wco = [
         (mid_mine[:, index * halves : (index + 1) * halves], mid_other[:, index * halves : (index + 1) * halves])
@@ -811,7 +812,7 @@
     grad_encoder = tick([lane_first, lane_second, lane_down, lane_keys], grad_encoder)
 
     partial_keys = weight_grad(encoder_rows, lane_encoder_rows.take()[0], keys_mine, lane_keys.take()[0])
-    partial_keys = tick([lane_second, lane_mid, lane_wide], partial_keys)
+    partial_keys = tick([lane_second, lane_mid], partial_keys)
     pairs_first, pairs_second = lane_first.take(), lane_second.take()
     mine = [joint([pairs_first[index], pairs_second[index]], axis=1) for index in range(2)]
     last_mine, last_away = grad_halves(mine[0], mine[1])

time: 593 us -> 594 us (level)
  starting transfers between devices: 97.2 us -> 120 us
  waiting for transfers between devices: 189 us -> 174 us
  Pallas kernels: 99.2 us -> 86.5 us
    ppermute x105, starting transfers between devices: 97.2 us -> 120 us  [cross(): return lax.ppermute(value, axis, partners(lax.axis_size(axis), bit))]
    ppermute x105, waiting for transfers between devices: 189 us -> 174 us  [cross(): return lax.ppermute(value, axis, partners(lax.axis_size(axis), bit))]
    pallas_call x3, Pallas kernels: 49.1 us -> 42.4 us  [attend_back(): pl.pallas_call(functools.partial(backward_kernel, masked), grid_spec=pltp...]
    pallas_call x2, Pallas kernels: 34.5 us -> 28.3 us  [attend(): pl.pallas_call(functools.partial(forward_kernel, masked), grid_spec=pltpu...]
    unnamed x230 -> x226, local copies, waits for them, and re-layouts: 17.2 us -> 17.8 us
  transfers between devices with their start and end apart: 105 -> 105, of which waited for: 43 -> 44; matrix products, arithmetic and copies ran while one was open for 28% -> 29% of each run, Pallas kernels for 14% -> 12%
where the time goes in v9:
time: 594 us; the launch traced here: 592 us
  waiting for transfers between devices  174 us (29%)
  starting transfers between devices  120 us (20%)
  Pallas kernels  86.5 us (15%)
  matrix products  79.7 us (13%)
  other arithmetic  65.7 us (11%)
  local copies, waits for them, and re-layouts  58.1 us (10%)
  between operations  7.67 us (1%)
    ppermute x105, waiting for transfers between devices, cross(): return lax.ppermute(value, axis, partners(lax.axis_size(axis), bit))  174 us
    ppermute x105, starting transfers between devices, cross(): return lax.ppermute(value, axis, partners(lax.axis_size(axis), bit))  120 us
    pallas_call x3, Pallas kernels, attend_back(): pl.pallas_call(functools.partial(backward_kernel, masked), grid_spec=pltp...  42.4 us
    dot_general x14, matrix products, nt(): lax.dot_general(left, right, (((1,), (1,)), ((), ())), preferred_element_...  31 us
    dot_general x14, matrix products, nn(): return jnp.dot(left, right, preferred_element_type=F32)  30 us
    pallas_call x2, Pallas kernels, attend(): pl.pallas_call(functools.partial(forward_kernel, masked), grid_spec=pltpu...  28.3 us
    unnamed x226, local copies, waits for them, and re-layouts  17.8 us
    dot_general x9, matrix products, tn(): lax.dot_general(left, right, (((0,), (0,)), ((), ())), preferred_element_...  17.3 us
  transfers between devices with their start and end apart: 105, of which 44 were waited for; matrix products, arithmetic and copies ran while one was open for 29% of the time, Pallas kernels for 12%

profile of v9, /device:TPU:0, one launch (start us, length us, event | category | flops | bytes accessed | tf_op | source)
XLA Modules:
  0.0 592.1 jit_solution(18313852209899134040)
XLA Ops:
  57.0 5.2 collective-permute-done.17.refs_2_
  64.0 11.2 %collective-permute-done.16 = bf16[256,1024]{1,0:T(8,128)(2,1)} collective-permute-done((bf16[256,1024]{1,0:T(8,128)(2,1)S(1)}, bf16[256,1024]{1,0:T(8,128)(2,1)}, u32[]{:S(2)}, u32[]{:S(2)}) %collective-permute-start.16) | collective-permute-done | bytes 524320 | tf_op jit(solution)/shard_map/ppermute | solution.py:349
  94.0 10.8 %collective-permute-done.23.refs_1_ = bf16[128,2816]{1,0:T(8,128)(2,1)} collective-permute-done((bf16[128,2816]{1,0:T(8,128)(2,1)}, bf16[128,2816]{1,0:T(8,128)(2,1)}, u32[]{:S(2)}, u32[]{:S(2)}) %collective-permute-start.23) | collective-permute-done | bytes 720928 | tf_op jit(solution)/shard_map/ppermute | solution.py:349
  105.1 5.3 collective-permute-done.21
  130.8 11.9 %attend_self.1 = (bf16[256,1024]{1,0:T(8,128)(2,1)}, f32[4,2,64,512]{3,2,1,0:T(8,128)}, f32[4,2,8,512]{3,2,1,0:T(8,128)}) custom-call(s32[20]{0:T(128)} %pad_add_fusion.1.table, bf16[256,1024]{1,0:T(8,128)(2,1)} %get-tuple-element.275.refs_0_, bf16[2048,1024]{1,0:T(8,128)(2,1)} %constant_dynamic-update-slice_fusion.refs_1_.refs_2_, ...), custom_call_target="tpu_custom_call" | custom-call | flops 2147483648 | bytes 8388608 | tf_op jit(solution)/shard_map/attend_self/pallas_call | solution.py:248
  144.9 12.0 %collective-permute-start.36 = (bf16[128,2816]{1,0:T(8,128)(2,1)}, bf16[128,2816]{1,0:T(8,128)(2,1)}, u32[]{:S(2)}, u32[]{:S(2)}) collective-permute-start(bf16[128,2816]{1,0:T(8,128)(2,1)} %collective-permute-done.24.refs_4_), channel_id=1, source_target_pairs={{0,1},{1,0},{2,3},{3,2},{4,5},{5,4},{6,7},{7,6},{8,9},{9,8},{10,11... | collective-permute-start | bytes 2162696 | tf_op jit(solution)/shard_map/ppermute | solution.py:349
  168.4 5.2 place.6
  180.7 6.5 %collective-permute-done.39.refs_2_ = bf16[352,512]{1,0:T(8,128)(2,1)S(1)} collective-permute-done((bf16[352,512]{1,0:T(8,128)(2,1)}, bf16[352,512]{1,0:T(8,128)(2,1)S(1)}, u32[]{:S(2)}, u32[]{:S(2)}) %collective-permute-start.39) | collective-permute-done | bytes 360480 | tf_op jit(solution)/shard_map/ppermute | solution.py:349
  193.0 16.4 %attend_cross.1 = (bf16[256,1024]{1,0:T(8,128)(2,1)}, f32[4,2,64,512]{3,2,1,0:T(8,128)}, f32[4,2,8,512]{3,2,1,0:T(8,128)}) custom-call(s32[20]{0:T(128)} %pad_add_fusion.1.table, bf16[256,1024]{1,0:T(8,128)(2,1)} %pad_maximum_fusion.10.refs_0_, bf16[512,1024]{1,0:T(8,128)(2,1)} %constant_dynamic-update-slice_fusion.5.refs_1_.refs_2_, ...), custom_call_target="tpu_custom_call" | custom-call | flops 536870912 | bytes 2097152 | tf_op jit(solution)/shard_map/attend_cross/pallas_call | solution.py:248
  220.6 4.7 fusion.334
  240.0 4.7 multiply_convert_fusion
  257.2 4.8 convolution_convert_fusion
  262.0 10.7 %collective-permute-done.51 = bf16[1,2,352,512]{3,2,1,0:T(8,128)(2,1)S(1)} collective-permute-done((bf16[1,2,352,512]{3,2,1,0:T(8,128)(2,1)S(1)}, bf16[1,2,352,512]{3,2,1,0:T(8,128)(2,1)S(1)}, u32[]{:S(2)}, u32[]{:S(2)}) %collective-permute-start.51) | collective-permute-done | bytes 720928 | tf_op jit(solution)/shard_map/ppermute | solution.py:349
  287.9 16.6 %attend_cross_back.1 = (bf16[256,1024]{1,0:T(8,128)(2,1)}, bf16[2,512,512]{2,1,0:T(8,128)(2,1)}) custom-call(s32[20]{0:T(128)} %pad_add_fusion.1.table, bf16[256,1024]{1,0:T(8,128)(2,1)} %pad_maximum_fusion.10.refs_0_, bf16[512,1024]{1,0:T(8,128)(2,1)} %constant_dynamic-update-slice_fusion.5.refs_1_.refs_2_, ...), custom_call_target="tpu_custom_call" | custom-call | flops 1342177280 | bytes 4194304 | tf_op jit(solution)/shard_map/attend_cross_back/pallas_call | solution.py:287
  305.9 9.9 %collective-permute-done.52 = bf16[1,352,512]{2,1,0:T(8,128)(2,1)} collective-permute-done((bf16[1,352,512]{2,1,0:T(8,128)(2,1)}, bf16[1,352,512]{2,1,0:T(8,128)(2,1)}, u32[]{:S(2)}, u32[]{:S(2)}) %collective-permute-start.52) | collective-permute-done | bytes 360480 | tf_op jit(solution)/shard_map/ppermute | solution.py:349
  345.8 12.7 %attend_self_back.2 = (bf16[256,512]{1,0:T(8,128)(2,1)}, bf16[2,2048,256]{2,1,0:T(8,128)(2,1)}, f32[2,4,512]{2,1,0:T(4,128)}) custom-call(s32[20]{0:T(128)} %pad_add_fusion.1.table, bf16[256,1024]{1,0:T(8,128)(2,1)} %get-tuple-element.275.refs_0_, bf16[2048,1024]{1,0:T(8,128)(2,1)} %constant_dynamic-update-slice_fusion.refs_1_.refs_2_, ...), custom_call_target="tpu_custom_call" | custom-call | flops 2684354560 | bytes 8388608 | tf_op jit(solution)/shard_map/attend_self_back/pallas_call | solution.py:287
  379.9 13.1 %attend_self_back.3 = (bf16[256,512]{1,0:T(8,128)(2,1)}, bf16[2,2048,256]{2,1,0:T(8,128)(2,1)}, f32[2,4,512]{2,1,0:T(4,128)}) custom-call(s32[20]{0:T(128)} %pad_add_fusion.1.table, bf16[256,1024]{1,0:T(8,128)(2,1)} %get-tuple-element.275.refs_0_, bf16[2048,1024]{1,0:T(8,128)(2,1)} %constant_dynamic-update-slice_fusion.refs_1_.refs_2_, ...), custom_call_target="tpu_custom_call" | custom-call | flops 2684354560 | bytes 8388608 | tf_op jit(solution)/shard_map/attend_self_back/pallas_call | solution.py:287
  423.3 10.1 %collective-permute-done.69 = bf16[2,2,256,256]{3,2,0,1:T(8,128)(2,1)} collective-permute-done((bf16[2,2,256,256]{3,2,0,1:T(8,128)(2,1)}, bf16[2,2,256,256]{3,2,0,1:T(8,128)(2,1)}, u32[]{:S(2)}, u32[]{:S(2)}) %collective-permute-start.69) | collective-permute-done | bytes 524320 | tf_op jit(solution)/shard_map/ppermute | solution.py:349
  466.1 9.2 %collective-permute-done.78 = bf16[2,1,256,256]{3,2,1,0:T(8,128)(2,1)S(1)} collective-permute-done((bf16[2,1,256,256]{3,2,1,0:T(8,128)(2,1)S(1)}, bf16[2,1,256,256]{3,2,1,0:T(8,128)(2,1)S(1)}, u32[]{:S(2)}, u32[]{:S(2)}) %collective-permute-start.78) | collective-permute-done | bytes 262176 | tf_op jit(solution)/shard_map/ppermute | solution.py:349
  475.4 6.2 %collective-permute-done.79 = bf16[4,2,128,512]{3,2,1,0:T(8,128)(2,1)S(1)} collective-permute-done((bf16[4,2,128,512]{3,2,1,0:T(8,128)(2,1)S(1)}, bf16[4,2,128,512]{3,2,1,0:T(8,128)(2,1)S(1)}, u32[]{:S(2)}, u32[]{:S(2)}) %collective-permute-start.79) | collective-permute-done | bytes 1048608 | tf_op jit(solution)/shard_map/ppermute | solution.py:349
  505.9 10.1 %collective-permute-done.88 = bf16[4,2,64,512]{3,2,0,1:T(8,128)(2,1)S(1)} collective-permute-done((bf16[4,2,64,512]{3,2,0,1:T(8,128)(2,1)S(1)}, bf16[4,2,64,512]{3,2,0,1:T(8,128)(2,1)S(1)}, u32[]{:S(2)}, u32[]{:S(2)}) %collective-permute-start.88) | collective-permute-done | bytes 524320 | tf_op jit(solution)/shard_map/ppermute | solution.py:349
  522.3 9.5 %collective-permute-done.91 = bf16[4,64,512]{2,1,0:T(8,128)(2,1)S(1)} collective-permute-done((bf16[4,64,512]{2,1,0:T(8,128)(2,1)S(1)}, bf16[4,64,512]{2,1,0:T(8,128)(2,1)S(1)}, u32[]{:S(2)}, u32[]{:S(2)}) %collective-permute-start.91) | collective-permute-done | bytes 262176 | tf_op jit(solution)/shard_map/ppermute | solution.py:349
  539.5 7.2 %collective-permute-done.94 = bf16[1,4,64,512]{3,2,0,1:T(8,128)(2,1)S(1)} collective-permute-done((bf16[1,4,64,512]{3,2,0,1:T(8,128)(2,1)S(1)}, bf16[1,4,64,512]{3,2,0,1:T(8,128)(2,1)S(1)}, u32[]{:S(2)}, u32[]{:S(2)}) %collective-permute-start.94) | collective-permute-done | bytes 262176 | tf_op jit(solution)/shard_map/ppermute | solution.py:349
  553.6 7.1 %collective-permute-done.96 = bf16[2,64,512]{2,1,0:T(8,128)(2,1)S(1)} collective-permute-done((bf16[2,64,512]{2,1,0:T(8,128)(2,1)S(1)}, bf16[2,64,512]{2,1,0:T(8,128)(2,1)S(1)}, u32[]{:S(2)}, u32[]{:S(2)}) %collective-permute-start.96) | collective-permute-done | bytes 131104 | tf_op jit(solution)/shard_map/ppermute | solution.py:349
  (690 shorter events, 363.4 us)
Async XLA Ops:
  50.4 24.8 %collective-permute-start.16 = (bf16[256,1024]{1,0:T(8,128)(2,1)S(1)}, bf16[256,1024]{1,0:T(8,128)(2,1)}, u32[]{:S(2)}, u32[]{:S(2)}) collective-permute-start(bf16[256,1024]{1,0:T(8,128)(2,1)S(1)} %get-tuple-element.261), channel_id=1, source_target_pairs={{0,16},{8,24},{16,0},{24,8},{1,17},{9,25},{17,1},{25,9},{2,18},{10... | collective-permute-start | bytes 1572872 | tf_op jit(solution)/shard_map/ppermute | solution.py:349
  79.5 30.9 %collective-permute-start.22 = (bf16[1024,2048]{1,0:T(8,128)(2,1)}, bf16[1024,2048]{1,0:T(8,128)(2,1)}, u32[]{:S(2)}, u32[]{:S(2)}) collective-permute-start(bf16[1024,2048]{1,0:T(8,128)(2,1)} %place.5), channel_id=1, source_target_pairs={{0,4},{4,0},{1,5},{5,1},{2,6},{6,2},{3,7},{7,3},{8,12},{12,8},{9,1... | collective-permute-start | bytes 12582920 | tf_op jit(solution)/shard_map/ppermute | solution.py:349
  84.5 25.9 %collective-permute-start.21 = (bf16[512,1024]{1,0:T(8,128)(2,1)}, bf16[512,1024]{1,0:T(8,128)(2,1)}, u32[]{:S(2)}, u32[]{:S(2)}) collective-permute-start(bf16[512,1024]{1,0:T(8,128)(2,1)} %pad_maximum_fusion.6), channel_id=1, source_target_pairs={{0,8},{8,0},{16,24},{24,16},{1,9},{9,1},{17,25},{25,17},{2,10},{10... | collective-permute-start | bytes 3145736 | tf_op jit(solution)/shard_map/ppermute | solution.py:349
  115.0 27.7 %collective-permute-start.28 = (bf16[128,2816]{1,0:T(8,128)(2,1)}, bf16[128,2816]{1,0:T(8,128)(2,1)S(1)}, u32[]{:S(2)}, u32[]{:S(2)}) collective-permute-start(bf16[128,2816]{1,0:T(8,128)(2,1)} %get-tuple-element.512), channel_id=1, source_target_pairs={{0,2},{1,3},{2,0},{3,1},{4,6},{5,7},{6,4},{7,5},{8,10},{9,11},{10,... | collective-permute-start | bytes 2162696 | tf_op jit(solution)/shard_map/ppermute | solution.py:349
  115.6 29.3 %collective-permute-start.29 = (bf16[128,2816]{1,0:T(8,128)(2,1)}, bf16[128,2816]{1,0:T(8,128)(2,1)}, u32[]{:S(2)}, u32[]{:S(2)}) collective-permute-start(bf16[128,2816]{1,0:T(8,128)(2,1)} %get-tuple-element.511), channel_id=1, source_target_pairs={{0,1},{1,0},{2,3},{3,2},{4,5},{5,4},{6,7},{7,6},{8,9},{9,8},{10,11... | collective-permute-start | bytes 2162696 | tf_op jit(solution)/shard_map/ppermute | solution.py:349
  124.6 32.3 %collective-permute-start.30 = (bf16[352,512]{1,0:T(8,128)(2,1)}, bf16[352,512]{1,0:T(8,128)(2,1)S(1)}, u32[]{:S(2)}, u32[]{:S(2)}) collective-permute-start(bf16[352,512]{1,0:T(8,128)(2,1)} %get-tuple-element.539), channel_id=1, source_target_pairs={{0,1},{1,0},{2,3},{3,2},{4,5},{5,4},{6,7},{7,6},{8,9},{9,8},{10,11... | collective-permute-start | bytes 1081352 | tf_op jit(solution)/shard_map/ppermute | solution.py:349
  125.5 31.5 %collective-permute-start.31 = (bf16[352,512]{1,0:T(8,128)(2,1)}, bf16[352,512]{1,0:T(8,128)(2,1)S(1)}, u32[]{:S(2)}, u32[]{:S(2)}) collective-permute-start(bf16[352,512]{1,0:T(8,128)(2,1)} %get-tuple-element.538), channel_id=1, source_target_pairs={{0,2},{1,3},{2,0},{3,1},{4,6},{5,7},{6,4},{7,5},{8,10},{9,11},{10,... | collective-permute-start | bytes 1081352 | tf_op jit(solution)/shard_map/ppermute | solution.py:349
  128.5 28.5 %collective-permute-start.26 = (bf16[64,1024]{1,0:T(8,128)(2,1)S(1)}, bf16[64,1024]{1,0:T(8,128)(2,1)S(1)}, u32[]{:S(2)}, u32[]{:S(2)}) collective-permute-start(bf16[64,1024]{1,0:T(8,128)(2,1)S(1)} %pad_maximum_fusion.23), channel_id=1, source_target_pairs={{0,16},{8,24},{16,0},{24,8},{1,17},{9,25},{17,1},{25,9},{2,18},{10... | collective-permute-start | bytes 393224 | tf_op jit(solution)/shard_map/ppermute | solution.py:349
  173.6 35.9 %collective-permute-start.38 = (bf16[1024,2816]{1,0:T(8,128)(2,1)}, bf16[1024,2816]{1,0:T(8,128)(2,1)}, u32[]{:S(2)}, u32[]{:S(2)}) collective-permute-start(bf16[1024,2816]{1,0:T(8,128)(2,1)} %place.6), channel_id=1, source_target_pairs={{0,4},{4,0},{1,5},{5,1},{2,6},{6,2},{3,7},{7,3},{8,12},{12,8},{9,1... | collective-permute-start | bytes 17301512 | tf_op jit(solution)/shard_map/ppermute | solution.py:349
  178.3 31.1 %collective-permute-start.43 = (bf16[256,1024]{1,0:T(8,128)(2,1)S(1)}, bf16[256,1024]{1,0:T(8,128)(2,1)}, u32[]{:S(2)}, u32[]{:S(2)}) collective-permute-start(bf16[256,1024]{1,0:T(8,128)(2,1)S(1)} %get-tuple-element.305), channel_id=1, source_target_pairs={{0,4},{4,0},{1,5},{5,1},{2,6},{6,2},{3,7},{7,3},{8,12},{12,8},{9,1... | collective-permute-start | bytes 1572872 | tf_op jit(solution)/shard_map/ppermute | solution.py:349
  178.3 31.1 %collective-permute-start.41 = (bf16[352,512]{1,0:T(8,128)(2,1)}, bf16[352,512]{1,0:T(8,128)(2,1)}, u32[]{:S(2)}, u32[]{:S(2)}) collective-permute-start(bf16[352,512]{1,0:T(8,128)(2,1)} %get-tuple-element.538), channel_id=1, source_target_pairs={{0,1},{1,0},{2,3},{3,2},{4,5},{5,4},{6,7},{7,6},{8,9},{9,8},{10,11... | collective-permute-start | bytes 1081352 | tf_op jit(solution)/shard_map/ppermute | solution.py:349
  275.0 40.7 %collective-permute-start.55 = (bf16[1,2,128,2816]{3,2,1,0:T(8,128)(2,1)}, bf16[1,2,128,2816]{3,2,1,0:T(8,128)(2,1)}, u32[]{:S(2)}, u32[]{:S(2)}) collective-permute-start(bf16[1,2,128,2816]{3,2,1,0:T(8,128)(2,1)} %dynamic-slice_bitcast_fusion), channel_id=1, source_target_pairs={{0,2},{1,3},{2,0},{3,1},{4,6},{5,7},{6,4},{7,5},{8,10},{9,11},{10,... | collective-permute-start | bytes 4325384 | tf_op jit(solution)/shard_map/ppermute | solution.py:349
  277.4 28.5 %collective-permute-start.53 = (bf16[1,352,512]{2,1,0:T(8,128)(2,1)}, bf16[1,352,512]{2,1,0:T(8,128)(2,1)}, u32[]{:S(2)}, u32[]{:S(2)}) collective-permute-start(bf16[1,352,512]{2,1,0:T(8,128)(2,1)} %dynamic-slice_bitcast_fusion.12), channel_id=1, source_target_pairs={{0,1},{1,0},{2,3},{3,2},{4,5},{5,4},{6,7},{7,6},{8,9},{9,8},{10,11... | collective-permute-start | bytes 1081352 | tf_op jit(solution)/shard_map/ppermute | solution.py:349
  279.0 38.8 %collective-permute-start.54 = (bf16[1,2,128,2816]{3,2,1,0:T(8,128)(2,1)}, bf16[1,2,128,2816]{3,2,1,0:T(8,128)(2,1)}, u32[]{:S(2)}, u32[]{:S(2)}) collective-permute-start(bf16[1,2,128,2816]{3,2,1,0:T(8,128)(2,1)} %dynamic-slice_bitcast_fusion.1), channel_id=1, source_target_pairs={{0,1},{1,0},{2,3},{3,2},{4,5},{5,4},{6,7},{7,6},{8,9},{9,8},{10,11... | collective-permute-start | bytes 4325384 | tf_op jit(solution)/shard_map/ppermute | solution.py:349
  281.7 34.1 %collective-permute-start.52 = (bf16[1,352,512]{2,1,0:T(8,128)(2,1)}, bf16[1,352,512]{2,1,0:T(8,128)(2,1)}, u32[]{:S(2)}, u32[]{:S(2)}) collective-permute-start(bf16[1,352,512]{2,1,0:T(8,128)(2,1)} %dynamic-slice_bitcast_fusion.13), channel_id=1, source_target_pairs={{0,2},{1,3},{2,0},{3,1},{4,6},{5,7},{6,4},{7,5},{8,10},{9,11},{10,... | collective-permute-start | bytes 1081352 | tf_op jit(solution)/shard_map/ppermute | solution.py:349
  339.1 24.4 %collective-permute-start.63 = (bf16[2,2,64,512]{3,2,1,0:T(8,128)(2,1)}, bf16[2,2,64,512]{3,2,1,0:T(8,128)(2,1)}, u32[]{:S(2)}, u32[]{:S(2)}) collective-permute-start(bf16[2,2,64,512]{3,2,1,0:T(8,128)(2,1)} %slice_bitcast_fusion.11), channel_id=1, source_target_pairs={{0,8},{8,0},{16,24},{24,16},{1,9},{9,1},{17,25},{25,17},{2,10},{10... | collective-permute-start | bytes 786440 | tf_op jit(solution)/shard_map/ppermute | solution.py:349
  366.7 29.9 %collective-permute-start.67 = (bf16[2,1,64,512]{3,2,0,1:T(8,128)(2,1)}, bf16[2,1,64,512]{3,2,0,1:T(8,128)(2,1)S(1)}, u32[]{:S(2)}, u32[]{:S(2)}) collective-permute-start(bf16[2,1,64,512]{3,2,0,1:T(8,128)(2,1)} %slice_bitcast_fusion.17), channel_id=1, source_target_pairs={{0,16},{8,24},{16,0},{24,8},{1,17},{9,25},{17,1},{25,9},{2,18},{10... | collective-permute-start | bytes 393224 | tf_op jit(solution)/shard_map/ppermute | solution.py:349
  372.0 28.5 %collective-permute-start.66 = (bf16[1,64,2816]{2,1,0:T(8,128)(2,1)}, bf16[1,64,2816]{2,1,0:T(8,128)(2,1)}, u32[]{:S(2)}, u32[]{:S(2)}) collective-permute-start(bf16[1,64,2816]{2,1,0:T(8,128)(2,1)} %dynamic-slice_bitcast_fusion.11), channel_id=1, source_target_pairs={{0,16},{8,24},{16,0},{24,8},{1,17},{9,25},{17,1},{25,9},{2,18},{10... | collective-permute-start | bytes 1081352 | tf_op jit(solution)/shard_map/ppermute | solution.py:349
  373.2 27.4 %collective-permute-start.68 = (bf16[2,4,256,256]{3,2,1,0:T(8,128)(2,1)}, bf16[2,4,256,256]{3,2,1,0:T(8,128)(2,1)S(1)}, u32[]{:S(2)}, u32[]{:S(2)}) collective-permute-start(bf16[2,4,256,256]{3,2,1,0:T(8,128)(2,1)} %slice_bitcast_fusion.3), channel_id=1, source_target_pairs={{0,4},{4,0},{1,5},{5,1},{2,6},{6,2},{3,7},{7,3},{8,12},{12,8},{9,1... | collective-permute-start | bytes 3145736 | tf_op jit(solution)/shard_map/ppermute | solution.py:349
  375.8 24.8 %collective-permute-start.65 = (bf16[1,1,176,512]{3,2,0,1:T(8,128)(2,1)S(1)}, bf16[1,1,176,512]{3,2,0,1:T(8,128)(2,1)S(1)}, u32[]{:S(2)}, u32[]{:S(2)}) collective-permute-start(bf16[1,1,176,512]{3,2,0,1:T(8,128)(2,1)S(1)} %fusion.191), channel_id=1, source_target_pairs={{0,16},{8,24},{16,0},{24,8},{1,17},{9,25},{17,1},{25,9},{2,18},{10... | collective-permute-start | bytes 540680 | tf_op jit(solution)/shard_map/ppermute | solution.py:349
  409.1 24.2 %collective-permute-start.69 = (bf16[2,2,256,256]{3,2,0,1:T(8,128)(2,1)}, bf16[2,2,256,256]{3,2,0,1:T(8,128)(2,1)}, u32[]{:S(2)}, u32[]{:S(2)}) collective-permute-start(bf16[2,2,256,256]{3,2,0,1:T(8,128)(2,1)} %bitcast.504), channel_id=1, source_target_pairs={{0,8},{8,0},{16,24},{24,16},{1,9},{9,1},{17,25},{25,17},{2,10},{10... | collective-permute-start | bytes 1572872 | tf_op jit(solution)/shard_map/ppermute | solution.py:349
  442.4 51.5 %collective-permute-start.84 = (bf16[2,1,64,2816]{3,2,0,1:T(8,128)(2,1)S(1)}, bf16[2,1,64,2816]{3,2,0,1:T(8,128)(2,1)S(1)}, u32[]{:S(2)}, u32[]{:S(2)}) collective-permute-start(bf16[2,1,64,2816]{3,2,0,1:T(8,128)(2,1)S(1)} %pad_maximum_fusion.9), channel_id=1, source_target_pairs={{0,8},{8,0},{16,24},{24,16},{1,9},{9,1},{17,25},{25,17},{2,10},{10... | collective-permute-start | bytes 2162696 | tf_op jit(solution)/shard_map/ppermute | solution.py:349
  450.1 25.3 %collective-permute-start.80 = (bf16[4,2,128,512]{3,2,1,0:T(8,128)(2,1)S(1)}, bf16[4,2,128,512]{3,2,1,0:T(8,128)(2,1)S(1)}, u32[]{:S(2)}, u32[]{:S(2)}) collective-permute-start(bf16[4,2,128,512]{3,2,1,0:T(8,128)(2,1)S(1)} %dynamic-slice_bitcast_fusion.2), channel_id=1, source_target_pairs={{0,2},{1,3},{2,0},{3,1},{4,6},{5,7},{6,4},{7,5},{8,10},{9,11},{10,... | collective-permute-start | bytes 3145736 | tf_op jit(solution)/shard_map/ppermute | solution.py:349
  454.4 27.3 %collective-permute-start.79 = (bf16[4,2,128,512]{3,2,1,0:T(8,128)(2,1)S(1)}, bf16[4,2,128,512]{3,2,1,0:T(8,128)(2,1)S(1)}, u32[]{:S(2)}, u32[]{:S(2)}) collective-permute-start(bf16[4,2,128,512]{3,2,1,0:T(8,128)(2,1)S(1)} %dynamic-slice_bitcast_fusion.3), channel_id=1, source_target_pairs={{0,1},{1,0},{2,3},{3,2},{4,5},{5,4},{6,7},{7,6},{8,9},{9,8},{10,11... | collective-permute-start | bytes 3145736 | tf_op jit(solution)/shard_map/ppermute | solution.py:349
  (182 other events, 1858.0 us)
